TPU v7x, 256 devices: a whole 4x4x8 slice. The times are simulated.
256 devices in a mesh: ifg: 8 (over x, core), rows: 32 (over y, z).
Axes of the slice: x: 4, y: 4, z: 8, core: 2. Of those that a mesh axis runs over, the one named last changes fastest.
Arguments:
- phase: bfloat16 [512, 256, 1024], P('ifg', 'rows')
- coherence: bfloat16 [512, 256, 1024], P('ifg', 'rows'), may hold values from 0.0996 to 0.95
- height: float32 [256, 1024], P('rows')
- gap_mask: int32 [512, 256], P('ifg', 'rows'), may hold values 0 or 1
- date_pairs: int32 [512, 2], replicated, may hold values from 0 to 299, as said below
Outputs:
- displacement: float32 [300, 256, 1024], P(None, 'rows', 'ifg')
- topo_slope: float32 [512], P('ifg')
Inputs may be any that keep to these rules, and one draw needn't show every extreme that they name: date_pairs[i, 0] < date_pairs[i, 1] for every interferogram.
All inputs are finite; a program needn't handle non-finite values. No bound on the sum of `gap_mask` on one device may be relied on, other than what follows from the above.
Results may differ from a plain program's by a relative error of at most 0.0028.
Values may be sent and summed in bfloat16 or wider, within the bound.
No kernel may reach another device: no remote copies, remote signals or barrier semaphores. Data moves between devices by JAX's collectives and lax.ppermute only.
A program may use at most 128 MiB of HBM per device.

v0:
```python
import jax
import jax.numpy as jnp
from jax import lax
from jax.sharding import PartitionSpec as P

DATES = 300
ITERS = 3


SMOOTHING_WEIGHT = 0.5
RIDGE_WEIGHT = 0.05
precise = lax.Precision.HIGHEST


def extended(block, sides, width):
    for axis, dim in sides:
        count = lax.axis_size(axis)
        forward = [(i, i + 1) for i in range(count - 1)]
        backward = [(target, source) for source, target in forward]
        low = lax.ppermute(
            lax.slice_in_dim(block, block.shape[dim] - width, None, axis=dim), axis, forward
        )
        high = lax.ppermute(lax.slice_in_dim(block, 0, width, axis=dim), axis, backward)
        block = jnp.concatenate([low, block, high], axis=dim)
    return block


def box_sum(padded):
    row_sum = padded[..., :-2, :] + padded[..., 1:-1, :] + padded[..., 2:, :]
    return row_sum[..., :-2] + row_sum[..., 1:-1] + row_sum[..., 2:]


def smooth_parts(padded):
    phase_pad = padded[0].astype(jnp.float32)
    coher_pad = padded[1].astype(jnp.float32)
    top_sum = box_sum(coher_pad * phase_pad)
    low_sum = box_sum(coher_pad)
    return (top_sum / low_sum, low_sum / 9.0)


def moments(smooth, mean_coh, terrain):
    top_sum = jnp.sum(mean_coh * smooth * terrain[None], axis=(1, 2))
    low_sum = jnp.sum(mean_coh * terrain[None] * terrain[None], axis=(1, 2))
    return (top_sum, low_sum)


def correct(smooth, mean_coh, topo_slope, terrain, mask_rows):
    corrected = (smooth - topo_slope[:, None, None] * terrain[None]).astype(jnp.bfloat16)
    weights = (mask_rows.astype(jnp.float32)[:, :, None] * mean_coh).astype(jnp.bfloat16)
    return (corrected, weights)


def residual_norm(current):
    return lax.psum(jnp.sum(current * current), ("ifg", "rows"))


def per_device(phase, coherence, height, gap_mask, date_pairs):
    stacked = jnp.stack([phase, coherence])
    padded = extended(stacked, (("rows", 2),), 1)
    padded = jnp.pad(padded, ((0, 0), (0, 0), (0, 0), (1, 1)))
    smooth, mean_coh = smooth_parts(padded)
    top_sum, low_sum = moments(smooth, mean_coh, height)
    top_sum, low_sum = lax.psum((top_sum, low_sum), "rows")
    topo_slope = top_sum / low_sum
    corrected, weights = correct(smooth, mean_coh, topo_slope, height, gap_mask)
    corrected, weights = (
        lax.all_to_all(corrected, "ifg", split_axis=2, concat_axis=0, tiled=True),
        lax.all_to_all(weights, "ifg", split_axis=2, concat_axis=0, tiled=True),
    )
    ifg_count, row_count, col_count = weights.shape
    pixels = row_count * col_count
    dates_axis = jnp.arange(DATES, dtype=jnp.int32)
    design = (dates_axis[None, :] == date_pairs[:, 1:2]).astype(jnp.float32) - (
        dates_axis[None, :] == date_pairs[:, 0:1]
    ).astype(jnp.float32)
    weight_flat = weights.reshape(ifg_count, pixels)

    def back_project(values):
        return lax.dot_general(
            design,
            values,
            (((0,), (0,)), ((), ())),
            precision=precise,
            preferred_element_type=jnp.float32,
        )

    right_side = back_project(
        weight_flat.astype(jnp.float32) * corrected.reshape(ifg_count, pixels).astype(jnp.float32)
    )
    displacement = jnp.zeros_like(right_side)
    residual = right_side
    direction = right_side
    norm_now = residual_norm(residual)
    for sweep_index in range(ITERS):
        cube_grid = direction.reshape(DATES, row_count, col_count)
        padded_cube = extended(cube_grid, (("ifg", 2), ("rows", 1)), 1)
        neighbours = (
            padded_cube[:, 2:, 1:-1]
            + padded_cube[:, :-2, 1:-1]
            + padded_cube[:, 1:-1, 2:]
            + padded_cube[:, 1:-1, :-2]
        )
        spread = (4.0 * cube_grid - neighbours).reshape(DATES, pixels)
        differences = jnp.dot(
            design, direction, precision=precise, preferred_element_type=jnp.float32
        )
        mapped = back_project(differences * weight_flat)
        mapped = mapped + SMOOTHING_WEIGHT * spread + RIDGE_WEIGHT * direction
        step_size = norm_now / lax.psum(jnp.sum(direction * mapped), ("ifg", "rows"))
        displacement = displacement + step_size * direction
        residual = residual - step_size * mapped
        norm_next = residual_norm(residual)
        direction = residual + norm_next / norm_now * direction
        norm_now = norm_next
    return (displacement.reshape(DATES, row_count, col_count), topo_slope)


def solution(mesh):
    placed = (
        P("ifg", "rows", None),
        P("ifg", "rows", None),
        P("rows", None),
        P("ifg", "rows"),
        P(),
    )
    return jax.shard_map(
        per_device,
        mesh=mesh,
        in_specs=placed,
        out_specs=(P(None, "rows", "ifg"), P("ifg")),
        check_vma=False,
    )
```

profile of v0, /device:TPU:6, one launch (start us, length us, event | category | flops | bytes accessed | tf_op | source)
XLA Modules:
  0.0 686.0 jit_solution(10291353964235521718)
XLA Ops:
  0.6 3.4 fusion.36
  7.0 5.3 collective-permute-start
  12.9 5.1 copy.95
  22.5 11.1 %fusion.5 = bf16[2,64,10,1026]{1,2,3,0:T(8,128)(2,1)S(1)} fusion(bf16[2,64,1,1024]{1,2,3,0:T(2,128)(2,1)S(1)} %copy.96, bf16[2,64,8,1024]{1,2,3,0:T(8,128)(2,1)} %copy.95, bf16[2,64,1,1024]{1,2,3,0:T(2,128)(2,1)S(1)} %copy.94), kind=kLoop, calls=%fused_computation.7 | loop fusion | flops 15759360 | bytes 5248000 | tf_op jit(solution)/shard_map/concatenate | solution.py:24
  36.2 2.4 slice_add_fusion
  38.6 2.6 multiply_convert_fusion
  41.2 2.6 reshape.56
  43.8 6.4 all-to-all-start
  50.2 10.1 %multiply_reduce_fusion = (f32[64]{0:T(128)S(1)}, f32[64]{0:T(128)S(1)}, f32[64,8,1024]{0,1,2:T(8,128)}) fusion(f32[64,8,1024]{0,1,2:T(8,128)} %get-tuple-element.13, f32[8,1024]{0,1:T(8,128)S(1)} %copy.99, f32[8,1024]{0,1:T(8,128)S(1)} %copy.98, f32[64,8,1026]{0,1,2:T(8,128)} %slice_add_fusion), kind=kLoop, calls=%fused_computation.22 | loop fusion | flops 5242752 | bytes 10551808 | tf_op jit(solution)/shard_map/reduce_sum | solution.py:43
  60.3 77.6 %all-reduce.2 = (f32[64]{0:T(128)S(1)}, f32[64]{0:T(128)S(1)}) all-reduce(f32[64]{0:T(128)S(1)} %get-tuple-element.3, f32[64]{0:T(128)S(1)} %get-tuple-element.2), channel_id=1, replica_groups=mesh['ifg'=8,'rows'=32] {'rows'}, use_global_device_ids=true, to_apply=%region_1.2 | all-reduce | flops 128 | bytes 1024 | tf_op jit(solution)/shard_map/psum | solution.py:63
  137.8 2.9 fusion.57
  140.7 2.7 reshape.54
  143.4 5.4 all-to-all-start.1
  148.8 4.3 reshape.57
  153.1 2.6 copy.97
  155.8 6.9 %all-to-all-done.1 = bf16[8,2,32768]{2,1,0:T(2,128)(2,1)S(1)} async-done(((bf16[8,2,32768]{2,1,0:T(2,128)(2,1)}), bf16[8,2,32768]{2,1,0:T(2,128)(2,1)S(1)}, u32[]{:S(2)}, u32[]{:S(2)}) %all-to-all-start.1) | async-done | bytes 1048608 | tf_op jit(solution)/shard_map/all_to_all | solution.py:67
  162.7 2.7 reshape.55
  165.3 3.5 copy.100
  168.8 4.5 fusion.8
  180.9 3.6 collective-permute-start.3
  184.5 2.4 slice.204
  186.9 2.9 copy.101
  192.3 4.9 collective-permute-start.5
  197.2 4.9 fusion.35
  203.8 2.9 copy.134
  206.7 6.4 multiply_reduce_fusion.6
  213.1 71.8 %all-reduce.1 = (f32[]{:T(128)}, f32[]{:T(128)}) all-reduce(f32[]{:T(128)} %get-tuple-element.5, f32[]{:T(128)} %get-tuple-element.4), channel_id=1, replica_groups=mesh['ifg'=8,'rows'=32] {'ifg','rows'}, use_global_device_ids=true, to_apply=%region_5.6 | all-reduce | flops 2 | bytes 16 | tf_op jit(solution)/shard_map/psum | solution.py:54
  286.2 3.7 multiply_reduce_fusion.5
  289.9 74.2 %psum.60 = f32[]{:T(128)} all-reduce(f32[]{:T(128)} %get-tuple-element.10), channel_id=1, replica_groups=mesh['ifg'=8,'rows'=32] {'ifg','rows'}, use_global_device_ids=true, to_apply=%region_9.10 | all-reduce | flops 1 | bytes 8 | tf_op jit(solution)/shard_map/psum | solution.py:54
  374.5 3.6 collective-permute-start.7
  378.1 2.4 slice.205
  380.5 2.9 copy.112
  385.9 4.9 collective-permute-start.9
  390.8 4.9 fusion.34
  397.5 2.9 copy.135
  400.4 6.9 %multiply_reduce_fusion.4 = (f32[]{:T(128)}, f32[300,1024]{1,0:T(8,128)}) fusion(f32[300,1024]{1,0:T(8,128)S(1)} %multiply_add_fusion.3, f32[300,1024]{1,0:T(8,128)} %copy.135, f32[512,1024]{1,0:T(8,128)} %fusion.34, f32[64,8,8,128]{3,2,1,0:T(8,128)} %bitcast.71, s32[512]{0:T(512)S(1)} %bitcast.104, s32[512]{0:T(512)S(1)} %bitcast.97), kind=kOutput, calls=%fused_computation.88 | convolution fusion | flops 1890265088 | bytes 7884804 | tf_op jit(solution)/shard_map/dot_general | solution.py:79
  407.3 74.9 %psum.61 = f32[]{:T(128)} all-reduce(f32[]{:T(128)} %get-tuple-element.32), channel_id=1, replica_groups=mesh['ifg'=8,'rows'=32] {'ifg','rows'}, use_global_device_ids=true, to_apply=%region_11.12 | all-reduce | flops 1 | bytes 8 | tf_op jit(solution)/shard_map/psum | solution.py:109
  483.4 3.1 multiply_reduce_fusion.3
  486.5 74.2 %psum.62 = f32[]{:T(128)} all-reduce(f32[]{:T(128)} %multiply_reduce_fusion.3), channel_id=1, replica_groups=mesh['ifg'=8,'rows'=32] {'ifg','rows'}, use_global_device_ids=true, to_apply=%region_13.14 | all-reduce | flops 1 | bytes 8 | tf_op jit(solution)/shard_map/psum | solution.py:54
  562.0 2.6 multiply_add_fusion.1
  572.4 3.9 collective-permute-start.11
  576.4 6.2 fusion.33
  583.6 2.9 copy.123
  589.0 4.7 collective-permute-start.13
  593.7 5.9 fusion.13
  601.3 2.9 copy.136
  604.2 3.0 multiply_reduce_fusion.2
  607.3 73.9 %psum.63 = f32[]{:T(128)} all-reduce(f32[]{:T(128)} %multiply_reduce_fusion.2), channel_id=1, replica_groups=mesh['ifg'=8,'rows'=32] {'ifg','rows'}, use_global_device_ids=true, to_apply=%region_15.16 | all-reduce | flops 1 | bytes 8 | tf_op jit(solution)/shard_map/psum | solution.py:109
  (95 shorter events, 51.6 us)
Async XLA Ops:
  0.6 11.6 %copy-start.10 = (bf16[64,8,1024]{2,1,0:T(8,128)(2,1)S(1)}, bf16[64,8,1024]{2,1,0:T(8,128)(2,1)}, u32[]{:S(2)}) copy-start(bf16[64,8,1024]{2,1,0:T(8,128)(2,1)} %param.6) | copy-start | bytes 3145732
  4.1 8.2 %copy-start.11 = (f32[8,1024]{1,0:T(8,128)S(1)}, f32[8,1024]{1,0:T(8,128)}, u32[]{:S(2)}) copy-start(f32[8,1024]{1,0:T(8,128)} %param.7) | copy-start | bytes 98308
  4.1 8.2 %copy-start.9 = (bf16[64,8,1024]{2,1,0:T(8,128)(2,1)S(1)}, bf16[64,8,1024]{2,1,0:T(8,128)(2,1)}, u32[]{:S(2)}) copy-start(bf16[64,8,1024]{2,1,0:T(8,128)(2,1)} %param.5) | copy-start | bytes 3145732
  4.9 15.4 %collective-permute-start.1 = (bf16[2,64,1,1024]{3,1,2,0:T(8,128)(2,1)}, bf16[2,64,1,1024]{3,1,2,0:T(8,128)(2,1)}, u32[]{:S(2)}, u32[]{:S(2)}) collective-permute-start(bf16[2,64,1,1024]{3,1,2,0:T(8,128)(2,1)} %copy.138), channel_id=1, source_target_pairs={{1,0},{2,1},{3,2},{4,3},{5,4},{6,5},{7,6},{8,7},{9,8},{10,9},{11,1... | collective-permute-start | bytes 786440 | tf_op jit(solution)/shard_map/ppermute | solution.py:23
  7.0 11.1 %collective-permute-start = (bf16[2,64,1,1024]{3,1,2,0:T(8,128)(2,1)}, bf16[2,64,1,1024]{3,1,2,0:T(8,128)(2,1)}, u32[]{:S(2)}, u32[]{:S(2)}) collective-permute-start(bf16[2,64,1,1024]{3,1,2,0:T(8,128)(2,1)} %copy.137), channel_id=1, source_target_pairs={{0,1},{1,2},{2,3},{3,4},{4,5},{5,6},{6,7},{7,8},{8,9},{9,10},{10,1... | collective-permute-start | bytes 786440 | tf_op jit(solution)/shard_map/ppermute | solution.py:20
  12.9 5.2 copy-start.12
  43.8 99.5 %all-to-all-start = ((bf16[8,2,32768]{2,1,0:T(2,128)(2,1)}), bf16[8,2,32768]{2,1,0:T(2,128)(2,1)}, u32[]{:S(2)}, u32[]{:S(2)}) async-start(bf16[8,2,32768]{2,1,0:T(2,128)(2,1)} %reshape.56), calls=%async_computation | async-start | bytes 2097152 | tf_op jit(solution)/shard_map/all_to_all | solution.py:68
  137.8 2.9 copy-start.14
  143.4 5.4 copy-start.13
  143.4 19.3 %all-to-all-start.1 = ((bf16[8,2,32768]{2,1,0:T(2,128)(2,1)}), bf16[8,2,32768]{2,1,0:T(2,128)(2,1)S(1)}, u32[]{:S(2)}, u32[]{:S(2)}) async-start(bf16[8,2,32768]{2,1,0:T(2,128)(2,1)} %reshape.54), calls=%async_computation.1 | async-start | bytes 2097152 | tf_op jit(solution)/shard_map/all_to_all | solution.py:67
  155.8 51.0 %copy-start = (f32[64,8,8,128]{3,1,0,2:T(8,128)}, f32[64,8,8,128]{3,1,0,2:T(8,128)S(1)}, u32[]{:S(2)}) copy-start(f32[64,8,8,128]{3,1,0,2:T(8,128)S(1)} %copy.97) | copy-start | bytes 6291460
  173.6 1.9 copy-start.4
  177.2 12.7 %collective-permute-start.2 = (f32[300,8,1]{0,1,2:T(8,128)S(1)}, f32[300,8,1]{0,1,2:T(8,128)S(1)}, u32[]{:S(2)}, u32[]{:S(2)}) collective-permute-start(f32[300,8,1]{0,1,2:T(8,128)S(1)} %copy.139), channel_id=1, source_target_pairs={{0,32},{32,64},{64,96},{96,128},{128,160},{160,192},{192,224},{1,3... | collective-permute-start | bytes 28808 | tf_op jit(solution)/shard_map/ppermute | solution.py:20
  180.9 9.0 %collective-permute-start.3 = (f32[300,8,1]{0,1,2:T(8,128)S(1)}, f32[300,8,1]{0,1,2:T(8,128)S(1)}, u32[]{:S(2)}, u32[]{:S(2)}) collective-permute-start(f32[300,8,1]{0,1,2:T(8,128)S(1)} %copy.140), channel_id=1, source_target_pairs={{32,0},{64,32},{96,64},{128,96},{160,128},{192,160},{224,192},{33,... | collective-permute-start | bytes 28808 | tf_op jit(solution)/shard_map/ppermute | solution.py:23
  191.0 11.1 %collective-permute-start.4 = (f32[300,1,130]{0,2,1:T(8,128)S(1)}, f32[300,1,130]{0,2,1:T(8,128)S(1)}, u32[]{:S(2)}, u32[]{:S(2)}) collective-permute-start(f32[300,1,130]{0,2,1:T(8,128)S(1)} %get-tuple-element.21), channel_id=1, source_target_pairs={{1,0},{2,1},{3,2},{4,3},{5,4},{6,5},{7,6},{8,7},{9,8},{10,9},{11,1... | collective-permute-start | bytes 468008 | tf_op jit(solution)/shard_map/ppermute | solution.py:23
  192.3 9.8 %copy-start.7 = (f32[300,8,128]{0,2,1:T(8,128)S(1)}, f32[300,8,128]{0,2,1:T(8,128)}, u32[]{:S(2)}) copy-start(f32[300,8,128]{0,2,1:T(8,128)} %copy.101) | copy-start | bytes 3686404
  192.3 9.8 %collective-permute-start.5 = (f32[300,1,130]{0,2,1:T(8,128)S(1)}, f32[300,1,130]{0,2,1:T(8,128)S(1)}, u32[]{:S(2)}, u32[]{:S(2)}) collective-permute-start(f32[300,1,130]{0,2,1:T(8,128)S(1)} %get-tuple-element.22), channel_id=1, source_target_pairs={{0,1},{1,2},{2,3},{3,4},{4,5},{5,6},{6,7},{7,8},{8,9},{9,10},{10,1... | collective-permute-start | bytes 468008 | tf_op jit(solution)/shard_map/ppermute | solution.py:20
  367.2 1.9 copy-start.5
  370.8 12.7 %collective-permute-start.6 = (f32[300,8,1]{0,1,2:T(8,128)S(1)}, f32[300,8,1]{0,1,2:T(8,128)S(1)}, u32[]{:S(2)}, u32[]{:S(2)}) collective-permute-start(f32[300,8,1]{0,1,2:T(8,128)S(1)} %copy.141), channel_id=1, source_target_pairs={{0,32},{32,64},{64,96},{96,128},{128,160},{160,192},{192,224},{1,3... | collective-permute-start | bytes 28808 | tf_op jit(solution)/shard_map/ppermute | solution.py:20
  374.5 9.0 %collective-permute-start.7 = (f32[300,8,1]{0,1,2:T(8,128)S(1)}, f32[300,8,1]{0,1,2:T(8,128)S(1)}, u32[]{:S(2)}, u32[]{:S(2)}) collective-permute-start(f32[300,8,1]{0,1,2:T(8,128)S(1)} %copy.142), channel_id=1, source_target_pairs={{32,0},{64,32},{96,64},{128,96},{160,128},{192,160},{224,192},{33,... | collective-permute-start | bytes 28808 | tf_op jit(solution)/shard_map/ppermute | solution.py:23
  384.6 11.1 %collective-permute-start.8 = (f32[300,1,130]{0,2,1:T(8,128)S(1)}, f32[300,1,130]{0,2,1:T(8,128)S(1)}, u32[]{:S(2)}, u32[]{:S(2)}) collective-permute-start(f32[300,1,130]{0,2,1:T(8,128)S(1)} %get-tuple-element.19), channel_id=1, source_target_pairs={{1,0},{2,1},{3,2},{4,3},{5,4},{6,5},{7,6},{8,7},{9,8},{10,9},{11,1... | collective-permute-start | bytes 468008 | tf_op jit(solution)/shard_map/ppermute | solution.py:23
  385.9 9.8 %copy-start.8 = (f32[300,8,128]{0,2,1:T(8,128)S(1)}, f32[300,8,128]{0,2,1:T(8,128)}, u32[]{:S(2)}) copy-start(f32[300,8,128]{0,2,1:T(8,128)} %copy.112) | copy-start | bytes 3686404
  385.9 9.8 %collective-permute-start.9 = (f32[300,1,130]{0,2,1:T(8,128)S(1)}, f32[300,1,130]{0,2,1:T(8,128)S(1)}, u32[]{:S(2)}, u32[]{:S(2)}) collective-permute-start(f32[300,1,130]{0,2,1:T(8,128)S(1)} %get-tuple-element.20), channel_id=1, source_target_pairs={{0,1},{1,2},{2,3},{3,4},{4,5},{5,6},{6,7},{7,8},{8,9},{9,10},{10,1... | collective-permute-start | bytes 468008 | tf_op jit(solution)/shard_map/ppermute | solution.py:20
  564.6 2.3 copy-start.1
  564.8 2.0 copy-start.2
  570.4 12.1 %copy-start.3 = (f32[38,8,8,128]{3,2,1,0:T(8,128)S(1)}, f32[38,8,8,128]{3,2,1,0:T(8,128)}, u32[]{:S(2)}) copy-start(f32[38,8,8,128]{3,2,1,0:T(8,128)} %copy-done.2) | copy-start | bytes 3735556
  570.4 16.2 %collective-permute-start.10 = (f32[300,8,1]{0,1,2:T(8,128)S(1)}, f32[300,8,1]{0,1,2:T(8,128)S(1)}, u32[]{:S(2)}, u32[]{:S(2)}) collective-permute-start(f32[300,8,1]{0,1,2:T(8,128)S(1)} %copy.143), channel_id=1, source_target_pairs={{0,32},{32,64},{64,96},{96,128},{128,160},{160,192},{192,224},{1,3... | collective-permute-start | bytes 28808 | tf_op jit(solution)/shard_map/ppermute | solution.py:20
  572.4 14.1 %collective-permute-start.11 = (f32[300,8,1]{0,1,2:T(8,128)S(1)}, f32[300,8,1]{0,1,2:T(8,128)S(1)}, u32[]{:S(2)}, u32[]{:S(2)}) collective-permute-start(f32[300,8,1]{0,1,2:T(8,128)S(1)} %copy.144), channel_id=1, source_target_pairs={{32,0},{64,32},{96,64},{128,96},{160,128},{192,160},{224,192},{33,... | collective-permute-start | bytes 28808 | tf_op jit(solution)/shard_map/ppermute | solution.py:23
  587.7 11.9 %collective-permute-start.12 = (f32[300,1,130]{0,2,1:T(8,128)S(1)}, f32[300,1,130]{0,2,1:T(8,128)S(1)}, u32[]{:S(2)}, u32[]{:S(2)}) collective-permute-start(f32[300,1,130]{0,2,1:T(8,128)S(1)} %get-tuple-element.17), channel_id=1, source_target_pairs={{1,0},{2,1},{3,2},{4,3},{5,4},{6,5},{7,6},{8,7},{9,8},{10,9},{11,1... | collective-permute-start | bytes 468008 | tf_op jit(solution)/shard_map/ppermute | solution.py:23
  589.0 10.6 %copy-start.6 = (f32[300,8,128]{0,2,1:T(8,128)S(1)}, f32[300,8,128]{0,2,1:T(8,128)}, u32[]{:S(2)}) copy-start(f32[300,8,128]{0,2,1:T(8,128)} %copy.123) | copy-start | bytes 3686404
  589.0 10.6 %collective-permute-start.13 = (f32[300,1,130]{0,2,1:T(8,128)S(1)}, f32[300,1,130]{0,2,1:T(8,128)S(1)}, u32[]{:S(2)}, u32[]{:S(2)}) collective-permute-start(f32[300,1,130]{0,2,1:T(8,128)S(1)} %get-tuple-element.18), channel_id=1, source_target_pairs={{0,1},{1,2},{2,3},{3,4},{4,5},{5,6},{6,7},{7,8},{8,9},{9,10},{10,1... | collective-permute-start | bytes 468008 | tf_op jit(solution)/shard_map/ppermute | solution.py:20
where the time goes:
time: 698 us; the launch traced here: 686 us
  blocking collectives  447 us (64%)
  local copies, waits for them, and re-layouts  71.9 us (10%)
  other arithmetic  59.4 us (9%)
  starting transfers between devices  53.7 us (8%)
  matrix products  39.5 us (6%)
  between operations  7.94 us (1%)
    psum x3, blocking collectives, residual_norm(): return lax.psum(jnp.sum(current * current), ('ifg', 'rows'))  220 us
    psum x2, blocking collectives, per_device(): lax.psum(jnp.sum(direction * mapped), ('ifg', 'rows'))  149 us
    psum x1, blocking collectives, per_device(): top_sum, low_sum = lax.psum((top_sum, low_sum), 'rows')  77.6 us
    unnamed x47, local copies, waits for them, and re-layouts  25.7 us
    ppermute x7, starting transfers between devices, extended(): lax.ppermute(lax.slice_in_dim(block, block.shape[dim] - width, None, axis...  25.6 us
    dot_general x4, matrix products, back_project(): lax.dot_general(design, values, (((0,), (0,)), ((), ())), precision=preci...  23.6 us
    ppermute x7, starting transfers between devices, extended(): lax.ppermute(lax.slice_in_dim(block, 0, width, axis=dim), axis, backward)  16.3 us
    dot_general x3, matrix products, per_device(): jnp.dot(design, direction, precision=precise, preferred_element_type=jnp....  15.9 us
  transfers between devices with their start and end apart: 16, of which 1 were waited for; matrix products, arithmetic and copies ran while one was open for 10% of the time, Pallas kernels for 0%

commit v1 on v0

v1 whole, which is shorter than its diff:
```python
import jax
import jax.numpy as jnp
from jax import lax
from jax.experimental import pallas as pl
from jax.experimental.pallas import tpu as pltpu
from jax.sharding import PartitionSpec as P

DATES = 300
DP = 304
SHIFT = 4.0
SMOOTHING_WEIGHT = 0.5
RIDGE_WEIGHT = 0.05
CENTRE = 4.0 * SMOOTHING_WEIGHT + RIDGE_WEIGHT - SHIFT
F32 = jnp.float32
BF16 = jnp.bfloat16
PARAMS = pltpu.CompilerParams(vmem_limit_bytes=48 * 1024 * 1024)


def sds(shape, dtype):
    return jax.ShapeDtypeStruct(shape, dtype)


def call(body, outs, *args, scratch=(), name=None):
    return pl.pallas_call(
        body,
        out_shape=outs,
        scratch_shapes=list(scratch),
        compiler_params=PARAMS,
        name=name,
    )(*args)


def dot(a, b):
    return jnp.dot(a, b, preferred_element_type=F32)


def split(values):
    high = values.astype(BF16)
    return high, (values - high.astype(F32)).astype(BF16)


def rows_first(phase, coher, phase_t, coher_t, first, last, wide):
    for part, (source, target) in enumerate(((phase, phase_t), (coher, coher_t))):
        for block in range(4):
            for tile in range(8):
                lanes = pl.ds(tile * 128, 128)
                wide[...] = source[pl.ds(block * 16, 16), :, lanes].astype(F32).reshape(128, 128)
                for row in range(8):
                    piece = wide[pl.ds(row, 16, stride=8), :].astype(BF16)
                    target[row, pl.ds(block * 16, 16), lanes] = piece
        first[pl.ds(part * 64, 64), :] = target[0]
        last[pl.ds(part * 64, 64), :] = target[7]


def shifted_sum(values, lane, last):
    left = jnp.where(lane == 0, 0.0, pltpu.roll(values, 1, 1))
    right = jnp.where(lane == last, 0.0, pltpu.roll(values, last, 1))
    return values + left + right


def regression_sums(phase_t, coher_t, height, above, below, out, box_one, box_two):
    lane = lax.broadcasted_iota(jnp.int32, (8, 1024), 1)
    sub = lax.broadcasted_iota(jnp.int32, (8, 1024), 0)
    here = height[...]
    up = jnp.where(sub == 0, above[...], pltpu.roll(here, 1, 0))
    down = jnp.where(sub == 7, below[...], pltpu.roll(here, 7, 0))
    box_one[...] = shifted_sum(here + up + down, lane, 1023)
    box_two[...] = shifted_sum(here * here + up * up + down * down, lane, 1023)
    tops, lows = [], []
    for block in range(4):
        top = jnp.zeros((16, 128), F32)
        low = jnp.zeros((16, 128), F32)
        for row in range(8):
            for tile in range(8):
                lanes = pl.ds(tile * 128, 128)
                coher = coher_t[row, pl.ds(block * 16, 16), lanes].astype(F32)
                phase = phase_t[row, pl.ds(block * 16, 16), lanes].astype(F32)
                top += coher * phase * box_one[pl.ds(row, 1), lanes]
                low += coher * box_two[pl.ds(row, 1), lanes]
        tops.append(top)
        lows.append(low)
    sums = jnp.sum(jnp.concatenate(tops + lows, axis=0).T, axis=0, keepdims=True)
    out[...] = jnp.broadcast_to(sums, out.shape)


def smoothing(phase_t, coher_t, above, below, mask, smooth, weights):
    lane = lax.broadcasted_iota(jnp.int32, (16, 1024), 1)

    def group(block, _):
        ifgs = pl.ds(pl.multiple_of(block * 16, 16), 16)
        cohers = pl.ds(pl.multiple_of(block * 16 + 64, 16), 16)
        masks = mask[ifgs, :]

        def load(row):
            if row < 0 or row > 7:
                edge = above if row < 0 else below
                coher = edge[cohers, :].astype(F32)
                return coher, coher * edge[ifgs, :].astype(F32)
            coher = coher_t[row, ifgs, :].astype(F32)
            return coher, coher * phase_t[row, ifgs, :].astype(F32)

        before, current = load(-1), load(0)
        for row in range(8):
            after = load(row + 1)
            denom = shifted_sum(before[0] + current[0] + after[0], lane, 1023)
            numer = shifted_sum(before[1] + current[1] + after[1], lane, 1023)
            smooth[row, ifgs, :] = numer / denom
            weight = (masks[:, row : row + 1] * (denom / 9.0)).astype(BF16)
            for tile in range(8):
                weights[tile, ifgs, pl.ds(row * 128, 128)] = weight[:, tile * 128 : tile * 128 + 128]
            before, current = current, after
        return 0

    lax.fori_loop(0, 4, group, 0)


def pick_blocks(source, owner, outs):
    for step, out in enumerate(outs):
        out[...] = source[(owner[0] + step) % 8]


def weight_blocks(owner, weights, *outs):
    pick_blocks(weights, owner, outs)


def correction(owner, sums, smooth, height, slope_row, *rest):
    outs, blocks = rest[:8], rest[8]
    total = sums[0] + sums[1] + sums[2] + sums[3]
    slope_row[...] = total / pltpu.roll(total, 64, 1)
    column = jnp.broadcast_to(total[0:1, :], (128, 128)).T
    slope = column[:64, :] / column[64:, :]
    for row in range(8):
        for tile in range(8):
            lanes = pl.ds(tile * 128, 128)
            value = smooth[row, :, lanes] - slope * height[pl.ds(row, 1), lanes]
            blocks[tile, :, pl.ds(row * 128, 128)] = value.astype(BF16)
    pick_blocks(blocks, owner, outs)


def column_selector():
    row = lax.broadcasted_iota(jnp.int32, (16, 1024), 0)
    pixel = lax.broadcasted_iota(jnp.int32, (16, 1024), 1)
    wanted = jnp.where(row < 8, row * 128, (row - 8) * 128 + 127)
    return (pixel == wanted).astype(BF16)


def write_edges(field, first, last, columns):
    first[...] = field[:, pl.ds(0, 128)].astype(BF16)
    last[...] = field[:, pl.ds(896, 128)].astype(BF16)
    picked = lax.dot_general(
        column_selector(), field[...].astype(BF16), (((1,), (1,)), ((), ())), preferred_element_type=F32
    )
    columns[...] = picked.astype(BF16)


def right_side(*refs):
    weight_parts, corrected_parts = refs[:8], refs[8:16]
    design_t, field, weights, first, last, columns = refs[16:]
    for part in range(8):
        weights[pl.ds(part * 64, 64), :] = weight_parts[part][...]
    for chunk in range(4):
        lanes = pl.ds(chunk * 256, 256)
        total = jnp.zeros((DP, 256), F32)
        scaled = jnp.concatenate(
            [
                weight_parts[part][:, lanes].astype(F32) * corrected_parts[part][:, lanes].astype(F32)
                for part in range(8)
            ],
            axis=0,
        )
        high, low = split(scaled)
        field[:, lanes] = dot(design_t[...], high) + dot(design_t[...], low)
    write_edges(field, first, last, columns)


def local_image(field, weights, design, design_t, chunk):
    lanes = pl.ds(chunk * 256, 256)
    high, low = split(field[:, lanes])
    scaled = (dot(design[...], high) + dot(design[...], low)) * weights[:, lanes].astype(F32)
    high, low = split(scaled)
    back = dot(design_t[...], high) + dot(design_t[...], low)
    lane = lax.broadcasted_iota(jnp.int32, (DP, 128), 1)
    parts = []
    for row in (2 * chunk, 2 * chunk + 1):
        here = field[:, pl.ds(row * 128, 128)]
        around = jnp.where(lane == 0, 0.0, pltpu.roll(here, 1, 1))
        around += jnp.where(lane == 127, 0.0, pltpu.roll(here, 127, 1))
        if row > 0:
            around += field[:, pl.ds((row - 1) * 128, 128)]
        if row < 7:
            around += field[:, pl.ds((row + 1) * 128, 128)]
        start = (row - 2 * chunk) * 128
        parts.append(back[:, start : start + 128] + CENTRE * here - SMOOTHING_WEIGHT * around)
    return parts


def fold(values):
    return jnp.sum(values.reshape(DP // 8, 8, 128), axis=0)


def apply_local(with_before, with_image, *refs):
    field, weights, design, design_t = refs[:4]
    refs = refs[4:]
    before = None
    if with_before:
        before, refs = refs[0], refs[1:]
    image = None
    if with_image:
        image, refs = refs[0], refs[1:]
    moments = refs[0]
    square = jnp.zeros((8, 128), F32)
    cross = jnp.zeros((8, 128), F32)
    ahead = jnp.zeros((8, 128), F32)
    for chunk in range(4):
        parts = local_image(field, weights, design, design_t, chunk)
        for offset, part in enumerate(parts):
            lanes = pl.ds((2 * chunk + offset) * 128, 128)
            here = field[:, lanes]
            square += fold(here * here)
            if with_before:
                cross += fold(here * before[:, lanes])
            if with_image:
                image[:, lanes] = part
            else:
                ahead += fold(here * part)
    moments[0] = square
    moments[1] = cross
    moments[2] = ahead


def spread_columns(columns, pixels):
    row = lax.broadcasted_iota(jnp.int32, (16, 128), 0)
    lane = lax.broadcasted_iota(jnp.int32, (16, 128), 1)
    wanted = jnp.where(row < 8, row, row - 8) == pixels
    place = (wanted & (lane == jnp.where(row < 8, 0, 127))).astype(BF16)
    return lax.dot_general(columns, place, (((0,), (0,)), ((), ())), preferred_element_type=F32)


def halo_part(row, above, below, columns):
    halo = spread_columns(columns, row)
    if row == 0:
        halo += above[...].astype(F32)
    if row == 7:
        halo += below[...].astype(F32)
    return halo


def join_columns(left, right):
    return jnp.concatenate([left[8:16, :], right[0:8, :]], axis=0)


def add_halo(image, above, below, left, right, field, first, last, columns):
    sides = join_columns(left, right)
    for row in range(8):
        lanes = pl.ds(row * 128, 128)
        field[:, lanes] = image[:, lanes] - SMOOTHING_WEIGHT * halo_part(row, above, below, sides)
    write_edges(field, first, last, columns)


def all_moments(field, above, below, left, right, zero, one, two, out):
    sides = join_columns(left, right)
    ahead = two[2]
    for row in range(8):
        lanes = pl.ds(row * 128, 128)
        ahead -= SMOOTHING_WEIGHT * fold(field[:, lanes] * halo_part(row, above, below, sides))
    rows = [zero[0], one[1], one[0], two[1], two[0], ahead]
    sums = [jnp.sum(values, axis=0, keepdims=True) for values in rows]
    out[...] = jnp.concatenate(sums + [jnp.zeros((2, 128), F32)], axis=0)


def combine(parts, zero, one, two, out):
    total = parts[0]
    for index in range(1, parts.shape[0]):
        total += parts[index]
    sums = jnp.sum(total, axis=1, keepdims=True)
    m0, m1, m2, m3, m4, m5 = (jnp.broadcast_to(sums[i : i + 1, :], (1, 128)) for i in range(6))
    t00, t01, t11 = m1 + SHIFT * m0, m2 + SHIFT * m1, m3 + SHIFT * m2
    t12, t22 = m4 + SHIFT * m3, m5 + SHIFT * m4
    l10, l20 = t01 / t00, t11 / t00
    pivot = t11 - l10 * t01
    off = t12 - l20 * t01
    keep = pivot > 1e-6 * t11
    safe = jnp.where(keep, pivot, 1.0)
    l21 = jnp.where(keep, off / safe, 0.0)
    last = t22 - l20 * t11 - l21 * off
    keep_last = keep & (last > 1e-6 * t22)
    y1 = m1 - l10 * m0
    y2 = m2 - l20 * m0 - l21 * y1
    c2 = jnp.where(keep_last, y2 / jnp.where(keep_last, last, 1.0), 0.0)
    c1 = jnp.where(keep, y1 / safe, 0.0) - l21 * c2
    c0 = m0 / t00 - l10 * c1 - l20 * c2
    for row in range(8):
        lanes = pl.ds(row * 128, 128)
        value = c0 * zero[:, lanes] + c1 * one[:, lanes] + c2 * two[:, lanes]
        out[pl.ds(row, DATES, stride=8), :] = value[:DATES, :]


def swap_sum(values, axis, groups, count):
    spread = jnp.broadcast_to(values[None], (count,) + values.shape)
    return lax.all_to_all(spread, axis, 0, 0, tiled=True, axis_index_groups=groups)


def per_device(phase, coherence, height, gap_mask, date_pairs):
    n_ifg, n_rows = lax.axis_size("ifg"), lax.axis_size("rows")
    me = lax.axis_index("ifg")
    owner = me.reshape(1).astype(jnp.int32)

    def forward(values, axis):
        return lax.ppermute(values, axis, [(i, i + 1) for i in range(lax.axis_size(axis) - 1)])

    def backward(values, axis):
        return lax.ppermute(values, axis, [(i + 1, i) for i in range(lax.axis_size(axis) - 1)])

    fast_groups = [[outer * 8 + inner for inner in range(8)] for outer in range(4)]
    slow_groups = [[outer * 8 + inner for outer in range(4)] for inner in range(8)]

    height_above = forward(height[7:8], "rows")
    height_below = backward(height[0:1], "rows")
    stacked = sds((8, 64, 1024), BF16)
    edge = sds((128, 1024), BF16)
    phase_t, coher_t, first, last = call(
        rows_first,
        (stacked, stacked, edge, edge),
        phase,
        coherence,
        scratch=(pltpu.VMEM((128, 128), F32),),
        name="rows_first",
    )
    above, below = forward(last, "rows"), backward(first, "rows")
    sums = call(
        regression_sums,
        sds((8, 128), F32),
        phase_t,
        coher_t,
        height,
        height_above,
        height_below,
        scratch=(pltpu.VMEM((8, 1024), F32), pltpu.VMEM((8, 1024), F32)),
        name="regression_sums",
    )
    sums = jnp.sum(swap_sum(sums, "rows", fast_groups, 8), axis=0)
    sums = swap_sum(sums[None], "rows", slow_groups, 4).reshape(4, 8, 128)

    smooth, weights = call(
        smoothing,
        (sds((8, 64, 1024), F32), stacked),
        phase_t,
        coher_t,
        above,
        below,
        gap_mask.astype(F32),
        name="smoothing",
    )
    block = sds((64, 1024), BF16)
    vmem = pl.BlockSpec(memory_space=pltpu.VMEM)
    smem = pl.BlockSpec(memory_space=pltpu.SMEM)
    weight_parts = pl.pallas_call(
        weight_blocks,
        out_shape=[block] * 8,
        in_specs=[smem, vmem],
        compiler_params=PARAMS,
        name="weight_blocks",
    )(owner, weights)
    slope_row, *corrected_parts = pl.pallas_call(
        correction,
        out_shape=[sds((8, 128), F32)] + [block] * 8,
        in_specs=[smem, vmem, vmem, vmem],
        scratch_shapes=[pltpu.VMEM((8, 64, 1024), BF16)],
        compiler_params=PARAMS,
        name="correction",
    )(owner, sums, smooth, height)

    def exchange(parts):
        return [parts[0]] + [
            lax.ppermute(parts[k], "ifg", [(i, (i + k) % n_ifg) for i in range(n_ifg)])
            for k in range(1, n_ifg)
        ]

    weight_parts, corrected_parts = exchange(weight_parts), exchange(corrected_parts)
    order = (me - jnp.arange(n_ifg)) % n_ifg
    pairs = date_pairs.reshape(n_ifg, -1, 2)[order].reshape(-1, 2)
    dates = jnp.arange(DP, dtype=jnp.int32)
    design = ((dates[None] == pairs[:, 1:2]).astype(F32) - (dates[None] == pairs[:, 0:1]).astype(F32)).astype(BF16)
    design_t = design.T

    field = sds((DP, 1024), F32)
    edges = (sds((DP, 128), BF16), sds((DP, 128), BF16), sds((16, DP), BF16))
    moments = sds((3, 8, 128), F32)
    k0, weights, *sides = call(
        right_side,
        (field, sds((512, 1024), BF16)) + edges,
        *weight_parts,
        *corrected_parts,
        design_t,
        name="right_side",
    )

    def halos(sides):
        first, last, columns = sides
        return (
            forward(last, "rows"),
            backward(first, "rows"),
            forward(columns, "ifg"),
            backward(columns, "ifg"),
        )

    def local(with_before, with_image, name, *args):
        outs = ((field,) if with_image else ()) + (moments,)
        body = lambda *refs: apply_local(with_before, with_image, *refs)
        return call(body, outs, *args, name=name)

    around = halos(sides)
    image, mom0 = local(False, True, "apply0", k0, weights, design, design_t)
    k1, *sides = call(add_halo, (field,) + edges, image, *around, name="add_halo1")
    around = halos(sides)
    image, mom1 = local(True, True, "apply1", k1, weights, design, design_t, k0)
    k2, *sides = call(add_halo, (field,) + edges, image, *around, name="add_halo2")
    around = halos(sides)
    (mom2,) = local(True, False, "apply2", k2, weights, design, design_t, k1)
    part = call(all_moments, sds((8, 128), F32), k2, *around, mom0, mom1, mom2, name="all_moments")
    for step in (1, 2, 4):
        part = part + lax.ppermute(part, "ifg", [(i, i ^ step) for i in range(n_ifg)])
    parts = swap_sum(part[None], "rows", None, n_rows).reshape(n_rows, 8, 128)
    displacement = call(combine, sds((DATES * 8, 128), F32), parts, k0, k1, k2, name="combine")
    return displacement.reshape(DATES, 8, 128), slope_row[0, :64]


def solution(mesh):
    placed = (
        P("ifg", "rows", None),
        P("ifg", "rows", None),
        P("rows", None),
        P("ifg", "rows"),
        P(),
    )
    return jax.shard_map(
        per_device,
        mesh=mesh,
        in_specs=placed,
        out_specs=(P(None, "rows", "ifg"), P("ifg")),
        check_vma=False,
    )
```

time: 698 us -> 155 us (0.22); the launches traced: 686 us -> 153 us
  blocking collectives: 447 us -> 0 us
  local copies, waits for them, and re-layouts: 71.9 us -> 9.94 us
  other arithmetic: 59.4 us -> 0.41 us
  matrix products: 39.5 us -> 0 us
  starting transfers between devices: 53.7 us -> 88.4 us
  waiting for transfers between devices: 6.94 us -> 30.8 us
  Pallas kernels: 0 us -> 22.1 us
    psum x6 -> x0, blocking collectives: 447 us -> none  [the longest x3 220 us: residual_norm(): return lax.psum(jnp.sum(current * current), ('ifg', 'rows'))]
    dot_general x7 -> x0, matrix products: 39.5 us -> none  [the longest x4 23.6 us: back_project(): lax.dot_general(design, values, (((0,), (0,)), ((), ())), precision=preci...]
    pallas_call x0 -> x13, Pallas kernels: none -> 22.1 us  [the longest x11 21.5 us: call(): pl.pallas_call(body, out_shape=outs, scratch_shapes=list(scratch), compil...]
    reduce_sum x4 -> x1, other arithmetic: 19.9 us -> 0.01 us  [per_device(): sums = jnp.sum(swap_sum(sums, 'rows', fast_groups, 8), axis=0)]
    ppermute x14 -> x33, starting transfers between devices: 42 us -> 61.2 us  [the longest x8 26.9 us: forward(): lax.ppermute(values, axis, [(i, i + 1) for i in range(lax.axis_size(axis)...]
    unnamed x47 -> x18, local copies, waits for them, and re-layouts: 25.7 us -> 6.68 us
    ppermute x14 -> x33, waiting for transfers between devices: 0.04 us -> 18 us  [the longest x14 10 us: exchange(): lax.ppermute(parts[k], 'ifg', [(i, (i + k) % n_ifg) for i in range(n_ifg)])]
    reshape x7 -> x3, local copies, waits for them, and re-layouts: 15.8 us -> 0.16 us  [per_device(): pairs = date_pairs.reshape(n_ifg, -1, 2)[order].reshape(-1, 2)]
  transfers between devices with their start and end apart: 16 -> 36, of which waited for: 1 -> 11; matrix products, arithmetic and copies ran while one was open for 10% -> 2% of each run, Pallas kernels for 0% -> 10%
where the time goes in v1:
time: 155 us; the launch traced here: 153 us
  starting transfers between devices  88.4 us (57%)
  waiting for transfers between devices  30.8 us (20%)
  Pallas kernels  22.1 us (14%)
  local copies, waits for them, and re-layouts  9.94 us (6%)
    all_to_all x3, starting transfers between devices, swap_sum(): lax.all_to_all(spread, axis, 0, 0, tiled=True, axis_index_groups=groups)  27.2 us
    ppermute x8, starting transfers between devices, forward(): lax.ppermute(values, axis, [(i, i + 1) for i in range(lax.axis_size(axis)...  26.9 us
    pallas_call x11, Pallas kernels, call(): pl.pallas_call(body, out_shape=outs, scratch_shapes=list(scratch), compil...  21.5 us
    ppermute x8, starting transfers between devices, backward(): lax.ppermute(values, axis, [(i + 1, i) for i in range(lax.axis_size(axis)...  15.9 us
    ppermute x14, starting transfers between devices, exchange(): lax.ppermute(parts[k], 'ifg', [(i, (i + k) % n_ifg) for i in range(n_ifg)])  13.6 us
    all_to_all x3, waiting for transfers between devices, swap_sum(): lax.all_to_all(spread, axis, 0, 0, tiled=True, axis_index_groups=groups)  12.8 us
    ppermute x14, waiting for transfers between devices, exchange(): lax.ppermute(parts[k], 'ifg', [(i, (i + k) % n_ifg) for i in range(n_ifg)])  10 us
    unnamed x18, local copies, waits for them, and re-layouts  6.68 us
  transfers between devices with their start and end apart: 36, of which 11 were waited for; matrix products, arithmetic and copies ran while one was open for 2% of the time, Pallas kernels for 10%

profile of v1, /device:TPU:6, one launch (start us, length us, event | category | flops | bytes accessed | tf_op | source)
XLA Modules:
  0.0 152.7 jit_solution(421513158407000790)
XLA Ops:
  0.6 1.2 copy-done.4
  1.9 1.2 copy-done.5
  3.1 1.3 rows_first.1
  4.4 3.8 %collective-permute-start = (bf16[128,1024]{1,0:T(8,128)(2,1)S(1)}, bf16[128,1024]{1,0:T(8,128)(2,1)S(1)}, u32[]{:S(2)}, u32[]{:S(2)}) collective-permute-start(bf16[128,1024]{1,0:T(8,128)(2,1)S(1)} %get-tuple-element.44), channel_id=1, source_target_pairs={{0,1},{1,2},{2,3},{3,4},{4,5},{5,6},{6,7},{7,8},{8,9},{9,10},{10,1... | collective-permute-start | bytes 786440 | tf_op jit(solution)/shard_map/ppermute | solution.py:309
  8.2 1.3 collective-permute-start.1
  9.6 1.3 collective-permute-start.10
  10.9 5.2 %collective-permute-start.9 = (f32[1,1024]{1,0:T(1,128)S(1)}, f32[1,1024]{1,0:T(1,128)S(1)}, u32[]{:S(2)}, u32[]{:S(2)}) collective-permute-start(f32[1,1024]{1,0:T(1,128)S(1)} %get-tuple-element.83), channel_id=1, source_target_pairs={{0,1},{1,2},{2,3},{3,4},{4,5},{5,6},{6,7},{7,8},{8,9},{9,10},{10,1... | collective-permute-start | bytes 12296 | tf_op jit(solution)/shard_map/ppermute | solution.py:309
  16.2 2.0 %collective-permute-done.10.below = f32[1,1024]{1,0:T(1,128)S(1)} collective-permute-done((f32[1,1024]{1,0:T(1,128)S(1)}, f32[1,1024]{1,0:T(1,128)S(1)}, u32[]{:S(2)}, u32[]{:S(2)}) %collective-permute-start.10) | collective-permute-done | bytes 4128 | tf_op jit(solution)/shard_map/ppermute | solution.py:312
  19.5 10.4 %all-to-all-start = ((f32[8,8,128]{2,1,0:T(8,128)}), f32[8,8,128]{2,1,0:T(8,128)S(1)}, u32[]{:S(2)}, u32[]{:S(2)}) async-start(f32[8,8,128]{2,1,0:T(8,128)} %broadcast_in_dim.6), calls=%async_computation | async-start | bytes 65536 | tf_op jit(solution)/shard_map/all_to_all | solution.py:300
  30.0 2.7 %smoothing.1 = (f32[8,64,1024]{2,1,0:T(8,128)S(1)}, bf16[8,64,1024]{2,1,0:T(8,128)(2,1)S(1)}) custom-call(bf16[8,64,1024]{2,1,0:T(8,128)(2,1)S(1)} %get-tuple-element.42.phase_t, bf16[8,64,1024]{2,1,0:T(8,128)(2,1)S(1)} %get-tuple-element.43.coher_t, bf16[128,1024]{1,0:T(8,128)(2,1)S(1)} %collective-permute-done.above, ...), custom_call_target="tpu_custom_call" | custom-call | tf_op jit(solution)/shard_map/smoothing/pallas_call | solution.py:24
  32.7 1.3 copy-done.2
  34.7 2.3 %collective-permute-start.4 = (bf16[64,1024]{1,0:T(8,128)(2,1)S(1)}, bf16[64,1024]{1,0:T(8,128)(2,1)S(1)}, u32[]{:S(2)}, u32[]{:S(2)}) collective-permute-start(bf16[64,1024]{1,0:T(8,128)(2,1)S(1)} %get-tuple-element.50), channel_id=1, source_target_pairs={{0,96},{32,128},{64,160},{96,192},{128,224},{160,0},{192,32},{224,... | collective-permute-start | bytes 393224 | tf_op jit(solution)/shard_map/ppermute | solution.py:375
  37.0 1.1 collective-permute-start.5
  38.8 4.9 %all-to-all-start.1 = ((f32[4,1,8,128]{3,2,1,0:T(8,128)}), f32[4,1,8,128]{3,2,1,0:T(8,128)S(1)}, u32[]{:S(2)}, u32[]{:S(2)}) async-start(f32[4,1,8,128]{3,2,1,0:T(8,128)} %broadcast_in_dim.7), calls=%async_computation.1 | async-start | bytes 32768 | tf_op jit(solution)/shard_map/all_to_all | solution.py:300
  44.4 1.7 %collective-permute-start.6 = (bf16[64,1024]{1,0:T(8,128)(2,1)S(1)}, bf16[64,1024]{1,0:T(8,128)(2,1)S(1)}, u32[]{:S(2)}, u32[]{:S(2)}) collective-permute-start(bf16[64,1024]{1,0:T(8,128)(2,1)S(1)} %get-tuple-element.52), channel_id=1, source_target_pairs={{0,160},{32,192},{64,224},{96,0},{128,32},{160,64},{192,96},{224,1... | collective-permute-start | bytes 393224 | tf_op jit(solution)/shard_map/ppermute | solution.py:375
  46.1 2.9 %all-to-all-done.1 = f32[4,1,8,128]{3,2,1,0:T(8,128)S(1)} async-done(((f32[4,1,8,128]{3,2,1,0:T(8,128)}), f32[4,1,8,128]{3,2,1,0:T(8,128)S(1)}, u32[]{:S(2)}, u32[]{:S(2)}) %all-to-all-start.1) | async-done | bytes 16416 | tf_op jit(solution)/shard_map/all_to_all | solution.py:300
  49.0 1.6 %copy-done.3 = f32[8,64,1024]{2,1,0:T(8,128)S(1)} copy-done((f32[8,64,1024]{2,1,0:T(8,128)S(1)}, f32[8,64,1024]{2,1,0:T(8,128)}, u32[]{:S(2)}) %copy-start.3) | copy-done | bytes 2097176
  52.7 2.3 %collective-permute-start.12 = (bf16[64,1024]{1,0:T(8,128)(2,1)S(1)}, bf16[64,1024]{1,0:T(8,128)(2,1)S(1)}, u32[]{:S(2)}, u32[]{:S(2)}) collective-permute-start(bf16[64,1024]{1,0:T(8,128)(2,1)S(1)} %get-tuple-element.58), channel_id=1, source_target_pairs={{0,64},{32,96},{64,128},{96,160},{128,192},{160,224},{192,0},{224,... | collective-permute-start | bytes 393224 | tf_op jit(solution)/shard_map/ppermute | solution.py:375
  55.8 1.6 %collective-permute-done.7.refs_6_ = bf16[64,1024]{1,0:T(8,128)(2,1)S(1)} collective-permute-done((bf16[64,1024]{1,0:T(8,128)(2,1)S(1)}, bf16[64,1024]{1,0:T(8,128)(2,1)S(1)}, u32[]{:S(2)}, u32[]{:S(2)}) %collective-permute-start.7) | collective-permute-done | bytes 131104 | tf_op jit(solution)/shard_map/ppermute | solution.py:375
  57.4 1.2 collective-permute-start.14
  58.6 1.1 collective-permute-start.15
  60.8 5.4 %collective-permute-done.13.refs_11_ = bf16[64,1024]{1,0:T(8,128)(2,1)S(1)} collective-permute-done((bf16[64,1024]{1,0:T(8,128)(2,1)S(1)}, bf16[64,1024]{1,0:T(8,128)(2,1)S(1)}, u32[]{:S(2)}, u32[]{:S(2)}) %collective-permute-start.13) | collective-permute-done | bytes 131104 | tf_op jit(solution)/shard_map/ppermute | solution.py:375
  66.6 2.6 %collective-permute-done.16.refs_14_ = bf16[64,1024]{1,0:T(8,128)(2,1)S(1)} collective-permute-done((bf16[64,1024]{1,0:T(8,128)(2,1)S(1)}, bf16[64,1024]{1,0:T(8,128)(2,1)S(1)}, u32[]{:S(2)}, u32[]{:S(2)}) %collective-permute-start.16) | collective-permute-done | bytes 131104 | tf_op jit(solution)/shard_map/ppermute | solution.py:375
  69.2 1.1 right_side.1
  70.3 3.3 %collective-permute-start.21 = (bf16[16,304]{1,0:T(8,128)(2,1)S(1)}, bf16[16,304]{1,0:T(8,128)(2,1)S(1)}, u32[]{:S(2)}, u32[]{:S(2)}) collective-permute-start(bf16[16,304]{1,0:T(8,128)(2,1)S(1)} %get-tuple-element.69), channel_id=1, source_target_pairs={{32,0},{64,32},{96,64},{128,96},{160,128},{192,160},{224,192},{33,... | collective-permute-start | bytes 29192 | tf_op jit(solution)/shard_map/ppermute | solution.py:312
  73.6 1.9 %collective-permute-start.20 = (bf16[16,304]{1,0:T(8,128)(2,1)S(1)}, bf16[16,304]{1,0:T(8,128)(2,1)S(1)}, u32[]{:S(2)}, u32[]{:S(2)}) collective-permute-start(bf16[16,304]{1,0:T(8,128)(2,1)S(1)} %get-tuple-element.69), channel_id=1, source_target_pairs={{0,32},{32,64},{64,96},{96,128},{128,160},{160,192},{192,224},{1,3... | collective-permute-start | bytes 29192 | tf_op jit(solution)/shard_map/ppermute | solution.py:309
  75.5 3.8 %collective-permute-start.18 = (bf16[304,128]{1,0:T(8,128)(2,1)S(1)}, bf16[304,128]{1,0:T(8,128)(2,1)S(1)}, u32[]{:S(2)}, u32[]{:S(2)}) collective-permute-start(bf16[304,128]{1,0:T(8,128)(2,1)S(1)} %get-tuple-element.67), channel_id=1, source_target_pairs={{0,1},{1,2},{2,3},{3,4},{4,5},{5,6},{6,7},{7,8},{8,9},{9,10},{10,1... | collective-permute-start | bytes 233480 | tf_op jit(solution)/shard_map/ppermute | solution.py:309
  79.4 1.3 collective-permute-start.19
  80.9 3.9 %apply0.1 = (f32[304,1024]{1,0:T(8,128)S(1)}, f32[3,8,128]{2,1,0:T(8,128)S(1)}) custom-call(f32[304,1024]{1,0:T(8,128)S(1)} %get-tuple-element.64.refs_0_.refs_4_.zero, bf16[512,1024]{1,0:T(8,128)(2,1)S(1)} %get-tuple-element.65.refs_1_, bf16[512,304]{1,0:T(8,128)(2,1)S(1)} %subtract_convert_fusion.refs_2_, ...), custom_call_target="tpu_custom_call" | custom-call | tf_op jit(solution)/shard_map/apply0/pallas_call | solution.py:24
  86.3 3.7 %collective-permute-start.22 = (bf16[304,128]{1,0:T(8,128)(2,1)S(1)}, bf16[304,128]{1,0:T(8,128)(2,1)S(1)}, u32[]{:S(2)}, u32[]{:S(2)}) collective-permute-start(bf16[304,128]{1,0:T(8,128)(2,1)S(1)} %get-tuple-element.72), channel_id=1, source_target_pairs={{0,1},{1,2},{2,3},{3,4},{4,5},{5,6},{6,7},{7,8},{8,9},{9,10},{10,1... | collective-permute-start | bytes 233480 | tf_op jit(solution)/shard_map/ppermute | solution.py:309
  90.1 1.3 collective-permute-start.23
  91.4 2.8 %collective-permute-start.25 = (bf16[16,304]{1,0:T(8,128)(2,1)S(1)}, bf16[16,304]{1,0:T(8,128)(2,1)S(1)}, u32[]{:S(2)}, u32[]{:S(2)}) collective-permute-start(bf16[16,304]{1,0:T(8,128)(2,1)S(1)} %get-tuple-element.74), channel_id=1, source_target_pairs={{32,0},{64,32},{96,64},{128,96},{160,128},{192,160},{224,192},{33,... | collective-permute-start | bytes 29192 | tf_op jit(solution)/shard_map/ppermute | solution.py:312
  94.2 1.9 %collective-permute-start.24 = (bf16[16,304]{1,0:T(8,128)(2,1)S(1)}, bf16[16,304]{1,0:T(8,128)(2,1)S(1)}, u32[]{:S(2)}, u32[]{:S(2)}) collective-permute-start(bf16[16,304]{1,0:T(8,128)(2,1)S(1)} %get-tuple-element.74), channel_id=1, source_target_pairs={{0,32},{32,64},{64,96},{96,128},{128,160},{160,192},{192,224},{1,3... | collective-permute-start | bytes 29192 | tf_op jit(solution)/shard_map/ppermute | solution.py:309
  96.1 3.9 %apply1.1 = (f32[304,1024]{1,0:T(8,128)S(1)}, f32[3,8,128]{2,1,0:T(8,128)S(1)}) custom-call(f32[304,1024]{1,0:T(8,128)S(1)} %get-tuple-element.70.refs_0_.refs_4_.one, bf16[512,1024]{1,0:T(8,128)(2,1)S(1)} %get-tuple-element.65.refs_1_, bf16[512,304]{1,0:T(8,128)(2,1)S(1)} %subtract_convert_fusion.refs_2_, ...), custom_call_target="tpu_custom_call" | custom-call | tf_op jit(solution)/shard_map/apply1/pallas_call | solution.py:24
  100.7 4.6 %collective-permute-start.26 = (bf16[304,128]{1,0:T(8,128)(2,1)S(1)}, bf16[304,128]{1,0:T(8,128)(2,1)S(1)}, u32[]{:S(2)}, u32[]{:S(2)}) collective-permute-start(bf16[304,128]{1,0:T(8,128)(2,1)S(1)} %get-tuple-element.76), channel_id=1, source_target_pairs={{0,1},{1,2},{2,3},{3,4},{4,5},{5,6},{6,7},{7,8},{8,9},{9,10},{10,1... | collective-permute-start | bytes 233480 | tf_op jit(solution)/shard_map/ppermute | solution.py:309
  105.3 1.3 collective-permute-start.27
  106.6 3.4 %collective-permute-start.29 = (bf16[16,304]{1,0:T(8,128)(2,1)S(1)}, bf16[16,304]{1,0:T(8,128)(2,1)S(1)}, u32[]{:S(2)}, u32[]{:S(2)}) collective-permute-start(bf16[16,304]{1,0:T(8,128)(2,1)S(1)} %get-tuple-element.78), channel_id=1, source_target_pairs={{32,0},{64,32},{96,64},{128,96},{160,128},{192,160},{224,192},{33,... | collective-permute-start | bytes 29192 | tf_op jit(solution)/shard_map/ppermute | solution.py:312
  110.0 1.9 %collective-permute-start.28 = (bf16[16,304]{1,0:T(8,128)(2,1)S(1)}, bf16[16,304]{1,0:T(8,128)(2,1)S(1)}, u32[]{:S(2)}, u32[]{:S(2)}) collective-permute-start(bf16[16,304]{1,0:T(8,128)(2,1)S(1)} %get-tuple-element.78), channel_id=1, source_target_pairs={{0,32},{32,64},{64,96},{96,128},{128,160},{160,192},{192,224},{1,3... | collective-permute-start | bytes 29192 | tf_op jit(solution)/shard_map/ppermute | solution.py:309
  111.9 4.0 %apply2.1.two = f32[3,8,128]{2,1,0:T(8,128)S(1)} custom-call(f32[304,1024]{1,0:T(8,128)S(1)} %get-tuple-element.75.refs_0_.field.two, bf16[512,1024]{1,0:T(8,128)(2,1)S(1)} %get-tuple-element.65.refs_1_, bf16[512,304]{1,0:T(8,128)(2,1)S(1)} %subtract_convert_fusion.refs_2_, bf16[304,512]{1,0:T(8,128)(2,1)S(1)} %subtract_convert_fusion.1.refs_16_.refs_3_, ...), custom_call_target="tpu_custom_call" | custom-call | tf_op jit(solution)/shard_map/apply2/pallas_call | solution.py:24
  116.6 1.2 collective-permute-done.30
  117.8 1.8 %collective-permute-start.31 = (f32[8,128]{1,0:T(8,128)S(1)}, f32[8,128]{1,0:T(8,128)S(1)}, u32[]{:S(2)}, u32[]{:S(2)}) collective-permute-start(f32[8,128]{1,0:T(8,128)S(1)} %add.34), channel_id=1, source_target_pairs={{0,64},{32,96},{64,0},{96,32},{128,192},{160,224},{192,128},{224,1... | collective-permute-start | bytes 12296 | tf_op jit(solution)/shard_map/ppermute | solution.py:422
  119.6 1.8 %collective-permute-done.31 = f32[8,128]{1,0:T(8,128)S(1)} collective-permute-done((f32[8,128]{1,0:T(8,128)S(1)}, f32[8,128]{1,0:T(8,128)S(1)}, u32[]{:S(2)}, u32[]{:S(2)}) %collective-permute-start.31) | collective-permute-done | bytes 4128 | tf_op jit(solution)/shard_map/ppermute | solution.py:422
  121.4 3.0 %collective-permute-start.32 = (f32[8,128]{1,0:T(8,128)S(1)}, f32[8,128]{1,0:T(8,128)S(1)}, u32[]{:S(2)}, u32[]{:S(2)}) collective-permute-start(f32[8,128]{1,0:T(8,128)S(1)} %add.35), channel_id=1, source_target_pairs={{0,128},{32,160},{64,192},{96,224},{128,0},{160,32},{192,64},{224,... | collective-permute-start | bytes 12296 | tf_op jit(solution)/shard_map/ppermute | solution.py:422
  124.4 2.1 %collective-permute-done.32 = f32[8,128]{1,0:T(8,128)S(1)} collective-permute-done((f32[8,128]{1,0:T(8,128)S(1)}, f32[8,128]{1,0:T(8,128)S(1)}, u32[]{:S(2)}, u32[]{:S(2)}) %collective-permute-start.32) | collective-permute-done | bytes 4128 | tf_op jit(solution)/shard_map/ppermute | solution.py:422
  127.2 11.9 %all-to-all-start.2 = ((f32[32,1,8,128]{3,2,1,0:T(8,128)}), f32[32,1,8,128]{3,2,1,0:T(8,128)S(1)}, u32[]{:S(2)}, u32[]{:S(2)}) async-start(f32[32,1,8,128]{3,2,1,0:T(8,128)} %broadcast_in_dim.8), calls=%async_computation.2 | async-start | bytes 262144 | tf_op jit(solution)/shard_map/all_to_all | solution.py:300
  139.6 9.9 %all-to-all-done.2 = f32[32,1,8,128]{3,2,1,0:T(8,128)S(1)} async-done(((f32[32,1,8,128]{3,2,1,0:T(8,128)}), f32[32,1,8,128]{3,2,1,0:T(8,128)S(1)}, u32[]{:S(2)}, u32[]{:S(2)}) %all-to-all-start.2) | async-done | bytes 131104 | tf_op jit(solution)/shard_map/all_to_all | solution.py:300
  149.5 1.3 copy-done.1
  150.8 2.0 %combine.1 = f32[2400,128]{1,0:T(8,128)} custom-call(f32[32,8,128]{2,1,0:T(8,128)S(1)} %bitcast.14, f32[304,1024]{1,0:T(8,128)S(1)} %get-tuple-element.64.refs_0_.refs_4_.zero, f32[304,1024]{1,0:T(8,128)S(1)} %get-tuple-element.70.refs_0_.refs_4_.one, f32[304,1024]{1,0:T(8,128)S(1)} %copy-done.1), custom_call_target="tpu_custom_call" | custom-call | tf_op jit(solution)/shard_map/combine/pallas_call | solution.py:24
  (76 shorter events, 12.1 us)
Async XLA Ops:
  0.6 1.2 copy-start.4
  1.9 1.2 copy-start.5
  3.1 6.5 %copy-start.6 = (f32[8,1024]{1,0:T(8,128)S(1)}, f32[8,1024]{1,0:T(8,128)}, u32[]{:S(2)}) copy-start(f32[8,1024]{1,0:T(8,128)} %height.3) | copy-start | bytes 98308
  3.1 13.0 %copy-start.8 = (s32[64,8]{0,1:T(8,128)S(1)}, s32[64,8]{0,1:T(8,128)}, u32[]{:S(2)}) copy-start(s32[64,8]{0,1:T(8,128)} %param.8) | copy-start | bytes 6148
  4.4 25.6 %collective-permute-start = (bf16[128,1024]{1,0:T(8,128)(2,1)S(1)}, bf16[128,1024]{1,0:T(8,128)(2,1)S(1)}, u32[]{:S(2)}, u32[]{:S(2)}) collective-permute-start(bf16[128,1024]{1,0:T(8,128)(2,1)S(1)} %get-tuple-element.44), channel_id=1, source_target_pairs={{0,1},{1,2},{2,3},{3,4},{4,5},{5,6},{6,7},{7,8},{8,9},{9,10},{10,1... | collective-permute-start | bytes 786440 | tf_op jit(solution)/shard_map/ppermute | solution.py:309
  8.2 21.7 %collective-permute-start.1 = (bf16[128,1024]{1,0:T(8,128)(2,1)S(1)}, bf16[128,1024]{1,0:T(8,128)(2,1)S(1)}, u32[]{:S(2)}, u32[]{:S(2)}) collective-permute-start(bf16[128,1024]{1,0:T(8,128)(2,1)S(1)} %get-tuple-element.45), channel_id=1, source_target_pairs={{1,0},{2,1},{3,2},{4,3},{5,4},{6,5},{7,6},{8,7},{9,8},{10,9},{11,1... | collective-permute-start | bytes 786440 | tf_op jit(solution)/shard_map/ppermute | solution.py:312
  9.6 8.6 %collective-permute-start.10 = (f32[1,1024]{1,0:T(1,128)S(1)}, f32[1,1024]{1,0:T(1,128)S(1)}, u32[]{:S(2)}, u32[]{:S(2)}) collective-permute-start(f32[1,1024]{1,0:T(1,128)S(1)} %get-tuple-element.82), channel_id=1, source_target_pairs={{1,0},{2,1},{3,2},{4,3},{5,4},{6,5},{7,6},{8,7},{9,8},{10,9},{11,1... | collective-permute-start | bytes 12296 | tf_op jit(solution)/shard_map/ppermute | solution.py:312
  10.9 7.3 %collective-permute-start.9 = (f32[1,1024]{1,0:T(1,128)S(1)}, f32[1,1024]{1,0:T(1,128)S(1)}, u32[]{:S(2)}, u32[]{:S(2)}) collective-permute-start(f32[1,1024]{1,0:T(1,128)S(1)} %get-tuple-element.83), channel_id=1, source_target_pairs={{0,1},{1,2},{2,3},{3,4},{4,5},{5,6},{6,7},{7,8},{8,9},{9,10},{10,1... | collective-permute-start | bytes 12296 | tf_op jit(solution)/shard_map/ppermute | solution.py:309
  19.5 18.6 %all-to-all-start = ((f32[8,8,128]{2,1,0:T(8,128)}), f32[8,8,128]{2,1,0:T(8,128)S(1)}, u32[]{:S(2)}, u32[]{:S(2)}) async-start(f32[8,8,128]{2,1,0:T(8,128)} %broadcast_in_dim.6), calls=%async_computation | async-start | bytes 65536 | tf_op jit(solution)/shard_map/all_to_all | solution.py:300
  30.0 13.7 %copy-start.7 = (s32[512,2]{0,1:T(2,128)S(1)}, s32[512,2]{0,1:T(2,128)}, u32[]{:S(2)}) copy-start(s32[512,2]{0,1:T(2,128)} %param.9) | copy-start | bytes 12292
  32.7 1.4 copy-start.2
  34.1 17.0 %collective-permute-start.2 = (bf16[64,1024]{1,0:T(8,128)(2,1)S(1)}, bf16[64,1024]{1,0:T(8,128)(2,1)S(1)}, u32[]{:S(2)}, u32[]{:S(2)}) collective-permute-start(bf16[64,1024]{1,0:T(8,128)(2,1)S(1)} %get-tuple-element.48), channel_id=1, source_target_pairs={{0,32},{32,64},{64,96},{96,128},{128,160},{160,192},{192,224},{224... | collective-permute-start | bytes 393224 | tf_op jit(solution)/shard_map/ppermute | solution.py:375
  34.2 18.0 %collective-permute-start.3 = (bf16[64,1024]{1,0:T(8,128)(2,1)S(1)}, bf16[64,1024]{1,0:T(8,128)(2,1)S(1)}, u32[]{:S(2)}, u32[]{:S(2)}) collective-permute-start(bf16[64,1024]{1,0:T(8,128)(2,1)S(1)} %get-tuple-element.49), channel_id=1, source_target_pairs={{0,64},{32,96},{64,128},{96,160},{128,192},{160,224},{192,0},{224,... | collective-permute-start | bytes 393224 | tf_op jit(solution)/shard_map/ppermute | solution.py:375
  34.7 17.5 %collective-permute-start.4 = (bf16[64,1024]{1,0:T(8,128)(2,1)S(1)}, bf16[64,1024]{1,0:T(8,128)(2,1)S(1)}, u32[]{:S(2)}, u32[]{:S(2)}) collective-permute-start(bf16[64,1024]{1,0:T(8,128)(2,1)S(1)} %get-tuple-element.50), channel_id=1, source_target_pairs={{0,96},{32,128},{64,160},{96,192},{128,224},{160,0},{192,32},{224,... | collective-permute-start | bytes 393224 | tf_op jit(solution)/shard_map/ppermute | solution.py:375
  37.0 15.6 %collective-permute-start.5 = (bf16[64,1024]{1,0:T(8,128)(2,1)S(1)}, bf16[64,1024]{1,0:T(8,128)(2,1)S(1)}, u32[]{:S(2)}, u32[]{:S(2)}) collective-permute-start(bf16[64,1024]{1,0:T(8,128)(2,1)S(1)} %get-tuple-element.51), channel_id=1, source_target_pairs={{0,128},{32,160},{64,192},{96,224},{128,0},{160,32},{192,64},{224,... | collective-permute-start | bytes 393224 | tf_op jit(solution)/shard_map/ppermute | solution.py:375
  38.8 10.2 %all-to-all-start.1 = ((f32[4,1,8,128]{3,2,1,0:T(8,128)}), f32[4,1,8,128]{3,2,1,0:T(8,128)S(1)}, u32[]{:S(2)}, u32[]{:S(2)}) async-start(f32[4,1,8,128]{3,2,1,0:T(8,128)} %broadcast_in_dim.7), calls=%async_computation.1 | async-start | bytes 32768 | tf_op jit(solution)/shard_map/all_to_all | solution.py:300
  44.4 10.5 %collective-permute-start.6 = (bf16[64,1024]{1,0:T(8,128)(2,1)S(1)}, bf16[64,1024]{1,0:T(8,128)(2,1)S(1)}, u32[]{:S(2)}, u32[]{:S(2)}) collective-permute-start(bf16[64,1024]{1,0:T(8,128)(2,1)S(1)} %get-tuple-element.52), channel_id=1, source_target_pairs={{0,160},{32,192},{64,224},{96,0},{128,32},{160,64},{192,96},{224,1... | collective-permute-start | bytes 393224 | tf_op jit(solution)/shard_map/ppermute | solution.py:375
  49.0 1.6 %copy-start.3 = (f32[8,64,1024]{2,1,0:T(8,128)S(1)}, f32[8,64,1024]{2,1,0:T(8,128)}, u32[]{:S(2)}) copy-start(f32[8,64,1024]{2,1,0:T(8,128)} %copy-done.2) | copy-start | bytes 6291460
  51.1 6.3 %collective-permute-start.7 = (bf16[64,1024]{1,0:T(8,128)(2,1)S(1)}, bf16[64,1024]{1,0:T(8,128)(2,1)S(1)}, u32[]{:S(2)}, u32[]{:S(2)}) collective-permute-start(bf16[64,1024]{1,0:T(8,128)(2,1)S(1)} %get-tuple-element.53), channel_id=1, source_target_pairs={{0,192},{32,224},{64,0},{96,32},{128,64},{160,96},{192,128},{224,1... | collective-permute-start | bytes 393224 | tf_op jit(solution)/shard_map/ppermute | solution.py:375
  52.2 6.4 %collective-permute-start.8 = (bf16[64,1024]{1,0:T(8,128)(2,1)S(1)}, bf16[64,1024]{1,0:T(8,128)(2,1)S(1)}, u32[]{:S(2)}, u32[]{:S(2)}) collective-permute-start(bf16[64,1024]{1,0:T(8,128)(2,1)S(1)} %get-tuple-element.54), channel_id=1, source_target_pairs={{0,224},{32,0},{64,32},{96,64},{128,96},{160,128},{192,160},{224,1... | collective-permute-start | bytes 393224 | tf_op jit(solution)/shard_map/ppermute | solution.py:375
  52.2 7.6 %collective-permute-start.11 = (bf16[64,1024]{1,0:T(8,128)(2,1)S(1)}, bf16[64,1024]{1,0:T(8,128)(2,1)S(1)}, u32[]{:S(2)}, u32[]{:S(2)}) collective-permute-start(bf16[64,1024]{1,0:T(8,128)(2,1)S(1)} %get-tuple-element.57), channel_id=1, source_target_pairs={{0,32},{32,64},{64,96},{96,128},{128,160},{160,192},{192,224},{224... | collective-permute-start | bytes 393224 | tf_op jit(solution)/shard_map/ppermute | solution.py:375
  52.7 7.6 %collective-permute-start.12 = (bf16[64,1024]{1,0:T(8,128)(2,1)S(1)}, bf16[64,1024]{1,0:T(8,128)(2,1)S(1)}, u32[]{:S(2)}, u32[]{:S(2)}) collective-permute-start(bf16[64,1024]{1,0:T(8,128)(2,1)S(1)} %get-tuple-element.58), channel_id=1, source_target_pairs={{0,64},{32,96},{64,128},{96,160},{128,192},{160,224},{192,0},{224,... | collective-permute-start | bytes 393224 | tf_op jit(solution)/shard_map/ppermute | solution.py:375
  55.0 11.3 %collective-permute-start.13 = (bf16[64,1024]{1,0:T(8,128)(2,1)S(1)}, bf16[64,1024]{1,0:T(8,128)(2,1)S(1)}, u32[]{:S(2)}, u32[]{:S(2)}) collective-permute-start(bf16[64,1024]{1,0:T(8,128)(2,1)S(1)} %get-tuple-element.59), channel_id=1, source_target_pairs={{0,96},{32,128},{64,160},{96,192},{128,224},{160,0},{192,32},{224,... | collective-permute-start | bytes 393224 | tf_op jit(solution)/shard_map/ppermute | solution.py:375
  57.4 8.9 %collective-permute-start.14 = (bf16[64,1024]{1,0:T(8,128)(2,1)S(1)}, bf16[64,1024]{1,0:T(8,128)(2,1)S(1)}, u32[]{:S(2)}, u32[]{:S(2)}) collective-permute-start(bf16[64,1024]{1,0:T(8,128)(2,1)S(1)} %get-tuple-element.60), channel_id=1, source_target_pairs={{0,128},{32,160},{64,192},{96,224},{128,0},{160,32},{192,64},{224,... | collective-permute-start | bytes 393224 | tf_op jit(solution)/shard_map/ppermute | solution.py:375
  58.6 8.0 %collective-permute-start.15 = (bf16[64,1024]{1,0:T(8,128)(2,1)S(1)}, bf16[64,1024]{1,0:T(8,128)(2,1)S(1)}, u32[]{:S(2)}, u32[]{:S(2)}) collective-permute-start(bf16[64,1024]{1,0:T(8,128)(2,1)S(1)} %get-tuple-element.61), channel_id=1, source_target_pairs={{0,160},{32,192},{64,224},{96,0},{128,32},{160,64},{192,96},{224,1... | collective-permute-start | bytes 393224 | tf_op jit(solution)/shard_map/ppermute | solution.py:375
  59.7 9.5 %collective-permute-start.16 = (bf16[64,1024]{1,0:T(8,128)(2,1)S(1)}, bf16[64,1024]{1,0:T(8,128)(2,1)S(1)}, u32[]{:S(2)}, u32[]{:S(2)}) collective-permute-start(bf16[64,1024]{1,0:T(8,128)(2,1)S(1)} %get-tuple-element.62), channel_id=1, source_target_pairs={{0,192},{32,224},{64,0},{96,32},{128,64},{160,96},{192,128},{224,1... | collective-permute-start | bytes 393224 | tf_op jit(solution)/shard_map/ppermute | solution.py:375
  60.3 8.9 %collective-permute-start.17 = (bf16[64,1024]{1,0:T(8,128)(2,1)S(1)}, bf16[64,1024]{1,0:T(8,128)(2,1)S(1)}, u32[]{:S(2)}, u32[]{:S(2)}) collective-permute-start(bf16[64,1024]{1,0:T(8,128)(2,1)S(1)} %get-tuple-element.63), channel_id=1, source_target_pairs={{0,224},{32,0},{64,32},{96,64},{128,96},{160,128},{192,160},{224,1... | collective-permute-start | bytes 393224 | tf_op jit(solution)/shard_map/ppermute | solution.py:375
  70.3 14.4 %collective-permute-start.21 = (bf16[16,304]{1,0:T(8,128)(2,1)S(1)}, bf16[16,304]{1,0:T(8,128)(2,1)S(1)}, u32[]{:S(2)}, u32[]{:S(2)}) collective-permute-start(bf16[16,304]{1,0:T(8,128)(2,1)S(1)} %get-tuple-element.69), channel_id=1, source_target_pairs={{32,0},{64,32},{96,64},{128,96},{160,128},{192,160},{224,192},{33,... | collective-permute-start | bytes 29192 | tf_op jit(solution)/shard_map/ppermute | solution.py:312
  73.6 11.2 %collective-permute-start.20 = (bf16[16,304]{1,0:T(8,128)(2,1)S(1)}, bf16[16,304]{1,0:T(8,128)(2,1)S(1)}, u32[]{:S(2)}, u32[]{:S(2)}) collective-permute-start(bf16[16,304]{1,0:T(8,128)(2,1)S(1)} %get-tuple-element.69), channel_id=1, source_target_pairs={{0,32},{32,64},{64,96},{96,128},{128,160},{160,192},{192,224},{1,3... | collective-permute-start | bytes 29192 | tf_op jit(solution)/shard_map/ppermute | solution.py:309
  75.5 9.2 %collective-permute-start.18 = (bf16[304,128]{1,0:T(8,128)(2,1)S(1)}, bf16[304,128]{1,0:T(8,128)(2,1)S(1)}, u32[]{:S(2)}, u32[]{:S(2)}) collective-permute-start(bf16[304,128]{1,0:T(8,128)(2,1)S(1)} %get-tuple-element.67), channel_id=1, source_target_pairs={{0,1},{1,2},{2,3},{3,4},{4,5},{5,6},{6,7},{7,8},{8,9},{9,10},{10,1... | collective-permute-start | bytes 233480 | tf_op jit(solution)/shard_map/ppermute | solution.py:309
  79.4 6.3 %collective-permute-start.19 = (bf16[304,128]{1,0:T(8,128)(2,1)S(1)}, bf16[304,128]{1,0:T(8,128)(2,1)S(1)}, u32[]{:S(2)}, u32[]{:S(2)}) collective-permute-start(bf16[304,128]{1,0:T(8,128)(2,1)S(1)} %get-tuple-element.68), channel_id=1, source_target_pairs={{1,0},{2,1},{3,2},{4,3},{5,4},{6,5},{7,6},{8,7},{9,8},{10,9},{11,1... | collective-permute-start | bytes 233480 | tf_op jit(solution)/shard_map/ppermute | solution.py:312
  86.3 13.6 %collective-permute-start.22 = (bf16[304,128]{1,0:T(8,128)(2,1)S(1)}, bf16[304,128]{1,0:T(8,128)(2,1)S(1)}, u32[]{:S(2)}, u32[]{:S(2)}) collective-permute-start(bf16[304,128]{1,0:T(8,128)(2,1)S(1)} %get-tuple-element.72), channel_id=1, source_target_pairs={{0,1},{1,2},{2,3},{3,4},{4,5},{5,6},{6,7},{7,8},{8,9},{9,10},{10,1... | collective-permute-start | bytes 233480 | tf_op jit(solution)/shard_map/ppermute | solution.py:309
  90.1 10.0 %collective-permute-start.23 = (bf16[304,128]{1,0:T(8,128)(2,1)S(1)}, bf16[304,128]{1,0:T(8,128)(2,1)S(1)}, u32[]{:S(2)}, u32[]{:S(2)}) collective-permute-start(bf16[304,128]{1,0:T(8,128)(2,1)S(1)} %get-tuple-element.73), channel_id=1, source_target_pairs={{1,0},{2,1},{3,2},{4,3},{5,4},{6,5},{7,6},{8,7},{9,8},{10,9},{11,1... | collective-permute-start | bytes 233480 | tf_op jit(solution)/shard_map/ppermute | solution.py:312
  91.4 8.6 %collective-permute-start.25 = (bf16[16,304]{1,0:T(8,128)(2,1)S(1)}, bf16[16,304]{1,0:T(8,128)(2,1)S(1)}, u32[]{:S(2)}, u32[]{:S(2)}) collective-permute-start(bf16[16,304]{1,0:T(8,128)(2,1)S(1)} %get-tuple-element.74), channel_id=1, source_target_pairs={{32,0},{64,32},{96,64},{128,96},{160,128},{192,160},{224,192},{33,... | collective-permute-start | bytes 29192 | tf_op jit(solution)/shard_map/ppermute | solution.py:312
  94.2 5.8 %collective-permute-start.24 = (bf16[16,304]{1,0:T(8,128)(2,1)S(1)}, bf16[16,304]{1,0:T(8,128)(2,1)S(1)}, u32[]{:S(2)}, u32[]{:S(2)}) collective-permute-start(bf16[16,304]{1,0:T(8,128)(2,1)S(1)} %get-tuple-element.74), channel_id=1, source_target_pairs={{0,32},{32,64},{64,96},{96,128},{128,160},{160,192},{192,224},{1,3... | collective-permute-start | bytes 29192 | tf_op jit(solution)/shard_map/ppermute | solution.py:309
  100.7 15.3 %copy-start = (f32[304,1024]{1,0:T(8,128)}, f32[304,1024]{1,0:T(8,128)S(1)}, u32[]{:S(2)}) copy-start(f32[304,1024]{1,0:T(8,128)S(1)} %get-tuple-element.75.refs_0_.field.two) | copy-start | bytes 3735556
  100.7 15.2 %collective-permute-start.26 = (bf16[304,128]{1,0:T(8,128)(2,1)S(1)}, bf16[304,128]{1,0:T(8,128)(2,1)S(1)}, u32[]{:S(2)}, u32[]{:S(2)}) collective-permute-start(bf16[304,128]{1,0:T(8,128)(2,1)S(1)} %get-tuple-element.76), channel_id=1, source_target_pairs={{0,1},{1,2},{2,3},{3,4},{4,5},{5,6},{6,7},{7,8},{8,9},{9,10},{10,1... | collective-permute-start | bytes 233480 | tf_op jit(solution)/shard_map/ppermute | solution.py:309
  105.3 10.7 %collective-permute-start.27 = (bf16[304,128]{1,0:T(8,128)(2,1)S(1)}, bf16[304,128]{1,0:T(8,128)(2,1)S(1)}, u32[]{:S(2)}, u32[]{:S(2)}) collective-permute-start(bf16[304,128]{1,0:T(8,128)(2,1)S(1)} %get-tuple-element.77), channel_id=1, source_target_pairs={{1,0},{2,1},{3,2},{4,3},{5,4},{6,5},{7,6},{8,7},{9,8},{10,9},{11,1... | collective-permute-start | bytes 233480 | tf_op jit(solution)/shard_map/ppermute | solution.py:312
  106.6 9.3 %collective-permute-start.29 = (bf16[16,304]{1,0:T(8,128)(2,1)S(1)}, bf16[16,304]{1,0:T(8,128)(2,1)S(1)}, u32[]{:S(2)}, u32[]{:S(2)}) collective-permute-start(bf16[16,304]{1,0:T(8,128)(2,1)S(1)} %get-tuple-element.78), channel_id=1, source_target_pairs={{32,0},{64,32},{96,64},{128,96},{160,128},{192,160},{224,192},{33,... | collective-permute-start | bytes 29192 | tf_op jit(solution)/shard_map/ppermute | solution.py:312
  110.0 6.0 %collective-permute-start.28 = (bf16[16,304]{1,0:T(8,128)(2,1)S(1)}, bf16[16,304]{1,0:T(8,128)(2,1)S(1)}, u32[]{:S(2)}, u32[]{:S(2)}) collective-permute-start(bf16[16,304]{1,0:T(8,128)(2,1)S(1)} %get-tuple-element.78), channel_id=1, source_target_pairs={{0,32},{32,64},{64,96},{96,128},{128,160},{160,192},{192,224},{1,3... | collective-permute-start | bytes 29192 | tf_op jit(solution)/shard_map/ppermute | solution.py:309
  116.5 1.3 collective-permute-start.30
  117.8 3.6 %collective-permute-start.31 = (f32[8,128]{1,0:T(8,128)S(1)}, f32[8,128]{1,0:T(8,128)S(1)}, u32[]{:S(2)}, u32[]{:S(2)}) collective-permute-start(f32[8,128]{1,0:T(8,128)S(1)} %add.34), channel_id=1, source_target_pairs={{0,64},{32,96},{64,0},{96,32},{128,192},{160,224},{192,128},{224,1... | collective-permute-start | bytes 12296 | tf_op jit(solution)/shard_map/ppermute | solution.py:422
  121.4 5.1 %collective-permute-start.32 = (f32[8,128]{1,0:T(8,128)S(1)}, f32[8,128]{1,0:T(8,128)S(1)}, u32[]{:S(2)}, u32[]{:S(2)}) collective-permute-start(f32[8,128]{1,0:T(8,128)S(1)} %add.35), channel_id=1, source_target_pairs={{0,128},{32,160},{64,192},{96,224},{128,0},{160,32},{192,64},{224,... | collective-permute-start | bytes 12296 | tf_op jit(solution)/shard_map/ppermute | solution.py:422
  127.2 22.3 %all-to-all-start.2 = ((f32[32,1,8,128]{3,2,1,0:T(8,128)}), f32[32,1,8,128]{3,2,1,0:T(8,128)S(1)}, u32[]{:S(2)}, u32[]{:S(2)}) async-start(f32[32,1,8,128]{3,2,1,0:T(8,128)} %broadcast_in_dim.8), calls=%async_computation.2 | async-start | bytes 262144 | tf_op jit(solution)/shard_map/all_to_all | solution.py:300
  149.5 1.3 copy-start.1

commit v2 on v1

v2 whole, which is shorter than its diff:
```python
import jax
import jax.numpy as jnp
from jax import lax
from jax.experimental import pallas as pl
from jax.experimental.pallas import tpu as pltpu
from jax.sharding import PartitionSpec as P

DATES = 300
DP = 304
SHIFT = 4.0
SMOOTHING_WEIGHT = 0.5
RIDGE_WEIGHT = 0.05
CENTRE = 4.0 * SMOOTHING_WEIGHT + RIDGE_WEIGHT - SHIFT
F32 = jnp.float32
BF16 = jnp.bfloat16


def sds(shape, dtype):
    return jax.ShapeDtypeStruct(shape, dtype)


def call(body, outs, *args, specs=None, scratch=(), name=None):
    places = specs or [pltpu.VMEM] * len(args)
    return pl.pallas_call(
        body,
        out_shape=outs,
        in_specs=[pl.BlockSpec(memory_space=place) for place in places],
        scratch_shapes=list(scratch),
        name=name,
    )(*args)


def dot(a, b):
    return jnp.dot(a, b, preferred_element_type=F32)


def split(values):
    high = values.astype(BF16)
    return high, (values - high.astype(F32)).astype(BF16)


def fetch(step, phase, coher, phase_in, coher_in, sems):
    ifgs = pl.ds(step * 16, 16)
    return [
        pltpu.make_async_copy(source.at[ifgs], target.at[ifgs], sems.at[part, step])
        for part, (source, target) in enumerate(((phase, phase_in), (coher, coher_in)))
    ]


def rows_first(phase, coher, phase_t, coher_t, first, last, phase_in, coher_in, wide, sems):
    copies = [fetch(step, phase, coher, phase_in, coher_in, sems) for step in range(4)]
    for pair in copies:
        for copy in pair:
            copy.start()
    for block in range(4):
        for part, (source, target) in enumerate(((phase_in, phase_t), (coher_in, coher_t))):
            copies[block][part].wait()
            for tile in range(8):
                lanes = pl.ds(tile * 128, 128)
                wide[part, tile] = source[pl.ds(block * 16, 16), :, lanes].astype(F32).reshape(128, 128)
                for row in range(8):
                    piece = wide[part, tile, pl.ds(row, 16, stride=8), :].astype(BF16)
                    target[row, pl.ds(block * 16, 16), lanes] = piece
    for part, target in enumerate((phase_t, coher_t)):
        first[pl.ds(part * 64, 64), :] = target[0]
        last[pl.ds(part * 64, 64), :] = target[7]


def shifted_sum(values, lane, last):
    left = jnp.where(lane == 0, 0.0, pltpu.roll(values, 1, 1))
    right = jnp.where(lane == last, 0.0, pltpu.roll(values, last, 1))
    return values + left + right


def fold_lanes(values):
    total = values[:, :128]
    for tile in range(1, 8):
        total += values[:, tile * 128 : tile * 128 + 128]
    return total


def smoothing(flags, owners, phase_t, coher_t, above, below, mask, height, smooth, sums, *rest):
    outs, weights, totals = rest[:8], rest[8], rest[9]
    lane = lax.broadcasted_iota(jnp.int32, (16, 1024), 1)
    edge_flag = {-1: flags[0] > 0, 8: flags[1] > 0}

    def group(block, _):
        ifgs = pl.ds(pl.multiple_of(block * 16, 16), 16)
        cohers = pl.ds(pl.multiple_of(block * 16 + 64, 16), 16)
        masks = mask[ifgs, :]

        def load(row):
            if row < 0 or row > 7:
                edge = above if row < 0 else below
                coher = jnp.where(edge_flag[row], edge[cohers, :].astype(F32), 0.0)
                return coher, coher * edge[ifgs, :].astype(F32)
            coher = coher_t[row, ifgs, :].astype(F32)
            return coher, coher * phase_t[row, ifgs, :].astype(F32)

        before, current = load(-1), load(0)
        top = jnp.zeros((16, 128), F32)
        low = jnp.zeros((16, 128), F32)
        for row in range(8):
            after = load(row + 1)
            denom = shifted_sum(before[0] + current[0] + after[0], lane, 1023)
            numer = shifted_sum(before[1] + current[1] + after[1], lane, 1023)
            terrain = height[pl.ds(row, 1), :]
            top += fold_lanes(numer * terrain)
            low += fold_lanes(denom * (terrain * terrain))
            smooth[row, ifgs, :] = numer / denom
            weight = (masks[:, row : row + 1] * (denom / 9.0)).astype(BF16)
            for tile in range(8):
                weights[tile, ifgs, pl.ds(row * 128, 128)] = weight[:, tile * 128 : tile * 128 + 128]
            before, current = current, after
        totals[ifgs, :] = top
        totals[cohers, :] = low
        return 0

    lax.fori_loop(0, 4, group, 0)
    sums[...] = jnp.broadcast_to(jnp.sum(totals[...].T, axis=0)[None, None, :], sums.shape)
    pick_blocks(weights, owners, outs)


def pick_blocks(source, owners, outs):
    for step, out in enumerate(outs):
        out[...] = source[owners[step]]


def correction(owners, sums, smooth, height, slope_row, *rest):
    outs, blocks = rest[:8], rest[8]
    total = sums[0]
    for index in range(1, sums.shape[0]):
        total += sums[index]
    slope_row[...] = total / pltpu.roll(total, 64, 1)
    column = jnp.broadcast_to(total[0:1, :], (128, 128)).T
    slope = column[:64, :] / column[64:, :]
    for row in range(8):
        for tile in range(8):
            lanes = pl.ds(tile * 128, 128)
            value = smooth[row, :, lanes] - slope * height[pl.ds(row, 1), lanes]
            blocks[tile, :, pl.ds(row * 128, 128)] = value.astype(BF16)
    pick_blocks(blocks, owners, outs)


def column_selector():
    row = lax.broadcasted_iota(jnp.int32, (16, 1024), 0)
    pixel = lax.broadcasted_iota(jnp.int32, (16, 1024), 1)
    wanted = jnp.where(row < 8, row * 128, (row - 8) * 128 + 127)
    return (pixel == wanted).astype(BF16)


def write_edges(field, first, last, columns):
    first[...] = field[:, pl.ds(0, 128)].astype(BF16)
    last[...] = field[:, pl.ds(896, 128)].astype(BF16)
    picked = lax.dot_general(
        column_selector(), field[...].astype(BF16), (((1,), (1,)), ((), ())), preferred_element_type=F32
    )
    columns[...] = picked.astype(BF16)


def right_side(*refs):
    weight_parts, corrected_parts = refs[:8], refs[8:16]
    design_t, field, weights, first, last, columns = refs[16:]
    for part in range(8):
        weights[pl.ds(part * 64, 64), :] = weight_parts[part][...]
    for chunk in range(4):
        lanes = pl.ds(chunk * 256, 256)
        total = jnp.zeros((DP, 256), F32)
        scaled = jnp.concatenate(
            [
                weight_parts[part][:, lanes].astype(F32) * corrected_parts[part][:, lanes].astype(F32)
                for part in range(8)
            ],
            axis=0,
        )
        high, low = split(scaled)
        field[:, lanes] = dot(design_t[...], high) + dot(design_t[...], low)
    write_edges(field, first, last, columns)


def local_image(field, weights, design, design_t, chunk):
    lanes = pl.ds(chunk * 256, 256)
    high, low = split(field[:, lanes])
    scaled = (dot(design[...], high) + dot(design[...], low)) * weights[:, lanes].astype(F32)
    high, low = split(scaled)
    back = dot(design_t[...], high) + dot(design_t[...], low)
    lane = lax.broadcasted_iota(jnp.int32, (DP, 128), 1)
    parts = []
    for row in (2 * chunk, 2 * chunk + 1):
        here = field[:, pl.ds(row * 128, 128)]
        around = jnp.where(lane == 0, 0.0, pltpu.roll(here, 1, 1))
        around += jnp.where(lane == 127, 0.0, pltpu.roll(here, 127, 1))
        if row > 0:
            around += field[:, pl.ds((row - 1) * 128, 128)]
        if row < 7:
            around += field[:, pl.ds((row + 1) * 128, 128)]
        start = (row - 2 * chunk) * 128
        parts.append(back[:, start : start + 128] + CENTRE * here - SMOOTHING_WEIGHT * around)
    return parts


def fold(values):
    return jnp.sum(values.reshape(DP // 8, 8, 128), axis=0)


def apply_local(with_before, with_image, *refs):
    field, weights, design, design_t = refs[:4]
    refs = refs[4:]
    before = None
    if with_before:
        before, refs = refs[0], refs[1:]
    image = None
    if with_image:
        image, refs = refs[0], refs[1:]
    moments = refs[0]
    square = jnp.zeros((8, 128), F32)
    cross = jnp.zeros((8, 128), F32)
    ahead = jnp.zeros((8, 128), F32)
    for chunk in range(4):
        parts = local_image(field, weights, design, design_t, chunk)
        for offset, part in enumerate(parts):
            lanes = pl.ds((2 * chunk + offset) * 128, 128)
            here = field[:, lanes]
            square += fold(here * here)
            if with_before:
                cross += fold(here * before[:, lanes])
            if with_image:
                image[:, lanes] = part
            else:
                ahead += fold(here * part)
    moments[0] = square
    moments[1] = cross
    moments[2] = ahead


def spread_columns(columns, pixels):
    row = lax.broadcasted_iota(jnp.int32, (16, 128), 0)
    lane = lax.broadcasted_iota(jnp.int32, (16, 128), 1)
    wanted = jnp.where(row < 8, row, row - 8) == pixels
    place = (wanted & (lane == jnp.where(row < 8, 0, 127))).astype(BF16)
    return lax.dot_general(columns, place, (((0,), (0,)), ((), ())), preferred_element_type=F32)


def keep(flag, values):
    return jnp.where(flag > 0, values.astype(F32), 0.0)


def add_halo(flags, image, above, below, left, right, field, first, last, columns):
    sides = jnp.concatenate([keep(flags[2], left[8:16, :]), keep(flags[3], right[0:8, :])], axis=0).astype(BF16)
    for row in range(8):
        lanes = pl.ds(row * 128, 128)
        halo = spread_columns(sides, row)
        if row == 0:
            halo += keep(flags[0], above[...])
        if row == 7:
            halo += keep(flags[1], below[...])
        field[:, lanes] = image[:, lanes] - SMOOTHING_WEIGHT * halo
    write_edges(field, first, last, columns)


def all_moments(flags, field, above, left, zero, one, two, out):
    sides = jnp.concatenate([keep(flags[2], left[8:16, :]), jnp.zeros((8, DP), F32)], axis=0).astype(BF16)
    ahead = two[2]
    for row in range(8):
        halo = spread_columns(sides, row)
        if row == 0:
            halo += keep(flags[0], above[...])
        ahead -= (2.0 * SMOOTHING_WEIGHT) * fold(field[:, pl.ds(row * 128, 128)] * halo)
    rows = [zero[0], one[1], one[0], two[1], two[0], ahead]
    sums = [jnp.sum(values, axis=0, keepdims=True) for values in rows]
    out[...] = jnp.concatenate(sums + [jnp.zeros((2, 128), F32)], axis=0)


def combine(parts, zero, one, two, out):
    total = parts[0]
    for index in range(1, parts.shape[0]):
        total += parts[index]
    sums = jnp.sum(total, axis=1, keepdims=True)
    m0, m1, m2, m3, m4, m5 = (jnp.broadcast_to(sums[i : i + 1, :], (1, 128)) for i in range(6))
    t00, t01, t11 = m1 + SHIFT * m0, m2 + SHIFT * m1, m3 + SHIFT * m2
    t12, t22 = m4 + SHIFT * m3, m5 + SHIFT * m4
    l10, l20 = t01 / t00, t11 / t00
    pivot = t11 - l10 * t01
    off = t12 - l20 * t01
    keep = pivot > 1e-6 * t11
    safe = jnp.where(keep, pivot, 1.0)
    l21 = jnp.where(keep, off / safe, 0.0)
    last = t22 - l20 * t11 - l21 * off
    keep_last = keep & (last > 1e-6 * t22)
    y1 = m1 - l10 * m0
    y2 = m2 - l20 * m0 - l21 * y1
    c2 = jnp.where(keep_last, y2 / jnp.where(keep_last, last, 1.0), 0.0)
    c1 = jnp.where(keep, y1 / safe, 0.0) - l21 * c2
    c0 = m0 / t00 - l10 * c1 - l20 * c2
    for row in range(8):
        lanes = pl.ds(row * 128, 128)
        value = c0 * zero[:, lanes] + c1 * one[:, lanes] + c2 * two[:, lanes]
        out[pl.ds(row, DATES, stride=8), :] = value[:DATES, :]


def per_device(phase, coherence, height, gap_mask, date_pairs):
    n_ifg, n_rows = lax.axis_size("ifg"), lax.axis_size("rows")
    n_chip = n_ifg // 2
    me, my_row = lax.axis_index("ifg"), lax.axis_index("rows")
    offsets = ((0, 0), (1, 0), (3, 0), (2, 0), (2, 1), (1, 1), (3, 1), (0, 1))

    def other(index, chips, core):
        return (index // 2 + chips) % n_chip * 2 + (index + core) % 2

    owners = jnp.stack([other(me, *offset) for offset in offsets]).astype(jnp.int32)
    flags = jnp.stack([my_row > 0, my_row < n_rows - 1, me > 0, me < n_ifg - 1]).astype(jnp.int32)

    def permute(values, axis, target):
        return lax.ppermute(values, axis, [(i, target(i)) for i in range(lax.axis_size(axis))])

    def forward(values, axis):
        return permute(values, axis, lambda i: (i + 1) % lax.axis_size(axis))

    def backward(values, axis):
        return permute(values, axis, lambda i: (i - 1) % lax.axis_size(axis))

    stacked = sds((8, 64, 1024), BF16)
    edge = sds((128, 1024), BF16)
    phase_t, coher_t, first, last = call(
        rows_first,
        (stacked, stacked, edge, edge),
        phase,
        coherence,
        specs=[pltpu.HBM] * 2,
        scratch=(
            pltpu.VMEM((64, 8, 1024), BF16),
            pltpu.VMEM((64, 8, 1024), BF16),
            pltpu.VMEM((2, 8, 128, 128), F32),
            pltpu.SemaphoreType.DMA((2, 4)),
        ),
        name="rows_first",
    )
    above, below = forward(last, "rows"), backward(first, "rows")
    block = sds((64, 1024), BF16)
    smooth, sums, *weight_parts = call(
        smoothing,
        [sds((8, 64, 1024), F32), sds((n_rows, 8, 128), F32)] + [block] * 8,
        flags,
        owners,
        phase_t,
        coher_t,
        above,
        below,
        gap_mask.astype(F32),
        height,
        specs=[pltpu.SMEM] * 2 + [pltpu.VMEM] * 6,
        scratch=(pltpu.VMEM((8, 64, 1024), BF16), pltpu.VMEM((128, 128), F32)),
        name="smoothing",
    )
    sums = lax.all_to_all(sums, "rows", 0, 0, tiled=True)

    def exchange(parts):
        return [parts[0]] + [
            permute(part, "ifg", lambda i: other(i, *offset))
            for part, offset in zip(parts[1:], offsets[1:])
        ]

    weight_parts = exchange(weight_parts)
    slope_row, *corrected_parts = call(
        correction,
        [sds((8, 128), F32)] + [block] * 8,
        owners,
        sums,
        smooth,
        height,
        specs=[pltpu.SMEM] + [pltpu.VMEM] * 3,
        scratch=(pltpu.VMEM((8, 64, 1024), BF16),),
        name="correction",
    )
    corrected_parts = exchange(corrected_parts)
    sources = jnp.stack([other(me, -chips, core) for chips, core in offsets])
    pairs = date_pairs.reshape(n_ifg, -1, 2)[sources].reshape(-1, 2)
    dates = jnp.arange(DP, dtype=jnp.int32)
    design = ((dates[None] == pairs[:, 1:2]).astype(F32) - (dates[None] == pairs[:, 0:1]).astype(F32)).astype(BF16)
    design_t = design.T

    field = sds((DP, 1024), F32)
    edges = (sds((DP, 128), BF16), sds((DP, 128), BF16), sds((16, DP), BF16))
    moments = sds((3, 8, 128), F32)
    k0, weights, first, last, columns = call(
        right_side,
        (field, sds((512, 1024), BF16)) + edges,
        *weight_parts,
        *corrected_parts,
        design_t,
        name="right_side",
    )

    def halos(first, last, columns):
        return (
            forward(last, "rows"),
            backward(first, "rows"),
            forward(columns, "ifg"),
            backward(columns, "ifg"),
        )

    def local(with_before, with_image, name, *args):
        outs = ((field,) if with_image else ()) + (moments,)
        body = lambda *refs: apply_local(with_before, with_image, *refs)
        return call(body, outs, *args, name=name)

    def joined(image, around, name):
        specs = [pltpu.SMEM] + [pltpu.VMEM] * 5
        return call(add_halo, (field,) + edges, flags, image, *around, specs=specs, name=name)

    around = halos(first, last, columns)
    image, mom0 = local(False, True, "apply0", k0, weights, design, design_t)
    k1, first, last, columns = joined(image, around, "add_halo1")
    around = halos(first, last, columns)
    image, mom1 = local(True, True, "apply1", k1, weights, design, design_t, k0)
    k2, first, last, columns = joined(image, around, "add_halo2")
    above, left = forward(last, "rows"), forward(columns, "ifg")
    (mom2,) = local(True, False, "apply2", k2, weights, design, design_t, k1)
    part = call(
        all_moments,
        sds((8, 128), F32),
        flags,
        k2,
        above,
        left,
        mom0,
        mom1,
        mom2,
        specs=[pltpu.SMEM] + [pltpu.VMEM] * 6,
        name="all_moments",
    )
    for target in (lambda i: i ^ 1, lambda i: i ^ 2, lambda i: i ^ 4):
        part = part + permute(part, "ifg", target)
    part = jnp.broadcast_to(part[None], (n_rows, 8, 128))
    parts = lax.all_to_all(part, "rows", 0, 0, tiled=True)
    displacement = call(combine, sds((DATES * 8, 128), F32), parts, k0, k1, k2, name="combine")
    return displacement.reshape(DATES, 8, 128), slope_row[0, :64]


def solution(mesh):
    placed = (
        P("ifg", "rows", None),
        P("ifg", "rows", None),
        P("rows", None),
        P("ifg", "rows"),
        P(),
    )
    return jax.shard_map(
        per_device,
        mesh=mesh,
        in_specs=placed,
        out_specs=(P(None, "rows", "ifg"), P("ifg")),
        check_vma=False,
    )
```

time: 155 us -> 151 us (0.974); the launches traced: 153 us -> 151 us
  starting transfers between devices: 88.4 us -> 55 us
  Pallas kernels: 22.1 us -> 49.8 us
  other arithmetic: 0.41 us -> 3.12 us
  waiting for transfers between devices: 30.8 us -> 33.3 us
    pallas_call x13 -> x11, Pallas kernels: 22.1 us -> 49.8 us  [call(): pl.pallas_call(body, out_shape=outs, in_specs=[pl.BlockSpec(memory_space=...]
    ppermute x33 -> x29, starting transfers between devices: 61.2 us -> 41.5 us  [permute(): lax.ppermute(values, axis, [(i, target(i)) for i in range(lax.axis_size(a...]
    all_to_all x3 -> x2, starting transfers between devices: 27.2 us -> 13.5 us  [the longest x1 6.74 us: per_device(): sums = lax.all_to_all(sums, 'rows', 0, 0, tiled=True)]
    ppermute x33 -> x29, waiting for transfers between devices: 18 us -> 21.5 us  [permute(): lax.ppermute(values, axis, [(i, target(i)) for i in range(lax.axis_size(a...]
    unnamed x18 -> x64, local copies, waits for them, and re-layouts: 6.68 us -> 4.63 us
    all_to_all x3 -> x2, waiting for transfers between devices: 12.8 us -> 11.8 us  [the longest x1 9.2 us: per_device(): parts = lax.all_to_all(part, 'rows', 0, 0, tiled=True)]
  transfers between devices with their start and end apart: 36 -> 31, of which waited for: 11 -> 10; matrix products, arithmetic and copies ran while one was open for 2% -> 4% of each run, Pallas kernels for 10% -> 16%
where the time goes in v2:
time: 151 us
  starting transfers between devices  55 us (36%)
  Pallas kernels  49.8 us (33%)
  waiting for transfers between devices  33.3 us (22%)
  local copies, waits for them, and re-layouts  8.65 us (6%)
  other arithmetic  3.12 us (2%)
    pallas_call x11, Pallas kernels, call(): pl.pallas_call(body, out_shape=outs, in_specs=[pl.BlockSpec(memory_space=...  49.8 us
    ppermute x29, starting transfers between devices, permute(): lax.ppermute(values, axis, [(i, target(i)) for i in range(lax.axis_size(a...  41.5 us
    ppermute x29, waiting for transfers between devices, permute(): lax.ppermute(values, axis, [(i, target(i)) for i in range(lax.axis_size(a...  21.5 us
    all_to_all x1, waiting for transfers between devices, per_device(): parts = lax.all_to_all(part, 'rows', 0, 0, tiled=True)  9.2 us
    all_to_all x1, starting transfers between devices, per_device(): sums = lax.all_to_all(sums, 'rows', 0, 0, tiled=True)  6.74 us
    all_to_all x1, starting transfers between devices, per_device(): parts = lax.all_to_all(part, 'rows', 0, 0, tiled=True)  6.72 us
    unnamed x64, local copies, waits for them, and re-layouts  4.63 us
  transfers between devices with their start and end apart: 31, of which 10 were waited for; matrix products, arithmetic and copies ran while one was open for 4% of the time, Pallas kernels for 16%

profile of v2, /device:TPU:6, one launch (start us, length us, event | category | flops | bytes accessed | tf_op | source)
XLA Modules:
  0.0 150.8 jit_solution(2505188952021978454)
XLA Ops:
  0.6 3.5 %rows_first.1 = (bf16[8,64,1024]{2,1,0:T(8,128)(2,1)}, bf16[8,64,1024]{2,1,0:T(8,128)(2,1)}, bf16[128,1024]{1,0:T(8,128)(2,1)}, bf16[128,1024]{1,0:T(8,128)(2,1)}) custom-call(bf16[64,8,1024]{2,1,0:T(8,128)(2,1)} %phase.1, bf16[64,8,1024]{2,1,0:T(8,128)(2,1)} %coher.1), custom_call_target="tpu_custom_call" | custom-call | tf_op jit(solution)/shard_map/rows_first/pallas_call | solution.py:24
  4.1 2.0 %collective-permute-start = (bf16[128,1024]{1,0:T(8,128)(2,1)}, bf16[128,1024]{1,0:T(8,128)(2,1)S(1)}, u32[]{:S(2)}, u32[]{:S(2)}) collective-permute-start(bf16[128,1024]{1,0:T(8,128)(2,1)} %get-tuple-element.43), channel_id=1, source_target_pairs={{0,1},{1,2},{2,3},{3,4},{4,5},{5,6},{6,7},{7,8},{8,9},{9,10},{10,1... | collective-permute-start | bytes 786440 | tf_op jit(solution)/shard_map/ppermute | solution.py:314
  6.1 6.5 %collective-permute-start.1 = (bf16[128,1024]{1,0:T(8,128)(2,1)}, bf16[128,1024]{1,0:T(8,128)(2,1)S(1)}, u32[]{:S(2)}, u32[]{:S(2)}) collective-permute-start(bf16[128,1024]{1,0:T(8,128)(2,1)} %get-tuple-element.44), channel_id=1, source_target_pairs={{0,31},{1,0},{2,1},{3,2},{4,3},{5,4},{6,5},{7,6},{8,7},{9,8},{10,9... | collective-permute-start | bytes 786440 | tf_op jit(solution)/shard_map/ppermute | solution.py:314
  12.6 0.7 copy.12.mask
  13.3 0.6 stack.82.owners
  14.0 0.6 add_convert_fusion.flags
  14.6 4.4 %collective-permute-done.above = bf16[128,1024]{1,0:T(8,128)(2,1)S(1)} collective-permute-done((bf16[128,1024]{1,0:T(8,128)(2,1)}, bf16[128,1024]{1,0:T(8,128)(2,1)S(1)}, u32[]{:S(2)}, u32[]{:S(2)}) %collective-permute-start) | collective-permute-done | bytes 262176 | tf_op jit(solution)/shard_map/ppermute | solution.py:314
  19.0 0.7 copy-done.2
  19.8 6.2 %smoothing.1 = (f32[8,64,1024]{2,1,0:T(8,128)}, f32[32,8,128]{2,1,0:T(8,128)}, bf16[64,1024]{1,0:T(8,128)(2,1)}, bf16[64,1024]{1,0:T(8,128)(2,1)}, bf16[64,1024]...) custom-call(s32[4]{0:T(128)} %add_convert_fusion.flags, ...), custom_call_target="tpu_custom_call" | custom-call | tf_op jit(solution)/shard_map/smoothing/pallas_call | solution.py:24
  26.0 6.7 %all-to-all-start = ((f32[32,8,128]{2,1,0:T(8,128)}), f32[32,8,128]{2,1,0:T(8,128)S(1)}, u32[]{:S(2)}, u32[]{:S(2)}) async-start(f32[32,8,128]{2,1,0:T(8,128)} %get-tuple-element.53), calls=%async_computation | async-start | bytes 262144 | tf_op jit(solution)/shard_map/all_to_all | solution.py:355
  33.3 1.5 %collective-permute-start.3 = (bf16[64,1024]{1,0:T(8,128)(2,1)}, bf16[64,1024]{1,0:T(8,128)(2,1)S(1)}, u32[]{:S(2)}, u32[]{:S(2)}) collective-permute-start(bf16[64,1024]{1,0:T(8,128)(2,1)} %get-tuple-element.47), channel_id=1, source_target_pairs={{0,192},{32,224},{64,0},{96,32},{128,64},{160,96},{192,128},{224,1... | collective-permute-start | bytes 393224 | tf_op jit(solution)/shard_map/ppermute | solution.py:314
  34.9 1.4 collective-permute-start.4
  36.4 0.6 gather_fusion
  37.1 3.5 %collective-permute-start.6 = (bf16[64,1024]{1,0:T(8,128)(2,1)}, bf16[64,1024]{1,0:T(8,128)(2,1)S(1)}, u32[]{:S(2)}, u32[]{:S(2)}) collective-permute-start(bf16[64,1024]{1,0:T(8,128)(2,1)} %get-tuple-element.50), channel_id=1, source_target_pairs={{0,96},{32,64},{64,160},{96,128},{128,224},{160,192},{192,32},{224... | collective-permute-start | bytes 393224 | tf_op jit(solution)/shard_map/ppermute | solution.py:314
  40.6 2.5 %all-to-all-done.sums = f32[32,8,128]{2,1,0:T(8,128)S(1)} async-done(((f32[32,8,128]{2,1,0:T(8,128)}), f32[32,8,128]{2,1,0:T(8,128)S(1)}, u32[]{:S(2)}, u32[]{:S(2)}) %all-to-all-start) | async-done | bytes 131104 | tf_op jit(solution)/shard_map/all_to_all | solution.py:355
  43.1 0.7 copy-done
  43.8 3.1 %correction.1 = (f32[8,128]{1,0:T(8,128)}, bf16[64,1024]{1,0:T(8,128)(2,1)}, bf16[64,1024]{1,0:T(8,128)(2,1)}, bf16[64,1024]{1,0:T(8,128)(2,1)}, bf16[64,1024]{1...) custom-call(s32[8]{0:T(128)} %stack.82.owners, ...), custom_call_target="tpu_custom_call" | custom-call | tf_op jit(solution)/shard_map/correction/pallas_call | solution.py:24
  47.0 1.0 collective-permute-start.8
  48.0 2.4 %collective-permute-start.9 = (bf16[64,1024]{1,0:T(8,128)(2,1)}, bf16[64,1024]{1,0:T(8,128)(2,1)S(1)}, u32[]{:S(2)}, u32[]{:S(2)}) collective-permute-start(bf16[64,1024]{1,0:T(8,128)(2,1)} %get-tuple-element.56), channel_id=1, source_target_pairs={{0,64},{32,96},{64,128},{96,160},{128,192},{160,224},{192,0},{224,... | collective-permute-start | bytes 393224 | tf_op jit(solution)/shard_map/ppermute | solution.py:314
  50.4 1.6 %collective-permute-start.11 = (bf16[64,1024]{1,0:T(8,128)(2,1)}, bf16[64,1024]{1,0:T(8,128)(2,1)S(1)}, u32[]{:S(2)}, u32[]{:S(2)}) collective-permute-start(bf16[64,1024]{1,0:T(8,128)(2,1)} %get-tuple-element.58), channel_id=1, source_target_pairs={{0,128},{32,160},{64,192},{96,224},{128,0},{160,32},{192,64},{224,... | collective-permute-start | bytes 393224 | tf_op jit(solution)/shard_map/ppermute | solution.py:314
  52.6 1.4 collective-permute-start.12
  53.9 3.1 %collective-permute-start.13 = (bf16[64,1024]{1,0:T(8,128)(2,1)}, bf16[64,1024]{1,0:T(8,128)(2,1)S(1)}, u32[]{:S(2)}, u32[]{:S(2)}) collective-permute-start(bf16[64,1024]{1,0:T(8,128)(2,1)} %get-tuple-element.60), channel_id=1, source_target_pairs={{0,96},{32,64},{64,160},{96,128},{128,224},{160,192},{192,32},{224... | collective-permute-start | bytes 393224 | tf_op jit(solution)/shard_map/ppermute | solution.py:314
  57.0 6.5 %collective-permute-done.10.refs_10_ = bf16[64,1024]{1,0:T(8,128)(2,1)S(1)} collective-permute-done((bf16[64,1024]{1,0:T(8,128)(2,1)}, bf16[64,1024]{1,0:T(8,128)(2,1)S(1)}, u32[]{:S(2)}, u32[]{:S(2)}) %collective-permute-start.10) | collective-permute-done | bytes 131104 | tf_op jit(solution)/shard_map/ppermute | solution.py:314
  63.5 0.9 subtract_convert_fusion.1.refs_16_.refs_3_
  65.7 4.1 %right_side.1 = (f32[304,1024]{1,0:T(8,128)}, bf16[512,1024]{1,0:T(8,128)(2,1)}, bf16[304,128]{1,0:T(8,128)(2,1)}, bf16[304,128]{1,0:T(8,128)(2,1)}, bf16[16,304]{1,0:T(8,128)(2,1)}) custom-call(bf16[64,1024]{1,0:T(8,128)(2,1)} %get-tuple-element.45.refs_0_, bf16[64,1024]{1,0:T(8,128)(2,1)} %copy-done.4, bf16[64,1024]{1,0:T(8,128)(2,1)} %copy-done.5, ...), custom_call_target="tpu_custom_call" | custom-call | tf_op jit(solution)/shard_map/right_side/pallas_call | solution.py:24
  70.3 1.1 collective-permute-start.16
  71.4 4.3 %collective-permute-start.17 = (bf16[304,128]{1,0:T(8,128)(2,1)}, bf16[304,128]{1,0:T(8,128)(2,1)S(1)}, u32[]{:S(2)}, u32[]{:S(2)}) collective-permute-start(bf16[304,128]{1,0:T(8,128)(2,1)} %get-tuple-element.67), channel_id=1, source_target_pairs={{0,31},{1,0},{2,1},{3,2},{4,3},{5,4},{6,5},{7,6},{8,7},{9,8},{10,9... | collective-permute-start | bytes 233480 | tf_op jit(solution)/shard_map/ppermute | solution.py:314
  75.7 1.0 subtract_convert_fusion.refs_2_
  76.6 6.6 %apply0.1 = (f32[304,1024]{1,0:T(8,128)}, f32[3,8,128]{2,1,0:T(8,128)}) custom-call(f32[304,1024]{1,0:T(8,128)} %get-tuple-element.63.refs_0_.refs_4_.zero, bf16[512,1024]{1,0:T(8,128)(2,1)} %get-tuple-element.64.refs_1_, bf16[512,304]{1,0:T(8,128)(2,1)} %subtract_convert_fusion.refs_2_, bf16[304,512]{1,0:T(8,128)(2,1)} %subtract_convert_fusion.1.refs_16_.refs_3_), custom_call_target="tpu_custom_call" | custom-call | tf_op jit(solution)/shard_map/apply0/pallas_call | solution.py:24
  84.0 3.0 %add_halo1.1 = (f32[304,1024]{1,0:T(8,128)}, bf16[304,128]{1,0:T(8,128)(2,1)}, bf16[304,128]{1,0:T(8,128)(2,1)}, bf16[16,304]{1,0:T(8,128)(2,1)}) custom-call(s32[4]{0:T(128)} %add_convert_fusion.flags, f32[304,1024]{1,0:T(8,128)} %get-tuple-element.65.image, bf16[304,128]{1,0:T(8,128)(2,1)} %copy-done.20, bf16[304,128]{1,0:T(8,128)(2,1)} %copy-done.22, ...), custom_call_target="tpu_custom_call" | custom-call | tf_op jit(solution)/shard_map/add_halo1/pallas_call | solution.py:24
  87.0 5.3 %collective-permute-start.21 = (bf16[304,128]{1,0:T(8,128)(2,1)}, bf16[304,128]{1,0:T(8,128)(2,1)S(1)}, u32[]{:S(2)}, u32[]{:S(2)}) collective-permute-start(bf16[304,128]{1,0:T(8,128)(2,1)} %get-tuple-element.72), channel_id=1, source_target_pairs={{0,31},{1,0},{2,1},{3,2},{4,3},{5,4},{6,5},{7,6},{8,7},{9,8},{10,9... | collective-permute-start | bytes 233480 | tf_op jit(solution)/shard_map/ppermute | solution.py:314
  92.5 1.5 collective-permute-start.22
  94.0 7.1 %apply1.1 = (f32[304,1024]{1,0:T(8,128)}, f32[3,8,128]{2,1,0:T(8,128)}) custom-call(f32[304,1024]{1,0:T(8,128)} %get-tuple-element.69.refs_0_.refs_4_.one, bf16[512,1024]{1,0:T(8,128)(2,1)} %get-tuple-element.64.refs_1_, bf16[512,304]{1,0:T(8,128)(2,1)} %subtract_convert_fusion.refs_2_, bf16[304,512]{1,0:T(8,128)(2,1)} %subtract_convert_fusion.1.refs_16_.refs_3_, ...), custom_call_target="tpu_custom_call" | custom-call | tf_op jit(solution)/shard_map/apply1/pallas_call | solution.py:24
  101.8 3.0 %add_halo2.1 = (f32[304,1024]{1,0:T(8,128)}, bf16[304,128]{1,0:T(8,128)(2,1)}, bf16[304,128]{1,0:T(8,128)(2,1)}, bf16[16,304]{1,0:T(8,128)(2,1)}) custom-call(s32[4]{0:T(128)} %add_convert_fusion.flags, f32[304,1024]{1,0:T(8,128)} %get-tuple-element.70.image, bf16[304,128]{1,0:T(8,128)(2,1)} %copy-done.19, bf16[304,128]{1,0:T(8,128)(2,1)} %copy-done.21, ...), custom_call_target="tpu_custom_call" | custom-call | tf_op jit(solution)/shard_map/add_halo2/pallas_call | solution.py:24
  104.8 3.0 %collective-permute-start.25 = (bf16[16,304]{1,0:T(8,128)(2,1)}, bf16[16,304]{1,0:T(8,128)(2,1)S(1)}, u32[]{:S(2)}, u32[]{:S(2)}) collective-permute-start(bf16[16,304]{1,0:T(8,128)(2,1)} %get-tuple-element.76), channel_id=1, source_target_pairs={{0,32},{32,64},{64,96},{96,128},{128,160},{160,192},{192,224},{224... | collective-permute-start | bytes 29192 | tf_op jit(solution)/shard_map/ppermute | solution.py:314
  107.8 6.7 %apply2.1.two = f32[3,8,128]{2,1,0:T(8,128)} custom-call(f32[304,1024]{1,0:T(8,128)} %get-tuple-element.74.refs_0_.field.two, bf16[512,1024]{1,0:T(8,128)(2,1)} %get-tuple-element.64.refs_1_, bf16[512,304]{1,0:T(8,128)(2,1)} %subtract_convert_fusion.refs_2_, bf16[304,512]{1,0:T(8,128)(2,1)} %subtract_convert_fusion.1.refs_16_.refs_3_, ...), custom_call_target="tpu_custom_call" | custom-call | tf_op jit(solution)/shard_map/apply2/pallas_call | solution.py:24
  114.5 0.6 copy-done.23
  115.1 2.5 %all_moments.1 = f32[8,128]{1,0:T(8,128)} custom-call(s32[4]{0:T(128)} %add_convert_fusion.flags, f32[304,1024]{1,0:T(8,128)} %get-tuple-element.74.refs_0_.field.two, bf16[304,128]{1,0:T(8,128)(2,1)} %copy-done.18, bf16[16,304]{1,0:T(8,128)(2,1)} %copy-done.23, f32[3,8,128]{2,1,0:T(8,128)} %get-tuple-element.77.zero, f32[3,8,128]{2,1,0:T(8,128)} %get-tuple-element.78.one, ...), custom_call_target="tpu_custom_call" | custom-call | tf_op jit(solution)/shard_map/all_moments/pallas_call | solution.py:24
  117.6 1.3 collective-permute-done.26
  118.9 0.7 add.180
  119.6 3.6 %collective-permute-done.27 = f32[8,128]{1,0:T(8,128)S(1)} collective-permute-done((f32[8,128]{1,0:T(8,128)S(1)}, f32[8,128]{1,0:T(8,128)S(1)}, u32[]{:S(2)}, u32[]{:S(2)}) %collective-permute-start.27) | collective-permute-done | bytes 4128 | tf_op jit(solution)/shard_map/ppermute | solution.py:314
  123.8 4.6 %collective-permute-done.28 = f32[8,128]{1,0:T(8,128)S(1)} collective-permute-done((f32[8,128]{1,0:T(8,128)S(1)}, f32[8,128]{1,0:T(8,128)S(1)}, u32[]{:S(2)}, u32[]{:S(2)}) %collective-permute-start.28) | collective-permute-done | bytes 4128 | tf_op jit(solution)/shard_map/ppermute | solution.py:314
  128.3 0.7 broadcast_in_dim.2
  129.0 6.7 %all-to-all-start.1 = ((f32[32,8,128]{2,1,0:T(8,128)}), f32[32,8,128]{2,1,0:T(8,128)S(1)}, u32[]{:S(2)}, u32[]{:S(2)}) async-start(f32[32,8,128]{2,1,0:T(8,128)} %broadcast_in_dim.2), calls=%async_computation.1 | async-start | bytes 262144 | tf_op jit(solution)/shard_map/all_to_all | solution.py:435
  135.7 1.2 slice_bitcast_fusion
  136.9 9.2 %all-to-all-done.1.parts = f32[32,8,128]{2,1,0:T(8,128)S(1)} async-done(((f32[32,8,128]{2,1,0:T(8,128)}), f32[32,8,128]{2,1,0:T(8,128)S(1)}, u32[]{:S(2)}, u32[]{:S(2)}) %all-to-all-start.1) | async-done | bytes 131104 | tf_op jit(solution)/shard_map/all_to_all | solution.py:435
  146.1 0.6 copy-done.1
  146.8 4.0 %combine.1 = f32[2400,128]{1,0:T(8,128)} custom-call(f32[32,8,128]{2,1,0:T(8,128)} %copy-done.1, f32[304,1024]{1,0:T(8,128)} %get-tuple-element.63.refs_0_.refs_4_.zero, f32[304,1024]{1,0:T(8,128)} %get-tuple-element.69.refs_0_.refs_4_.one, f32[304,1024]{1,0:T(8,128)} %get-tuple-element.74.refs_0_.field.two), custom_call_target="tpu_custom_call" | custom-call | tf_op jit(solution)/shard_map/combine/pallas_call | solution.py:24
  (109 shorter events, 5.4 us)
Async XLA Ops:
  0.6 11.9 %copy-start.29 = (s32[64,8]{0,1:T(8,128)S(1)}, s32[64,8]{0,1:T(8,128)}, u32[]{:S(2)}) copy-start(s32[64,8]{0,1:T(8,128)} %param.8) | copy-start | bytes 6148
  4.1 14.9 %collective-permute-start = (bf16[128,1024]{1,0:T(8,128)(2,1)}, bf16[128,1024]{1,0:T(8,128)(2,1)S(1)}, u32[]{:S(2)}, u32[]{:S(2)}) collective-permute-start(bf16[128,1024]{1,0:T(8,128)(2,1)} %get-tuple-element.43), channel_id=1, source_target_pairs={{0,1},{1,2},{2,3},{3,4},{4,5},{5,6},{6,7},{7,8},{8,9},{9,10},{10,1... | collective-permute-start | bytes 786440 | tf_op jit(solution)/shard_map/ppermute | solution.py:314
  6.1 12.9 %collective-permute-start.1 = (bf16[128,1024]{1,0:T(8,128)(2,1)}, bf16[128,1024]{1,0:T(8,128)(2,1)S(1)}, u32[]{:S(2)}, u32[]{:S(2)}) collective-permute-start(bf16[128,1024]{1,0:T(8,128)(2,1)} %get-tuple-element.44), channel_id=1, source_target_pairs={{0,31},{1,0},{2,1},{3,2},{4,3},{5,4},{6,5},{7,6},{8,7},{9,8},{10,9... | collective-permute-start | bytes 786440 | tf_op jit(solution)/shard_map/ppermute | solution.py:314
  19.0 0.8 copy-start.3
  19.8 16.5 %copy-start.28 = (s32[512,2]{0,1:T(2,128)S(1)}, s32[512,2]{0,1:T(2,128)}, u32[]{:S(2)}) copy-start(s32[512,2]{0,1:T(2,128)} %param.9) | copy-start | bytes 12292
  26.0 17.1 %all-to-all-start = ((f32[32,8,128]{2,1,0:T(8,128)}), f32[32,8,128]{2,1,0:T(8,128)S(1)}, u32[]{:S(2)}, u32[]{:S(2)}) async-start(f32[32,8,128]{2,1,0:T(8,128)} %get-tuple-element.53), calls=%async_computation | async-start | bytes 262144 | tf_op jit(solution)/shard_map/all_to_all | solution.py:355
  32.8 14.1 %collective-permute-start.2 = (bf16[64,1024]{1,0:T(8,128)(2,1)}, bf16[64,1024]{1,0:T(8,128)(2,1)S(1)}, u32[]{:S(2)}, u32[]{:S(2)}) collective-permute-start(bf16[64,1024]{1,0:T(8,128)(2,1)} %get-tuple-element.46), channel_id=1, source_target_pairs={{0,64},{32,96},{64,128},{96,160},{128,192},{160,224},{192,0},{224,... | collective-permute-start | bytes 393224 | tf_op jit(solution)/shard_map/ppermute | solution.py:314
  33.3 13.7 %collective-permute-start.3 = (bf16[64,1024]{1,0:T(8,128)(2,1)}, bf16[64,1024]{1,0:T(8,128)(2,1)S(1)}, u32[]{:S(2)}, u32[]{:S(2)}) collective-permute-start(bf16[64,1024]{1,0:T(8,128)(2,1)} %get-tuple-element.47), channel_id=1, source_target_pairs={{0,192},{32,224},{64,0},{96,32},{128,64},{160,96},{192,128},{224,1... | collective-permute-start | bytes 393224 | tf_op jit(solution)/shard_map/ppermute | solution.py:314
  34.9 13.1 %collective-permute-start.4 = (bf16[64,1024]{1,0:T(8,128)(2,1)}, bf16[64,1024]{1,0:T(8,128)(2,1)S(1)}, u32[]{:S(2)}, u32[]{:S(2)}) collective-permute-start(bf16[64,1024]{1,0:T(8,128)(2,1)} %get-tuple-element.48), channel_id=1, source_target_pairs={{0,128},{32,160},{64,192},{96,224},{128,0},{160,32},{192,64},{224,... | collective-permute-start | bytes 393224 | tf_op jit(solution)/shard_map/ppermute | solution.py:314
  36.3 14.1 %collective-permute-start.5 = (bf16[64,1024]{1,0:T(8,128)(2,1)}, bf16[64,1024]{1,0:T(8,128)(2,1)S(1)}, u32[]{:S(2)}, u32[]{:S(2)}) collective-permute-start(bf16[64,1024]{1,0:T(8,128)(2,1)} %get-tuple-element.49), channel_id=1, source_target_pairs={{0,160},{32,128},{64,224},{96,192},{128,32},{160,0},{192,96},{224,... | collective-permute-start | bytes 393224 | tf_op jit(solution)/shard_map/ppermute | solution.py:314
  36.9 9.9 %copy-start.31 = (bf16[64,1024]{1,0:T(8,128)(2,1)S(1)}, bf16[64,1024]{1,0:T(8,128)(2,1)}, u32[]{:S(2)}) copy-start(bf16[64,1024]{1,0:T(8,128)(2,1)} %get-tuple-element.51) | copy-start | bytes 393220
  37.0 10.0 %copy-start.30 = (bf16[64,1024]{1,0:T(8,128)(2,1)S(1)}, bf16[64,1024]{1,0:T(8,128)(2,1)}, u32[]{:S(2)}) copy-start(bf16[64,1024]{1,0:T(8,128)(2,1)} %get-tuple-element.52) | copy-start | bytes 393220
  37.1 13.4 %collective-permute-start.6 = (bf16[64,1024]{1,0:T(8,128)(2,1)}, bf16[64,1024]{1,0:T(8,128)(2,1)S(1)}, u32[]{:S(2)}, u32[]{:S(2)}) collective-permute-start(bf16[64,1024]{1,0:T(8,128)(2,1)} %get-tuple-element.50), channel_id=1, source_target_pairs={{0,96},{32,64},{64,160},{96,128},{128,224},{160,192},{192,32},{224... | collective-permute-start | bytes 393224 | tf_op jit(solution)/shard_map/ppermute | solution.py:314
  46.9 18.2 %copy-start.4 = (bf16[64,1024]{1,0:T(8,128)(2,1)}, bf16[64,1024]{1,0:T(8,128)(2,1)S(1)}, u32[]{:S(2)}) copy-start(bf16[64,1024]{1,0:T(8,128)(2,1)S(1)} %collective-permute-done.2.refs_1_) | copy-start | bytes 393220
  46.9 5.7 %collective-permute-start.7 = (bf16[64,1024]{1,0:T(8,128)(2,1)S(1)}, bf16[64,1024]{1,0:T(8,128)(2,1)S(1)}, u32[]{:S(2)}, u32[]{:S(2)}) collective-permute-start(bf16[64,1024]{1,0:T(8,128)(2,1)S(1)} %copy-done.31), channel_id=1, source_target_pairs={{0,224},{32,192},{64,32},{96,0},{128,96},{160,64},{192,160},{224,1... | collective-permute-start | bytes 393224 | tf_op jit(solution)/shard_map/ppermute | solution.py:314
  47.0 18.1 %copy-start.5 = (bf16[64,1024]{1,0:T(8,128)(2,1)}, bf16[64,1024]{1,0:T(8,128)(2,1)S(1)}, u32[]{:S(2)}) copy-start(bf16[64,1024]{1,0:T(8,128)(2,1)S(1)} %collective-permute-done.3.refs_2_) | copy-start | bytes 393220
  47.0 6.9 %collective-permute-start.8 = (bf16[64,1024]{1,0:T(8,128)(2,1)S(1)}, bf16[64,1024]{1,0:T(8,128)(2,1)S(1)}, u32[]{:S(2)}, u32[]{:S(2)}) collective-permute-start(bf16[64,1024]{1,0:T(8,128)(2,1)S(1)} %copy-done.30), channel_id=1, source_target_pairs={{0,32},{32,0},{64,96},{96,64},{128,160},{160,128},{192,224},{224,1... | collective-permute-start | bytes 393224 | tf_op jit(solution)/shard_map/ppermute | solution.py:314
  48.0 17.1 %copy-start.6 = (bf16[64,1024]{1,0:T(8,128)(2,1)}, bf16[64,1024]{1,0:T(8,128)(2,1)S(1)}, u32[]{:S(2)}) copy-start(bf16[64,1024]{1,0:T(8,128)(2,1)S(1)} %collective-permute-done.4.refs_3_) | copy-start | bytes 393220
  48.0 9.0 %collective-permute-start.9 = (bf16[64,1024]{1,0:T(8,128)(2,1)}, bf16[64,1024]{1,0:T(8,128)(2,1)S(1)}, u32[]{:S(2)}, u32[]{:S(2)}) collective-permute-start(bf16[64,1024]{1,0:T(8,128)(2,1)} %get-tuple-element.56), channel_id=1, source_target_pairs={{0,64},{32,96},{64,128},{96,160},{128,192},{160,224},{192,0},{224,... | collective-permute-start | bytes 393224 | tf_op jit(solution)/shard_map/ppermute | solution.py:314
  50.4 14.7 %copy-start.7 = (bf16[64,1024]{1,0:T(8,128)(2,1)}, bf16[64,1024]{1,0:T(8,128)(2,1)S(1)}, u32[]{:S(2)}) copy-start(bf16[64,1024]{1,0:T(8,128)(2,1)S(1)} %collective-permute-done.5.refs_4_) | copy-start | bytes 393220
  50.4 13.1 %collective-permute-start.10 = (bf16[64,1024]{1,0:T(8,128)(2,1)}, bf16[64,1024]{1,0:T(8,128)(2,1)S(1)}, u32[]{:S(2)}, u32[]{:S(2)}) collective-permute-start(bf16[64,1024]{1,0:T(8,128)(2,1)} %get-tuple-element.57), channel_id=1, source_target_pairs={{0,192},{32,224},{64,0},{96,32},{128,64},{160,96},{192,128},{224,1... | collective-permute-start | bytes 393224 | tf_op jit(solution)/shard_map/ppermute | solution.py:314
  50.4 14.6 %copy-start.8 = (bf16[64,1024]{1,0:T(8,128)(2,1)}, bf16[64,1024]{1,0:T(8,128)(2,1)S(1)}, u32[]{:S(2)}) copy-start(bf16[64,1024]{1,0:T(8,128)(2,1)S(1)} %collective-permute-done.6.refs_5_) | copy-start | bytes 393220
  50.4 13.9 %collective-permute-start.11 = (bf16[64,1024]{1,0:T(8,128)(2,1)}, bf16[64,1024]{1,0:T(8,128)(2,1)S(1)}, u32[]{:S(2)}, u32[]{:S(2)}) collective-permute-start(bf16[64,1024]{1,0:T(8,128)(2,1)} %get-tuple-element.58), channel_id=1, source_target_pairs={{0,128},{32,160},{64,192},{96,224},{128,0},{160,32},{192,64},{224,... | collective-permute-start | bytes 393224 | tf_op jit(solution)/shard_map/ppermute | solution.py:314
  52.6 12.5 %copy-start.9 = (bf16[64,1024]{1,0:T(8,128)(2,1)}, bf16[64,1024]{1,0:T(8,128)(2,1)S(1)}, u32[]{:S(2)}) copy-start(bf16[64,1024]{1,0:T(8,128)(2,1)S(1)} %collective-permute-done.7.refs_6_) | copy-start | bytes 393220
  52.6 11.8 %collective-permute-start.12 = (bf16[64,1024]{1,0:T(8,128)(2,1)}, bf16[64,1024]{1,0:T(8,128)(2,1)S(1)}, u32[]{:S(2)}, u32[]{:S(2)}) collective-permute-start(bf16[64,1024]{1,0:T(8,128)(2,1)} %get-tuple-element.59), channel_id=1, source_target_pairs={{0,160},{32,128},{64,224},{96,192},{128,32},{160,0},{192,96},{224,... | collective-permute-start | bytes 393224 | tf_op jit(solution)/shard_map/ppermute | solution.py:314
  53.9 11.2 %copy-start.10 = (bf16[64,1024]{1,0:T(8,128)(2,1)}, bf16[64,1024]{1,0:T(8,128)(2,1)S(1)}, u32[]{:S(2)}) copy-start(bf16[64,1024]{1,0:T(8,128)(2,1)S(1)} %collective-permute-done.8.refs_7_) | copy-start | bytes 393220
  53.9 10.5 %collective-permute-start.13 = (bf16[64,1024]{1,0:T(8,128)(2,1)}, bf16[64,1024]{1,0:T(8,128)(2,1)S(1)}, u32[]{:S(2)}, u32[]{:S(2)}) collective-permute-start(bf16[64,1024]{1,0:T(8,128)(2,1)} %get-tuple-element.60), channel_id=1, source_target_pairs={{0,96},{32,64},{64,160},{96,128},{128,224},{160,192},{192,32},{224... | collective-permute-start | bytes 393224 | tf_op jit(solution)/shard_map/ppermute | solution.py:314
  57.0 8.1 %copy-start.11 = (bf16[64,1024]{1,0:T(8,128)(2,1)}, bf16[64,1024]{1,0:T(8,128)(2,1)S(1)}, u32[]{:S(2)}) copy-start(bf16[64,1024]{1,0:T(8,128)(2,1)S(1)} %collective-permute-done.9.refs_9_) | copy-start | bytes 393220
  57.0 7.6 %collective-permute-start.14 = (bf16[64,1024]{1,0:T(8,128)(2,1)}, bf16[64,1024]{1,0:T(8,128)(2,1)S(1)}, u32[]{:S(2)}, u32[]{:S(2)}) collective-permute-start(bf16[64,1024]{1,0:T(8,128)(2,1)} %get-tuple-element.61), channel_id=1, source_target_pairs={{0,224},{32,192},{64,32},{96,0},{128,96},{160,64},{192,160},{224,1... | collective-permute-start | bytes 393224 | tf_op jit(solution)/shard_map/ppermute | solution.py:314
  63.5 1.6 %copy-start.12 = (bf16[64,1024]{1,0:T(8,128)(2,1)}, bf16[64,1024]{1,0:T(8,128)(2,1)S(1)}, u32[]{:S(2)}) copy-start(bf16[64,1024]{1,0:T(8,128)(2,1)S(1)} %collective-permute-done.10.refs_10_) | copy-start | bytes 393220
  63.5 1.6 %collective-permute-start.15 = (bf16[64,1024]{1,0:T(8,128)(2,1)}, bf16[64,1024]{1,0:T(8,128)(2,1)S(1)}, u32[]{:S(2)}, u32[]{:S(2)}) collective-permute-start(bf16[64,1024]{1,0:T(8,128)(2,1)} %get-tuple-element.62), channel_id=1, source_target_pairs={{0,32},{32,0},{64,96},{96,64},{128,160},{160,128},{192,224},{224,1... | collective-permute-start | bytes 393224 | tf_op jit(solution)/shard_map/ppermute | solution.py:314
  64.4 0.7 copy-start.13
  64.4 0.7 copy-start.14
  64.4 0.7 copy-start.15
  69.8 13.5 %collective-permute-start.19 = (bf16[16,304]{1,0:T(8,128)(2,1)}, bf16[16,304]{1,0:T(8,128)(2,1)S(1)}, u32[]{:S(2)}, u32[]{:S(2)}) collective-permute-start(bf16[16,304]{1,0:T(8,128)(2,1)} %get-tuple-element.68), channel_id=1, source_target_pairs={{0,224},{32,0},{64,32},{96,64},{128,96},{160,128},{192,160},{224,1... | collective-permute-start | bytes 29192 | tf_op jit(solution)/shard_map/ppermute | solution.py:314
  69.8 13.5 %collective-permute-start.18 = (bf16[16,304]{1,0:T(8,128)(2,1)}, bf16[16,304]{1,0:T(8,128)(2,1)S(1)}, u32[]{:S(2)}, u32[]{:S(2)}) collective-permute-start(bf16[16,304]{1,0:T(8,128)(2,1)} %get-tuple-element.68), channel_id=1, source_target_pairs={{0,32},{32,64},{64,96},{96,128},{128,160},{160,192},{192,224},{224... | collective-permute-start | bytes 29192 | tf_op jit(solution)/shard_map/ppermute | solution.py:314
  70.3 13.0 %collective-permute-start.16 = (bf16[304,128]{1,0:T(8,128)(2,1)}, bf16[304,128]{1,0:T(8,128)(2,1)S(1)}, u32[]{:S(2)}, u32[]{:S(2)}) collective-permute-start(bf16[304,128]{1,0:T(8,128)(2,1)} %get-tuple-element.66), channel_id=1, source_target_pairs={{0,1},{1,2},{2,3},{3,4},{4,5},{5,6},{6,7},{7,8},{8,9},{9,10},{10,1... | collective-permute-start | bytes 233480 | tf_op jit(solution)/shard_map/ppermute | solution.py:314
  71.4 11.9 %collective-permute-start.17 = (bf16[304,128]{1,0:T(8,128)(2,1)}, bf16[304,128]{1,0:T(8,128)(2,1)S(1)}, u32[]{:S(2)}, u32[]{:S(2)}) collective-permute-start(bf16[304,128]{1,0:T(8,128)(2,1)} %get-tuple-element.67), channel_id=1, source_target_pairs={{0,31},{1,0},{2,1},{3,2},{4,3},{5,4},{6,5},{7,6},{8,7},{9,8},{10,9... | collective-permute-start | bytes 233480 | tf_op jit(solution)/shard_map/ppermute | solution.py:314
  87.0 14.1 %collective-permute-start.20 = (bf16[304,128]{1,0:T(8,128)(2,1)}, bf16[304,128]{1,0:T(8,128)(2,1)S(1)}, u32[]{:S(2)}, u32[]{:S(2)}) collective-permute-start(bf16[304,128]{1,0:T(8,128)(2,1)} %get-tuple-element.71), channel_id=1, source_target_pairs={{0,1},{1,2},{2,3},{3,4},{4,5},{5,6},{6,7},{7,8},{8,9},{9,10},{10,1... | collective-permute-start | bytes 233480 | tf_op jit(solution)/shard_map/ppermute | solution.py:314
  87.0 14.1 %collective-permute-start.21 = (bf16[304,128]{1,0:T(8,128)(2,1)}, bf16[304,128]{1,0:T(8,128)(2,1)S(1)}, u32[]{:S(2)}, u32[]{:S(2)}) collective-permute-start(bf16[304,128]{1,0:T(8,128)(2,1)} %get-tuple-element.72), channel_id=1, source_target_pairs={{0,31},{1,0},{2,1},{3,2},{4,3},{5,4},{6,5},{7,6},{8,7},{9,8},{10,9... | collective-permute-start | bytes 233480 | tf_op jit(solution)/shard_map/ppermute | solution.py:314
  92.4 8.7 %collective-permute-start.23 = (bf16[16,304]{1,0:T(8,128)(2,1)}, bf16[16,304]{1,0:T(8,128)(2,1)S(1)}, u32[]{:S(2)}, u32[]{:S(2)}) collective-permute-start(bf16[16,304]{1,0:T(8,128)(2,1)} %get-tuple-element.73), channel_id=1, source_target_pairs={{0,224},{32,0},{64,32},{96,64},{128,96},{160,128},{192,160},{224,1... | collective-permute-start | bytes 29192 | tf_op jit(solution)/shard_map/ppermute | solution.py:314
  92.5 8.6 %collective-permute-start.22 = (bf16[16,304]{1,0:T(8,128)(2,1)}, bf16[16,304]{1,0:T(8,128)(2,1)S(1)}, u32[]{:S(2)}, u32[]{:S(2)}) collective-permute-start(bf16[16,304]{1,0:T(8,128)(2,1)} %get-tuple-element.73), channel_id=1, source_target_pairs={{0,32},{32,64},{64,96},{96,128},{128,160},{160,192},{192,224},{224... | collective-permute-start | bytes 29192 | tf_op jit(solution)/shard_map/ppermute | solution.py:314
  104.8 9.6 %collective-permute-start.24 = (bf16[304,128]{1,0:T(8,128)(2,1)}, bf16[304,128]{1,0:T(8,128)(2,1)S(1)}, u32[]{:S(2)}, u32[]{:S(2)}) collective-permute-start(bf16[304,128]{1,0:T(8,128)(2,1)} %get-tuple-element.75), channel_id=1, source_target_pairs={{0,1},{1,2},{2,3},{3,4},{4,5},{5,6},{6,7},{7,8},{8,9},{9,10},{10,1... | collective-permute-start | bytes 233480 | tf_op jit(solution)/shard_map/ppermute | solution.py:314
  104.8 9.6 %collective-permute-start.25 = (bf16[16,304]{1,0:T(8,128)(2,1)}, bf16[16,304]{1,0:T(8,128)(2,1)S(1)}, u32[]{:S(2)}, u32[]{:S(2)}) collective-permute-start(bf16[16,304]{1,0:T(8,128)(2,1)} %get-tuple-element.76), channel_id=1, source_target_pairs={{0,32},{32,64},{64,96},{96,128},{128,160},{160,192},{192,224},{224... | collective-permute-start | bytes 29192 | tf_op jit(solution)/shard_map/ppermute | solution.py:314
  117.6 1.4 collective-permute-start.26
  119.6 3.6 %collective-permute-start.27 = (f32[8,128]{1,0:T(8,128)S(1)}, f32[8,128]{1,0:T(8,128)S(1)}, u32[]{:S(2)}, u32[]{:S(2)}) collective-permute-start(f32[8,128]{1,0:T(8,128)S(1)} %add.180), channel_id=1, source_target_pairs={{0,64},{32,96},{64,0},{96,32},{128,192},{160,224},{192,128},{224,1... | collective-permute-start | bytes 12296 | tf_op jit(solution)/shard_map/ppermute | solution.py:314
  123.2 5.1 %collective-permute-start.28 = (f32[8,128]{1,0:T(8,128)S(1)}, f32[8,128]{1,0:T(8,128)S(1)}, u32[]{:S(2)}, u32[]{:S(2)}) collective-permute-start(f32[8,128]{1,0:T(8,128)S(1)} %add.181), channel_id=1, source_target_pairs={{0,128},{32,160},{64,192},{96,224},{128,0},{160,32},{192,64},{224,... | collective-permute-start | bytes 12296 | tf_op jit(solution)/shard_map/ppermute | solution.py:314
  129.0 17.1 %all-to-all-start.1 = ((f32[32,8,128]{2,1,0:T(8,128)}), f32[32,8,128]{2,1,0:T(8,128)S(1)}, u32[]{:S(2)}, u32[]{:S(2)}) async-start(f32[32,8,128]{2,1,0:T(8,128)} %broadcast_in_dim.2), calls=%async_computation.1 | async-start | bytes 262144 | tf_op jit(solution)/shard_map/all_to_all | solution.py:435
  (15 other events, 9.5 us)

commit v3 on v2

--- a/solution.py
+++ b/solution.py
@@ -19,13 +19,21 @@
     return jax.ShapeDtypeStruct(shape, dtype)
 
 
-def call(body, outs, *args, specs=None, scratch=(), name=None):
+def in_hbm(shape, dtype):
+    return pltpu.HBM(shape, dtype)
+
+
+def call(body, outs, *args, specs=None, out_specs=None, scratch=(), name=None):
+    flat = outs if isinstance(outs, (list, tuple)) else [outs]
     places = specs or [pltpu.VMEM] * len(args)
+    out_places = [pl.BlockSpec(memory_space=place) for place in out_specs or [pltpu.VMEM] * len(flat)]
     return pl.pallas_call(
         body,
         out_shape=outs,
         in_specs=[pl.BlockSpec(memory_space=place) for place in places],
+        out_specs=out_places if isinstance(outs, (list, tuple)) else out_places[0],
         scratch_shapes=list(scratch),
+        compiler_params=pltpu.CompilerParams(vmem_limit_bytes=16 * 1024 * 1024),
         name=name,
     )(*args)
 
@@ -39,28 +47,18 @@
     return high, (values - high.astype(F32)).astype(BF16)
 
 
-def fetch(step, phase, coher, phase_in, coher_in, sems):
-    ifgs = pl.ds(step * 16, 16)
-    return [
-        pltpu.make_async_copy(source.at[ifgs], target.at[ifgs], sems.at[part, step])
-        for part, (source, target) in enumerate(((phase, phase_in), (coher, coher_in)))
-    ]
-
-
-def rows_first(phase, coher, phase_t, coher_t, first, last, phase_in, coher_in, wide, sems):
-    copies = [fetch(step, phase, coher, phase_in, coher_in, sems) for step in range(4)]
-    for pair in copies:
-        for copy in pair:
-            copy.start()
-    for block in range(4):
-        for part, (source, target) in enumerate(((phase_in, phase_t), (coher_in, coher_t))):
-            copies[block][part].wait()
+def rows_first(phase, coher, phase_t, coher_t, first, last, wide):
+    def group(block, _):
+        ifgs = pl.ds(pl.multiple_of(block * 16, 16), 16)
+        for part, (source, target) in enumerate(((phase, phase_t), (coher, coher_t))):
             for tile in range(8):
                 lanes = pl.ds(tile * 128, 128)
-                wide[part, tile] = source[pl.ds(block * 16, 16), :, lanes].astype(F32).reshape(128, 128)
+                wide[part, tile] = source[ifgs, :, lanes].astype(F32).reshape(128, 128)
                 for row in range(8):
-                    piece = wide[part, tile, pl.ds(row, 16, stride=8), :].astype(BF16)
-                    target[row, pl.ds(block * 16, 16), lanes] = piece
+                    target[row, ifgs, lanes] = wide[part, tile, pl.ds(row, 16, stride=8), :].astype(BF16)
+        return 0
+
+    lax.fori_loop(0, 4, group, 0)
     for part, target in enumerate((phase_t, coher_t)):
         first[pl.ds(part * 64, 64), :] = target[0]
         last[pl.ds(part * 64, 64), :] = target[7]
@@ -79,10 +77,17 @@
     return total
 
 
-def smoothing(flags, owners, phase_t, coher_t, above, below, mask, height, smooth, sums, *rest):
-    outs, weights, totals = rest[:8], rest[8], rest[9]
+def smoothing(flags, owners, phase_t, coher_t, above, below, mask, height, smooth_out, sums, *rest):
+    outs, weights, totals, smooth, sems = rest[:8], rest[8], rest[9], rest[10], rest[11]
     lane = lax.broadcasted_iota(jnp.int32, (16, 1024), 1)
     edge_flag = {-1: flags[0] > 0, 8: flags[1] > 0}
+
+    def copies(block):
+        ifgs = pl.ds(pl.multiple_of(block * 16, 16), 16)
+        return [
+            pltpu.make_async_copy(weights.at[owners[step], ifgs], out.at[ifgs], sems.at[block, step])
+            for step, out in enumerate(outs)
+        ] + [pltpu.make_async_copy(smooth.at[:, ifgs], smooth_out.at[:, ifgs], sems.at[block, 8])]
 
     def group(block, _):
         ifgs = pl.ds(pl.multiple_of(block * 16, 16), 16)
@@ -114,11 +119,15 @@
             before, current = current, after
         totals[ifgs, :] = top
         totals[cohers, :] = low
+        for copy in copies(block):
+            copy.start()
         return 0
 
     lax.fori_loop(0, 4, group, 0)
-    sums[...] = jnp.broadcast_to(jnp.sum(totals[...].T, axis=0)[None, None, :], sums.shape)
-    pick_blocks(weights, owners, outs)
+    sums[...] = jnp.broadcast_to(jnp.sum(totals[...].T, axis=0, keepdims=True), sums.shape)
+    for block in range(4):
+        for copy in copies(block):
+            copy.wait()
 
 
 def pick_blocks(source, owners, outs):
@@ -128,17 +137,19 @@
 
 def correction(owners, sums, smooth, height, slope_row, *rest):
     outs, blocks = rest[:8], rest[8]
-    total = sums[0]
-    for index in range(1, sums.shape[0]):
-        total += sums[index]
+    total = sums[...]
     slope_row[...] = total / pltpu.roll(total, 64, 1)
     column = jnp.broadcast_to(total[0:1, :], (128, 128)).T
     slope = column[:64, :] / column[64:, :]
-    for row in range(8):
-        for tile in range(8):
-            lanes = pl.ds(tile * 128, 128)
+
+    def one_tile(tile, _):
+        lanes = pl.ds(pl.multiple_of(tile * 128, 128), 128)
+        for row in range(8):
             value = smooth[row, :, lanes] - slope * height[pl.ds(row, 1), lanes]
             blocks[tile, :, pl.ds(row * 128, 128)] = value.astype(BF16)
+        return 0
+
+    lax.fori_loop(0, 8, one_tile, 0)
     pick_blocks(blocks, owners, outs)
 
 
@@ -163,9 +174,9 @@
     design_t, field, weights, first, last, columns = refs[16:]
     for part in range(8):
         weights[pl.ds(part * 64, 64), :] = weight_parts[part][...]
-    for chunk in range(4):
-        lanes = pl.ds(chunk * 256, 256)
-        total = jnp.zeros((DP, 256), F32)
+
+    def one_chunk(chunk, _):
+        lanes = pl.ds(pl.multiple_of(chunk * 256, 256), 256)
         scaled = jnp.concatenate(
             [
                 weight_parts[part][:, lanes].astype(F32) * corrected_parts[part][:, lanes].astype(F32)
@@ -175,27 +186,33 @@
         )
         high, low = split(scaled)
         field[:, lanes] = dot(design_t[...], high) + dot(design_t[...], low)
+        return 0
+
+    lax.fori_loop(0, 4, one_chunk, 0)
     write_edges(field, first, last, columns)
 
 
+def row_lanes(row):
+    return pl.ds(pl.multiple_of(row * 128, 128), 128)
+
+
 def local_image(field, weights, design, design_t, chunk):
-    lanes = pl.ds(chunk * 256, 256)
+    lanes = pl.ds(pl.multiple_of(chunk * 256, 256), 256)
     high, low = split(field[:, lanes])
     scaled = (dot(design[...], high) + dot(design[...], low)) * weights[:, lanes].astype(F32)
     high, low = split(scaled)
     back = dot(design_t[...], high) + dot(design_t[...], low)
     lane = lax.broadcasted_iota(jnp.int32, (DP, 128), 1)
     parts = []
-    for row in (2 * chunk, 2 * chunk + 1):
-        here = field[:, pl.ds(row * 128, 128)]
+    for offset in range(2):
+        row = 2 * chunk + offset
+        here = field[:, row_lanes(row)]
         around = jnp.where(lane == 0, 0.0, pltpu.roll(here, 1, 1))
         around += jnp.where(lane == 127, 0.0, pltpu.roll(here, 127, 1))
-        if row > 0:
-            around += field[:, pl.ds((row - 1) * 128, 128)]
-        if row < 7:
-            around += field[:, pl.ds((row + 1) * 128, 128)]
-        start = (row - 2 * chunk) * 128
-        parts.append(back[:, start : start + 128] + CENTRE * here - SMOOTHING_WEIGHT * around)
+        around += jnp.where(row > 0, field[:, row_lanes(jnp.maximum(row - 1, 0))], 0.0)
+        around += jnp.where(row < 7, field[:, row_lanes(jnp.minimum(row + 1, 7))], 0.0)
+        part = back[:, offset * 128 : offset * 128 + 128] + CENTRE * here - SMOOTHING_WEIGHT * around
+        parts.append((row, part))
     return parts
 
 
@@ -213,24 +230,24 @@
     if with_image:
         image, refs = refs[0], refs[1:]
     moments = refs[0]
-    square = jnp.zeros((8, 128), F32)
-    cross = jnp.zeros((8, 128), F32)
-    ahead = jnp.zeros((8, 128), F32)
-    for chunk in range(4):
-        parts = local_image(field, weights, design, design_t, chunk)
-        for offset, part in enumerate(parts):
-            lanes = pl.ds((2 * chunk + offset) * 128, 128)
-            here = field[:, lanes]
+
+    def one_chunk(chunk, totals):
+        square, cross, ahead = totals
+        for row, part in local_image(field, weights, design, design_t, chunk):
+            here = field[:, row_lanes(row)]
             square += fold(here * here)
             if with_before:
-                cross += fold(here * before[:, lanes])
+                cross += fold(here * before[:, row_lanes(row)])
             if with_image:
-                image[:, lanes] = part
+                image[:, row_lanes(row)] = part
             else:
                 ahead += fold(here * part)
-    moments[0] = square
-    moments[1] = cross
-    moments[2] = ahead
+        return square, cross, ahead
+
+    zero = jnp.zeros((8, 128), F32)
+    totals = lax.fori_loop(0, 4, one_chunk, (zero, zero, zero))
+    for index in range(3):
+        moments[index] = totals[index]
 
 
 def spread_columns(columns, pixels):
@@ -271,11 +288,8 @@
     out[...] = jnp.concatenate(sums + [jnp.zeros((2, 128), F32)], axis=0)
 
 
-def combine(parts, zero, one, two, out):
-    total = parts[0]
-    for index in range(1, parts.shape[0]):
-        total += parts[index]
-    sums = jnp.sum(total, axis=1, keepdims=True)
+def combine(total, zero, one, two, out):
+    sums = jnp.sum(total[...], axis=1, keepdims=True)
     m0, m1, m2, m3, m4, m5 = (jnp.broadcast_to(sums[i : i + 1, :], (1, 128)) for i in range(6))
     t00, t01, t11 = m1 + SHIFT * m0, m2 + SHIFT * m1, m3 + SHIFT * m2
     t12, t22 = m4 + SHIFT * m3, m5 + SHIFT * m4
@@ -305,7 +319,7 @@
     offsets = ((0, 0), (1, 0), (3, 0), (2, 0), (2, 1), (1, 1), (3, 1), (0, 1))
 
     def other(index, chips, core):
-        return (index // 2 + chips) % n_chip * 2 + (index + core) % 2
+        return (((index >> 1) + chips) & (n_chip - 1)) * 2 + ((index & 1) ^ core)
 
     owners = jnp.stack([other(me, *offset) for offset in offsets]).astype(jnp.int32)
     flags = jnp.stack([my_row > 0, my_row < n_rows - 1, me > 0, me < n_ifg - 1]).astype(jnp.int32)
@@ -318,6 +332,15 @@
 
     def backward(values, axis):
         return permute(values, axis, lambda i: (i - 1) % lax.axis_size(axis))
+
+    def ring_of_four(values, axis, target):
+        moved = [permute(values, axis, lambda i: target(i, k)) for k in (1, 2, 3)]
+        return (values + moved[1]) + (moved[0] + moved[2])
+
+    def sum_rows(values):
+        values = ring_of_four(values, "rows", lambda i, k: (i + 8 * k) % n_rows)
+        values = values + permute(values, "rows", lambda i: i ^ 1)
+        return ring_of_four(values, "rows", lambda i, k: i // 8 * 8 + (i + 2 * k) % 8)
 
     stacked = sds((8, 64, 1024), BF16)
     edge = sds((128, 1024), BF16)
@@ -326,20 +349,14 @@
         (stacked, stacked, edge, edge),
         phase,
         coherence,
-        specs=[pltpu.HBM] * 2,
-        scratch=(
-            pltpu.VMEM((64, 8, 1024), BF16),
-            pltpu.VMEM((64, 8, 1024), BF16),
-            pltpu.VMEM((2, 8, 128, 128), F32),
-            pltpu.SemaphoreType.DMA((2, 4)),
-        ),
+        scratch=(pltpu.VMEM((2, 8, 128, 128), F32),),
         name="rows_first",
     )
     above, below = forward(last, "rows"), backward(first, "rows")
     block = sds((64, 1024), BF16)
     smooth, sums, *weight_parts = call(
         smoothing,
-        [sds((8, 64, 1024), F32), sds((n_rows, 8, 128), F32)] + [block] * 8,
+        [in_hbm((8, 64, 1024), F32), sds((8, 128), F32)] + [in_hbm((64, 1024), BF16)] * 8,
         flags,
         owners,
         phase_t,
@@ -349,10 +366,16 @@
         gap_mask.astype(F32),
         height,
         specs=[pltpu.SMEM] * 2 + [pltpu.VMEM] * 6,
-        scratch=(pltpu.VMEM((8, 64, 1024), BF16), pltpu.VMEM((128, 128), F32)),
+        out_specs=[pltpu.HBM, pltpu.VMEM] + [pltpu.HBM] * 8,
+        scratch=(
+            pltpu.VMEM((8, 64, 1024), BF16),
+            pltpu.VMEM((128, 128), F32),
+            pltpu.VMEM((8, 64, 1024), F32),
+            pltpu.SemaphoreType.DMA((4, 9)),
+        ),
         name="smoothing",
     )
-    sums = lax.all_to_all(sums, "rows", 0, 0, tiled=True)
+    sums = sum_rows(sums)
 
     def exchange(parts):
         return [parts[0]] + [
@@ -373,7 +396,7 @@
         name="correction",
     )
     corrected_parts = exchange(corrected_parts)
-    sources = jnp.stack([other(me, -chips, core) for chips, core in offsets])
+    sources = jnp.stack([other(me, n_chip - chips, core) for chips, core in offsets])
     pairs = date_pairs.reshape(n_ifg, -1, 2)[sources].reshape(-1, 2)
     dates = jnp.arange(DP, dtype=jnp.int32)
     design = ((dates[None] == pairs[:, 1:2]).astype(F32) - (dates[None] == pairs[:, 0:1]).astype(F32)).astype(BF16)
@@ -429,11 +452,9 @@
         specs=[pltpu.SMEM] + [pltpu.VMEM] * 6,
         name="all_moments",
     )
-    for target in (lambda i: i ^ 1, lambda i: i ^ 2, lambda i: i ^ 4):
-        part = part + permute(part, "ifg", target)
-    part = jnp.broadcast_to(part[None], (n_rows, 8, 128))
-    parts = lax.all_to_all(part, "rows", 0, 0, tiled=True)
-    displacement = call(combine, sds((DATES * 8, 128), F32), parts, k0, k1, k2, name="combine")
+    part = part + permute(part, "ifg", lambda i: i ^ 1)
+    part = sum_rows(ring_of_four(part, "ifg", lambda i, k: (i + 2 * k) % n_ifg))
+    displacement = call(combine, sds((DATES * 8, 128), F32), part, k0, k1, k2, name="combine")
     return displacement.reshape(DATES, 8, 128), slope_row[0, :64]
 
 

time: 151 us -> 140 us (0.927)
  Pallas kernels: 49.8 us -> 27.5 us
  waiting for transfers between devices: 33.3 us -> 44.1 us
  starting transfers between devices: 55 us -> 61.2 us
  local copies, waits for them, and re-layouts: 8.65 us -> 5.59 us
  other arithmetic: 3.12 us -> 0.49 us
    ppermute x29 -> x44, waiting for transfers between devices: 21.5 us -> 44.1 us  [permute(): lax.ppermute(values, axis, [(i, target(i)) for i in range(lax.axis_size(a...]
    pallas_call x11, Pallas kernels: 49.8 us -> 27.5 us  [call(): pl.pallas_call(body, out_shape=outs, in_specs=[pl.BlockSpec(memory_space=...]
    ppermute x29 -> x44, starting transfers between devices: 41.5 us -> 61.2 us  [permute(): lax.ppermute(values, axis, [(i, target(i)) for i in range(lax.axis_size(a...]
    all_to_all x2 -> x0, starting transfers between devices: 13.5 us -> none  [the longest x1 6.74 us: per_device(): sums = lax.all_to_all(sums, 'rows', 0, 0, tiled=True)]
    all_to_all x2 -> x0, waiting for transfers between devices: 11.8 us -> none  [the longest x1 9.2 us: per_device(): parts = lax.all_to_all(part, 'rows', 0, 0, tiled=True)]
    unnamed x64 -> x18, local copies, waits for them, and re-layouts: 4.63 us -> 4.05 us
  transfers between devices with their start and end apart: 31 -> 44, of which waited for: 10 -> 22; matrix products, arithmetic and copies ran while one was open for 4% -> 1% of each run, Pallas kernels for 16% -> 10%
where the time goes in v3:
time: 140 us
  starting transfers between devices  61.2 us (44%)
  waiting for transfers between devices  44.1 us (32%)
  Pallas kernels  27.5 us (20%)
  local copies, waits for them, and re-layouts  5.59 us (4%)
    ppermute x44, starting transfers between devices, permute(): lax.ppermute(values, axis, [(i, target(i)) for i in range(lax.axis_size(a...  61.2 us
    ppermute x44, waiting for transfers between devices, permute(): lax.ppermute(values, axis, [(i, target(i)) for i in range(lax.axis_size(a...  44.1 us
    pallas_call x11, Pallas kernels, call(): pl.pallas_call(body, out_shape=outs, in_specs=[pl.BlockSpec(memory_space=...  27.5 us
    unnamed x18, local copies, waits for them, and re-layouts  4.05 us
  transfers between devices with their start and end apart: 44, of which 22 were waited for; matrix products, arithmetic and copies ran while one was open for 1% of the time, Pallas kernels for 10%

profile of v3, /device:TPU:6, one launch (start us, length us, event | category | flops | bytes accessed | tf_op | source)
XLA Modules:
  0.0 139.8 jit_solution(13578741317190218954)
XLA Ops:
  0.6 1.2 copy-done.1
  1.9 1.2 copy-done.2
  3.1 1.1 rows_first.1
  4.2 2.0 %collective-permute-start = (bf16[128,1024]{1,0:T(8,128)(2,1)S(1)}, bf16[128,1024]{1,0:T(8,128)(2,1)S(1)}, u32[]{:S(2)}, u32[]{:S(2)}) collective-permute-start(bf16[128,1024]{1,0:T(8,128)(2,1)S(1)} %get-tuple-element.43), channel_id=1, source_target_pairs={{0,1},{1,2},{2,3},{3,4},{4,5},{5,6},{6,7},{7,8},{8,9},{9,10},{10,1... | collective-permute-start | bytes 786440 | tf_op jit(solution)/shard_map/ppermute | solution.py:328
  6.2 6.5 %collective-permute-start.1 = (bf16[128,1024]{1,0:T(8,128)(2,1)S(1)}, bf16[128,1024]{1,0:T(8,128)(2,1)S(1)}, u32[]{:S(2)}, u32[]{:S(2)}) collective-permute-start(bf16[128,1024]{1,0:T(8,128)(2,1)S(1)} %get-tuple-element.44), channel_id=1, source_target_pairs={{0,31},{1,0},{2,1},{3,2},{4,3},{5,4},{6,5},{7,6},{8,7},{9,8},{10,9... | collective-permute-start | bytes 786440 | tf_op jit(solution)/shard_map/ppermute | solution.py:328
  12.9 6.0 %collective-permute-done.above = bf16[128,1024]{1,0:T(8,128)(2,1)S(1)} collective-permute-done((bf16[128,1024]{1,0:T(8,128)(2,1)S(1)}, bf16[128,1024]{1,0:T(8,128)(2,1)S(1)}, u32[]{:S(2)}, u32[]{:S(2)}) %collective-permute-start) | collective-permute-done | bytes 262176 | tf_op jit(solution)/shard_map/ppermute | solution.py:328
  18.9 4.5 %smoothing.1 = (f32[8,64,1024]{2,1,0:T(8,128)}, f32[8,128]{1,0:T(8,128)S(1)}, bf16[64,1024]{1,0:T(8,128)(2,1)}, bf16[64,1024]{1,0:T(8,128)(2,1)}, bf16[64,1024]{...) custom-call(s32[4]{0:T(128)S(1)} %add_convert_fusion.flags, ...), custom_call_target="tpu_custom_call" | custom-call | tf_op jit(solution)/shard_map/smoothing/pallas_call | solution.py:30
  24.2 1.3 collective-permute-start.10
  27.1 2.0 %collective-permute-done.10 = f32[8,128]{1,0:T(8,128)S(1)} collective-permute-done((f32[8,128]{1,0:T(8,128)S(1)}, f32[8,128]{1,0:T(8,128)S(1)}, u32[]{:S(2)}, u32[]{:S(2)}) %collective-permute-start.10) | collective-permute-done | bytes 4128 | tf_op jit(solution)/shard_map/ppermute | solution.py:328
  29.0 1.6 %collective-permute-done.9 = f32[8,128]{1,0:T(8,128)S(1)} collective-permute-done((f32[8,128]{1,0:T(8,128)S(1)}, f32[8,128]{1,0:T(8,128)S(1)}, u32[]{:S(2)}, u32[]{:S(2)}) %collective-permute-start.9) | collective-permute-done | bytes 4128 | tf_op jit(solution)/shard_map/ppermute | solution.py:328
  30.6 3.6 %collective-permute-done.12 = f32[8,128]{1,0:T(8,128)S(1)} collective-permute-done((f32[8,128]{1,0:T(8,128)S(1)}, f32[8,128]{1,0:T(8,128)S(1)}, u32[]{:S(2)}, u32[]{:S(2)}) %collective-permute-start.12) | collective-permute-done | bytes 4128 | tf_op jit(solution)/shard_map/ppermute | solution.py:328
  34.2 3.1 %collective-permute-start.15 = (f32[8,128]{1,0:T(8,128)S(1)}, f32[8,128]{1,0:T(8,128)S(1)}, u32[]{:S(2)}, u32[]{:S(2)}) collective-permute-start(f32[8,128]{1,0:T(8,128)S(1)} %add.136), channel_id=1, source_target_pairs={{0,6},{1,7},{2,0},{3,1},{4,2},{5,3},{6,4},{7,5},{8,14},{9,15},{10,... | collective-permute-start | bytes 12296 | tf_op jit(solution)/shard_map/ppermute | solution.py:328
  37.4 2.6 %collective-permute-start.13 = (f32[8,128]{1,0:T(8,128)S(1)}, f32[8,128]{1,0:T(8,128)S(1)}, u32[]{:S(2)}, u32[]{:S(2)}) collective-permute-start(f32[8,128]{1,0:T(8,128)S(1)} %add.136), channel_id=1, source_target_pairs={{0,4},{1,5},{2,6},{3,7},{4,0},{5,1},{6,2},{7,3},{8,12},{9,13},{10,... | collective-permute-start | bytes 12296 | tf_op jit(solution)/shard_map/ppermute | solution.py:328
  41.2 1.5 %collective-permute-start.3 = (bf16[64,1024]{1,0:T(8,128)(2,1)}, bf16[64,1024]{1,0:T(8,128)(2,1)S(1)}, u32[]{:S(2)}, u32[]{:S(2)}) collective-permute-start(bf16[64,1024]{1,0:T(8,128)(2,1)} %get-tuple-element.47), channel_id=1, source_target_pairs={{0,192},{32,224},{64,0},{96,32},{128,64},{160,96},{192,128},{224,1... | collective-permute-start | bytes 393224 | tf_op jit(solution)/shard_map/ppermute | solution.py:328
  42.8 1.4 %collective-permute-start.4 = (bf16[64,1024]{1,0:T(8,128)(2,1)}, bf16[64,1024]{1,0:T(8,128)(2,1)S(1)}, u32[]{:S(2)}, u32[]{:S(2)}) collective-permute-start(bf16[64,1024]{1,0:T(8,128)(2,1)} %get-tuple-element.48), channel_id=1, source_target_pairs={{0,128},{32,160},{64,192},{96,224},{128,0},{160,32},{192,64},{224,... | collective-permute-start | bytes 393224 | tf_op jit(solution)/shard_map/ppermute | solution.py:328
  44.9 2.9 %collective-permute-start.6 = (bf16[64,1024]{1,0:T(8,128)(2,1)}, bf16[64,1024]{1,0:T(8,128)(2,1)S(1)}, u32[]{:S(2)}, u32[]{:S(2)}) collective-permute-start(bf16[64,1024]{1,0:T(8,128)(2,1)} %get-tuple-element.50), channel_id=1, source_target_pairs={{0,96},{32,64},{64,160},{96,128},{128,224},{160,192},{192,32},{224... | collective-permute-start | bytes 393224 | tf_op jit(solution)/shard_map/ppermute | solution.py:328
  47.8 1.6 %copy-done = f32[8,64,1024]{2,1,0:T(8,128)S(1)} copy-done((f32[8,64,1024]{2,1,0:T(8,128)S(1)}, f32[8,64,1024]{2,1,0:T(8,128)}, u32[]{:S(2)}) %copy-start) | copy-done | bytes 2097176
  49.3 1.1 correction.1
  51.0 2.9 %collective-permute-start.16 = (bf16[64,1024]{1,0:T(8,128)(2,1)S(1)}, bf16[64,1024]{1,0:T(8,128)(2,1)S(1)}, u32[]{:S(2)}, u32[]{:S(2)}) collective-permute-start(bf16[64,1024]{1,0:T(8,128)(2,1)S(1)} %get-tuple-element.56), channel_id=1, source_target_pairs={{0,64},{32,96},{64,128},{96,160},{128,192},{160,224},{192,0},{224,... | collective-permute-start | bytes 393224 | tf_op jit(solution)/shard_map/ppermute | solution.py:328
  54.0 2.3 %collective-permute-start.18 = (bf16[64,1024]{1,0:T(8,128)(2,1)S(1)}, bf16[64,1024]{1,0:T(8,128)(2,1)S(1)}, u32[]{:S(2)}, u32[]{:S(2)}) collective-permute-start(bf16[64,1024]{1,0:T(8,128)(2,1)S(1)} %get-tuple-element.58), channel_id=1, source_target_pairs={{0,128},{32,160},{64,192},{96,224},{128,0},{160,32},{192,64},{224,... | collective-permute-start | bytes 393224 | tf_op jit(solution)/shard_map/ppermute | solution.py:328
  57.0 3.5 %collective-permute-start.20 = (bf16[64,1024]{1,0:T(8,128)(2,1)S(1)}, bf16[64,1024]{1,0:T(8,128)(2,1)S(1)}, u32[]{:S(2)}, u32[]{:S(2)}) collective-permute-start(bf16[64,1024]{1,0:T(8,128)(2,1)S(1)} %get-tuple-element.60), channel_id=1, source_target_pairs={{0,96},{32,64},{64,160},{96,128},{128,224},{160,192},{192,32},{224... | collective-permute-start | bytes 393224 | tf_op jit(solution)/shard_map/ppermute | solution.py:328
  60.5 6.4 %collective-permute-done.17.refs_10_ = bf16[64,1024]{1,0:T(8,128)(2,1)S(1)} collective-permute-done((bf16[64,1024]{1,0:T(8,128)(2,1)S(1)}, bf16[64,1024]{1,0:T(8,128)(2,1)S(1)}, u32[]{:S(2)}, u32[]{:S(2)}) %collective-permute-start.17) | collective-permute-done | bytes 131104 | tf_op jit(solution)/shard_map/ppermute | solution.py:328
  68.2 1.8 %right_side.1 = (f32[304,1024]{1,0:T(8,128)S(1)}, bf16[512,1024]{1,0:T(8,128)(2,1)S(1)}, bf16[304,128]{1,0:T(8,128)(2,1)S(1)}, bf16[304,128]{1,0:T(8,128)(2,1)S(1)}, bf16[16,304]{1,0:T(8,128)(2,1)S(1)}) custom-call(bf16[64,1024]{1,0:T(8,128)(2,1)S(1)} %copy-done.4, bf16[64,1024]{1,0:T(8,128)(2,1)S(1)} %collective-permute-done.2.refs_1_, ...), custom_call_target="tpu_custom_call" | custom-call | tf_op jit(solution)/shard_map/right_side/pallas_call | solution.py:30
  70.5 1.7 %collective-permute-start.23 = (bf16[304,128]{1,0:T(8,128)(2,1)S(1)}, bf16[304,128]{1,0:T(8,128)(2,1)S(1)}, u32[]{:S(2)}, u32[]{:S(2)}) collective-permute-start(bf16[304,128]{1,0:T(8,128)(2,1)S(1)} %get-tuple-element.66), channel_id=1, source_target_pairs={{0,1},{1,2},{2,3},{3,4},{4,5},{5,6},{6,7},{7,8},{8,9},{9,10},{10,1... | collective-permute-start | bytes 233480 | tf_op jit(solution)/shard_map/ppermute | solution.py:328
  72.2 5.1 %collective-permute-start.24 = (bf16[304,128]{1,0:T(8,128)(2,1)S(1)}, bf16[304,128]{1,0:T(8,128)(2,1)S(1)}, u32[]{:S(2)}, u32[]{:S(2)}) collective-permute-start(bf16[304,128]{1,0:T(8,128)(2,1)S(1)} %get-tuple-element.67), channel_id=1, source_target_pairs={{0,31},{1,0},{2,1},{3,2},{4,3},{5,4},{6,5},{7,6},{8,7},{9,8},{10,9... | collective-permute-start | bytes 233480 | tf_op jit(solution)/shard_map/ppermute | solution.py:328
  77.5 4.4 %apply0.1 = (f32[304,1024]{1,0:T(8,128)S(1)}, f32[3,8,128]{2,1,0:T(8,128)S(1)}) custom-call(f32[304,1024]{1,0:T(8,128)S(1)} %get-tuple-element.63.refs_0_.refs_4_.zero, bf16[512,1024]{1,0:T(8,128)(2,1)S(1)} %get-tuple-element.64.refs_1_, bf16[512,304]{1,0:T(8,128)(2,1)S(1)} %subtract_convert_fusion.refs_2_, ...), custom_call_target="tpu_custom_call" | custom-call | tf_op jit(solution)/shard_map/apply0/pallas_call | solution.py:30
  82.0 1.2 add_halo1.1
  83.2 5.4 %collective-permute-start.28 = (bf16[304,128]{1,0:T(8,128)(2,1)S(1)}, bf16[304,128]{1,0:T(8,128)(2,1)S(1)}, u32[]{:S(2)}, u32[]{:S(2)}) collective-permute-start(bf16[304,128]{1,0:T(8,128)(2,1)S(1)} %get-tuple-element.72), channel_id=1, source_target_pairs={{0,31},{1,0},{2,1},{3,2},{4,3},{5,4},{6,5},{7,6},{8,7},{9,8},{10,9... | collective-permute-start | bytes 233480 | tf_op jit(solution)/shard_map/ppermute | solution.py:328
  89.1 1.4 %collective-permute-start.29 = (bf16[16,304]{1,0:T(8,128)(2,1)S(1)}, bf16[16,304]{1,0:T(8,128)(2,1)S(1)}, u32[]{:S(2)}, u32[]{:S(2)}) collective-permute-start(bf16[16,304]{1,0:T(8,128)(2,1)S(1)} %get-tuple-element.73), channel_id=1, source_target_pairs={{0,32},{32,64},{64,96},{96,128},{128,160},{160,192},{192,224},{224... | collective-permute-start | bytes 29192 | tf_op jit(solution)/shard_map/ppermute | solution.py:328
  90.6 4.5 %apply1.1 = (f32[304,1024]{1,0:T(8,128)S(1)}, f32[3,8,128]{2,1,0:T(8,128)S(1)}) custom-call(f32[304,1024]{1,0:T(8,128)S(1)} %get-tuple-element.69.refs_0_.refs_4_.one, bf16[512,1024]{1,0:T(8,128)(2,1)S(1)} %get-tuple-element.64.refs_1_, bf16[512,304]{1,0:T(8,128)(2,1)S(1)} %subtract_convert_fusion.refs_2_, ...), custom_call_target="tpu_custom_call" | custom-call | tf_op jit(solution)/shard_map/apply1/pallas_call | solution.py:30
  95.1 1.7 %add_halo2.1 = (f32[304,1024]{1,0:T(8,128)S(1)}, bf16[304,128]{1,0:T(8,128)(2,1)}, bf16[304,128]{1,0:T(8,128)(2,1)S(1)}, bf16[16,304]{1,0:T(8,128)(2,1)S(1)}) custom-call(s32[4]{0:T(128)S(1)} %add_convert_fusion.flags, f32[304,1024]{1,0:T(8,128)S(1)} %get-tuple-element.70.image, bf16[304,128]{1,0:T(8,128)(2,1)S(1)} %collective-permute-done.27.above, ...), custom_call_target="tpu_custom_call" | custom-call | tf_op jit(solution)/shard_map/add_halo2/pallas_call | solution.py:30
  96.7 3.0 %collective-permute-start.32 = (bf16[16,304]{1,0:T(8,128)(2,1)S(1)}, bf16[16,304]{1,0:T(8,128)(2,1)S(1)}, u32[]{:S(2)}, u32[]{:S(2)}) collective-permute-start(bf16[16,304]{1,0:T(8,128)(2,1)S(1)} %get-tuple-element.76), channel_id=1, source_target_pairs={{0,32},{32,64},{64,96},{96,128},{128,160},{160,192},{192,224},{224... | collective-permute-start | bytes 29192 | tf_op jit(solution)/shard_map/ppermute | solution.py:328
  99.7 4.3 %apply2.1.two = f32[3,8,128]{2,1,0:T(8,128)S(1)} custom-call(f32[304,1024]{1,0:T(8,128)S(1)} %get-tuple-element.74.refs_0_.field.two, bf16[512,1024]{1,0:T(8,128)(2,1)S(1)} %get-tuple-element.64.refs_1_, bf16[512,304]{1,0:T(8,128)(2,1)S(1)} %subtract_convert_fusion.refs_2_, bf16[304,512]{1,0:T(8,128)(2,1)S(1)} %subtract_convert_fusion.1.refs_16_.refs_3_, ...), custom_call_target="tpu_custom_call" | custom-call | tf_op jit(solution)/shard_map/apply2/pallas_call | solution.py:30
  104.4 1.1 all_moments.1
  105.5 1.9 %collective-permute-start.33 = (f32[8,128]{1,0:T(8,128)S(1)}, f32[8,128]{1,0:T(8,128)S(1)}, u32[]{:S(2)}, u32[]{:S(2)}) collective-permute-start(f32[8,128]{1,0:T(8,128)S(1)} %all_moments.1), channel_id=1, source_target_pairs={{0,32},{32,0},{64,96},{96,64},{128,160},{160,128},{192,224},{224,1... | collective-permute-start | bytes 12296 | tf_op jit(solution)/shard_map/ppermute | solution.py:328
  108.2 3.2 %collective-permute-start.35 = (f32[8,128]{1,0:T(8,128)S(1)}, f32[8,128]{1,0:T(8,128)S(1)}, u32[]{:S(2)}, u32[]{:S(2)}) collective-permute-start(f32[8,128]{1,0:T(8,128)S(1)} %add.144), channel_id=1, source_target_pairs={{0,64},{32,96},{64,128},{96,160},{128,192},{160,224},{192,0},{224,... | collective-permute-start | bytes 12296 | tf_op jit(solution)/shard_map/ppermute | solution.py:328
  111.5 1.6 %collective-permute-done.36 = f32[8,128]{1,0:T(8,128)S(1)} collective-permute-done((f32[8,128]{1,0:T(8,128)S(1)}, f32[8,128]{1,0:T(8,128)S(1)}, u32[]{:S(2)}, u32[]{:S(2)}) %collective-permute-start.36) | collective-permute-done | bytes 4128 | tf_op jit(solution)/shard_map/ppermute | solution.py:328
  113.0 3.5 %collective-permute-done.34 = f32[8,128]{1,0:T(8,128)S(1)} collective-permute-done((f32[8,128]{1,0:T(8,128)S(1)}, f32[8,128]{1,0:T(8,128)S(1)}, u32[]{:S(2)}, u32[]{:S(2)}) %collective-permute-start.34) | collective-permute-done | bytes 4128 | tf_op jit(solution)/shard_map/ppermute | solution.py:328
  116.6 2.0 %collective-permute-start.38 = (f32[8,128]{1,0:T(8,128)S(1)}, f32[8,128]{1,0:T(8,128)S(1)}, u32[]{:S(2)}, u32[]{:S(2)}) collective-permute-start(f32[8,128]{1,0:T(8,128)S(1)} %add_add_fusion.2), channel_id=1, source_target_pairs={{0,8},{1,9},{2,10},{3,11},{4,12},{5,13},{6,14},{7,15},{8,16},{9,17... | collective-permute-start | bytes 12296 | tf_op jit(solution)/shard_map/ppermute | solution.py:328
  118.6 1.6 %collective-permute-done.39 = f32[8,128]{1,0:T(8,128)S(1)} collective-permute-done((f32[8,128]{1,0:T(8,128)S(1)}, f32[8,128]{1,0:T(8,128)S(1)}, u32[]{:S(2)}, u32[]{:S(2)}) %collective-permute-start.39) | collective-permute-done | bytes 4128 | tf_op jit(solution)/shard_map/ppermute | solution.py:328
  120.2 1.3 collective-permute-done.38
  121.5 2.2 %collective-permute-done.37 = f32[8,128]{1,0:T(8,128)S(1)} collective-permute-done((f32[8,128]{1,0:T(8,128)S(1)}, f32[8,128]{1,0:T(8,128)S(1)}, u32[]{:S(2)}, u32[]{:S(2)}) %collective-permute-start.37) | collective-permute-done | bytes 4128 | tf_op jit(solution)/shard_map/ppermute | solution.py:328
  123.7 3.6 %collective-permute-done.40 = f32[8,128]{1,0:T(8,128)S(1)} collective-permute-done((f32[8,128]{1,0:T(8,128)S(1)}, f32[8,128]{1,0:T(8,128)S(1)}, u32[]{:S(2)}, u32[]{:S(2)}) %collective-permute-start.40) | collective-permute-done | bytes 4128 | tf_op jit(solution)/shard_map/ppermute | solution.py:328
  127.3 1.1 collective-permute-start.43
  128.4 1.8 %collective-permute-start.42 = (f32[8,128]{1,0:T(8,128)S(1)}, f32[8,128]{1,0:T(8,128)S(1)}, u32[]{:S(2)}, u32[]{:S(2)}) collective-permute-start(f32[8,128]{1,0:T(8,128)S(1)} %add.151), channel_id=1, source_target_pairs={{0,2},{1,3},{2,4},{3,5},{4,6},{5,7},{6,0},{7,1},{8,10},{9,11},{10,... | collective-permute-start | bytes 12296 | tf_op jit(solution)/shard_map/ppermute | solution.py:328
  131.9 2.3 %collective-permute-done.42 = f32[8,128]{1,0:T(8,128)S(1)} collective-permute-done((f32[8,128]{1,0:T(8,128)S(1)}, f32[8,128]{1,0:T(8,128)S(1)}, u32[]{:S(2)}, u32[]{:S(2)}) %collective-permute-start.42) | collective-permute-done | bytes 4128 | tf_op jit(solution)/shard_map/ppermute | solution.py:328
  134.2 3.6 %collective-permute-done.41 = f32[8,128]{1,0:T(8,128)S(1)} collective-permute-done((f32[8,128]{1,0:T(8,128)S(1)}, f32[8,128]{1,0:T(8,128)S(1)}, u32[]{:S(2)}, u32[]{:S(2)}) %collective-permute-start.41) | collective-permute-done | bytes 4128 | tf_op jit(solution)/shard_map/ppermute | solution.py:328
  137.8 2.0 %combine.1 = f32[2400,128]{1,0:T(8,128)} custom-call(f32[8,128]{1,0:T(8,128)S(1)} %add_add_fusion.total, f32[304,1024]{1,0:T(8,128)S(1)} %get-tuple-element.63.refs_0_.refs_4_.zero, f32[304,1024]{1,0:T(8,128)S(1)} %get-tuple-element.69.refs_0_.refs_4_.one, f32[304,1024]{1,0:T(8,128)S(1)} %get-tuple-element.74.refs_0_.field.two), custom_call_target="tpu_custom_call" | custom-call | tf_op jit(solution)/shard_map/combine/pallas_call | solution.py:30
  (93 shorter events, 11.6 us)
Async XLA Ops:
  3.1 15.8 %copy-start.3 = (f32[8,1024]{1,0:T(8,128)S(1)}, f32[8,1024]{1,0:T(8,128)}, u32[]{:S(2)}) copy-start(f32[8,1024]{1,0:T(8,128)} %height.3) | copy-start | bytes 98308
  4.2 14.7 %collective-permute-start = (bf16[128,1024]{1,0:T(8,128)(2,1)S(1)}, bf16[128,1024]{1,0:T(8,128)(2,1)S(1)}, u32[]{:S(2)}, u32[]{:S(2)}) collective-permute-start(bf16[128,1024]{1,0:T(8,128)(2,1)S(1)} %get-tuple-element.43), channel_id=1, source_target_pairs={{0,1},{1,2},{2,3},{3,4},{4,5},{5,6},{6,7},{7,8},{8,9},{9,10},{10,1... | collective-permute-start | bytes 786440 | tf_op jit(solution)/shard_map/ppermute | solution.py:328
  6.2 12.7 %collective-permute-start.1 = (bf16[128,1024]{1,0:T(8,128)(2,1)S(1)}, bf16[128,1024]{1,0:T(8,128)(2,1)S(1)}, u32[]{:S(2)}, u32[]{:S(2)}) collective-permute-start(bf16[128,1024]{1,0:T(8,128)(2,1)S(1)} %get-tuple-element.44), channel_id=1, source_target_pairs={{0,31},{1,0},{2,1},{3,2},{4,3},{5,4},{6,5},{7,6},{8,7},{9,8},{10,9... | collective-permute-start | bytes 786440 | tf_op jit(solution)/shard_map/ppermute | solution.py:328
  18.9 21.1 %copy-start.5 = (s32[512,2]{0,1:T(2,128)S(1)}, s32[512,2]{0,1:T(2,128)}, u32[]{:S(2)}) copy-start(s32[512,2]{0,1:T(2,128)} %param.9) | copy-start | bytes 12292
  23.4 3.7 %collective-permute-start.11 = (f32[8,128]{1,0:T(8,128)S(1)}, f32[8,128]{1,0:T(8,128)S(1)}, u32[]{:S(2)}, u32[]{:S(2)}) collective-permute-start(f32[8,128]{1,0:T(8,128)S(1)} %get-tuple-element.53), channel_id=1, source_target_pairs={{0,24},{1,25},{2,26},{3,27},{4,28},{5,29},{6,30},{7,31},{8,0},{9,1... | collective-permute-start | bytes 12296 | tf_op jit(solution)/shard_map/ppermute | solution.py:328
  24.2 4.8 %collective-permute-start.10 = (f32[8,128]{1,0:T(8,128)S(1)}, f32[8,128]{1,0:T(8,128)S(1)}, u32[]{:S(2)}, u32[]{:S(2)}) collective-permute-start(f32[8,128]{1,0:T(8,128)S(1)} %get-tuple-element.53), channel_id=1, source_target_pairs={{0,8},{1,9},{2,10},{3,11},{4,12},{5,13},{6,14},{7,15},{8,16},{9,17... | collective-permute-start | bytes 12296 | tf_op jit(solution)/shard_map/ppermute | solution.py:328
  25.5 5.1 %collective-permute-start.9 = (f32[8,128]{1,0:T(8,128)S(1)}, f32[8,128]{1,0:T(8,128)S(1)}, u32[]{:S(2)}, u32[]{:S(2)}) collective-permute-start(f32[8,128]{1,0:T(8,128)S(1)} %get-tuple-element.53), channel_id=1, source_target_pairs={{0,16},{1,17},{2,18},{3,19},{4,20},{5,21},{6,22},{7,23},{8,24},{9,... | collective-permute-start | bytes 12296 | tf_op jit(solution)/shard_map/ppermute | solution.py:328
  30.6 3.6 %collective-permute-start.12 = (f32[8,128]{1,0:T(8,128)S(1)}, f32[8,128]{1,0:T(8,128)S(1)}, u32[]{:S(2)}, u32[]{:S(2)}) collective-permute-start(f32[8,128]{1,0:T(8,128)S(1)} %add_add_fusion.4), channel_id=1, source_target_pairs={{0,1},{1,0},{2,3},{3,2},{4,5},{5,4},{6,7},{7,6},{8,9},{9,8},{10,11... | collective-permute-start | bytes 12296 | tf_op jit(solution)/shard_map/ppermute | solution.py:328
  34.2 8.6 %collective-permute-start.15 = (f32[8,128]{1,0:T(8,128)S(1)}, f32[8,128]{1,0:T(8,128)S(1)}, u32[]{:S(2)}, u32[]{:S(2)}) collective-permute-start(f32[8,128]{1,0:T(8,128)S(1)} %add.136), channel_id=1, source_target_pairs={{0,6},{1,7},{2,0},{3,1},{4,2},{5,3},{6,4},{7,5},{8,14},{9,15},{10,... | collective-permute-start | bytes 12296 | tf_op jit(solution)/shard_map/ppermute | solution.py:328
  37.4 6.9 %collective-permute-start.14 = (f32[8,128]{1,0:T(8,128)S(1)}, f32[8,128]{1,0:T(8,128)S(1)}, u32[]{:S(2)}, u32[]{:S(2)}) collective-permute-start(f32[8,128]{1,0:T(8,128)S(1)} %add.136), channel_id=1, source_target_pairs={{0,2},{1,3},{2,4},{3,5},{4,6},{5,7},{6,0},{7,1},{8,10},{9,11},{10,... | collective-permute-start | bytes 12296 | tf_op jit(solution)/shard_map/ppermute | solution.py:328
  37.4 7.5 %collective-permute-start.13 = (f32[8,128]{1,0:T(8,128)S(1)}, f32[8,128]{1,0:T(8,128)S(1)}, u32[]{:S(2)}, u32[]{:S(2)}) collective-permute-start(f32[8,128]{1,0:T(8,128)S(1)} %add.136), channel_id=1, source_target_pairs={{0,4},{1,5},{2,6},{3,7},{4,0},{5,1},{6,2},{7,3},{8,12},{9,13},{10,... | collective-permute-start | bytes 12296 | tf_op jit(solution)/shard_map/ppermute | solution.py:328
  40.1 10.4 %copy-start.7 = (bf16[64,1024]{1,0:T(8,128)(2,1)S(1)}, bf16[64,1024]{1,0:T(8,128)(2,1)}, u32[]{:S(2)}) copy-start(bf16[64,1024]{1,0:T(8,128)(2,1)} %get-tuple-element.52) | copy-start | bytes 393220
  40.8 9.7 %collective-permute-start.2 = (bf16[64,1024]{1,0:T(8,128)(2,1)}, bf16[64,1024]{1,0:T(8,128)(2,1)S(1)}, u32[]{:S(2)}, u32[]{:S(2)}) collective-permute-start(bf16[64,1024]{1,0:T(8,128)(2,1)} %get-tuple-element.46), channel_id=1, source_target_pairs={{0,64},{32,96},{64,128},{96,160},{128,192},{160,224},{192,0},{224,... | collective-permute-start | bytes 393224 | tf_op jit(solution)/shard_map/ppermute | solution.py:328
  41.2 9.3 %collective-permute-start.3 = (bf16[64,1024]{1,0:T(8,128)(2,1)}, bf16[64,1024]{1,0:T(8,128)(2,1)S(1)}, u32[]{:S(2)}, u32[]{:S(2)}) collective-permute-start(bf16[64,1024]{1,0:T(8,128)(2,1)} %get-tuple-element.47), channel_id=1, source_target_pairs={{0,192},{32,224},{64,0},{96,32},{128,64},{160,96},{192,128},{224,1... | collective-permute-start | bytes 393224 | tf_op jit(solution)/shard_map/ppermute | solution.py:328
  42.8 8.2 %collective-permute-start.4 = (bf16[64,1024]{1,0:T(8,128)(2,1)}, bf16[64,1024]{1,0:T(8,128)(2,1)S(1)}, u32[]{:S(2)}, u32[]{:S(2)}) collective-permute-start(bf16[64,1024]{1,0:T(8,128)(2,1)} %get-tuple-element.48), channel_id=1, source_target_pairs={{0,128},{32,160},{64,192},{96,224},{128,0},{160,32},{192,64},{224,... | collective-permute-start | bytes 393224 | tf_op jit(solution)/shard_map/ppermute | solution.py:328
  44.2 9.7 %collective-permute-start.5 = (bf16[64,1024]{1,0:T(8,128)(2,1)}, bf16[64,1024]{1,0:T(8,128)(2,1)S(1)}, u32[]{:S(2)}, u32[]{:S(2)}) collective-permute-start(bf16[64,1024]{1,0:T(8,128)(2,1)} %get-tuple-element.49), channel_id=1, source_target_pairs={{0,160},{32,128},{64,224},{96,192},{128,32},{160,0},{192,96},{224,... | collective-permute-start | bytes 393224 | tf_op jit(solution)/shard_map/ppermute | solution.py:328
  44.9 9.2 %collective-permute-start.6 = (bf16[64,1024]{1,0:T(8,128)(2,1)}, bf16[64,1024]{1,0:T(8,128)(2,1)S(1)}, u32[]{:S(2)}, u32[]{:S(2)}) collective-permute-start(bf16[64,1024]{1,0:T(8,128)(2,1)} %get-tuple-element.50), channel_id=1, source_target_pairs={{0,96},{32,64},{64,160},{96,128},{128,224},{160,192},{192,32},{224... | collective-permute-start | bytes 393224 | tf_op jit(solution)/shard_map/ppermute | solution.py:328
  49.3 18.8 %copy-start.4 = (bf16[64,1024]{1,0:T(8,128)(2,1)S(1)}, bf16[64,1024]{1,0:T(8,128)(2,1)}, u32[]{:S(2)}) copy-start(bf16[64,1024]{1,0:T(8,128)(2,1)} %get-tuple-element.45.refs_0_) | copy-start | bytes 393220
  50.4 6.0 %collective-permute-start.7 = (bf16[64,1024]{1,0:T(8,128)(2,1)S(1)}, bf16[64,1024]{1,0:T(8,128)(2,1)S(1)}, u32[]{:S(2)}, u32[]{:S(2)}) collective-permute-start(bf16[64,1024]{1,0:T(8,128)(2,1)S(1)} %copy-done.8), channel_id=1, source_target_pairs={{0,224},{32,192},{64,32},{96,0},{128,96},{160,64},{192,160},{224,1... | collective-permute-start | bytes 393224 | tf_op jit(solution)/shard_map/ppermute | solution.py:328
  50.5 6.5 %collective-permute-start.8 = (bf16[64,1024]{1,0:T(8,128)(2,1)S(1)}, bf16[64,1024]{1,0:T(8,128)(2,1)S(1)}, u32[]{:S(2)}, u32[]{:S(2)}) collective-permute-start(bf16[64,1024]{1,0:T(8,128)(2,1)S(1)} %copy-done.7), channel_id=1, source_target_pairs={{0,32},{32,0},{64,96},{96,64},{128,160},{160,128},{192,224},{224,1... | collective-permute-start | bytes 393224 | tf_op jit(solution)/shard_map/ppermute | solution.py:328
  51.0 9.5 %collective-permute-start.16 = (bf16[64,1024]{1,0:T(8,128)(2,1)S(1)}, bf16[64,1024]{1,0:T(8,128)(2,1)S(1)}, u32[]{:S(2)}, u32[]{:S(2)}) collective-permute-start(bf16[64,1024]{1,0:T(8,128)(2,1)S(1)} %get-tuple-element.56), channel_id=1, source_target_pairs={{0,64},{32,96},{64,128},{96,160},{128,192},{160,224},{192,0},{224,... | collective-permute-start | bytes 393224 | tf_op jit(solution)/shard_map/ppermute | solution.py:328
  53.9 13.0 %collective-permute-start.17 = (bf16[64,1024]{1,0:T(8,128)(2,1)S(1)}, bf16[64,1024]{1,0:T(8,128)(2,1)S(1)}, u32[]{:S(2)}, u32[]{:S(2)}) collective-permute-start(bf16[64,1024]{1,0:T(8,128)(2,1)S(1)} %get-tuple-element.57), channel_id=1, source_target_pairs={{0,192},{32,224},{64,0},{96,32},{128,64},{160,96},{192,128},{224,1... | collective-permute-start | bytes 393224 | tf_op jit(solution)/shard_map/ppermute | solution.py:328
  54.0 13.0 %collective-permute-start.18 = (bf16[64,1024]{1,0:T(8,128)(2,1)S(1)}, bf16[64,1024]{1,0:T(8,128)(2,1)S(1)}, u32[]{:S(2)}, u32[]{:S(2)}) collective-permute-start(bf16[64,1024]{1,0:T(8,128)(2,1)S(1)} %get-tuple-element.58), channel_id=1, source_target_pairs={{0,128},{32,160},{64,192},{96,224},{128,0},{160,32},{192,64},{224,... | collective-permute-start | bytes 393224 | tf_op jit(solution)/shard_map/ppermute | solution.py:328
  56.5 10.6 %collective-permute-start.19 = (bf16[64,1024]{1,0:T(8,128)(2,1)S(1)}, bf16[64,1024]{1,0:T(8,128)(2,1)S(1)}, u32[]{:S(2)}, u32[]{:S(2)}) collective-permute-start(bf16[64,1024]{1,0:T(8,128)(2,1)S(1)} %get-tuple-element.59), channel_id=1, source_target_pairs={{0,160},{32,128},{64,224},{96,192},{128,32},{160,0},{192,96},{224,... | collective-permute-start | bytes 393224 | tf_op jit(solution)/shard_map/ppermute | solution.py:328
  57.0 10.0 %collective-permute-start.20 = (bf16[64,1024]{1,0:T(8,128)(2,1)S(1)}, bf16[64,1024]{1,0:T(8,128)(2,1)S(1)}, u32[]{:S(2)}, u32[]{:S(2)}) collective-permute-start(bf16[64,1024]{1,0:T(8,128)(2,1)S(1)} %get-tuple-element.60), channel_id=1, source_target_pairs={{0,96},{32,64},{64,160},{96,128},{128,224},{160,192},{192,32},{224... | collective-permute-start | bytes 393224 | tf_op jit(solution)/shard_map/ppermute | solution.py:328
  60.5 7.3 %collective-permute-start.21 = (bf16[64,1024]{1,0:T(8,128)(2,1)S(1)}, bf16[64,1024]{1,0:T(8,128)(2,1)S(1)}, u32[]{:S(2)}, u32[]{:S(2)}) collective-permute-start(bf16[64,1024]{1,0:T(8,128)(2,1)S(1)} %get-tuple-element.61), channel_id=1, source_target_pairs={{0,224},{32,192},{64,32},{96,0},{128,96},{160,64},{192,160},{224,1... | collective-permute-start | bytes 393224 | tf_op jit(solution)/shard_map/ppermute | solution.py:328
  66.8 1.3 collective-permute-start.22
  70.0 12.0 %collective-permute-start.26 = (bf16[16,304]{1,0:T(8,128)(2,1)S(1)}, bf16[16,304]{1,0:T(8,128)(2,1)S(1)}, u32[]{:S(2)}, u32[]{:S(2)}) collective-permute-start(bf16[16,304]{1,0:T(8,128)(2,1)S(1)} %get-tuple-element.68), channel_id=1, source_target_pairs={{0,224},{32,0},{64,32},{96,64},{128,96},{160,128},{192,160},{224,1... | collective-permute-start | bytes 29192 | tf_op jit(solution)/shard_map/ppermute | solution.py:328
  70.1 11.8 %collective-permute-start.25 = (bf16[16,304]{1,0:T(8,128)(2,1)S(1)}, bf16[16,304]{1,0:T(8,128)(2,1)S(1)}, u32[]{:S(2)}, u32[]{:S(2)}) collective-permute-start(bf16[16,304]{1,0:T(8,128)(2,1)S(1)} %get-tuple-element.68), channel_id=1, source_target_pairs={{0,32},{32,64},{64,96},{96,128},{128,160},{160,192},{192,224},{224... | collective-permute-start | bytes 29192 | tf_op jit(solution)/shard_map/ppermute | solution.py:328
  70.5 11.5 %collective-permute-start.23 = (bf16[304,128]{1,0:T(8,128)(2,1)S(1)}, bf16[304,128]{1,0:T(8,128)(2,1)S(1)}, u32[]{:S(2)}, u32[]{:S(2)}) collective-permute-start(bf16[304,128]{1,0:T(8,128)(2,1)S(1)} %get-tuple-element.66), channel_id=1, source_target_pairs={{0,1},{1,2},{2,3},{3,4},{4,5},{5,6},{6,7},{7,8},{8,9},{9,10},{10,1... | collective-permute-start | bytes 233480 | tf_op jit(solution)/shard_map/ppermute | solution.py:328
  72.2 9.7 %collective-permute-start.24 = (bf16[304,128]{1,0:T(8,128)(2,1)S(1)}, bf16[304,128]{1,0:T(8,128)(2,1)S(1)}, u32[]{:S(2)}, u32[]{:S(2)}) collective-permute-start(bf16[304,128]{1,0:T(8,128)(2,1)S(1)} %get-tuple-element.67), channel_id=1, source_target_pairs={{0,31},{1,0},{2,1},{3,2},{4,3},{5,4},{6,5},{7,6},{8,7},{9,8},{10,9... | collective-permute-start | bytes 233480 | tf_op jit(solution)/shard_map/ppermute | solution.py:328
  83.2 11.8 %collective-permute-start.27 = (bf16[304,128]{1,0:T(8,128)(2,1)S(1)}, bf16[304,128]{1,0:T(8,128)(2,1)S(1)}, u32[]{:S(2)}, u32[]{:S(2)}) collective-permute-start(bf16[304,128]{1,0:T(8,128)(2,1)S(1)} %get-tuple-element.71), channel_id=1, source_target_pairs={{0,1},{1,2},{2,3},{3,4},{4,5},{5,6},{6,7},{7,8},{8,9},{9,10},{10,1... | collective-permute-start | bytes 233480 | tf_op jit(solution)/shard_map/ppermute | solution.py:328
  83.2 11.8 %collective-permute-start.28 = (bf16[304,128]{1,0:T(8,128)(2,1)S(1)}, bf16[304,128]{1,0:T(8,128)(2,1)S(1)}, u32[]{:S(2)}, u32[]{:S(2)}) collective-permute-start(bf16[304,128]{1,0:T(8,128)(2,1)S(1)} %get-tuple-element.72), channel_id=1, source_target_pairs={{0,31},{1,0},{2,1},{3,2},{4,3},{5,4},{6,5},{7,6},{8,7},{9,8},{10,9... | collective-permute-start | bytes 233480 | tf_op jit(solution)/shard_map/ppermute | solution.py:328
  88.6 6.4 %collective-permute-start.30 = (bf16[16,304]{1,0:T(8,128)(2,1)S(1)}, bf16[16,304]{1,0:T(8,128)(2,1)S(1)}, u32[]{:S(2)}, u32[]{:S(2)}) collective-permute-start(bf16[16,304]{1,0:T(8,128)(2,1)S(1)} %get-tuple-element.73), channel_id=1, source_target_pairs={{0,224},{32,0},{64,32},{96,64},{128,96},{160,128},{192,160},{224,1... | collective-permute-start | bytes 29192 | tf_op jit(solution)/shard_map/ppermute | solution.py:328
  89.1 5.9 %collective-permute-start.29 = (bf16[16,304]{1,0:T(8,128)(2,1)S(1)}, bf16[16,304]{1,0:T(8,128)(2,1)S(1)}, u32[]{:S(2)}, u32[]{:S(2)}) collective-permute-start(bf16[16,304]{1,0:T(8,128)(2,1)S(1)} %get-tuple-element.73), channel_id=1, source_target_pairs={{0,32},{32,64},{64,96},{96,128},{128,160},{160,192},{192,224},{224... | collective-permute-start | bytes 29192 | tf_op jit(solution)/shard_map/ppermute | solution.py:328
  96.7 7.7 %collective-permute-start.31 = (bf16[304,128]{1,0:T(8,128)(2,1)S(1)}, bf16[304,128]{1,0:T(8,128)(2,1)S(1)}, u32[]{:S(2)}, u32[]{:S(2)}) collective-permute-start(bf16[304,128]{1,0:T(8,128)(2,1)S(1)} %get-tuple-element.75), channel_id=1, source_target_pairs={{0,1},{1,2},{2,3},{3,4},{4,5},{5,6},{6,7},{7,8},{8,9},{9,10},{10,1... | collective-permute-start | bytes 233480 | tf_op jit(solution)/shard_map/ppermute | solution.py:328
  96.7 7.2 %collective-permute-start.32 = (bf16[16,304]{1,0:T(8,128)(2,1)S(1)}, bf16[16,304]{1,0:T(8,128)(2,1)S(1)}, u32[]{:S(2)}, u32[]{:S(2)}) collective-permute-start(bf16[16,304]{1,0:T(8,128)(2,1)S(1)} %get-tuple-element.76), channel_id=1, source_target_pairs={{0,32},{32,64},{64,96},{96,128},{128,160},{160,192},{192,224},{224... | collective-permute-start | bytes 29192 | tf_op jit(solution)/shard_map/ppermute | solution.py:328
  105.5 2.7 %collective-permute-start.33 = (f32[8,128]{1,0:T(8,128)S(1)}, f32[8,128]{1,0:T(8,128)S(1)}, u32[]{:S(2)}, u32[]{:S(2)}) collective-permute-start(f32[8,128]{1,0:T(8,128)S(1)} %all_moments.1), channel_id=1, source_target_pairs={{0,32},{32,0},{64,96},{96,64},{128,160},{160,128},{192,224},{224,1... | collective-permute-start | bytes 12296 | tf_op jit(solution)/shard_map/ppermute | solution.py:328
  108.2 4.8 %collective-permute-start.36 = (f32[8,128]{1,0:T(8,128)S(1)}, f32[8,128]{1,0:T(8,128)S(1)}, u32[]{:S(2)}, u32[]{:S(2)}) collective-permute-start(f32[8,128]{1,0:T(8,128)S(1)} %add.144), channel_id=1, source_target_pairs={{0,192},{32,224},{64,0},{96,32},{128,64},{160,96},{192,128},{224,1... | collective-permute-start | bytes 12296 | tf_op jit(solution)/shard_map/ppermute | solution.py:328
  108.2 4.8 %collective-permute-start.35 = (f32[8,128]{1,0:T(8,128)S(1)}, f32[8,128]{1,0:T(8,128)S(1)}, u32[]{:S(2)}, u32[]{:S(2)}) collective-permute-start(f32[8,128]{1,0:T(8,128)S(1)} %add.144), channel_id=1, source_target_pairs={{0,64},{32,96},{64,128},{96,160},{128,192},{160,224},{192,0},{224,... | collective-permute-start | bytes 12296 | tf_op jit(solution)/shard_map/ppermute | solution.py:328
  111.5 5.1 %collective-permute-start.34 = (f32[8,128]{1,0:T(8,128)S(1)}, f32[8,128]{1,0:T(8,128)S(1)}, u32[]{:S(2)}, u32[]{:S(2)}) collective-permute-start(f32[8,128]{1,0:T(8,128)S(1)} %add.144), channel_id=1, source_target_pairs={{0,128},{32,160},{64,192},{96,224},{128,0},{160,32},{192,64},{224,... | collective-permute-start | bytes 12296 | tf_op jit(solution)/shard_map/ppermute | solution.py:328
  116.6 3.6 %collective-permute-start.39 = (f32[8,128]{1,0:T(8,128)S(1)}, f32[8,128]{1,0:T(8,128)S(1)}, u32[]{:S(2)}, u32[]{:S(2)}) collective-permute-start(f32[8,128]{1,0:T(8,128)S(1)} %add_add_fusion.2), channel_id=1, source_target_pairs={{0,24},{1,25},{2,26},{3,27},{4,28},{5,29},{6,30},{7,31},{8,0},{9,1... | collective-permute-start | bytes 12296 | tf_op jit(solution)/shard_map/ppermute | solution.py:328
  116.6 4.9 %collective-permute-start.38 = (f32[8,128]{1,0:T(8,128)S(1)}, f32[8,128]{1,0:T(8,128)S(1)}, u32[]{:S(2)}, u32[]{:S(2)}) collective-permute-start(f32[8,128]{1,0:T(8,128)S(1)} %add_add_fusion.2), channel_id=1, source_target_pairs={{0,8},{1,9},{2,10},{3,11},{4,12},{5,13},{6,14},{7,15},{8,16},{9,17... | collective-permute-start | bytes 12296 | tf_op jit(solution)/shard_map/ppermute | solution.py:328
  118.6 5.1 %collective-permute-start.37 = (f32[8,128]{1,0:T(8,128)S(1)}, f32[8,128]{1,0:T(8,128)S(1)}, u32[]{:S(2)}, u32[]{:S(2)}) collective-permute-start(f32[8,128]{1,0:T(8,128)S(1)} %add_add_fusion.2), channel_id=1, source_target_pairs={{0,16},{1,17},{2,18},{3,19},{4,20},{5,21},{6,22},{7,23},{8,24},{9,... | collective-permute-start | bytes 12296 | tf_op jit(solution)/shard_map/ppermute | solution.py:328
  123.7 3.6 %collective-permute-start.40 = (f32[8,128]{1,0:T(8,128)S(1)}, f32[8,128]{1,0:T(8,128)S(1)}, u32[]{:S(2)}, u32[]{:S(2)}) collective-permute-start(f32[8,128]{1,0:T(8,128)S(1)} %add_add_fusion.1), channel_id=1, source_target_pairs={{0,1},{1,0},{2,3},{3,2},{4,5},{5,4},{6,7},{7,6},{8,9},{9,8},{10,11... | collective-permute-start | bytes 12296 | tf_op jit(solution)/shard_map/ppermute | solution.py:328
  127.3 4.5 %collective-permute-start.43 = (f32[8,128]{1,0:T(8,128)S(1)}, f32[8,128]{1,0:T(8,128)S(1)}, u32[]{:S(2)}, u32[]{:S(2)}) collective-permute-start(f32[8,128]{1,0:T(8,128)S(1)} %add.151), channel_id=1, source_target_pairs={{0,6},{1,7},{2,0},{3,1},{4,2},{5,3},{6,4},{7,5},{8,14},{9,15},{10,... | collective-permute-start | bytes 12296 | tf_op jit(solution)/shard_map/ppermute | solution.py:328
  128.4 5.7 %collective-permute-start.42 = (f32[8,128]{1,0:T(8,128)S(1)}, f32[8,128]{1,0:T(8,128)S(1)}, u32[]{:S(2)}, u32[]{:S(2)}) collective-permute-start(f32[8,128]{1,0:T(8,128)S(1)} %add.151), channel_id=1, source_target_pairs={{0,2},{1,3},{2,4},{3,5},{4,6},{5,7},{6,0},{7,1},{8,10},{9,11},{10,... | collective-permute-start | bytes 12296 | tf_op jit(solution)/shard_map/ppermute | solution.py:328
  130.3 7.5 %collective-permute-start.41 = (f32[8,128]{1,0:T(8,128)S(1)}, f32[8,128]{1,0:T(8,128)S(1)}, u32[]{:S(2)}, u32[]{:S(2)}) collective-permute-start(f32[8,128]{1,0:T(8,128)S(1)} %add.151), channel_id=1, source_target_pairs={{0,4},{1,5},{2,6},{3,7},{4,0},{5,1},{6,2},{7,3},{8,12},{9,13},{10,... | collective-permute-start | bytes 12296 | tf_op jit(solution)/shard_map/ppermute | solution.py:328
  (5 other events, 23.9 us)

commit v4 on v3

--- a/solution.py
+++ b/solution.py
@@ -23,7 +23,7 @@
     return pltpu.HBM(shape, dtype)
 
 
-def call(body, outs, *args, specs=None, out_specs=None, scratch=(), name=None):
+def call(body, outs, *args, specs=None, out_specs=None, scratch=(), aliases=None, name=None):
     flat = outs if isinstance(outs, (list, tuple)) else [outs]
     places = specs or [pltpu.VMEM] * len(args)
     out_places = [pl.BlockSpec(memory_space=place) for place in out_specs or [pltpu.VMEM] * len(flat)]
@@ -33,6 +33,7 @@
         in_specs=[pl.BlockSpec(memory_space=place) for place in places],
         out_specs=out_places if isinstance(outs, (list, tuple)) else out_places[0],
         scratch_shapes=list(scratch),
+        input_output_aliases=aliases or {},
         compiler_params=pltpu.CompilerParams(vmem_limit_bytes=16 * 1024 * 1024),
         name=name,
     )(*args)
@@ -77,67 +78,125 @@
     return total
 
 
-def smoothing(flags, owners, phase_t, coher_t, above, below, mask, height, smooth_out, sums, *rest):
-    outs, weights, totals, smooth, sems = rest[:8], rest[8], rest[9], rest[10], rest[11]
+OFFSETS = ((0, 0), (1, 0), (3, 0), (2, 0), (2, 1), (1, 1), (3, 1), (0, 1))
+
+
+def other(index, chips, core):
+    return (((index >> 1) + chips) & 3) * 2 + ((index & 1) ^ core)
+
+
+def owner(step):
+    return other(lax.axis_index("ifg"), *OFFSETS[step])
+
+
+def smooth_row(rows, lane, mask, terrain):
+    denom = shifted_sum(rows[0][0] + rows[1][0] + rows[2][0], lane, 1023)
+    numer = shifted_sum(rows[0][1] + rows[1][1] + rows[2][1], lane, 1023)
+    top = fold_lanes(numer * terrain)
+    low = fold_lanes(denom * (terrain * terrain))
+    return numer / denom, (mask * (denom / 9.0)).astype(BF16), top, low
+
+
+def load_row(phase_t, coher_t, row, ifgs):
+    coher = coher_t[row, ifgs, :].astype(F32)
+    return coher, coher * phase_t[row, ifgs, :].astype(F32)
+
+
+def block_of(block):
+    return pl.ds(pl.multiple_of(block * 16, 16), 16), pl.ds(pl.multiple_of(block * 16 + 64, 16), 16)
+
+
+def inner_rows(phase_t, coher_t, mask, height, smooth_out, totals, *rest):
+    outs, weights, smooth, sems = rest[:8], rest[8], rest[9], rest[10]
     lane = lax.broadcasted_iota(jnp.int32, (16, 1024), 1)
-    edge_flag = {-1: flags[0] > 0, 8: flags[1] > 0}
 
     def copies(block):
-        ifgs = pl.ds(pl.multiple_of(block * 16, 16), 16)
+        ifgs, _ = block_of(block)
         return [
-            pltpu.make_async_copy(weights.at[owners[step], ifgs], out.at[ifgs], sems.at[block, step])
+            pltpu.make_async_copy(
+                weights.at[owner(step), ifgs], out.at[ifgs, pl.ds(128, 768)], sems.at[block, step]
+            )
             for step, out in enumerate(outs)
-        ] + [pltpu.make_async_copy(smooth.at[:, ifgs], smooth_out.at[:, ifgs], sems.at[block, 8])]
+        ] + [pltpu.make_async_copy(smooth.at[:, ifgs], smooth_out.at[pl.ds(1, 6), ifgs], sems.at[block, 8])]
 
     def group(block, _):
-        ifgs = pl.ds(pl.multiple_of(block * 16, 16), 16)
-        cohers = pl.ds(pl.multiple_of(block * 16 + 64, 16), 16)
+        ifgs, lows = block_of(block)
         masks = mask[ifgs, :]
-
-        def load(row):
-            if row < 0 or row > 7:
-                edge = above if row < 0 else below
-                coher = jnp.where(edge_flag[row], edge[cohers, :].astype(F32), 0.0)
-                return coher, coher * edge[ifgs, :].astype(F32)
-            coher = coher_t[row, ifgs, :].astype(F32)
-            return coher, coher * phase_t[row, ifgs, :].astype(F32)
-
-        before, current = load(-1), load(0)
+        rows = [load_row(phase_t, coher_t, row, ifgs) for row in (0, 1)]
         top = jnp.zeros((16, 128), F32)
         low = jnp.zeros((16, 128), F32)
-        for row in range(8):
-            after = load(row + 1)
-            denom = shifted_sum(before[0] + current[0] + after[0], lane, 1023)
-            numer = shifted_sum(before[1] + current[1] + after[1], lane, 1023)
-            terrain = height[pl.ds(row, 1), :]
-            top += fold_lanes(numer * terrain)
-            low += fold_lanes(denom * (terrain * terrain))
-            smooth[row, ifgs, :] = numer / denom
-            weight = (masks[:, row : row + 1] * (denom / 9.0)).astype(BF16)
+        for row in range(1, 7):
+            rows.append(load_row(phase_t, coher_t, row + 1, ifgs))
+            value, weight, more_top, more_low = smooth_row(
+                rows, lane, masks[:, row : row + 1], height[pl.ds(row, 1), :]
+            )
+            rows = rows[1:]
+            top += more_top
+            low += more_low
+            smooth[row - 1, ifgs, :] = value
             for tile in range(8):
-                weights[tile, ifgs, pl.ds(row * 128, 128)] = weight[:, tile * 128 : tile * 128 + 128]
-            before, current = current, after
+                weights[tile, ifgs, pl.ds((row - 1) * 128, 128)] = weight[:, tile * 128 : tile * 128 + 128]
         totals[ifgs, :] = top
-        totals[cohers, :] = low
+        totals[lows, :] = low
         for copy in copies(block):
             copy.start()
         return 0
 
     lax.fori_loop(0, 4, group, 0)
-    sums[...] = jnp.broadcast_to(jnp.sum(totals[...].T, axis=0, keepdims=True), sums.shape)
     for block in range(4):
         for copy in copies(block):
             copy.wait()
 
 
-def pick_blocks(source, owners, outs):
-    for step, out in enumerate(outs):
-        out[...] = source[owners[step]]
-
-
-def correction(owners, sums, smooth, height, slope_row, *rest):
+def border_rows(phase_t, coher_t, above, below, mask, height, totals, *rest):
+    smooth_out, sums, outs = rest[9], rest[10], rest[11:19]
+    weights, smooth, added, sems = rest[19:]
+    lane = lax.broadcasted_iota(jnp.int32, (16, 1024), 1)
+    my_row = lax.axis_index("rows")
+    valid = (my_row > 0, my_row < lax.axis_size("rows") - 1)
+
+    def group(block, _):
+        ifgs, lows = block_of(block)
+        masks = mask[ifgs, :]
+        top = totals[ifgs, :]
+        low = totals[lows, :]
+        for side, (edge, row) in enumerate(((above, 0), (below, 7))):
+            coher = jnp.where(valid[side], edge[lows, :].astype(F32), 0.0)
+            rows = [(coher, coher * edge[ifgs, :].astype(F32))]
+            rows += [load_row(phase_t, coher_t, near, ifgs) for near in (row, 1 if row == 0 else 6)]
+            value, weight, more_top, more_low = smooth_row(
+                rows, lane, masks[:, row : row + 1], height[pl.ds(row, 1), :]
+            )
+            top += more_top
+            low += more_low
+            smooth[side, ifgs, :] = value
+            for tile in range(8):
+                weights[side, tile, ifgs, :] = weight[:, tile * 128 : tile * 128 + 128]
+        added[ifgs, :] = top
+        added[lows, :] = low
+        return 0
+
+    lax.fori_loop(0, 4, group, 0)
+    copies = []
+    for side, row in ((0, 0), (1, 7)):
+        copies.append(pltpu.make_async_copy(smooth.at[side], smooth_out.at[row], sems.at[side, 8]))
+        for step, out in enumerate(outs):
+            lanes = pl.ds(row * 128, 128)
+            copies.append(
+                pltpu.make_async_copy(weights.at[side, owner(step)], out.at[:, lanes], sems.at[side, step])
+            )
+    for copy in copies:
+        copy.start()
+    sums[...] = jnp.broadcast_to(jnp.sum(added[...].T, axis=0)[None, None, :], sums.shape)
+    for copy in copies:
+        copy.wait()
+
+
+def correction(sums, smooth, height, slope_row, *rest):
     outs, blocks = rest[:8], rest[8]
-    total = sums[...]
+    total = sums[0]
+    for index in range(1, sums.shape[0]):
+        total += sums[index]
     slope_row[...] = total / pltpu.roll(total, 64, 1)
     column = jnp.broadcast_to(total[0:1, :], (128, 128)).T
     slope = column[:64, :] / column[64:, :]
@@ -150,7 +209,8 @@
         return 0
 
     lax.fori_loop(0, 8, one_tile, 0)
-    pick_blocks(blocks, owners, outs)
+    for step, out in enumerate(outs):
+        out[...] = blocks[owner(step)]
 
 
 def column_selector():
@@ -259,10 +319,16 @@
 
 
 def keep(flag, values):
-    return jnp.where(flag > 0, values.astype(F32), 0.0)
-
-
-def add_halo(flags, image, above, below, left, right, field, first, last, columns):
+    return jnp.where(flag, values.astype(F32), 0.0)
+
+
+def inside():
+    row, col = lax.axis_index("rows"), lax.axis_index("ifg")
+    return row > 0, row < lax.axis_size("rows") - 1, col > 0, col < lax.axis_size("ifg") - 1
+
+
+def add_halo(image, above, below, left, right, field, first, last, columns):
+    flags = inside()
     sides = jnp.concatenate([keep(flags[2], left[8:16, :]), keep(flags[3], right[0:8, :])], axis=0).astype(BF16)
     for row in range(8):
         lanes = pl.ds(row * 128, 128)
@@ -275,7 +341,8 @@
     write_edges(field, first, last, columns)
 
 
-def all_moments(flags, field, above, left, zero, one, two, out):
+def all_moments(field, above, left, zero, one, two, out):
+    flags = inside()
     sides = jnp.concatenate([keep(flags[2], left[8:16, :]), jnp.zeros((8, DP), F32)], axis=0).astype(BF16)
     ahead = two[2]
     for row in range(8):
@@ -288,8 +355,15 @@
     out[...] = jnp.concatenate(sums + [jnp.zeros((2, 128), F32)], axis=0)
 
 
-def combine(total, zero, one, two, out):
-    sums = jnp.sum(total[...], axis=1, keepdims=True)
+def add_and_spread(one, two, out):
+    out[...] = jnp.broadcast_to((one[...] + two[...])[None], out.shape)
+
+
+def combine(parts, zero, one, two, out):
+    total = parts[0]
+    for index in range(1, parts.shape[0]):
+        total += parts[index]
+    sums = jnp.sum(total, axis=1, keepdims=True)
     m0, m1, m2, m3, m4, m5 = (jnp.broadcast_to(sums[i : i + 1, :], (1, 128)) for i in range(6))
     t00, t01, t11 = m1 + SHIFT * m0, m2 + SHIFT * m1, m3 + SHIFT * m2
     t12, t22 = m4 + SHIFT * m3, m5 + SHIFT * m4
@@ -314,15 +388,7 @@
 
 def per_device(phase, coherence, height, gap_mask, date_pairs):
     n_ifg, n_rows = lax.axis_size("ifg"), lax.axis_size("rows")
-    n_chip = n_ifg // 2
-    me, my_row = lax.axis_index("ifg"), lax.axis_index("rows")
-    offsets = ((0, 0), (1, 0), (3, 0), (2, 0), (2, 1), (1, 1), (3, 1), (0, 1))
-
-    def other(index, chips, core):
-        return (((index >> 1) + chips) & (n_chip - 1)) * 2 + ((index & 1) ^ core)
-
-    owners = jnp.stack([other(me, *offset) for offset in offsets]).astype(jnp.int32)
-    flags = jnp.stack([my_row > 0, my_row < n_rows - 1, me > 0, me < n_ifg - 1]).astype(jnp.int32)
+    me = lax.axis_index("ifg")
 
     def permute(values, axis, target):
         return lax.ppermute(values, axis, [(i, target(i)) for i in range(lax.axis_size(axis))])
@@ -332,15 +398,6 @@
 
     def backward(values, axis):
         return permute(values, axis, lambda i: (i - 1) % lax.axis_size(axis))
-
-    def ring_of_four(values, axis, target):
-        moved = [permute(values, axis, lambda i: target(i, k)) for k in (1, 2, 3)]
-        return (values + moved[1]) + (moved[0] + moved[2])
-
-    def sum_rows(values):
-        values = ring_of_four(values, "rows", lambda i, k: (i + 8 * k) % n_rows)
-        values = values + permute(values, "rows", lambda i: i ^ 1)
-        return ring_of_four(values, "rows", lambda i, k: i // 8 * 8 + (i + 2 * k) % 8)
 
     stacked = sds((8, 64, 1024), BF16)
     edge = sds((128, 1024), BF16)
@@ -354,49 +411,67 @@
     )
     above, below = forward(last, "rows"), backward(first, "rows")
     block = sds((64, 1024), BF16)
+    mask = gap_mask.astype(F32)
+    pieces = [in_hbm((64, 1024), BF16)] * 8
+    smooth, totals, *weight_parts = call(
+        inner_rows,
+        [in_hbm((8, 64, 1024), F32), sds((128, 128), F32)] + pieces,
+        phase_t,
+        coher_t,
+        mask,
+        height,
+        out_specs=[pltpu.HBM, pltpu.VMEM] + [pltpu.HBM] * 8,
+        scratch=(
+            pltpu.VMEM((8, 64, 768), BF16),
+            pltpu.VMEM((6, 64, 1024), F32),
+            pltpu.SemaphoreType.DMA((4, 9)),
+        ),
+        name="inner_rows",
+    )
     smooth, sums, *weight_parts = call(
-        smoothing,
-        [in_hbm((8, 64, 1024), F32), sds((8, 128), F32)] + [in_hbm((64, 1024), BF16)] * 8,
-        flags,
-        owners,
+        border_rows,
+        [in_hbm((8, 64, 1024), F32), sds((n_rows, 8, 128), F32)] + pieces,
         phase_t,
         coher_t,
         above,
         below,
-        gap_mask.astype(F32),
+        mask,
         height,
-        specs=[pltpu.SMEM] * 2 + [pltpu.VMEM] * 6,
+        totals,
+        smooth,
+        *weight_parts,
+        specs=[pltpu.VMEM] * 7 + [pltpu.HBM] * 9,
         out_specs=[pltpu.HBM, pltpu.VMEM] + [pltpu.HBM] * 8,
         scratch=(
-            pltpu.VMEM((8, 64, 1024), BF16),
+            pltpu.VMEM((2, 8, 64, 128), BF16),
+            pltpu.VMEM((2, 64, 1024), F32),
             pltpu.VMEM((128, 128), F32),
-            pltpu.VMEM((8, 64, 1024), F32),
-            pltpu.SemaphoreType.DMA((4, 9)),
+            pltpu.SemaphoreType.DMA((2, 9)),
         ),
-        name="smoothing",
-    )
-    sums = sum_rows(sums)
+        aliases={7: 0, **{8 + step: 2 + step for step in range(8)}},
+        name="border_rows",
+    )
 
     def exchange(parts):
         return [parts[0]] + [
             permute(part, "ifg", lambda i: other(i, *offset))
-            for part, offset in zip(parts[1:], offsets[1:])
+            for part, offset in zip(parts[1:], OFFSETS[1:])
         ]
 
     weight_parts = exchange(weight_parts)
+    sums, weight_parts[7] = lax.optimization_barrier((sums, weight_parts[7]))
+    sums = lax.all_to_all(sums, "rows", 0, 0, tiled=True)
     slope_row, *corrected_parts = call(
         correction,
         [sds((8, 128), F32)] + [block] * 8,
-        owners,
         sums,
         smooth,
         height,
-        specs=[pltpu.SMEM] + [pltpu.VMEM] * 3,
         scratch=(pltpu.VMEM((8, 64, 1024), BF16),),
         name="correction",
     )
     corrected_parts = exchange(corrected_parts)
-    sources = jnp.stack([other(me, n_chip - chips, core) for chips, core in offsets])
+    sources = jnp.stack([other(me, 4 - chips, core) for chips, core in OFFSETS])
     pairs = date_pairs.reshape(n_ifg, -1, 2)[sources].reshape(-1, 2)
     dates = jnp.arange(DP, dtype=jnp.int32)
     design = ((dates[None] == pairs[:, 1:2]).astype(F32) - (dates[None] == pairs[:, 0:1]).astype(F32)).astype(BF16)
@@ -428,8 +503,7 @@
         return call(body, outs, *args, name=name)
 
     def joined(image, around, name):
-        specs = [pltpu.SMEM] + [pltpu.VMEM] * 5
-        return call(add_halo, (field,) + edges, flags, image, *around, specs=specs, name=name)
+        return call(add_halo, (field,) + edges, image, *around, name=name)
 
     around = halos(first, last, columns)
     image, mom0 = local(False, True, "apply0", k0, weights, design, design_t)
@@ -442,19 +516,25 @@
     part = call(
         all_moments,
         sds((8, 128), F32),
-        flags,
         k2,
         above,
         left,
         mom0,
         mom1,
         mom2,
-        specs=[pltpu.SMEM] + [pltpu.VMEM] * 6,
         name="all_moments",
     )
-    part = part + permute(part, "ifg", lambda i: i ^ 1)
-    part = sum_rows(ring_of_four(part, "ifg", lambda i, k: (i + 2 * k) % n_ifg))
-    displacement = call(combine, sds((DATES * 8, 128), F32), part, k0, k1, k2, name="combine")
+    for step in (1, 2):
+        part = part + permute(part, "ifg", lambda i: i ^ step)
+    parts = call(
+        add_and_spread,
+        sds((n_rows, 8, 128), F32),
+        part,
+        permute(part, "ifg", lambda i: i ^ 4),
+        name="add_and_spread",
+    )
+    parts = lax.all_to_all(parts, "rows", 0, 0, tiled=True)
+    displacement = call(combine, sds((DATES * 8, 128), F32), parts, k0, k1, k2, name="combine")
     return displacement.reshape(DATES, 8, 128), slope_row[0, :64]
 
 

time: 140 us -> 130 us (0.929)
  waiting for transfers between devices: 44.1 us -> 38 us
  starting transfers between devices: 61.2 us -> 55.6 us
    ppermute x44 -> x29, waiting for transfers between devices: 44.1 us -> 22.2 us  [permute(): lax.ppermute(values, axis, [(i, target(i)) for i in range(lax.axis_size(a...]
    ppermute x44 -> x29, starting transfers between devices: 61.2 us -> 42 us  [permute(): lax.ppermute(values, axis, [(i, target(i)) for i in range(lax.axis_size(a...]
    all_to_all x0 -> x2, waiting for transfers between devices: none -> 15.8 us  [the longest x1 9.89 us: per_device(): parts = lax.all_to_all(parts, 'rows', 0, 0, tiled=True)]
    all_to_all x0 -> x2, starting transfers between devices: none -> 13.6 us  [the longest x1 6.81 us: per_device(): sums = lax.all_to_all(sums, 'rows', 0, 0, tiled=True)]
    unnamed x18 -> x21, local copies, waits for them, and re-layouts: 4.05 us -> 5.43 us
    pallas_call x11 -> x13, Pallas kernels: 27.5 us -> 27.5 us  [call(): pl.pallas_call(body, out_shape=outs, in_specs=[pl.BlockSpec(memory_space=...]
  transfers between devices with their start and end apart: 44 -> 31, of which waited for: 22 -> 12; matrix products, arithmetic and copies ran while one was open for 1% -> 1% of each run, Pallas kernels for 10% -> 13%
where the time goes in v4:
time: 130 us; the launch traced here: 129 us
  starting transfers between devices  55.6 us (43%)
  waiting for transfers between devices  38 us (29%)
  Pallas kernels  27.5 us (21%)
  local copies, waits for them, and re-layouts  6.8 us (5%)
    ppermute x29, starting transfers between devices, permute(): lax.ppermute(values, axis, [(i, target(i)) for i in range(lax.axis_size(a...  42 us
    pallas_call x13, Pallas kernels, call(): pl.pallas_call(body, out_shape=outs, in_specs=[pl.BlockSpec(memory_space=...  27.5 us
    ppermute x29, waiting for transfers between devices, permute(): lax.ppermute(values, axis, [(i, target(i)) for i in range(lax.axis_size(a...  22.2 us
    all_to_all x1, waiting for transfers between devices, per_device(): parts = lax.all_to_all(parts, 'rows', 0, 0, tiled=True)  9.89 us
    all_to_all x1, starting transfers between devices, per_device(): sums = lax.all_to_all(sums, 'rows', 0, 0, tiled=True)  6.81 us
    all_to_all x1, starting transfers between devices, per_device(): parts = lax.all_to_all(parts, 'rows', 0, 0, tiled=True)  6.78 us
    all_to_all x1, waiting for transfers between devices, per_device(): sums = lax.all_to_all(sums, 'rows', 0, 0, tiled=True)  5.93 us
    unnamed x21, local copies, waits for them, and re-layouts  5.43 us
  transfers between devices with their start and end apart: 31, of which 12 were waited for; matrix products, arithmetic and copies ran while one was open for 1% of the time, Pallas kernels for 13%

profile of v4, /device:TPU:6, one launch (start us, length us, event | category | flops | bytes accessed | tf_op | source)
XLA Modules:
  0.0 129.2 jit_solution(11107975431817371867)
XLA Ops:
  0.6 1.2 copy-done.3
  1.9 1.2 copy-done.4
  3.1 1.1 rows_first.1
  4.2 2.0 %collective-permute-start = (bf16[128,1024]{1,0:T(8,128)(2,1)S(1)}, bf16[128,1024]{1,0:T(8,128)(2,1)S(1)}, u32[]{:S(2)}, u32[]{:S(2)}) collective-permute-start(bf16[128,1024]{1,0:T(8,128)(2,1)S(1)} %get-tuple-element.55), channel_id=1, source_target_pairs={{0,1},{1,2},{2,3},{3,4},{4,5},{5,6},{6,7},{7,8},{8,9},{9,10},{10,1... | collective-permute-start | bytes 786440 | tf_op jit(solution)/shard_map/ppermute | solution.py:394
  6.2 6.5 %collective-permute-start.1 = (bf16[128,1024]{1,0:T(8,128)(2,1)S(1)}, bf16[128,1024]{1,0:T(8,128)(2,1)S(1)}, u32[]{:S(2)}, u32[]{:S(2)}) collective-permute-start(bf16[128,1024]{1,0:T(8,128)(2,1)S(1)} %get-tuple-element.56), channel_id=1, source_target_pairs={{0,31},{1,0},{2,1},{3,2},{4,3},{5,4},{6,5},{7,6},{8,7},{9,8},{10,9... | collective-permute-start | bytes 786440 | tf_op jit(solution)/shard_map/ppermute | solution.py:394
  12.8 3.3 %inner_rows.1 = (f32[8,64,1024]{2,1,0:T(8,128)}, f32[128,128]{1,0:T(8,128)S(1)}, bf16[64,1024]{1,0:T(8,128)(2,1)}, bf16[64,1024]{1,0:T(8,128)(2,1)}, bf16[64,102...) custom-call(bf16[8,64,1024]{2,1,0:T(8,128)(2,1)S(1)} %get-tuple-elem, ...), custom_call_target="tpu_custom_call" | custom-call | tf_op jit(solution)/shard_map/inner_rows/pallas_call | solution.py:30
  16.0 2.8 %collective-permute-done.above = bf16[128,1024]{1,0:T(8,128)(2,1)S(1)} collective-permute-done((bf16[128,1024]{1,0:T(8,128)(2,1)S(1)}, bf16[128,1024]{1,0:T(8,128)(2,1)S(1)}, u32[]{:S(2)}, u32[]{:S(2)}) %collective-permute-start) | collective-permute-done | bytes 262176 | tf_op jit(solution)/shard_map/ppermute | solution.py:394
  18.9 2.6 %border_rows.1 = (f32[8,64,1024]{2,1,0:T(8,128)}, f32[32,8,128]{2,1,0:T(8,128)}, bf16[64,1024]{1,0:T(8,128)(2,1)}, bf16[64,1024]{1,0:T(8,128)(2,1)}, bf16[64,102...) custom-call(bf16[8,64,1024]{2,1,0:T(8,128)(2,1)S(1)} %get-tuple-elem, ...), custom_call_target="tpu_custom_call", output_to_operand_aliasing={{0}: (7, {}), {2}: (8, {}), {3}: (9, {}), {4}: (10, {}), {5... | custom-call | tf_op jit(solution)/shard_map/border_rows/pallas_call | solution.py:30
  22.2 1.5 %collective-permute-start.3 = (bf16[64,1024]{1,0:T(8,128)(2,1)}, bf16[64,1024]{1,0:T(8,128)(2,1)S(1)}, u32[]{:S(2)}, u32[]{:S(2)}) collective-permute-start(bf16[64,1024]{1,0:T(8,128)(2,1)} %get-tuple-element.69), channel_id=1, source_target_pairs={{0,192},{32,224},{64,0},{96,32},{128,64},{160,96},{192,128},{224,1... | collective-permute-start | bytes 393224 | tf_op jit(solution)/shard_map/ppermute | solution.py:394
  23.7 1.4 %collective-permute-start.4 = (bf16[64,1024]{1,0:T(8,128)(2,1)}, bf16[64,1024]{1,0:T(8,128)(2,1)S(1)}, u32[]{:S(2)}, u32[]{:S(2)}) collective-permute-start(bf16[64,1024]{1,0:T(8,128)(2,1)} %get-tuple-element.70), channel_id=1, source_target_pairs={{0,128},{32,160},{64,192},{96,224},{128,0},{160,32},{192,64},{224,... | collective-permute-start | bytes 393224 | tf_op jit(solution)/shard_map/ppermute | solution.py:394
  25.1 6.8 %all-to-all-start = ((f32[32,8,128]{2,1,0:T(8,128)}), f32[32,8,128]{2,1,0:T(8,128)S(1)}, u32[]{:S(2)}, u32[]{:S(2)}) async-start(f32[32,8,128]{2,1,0:T(8,128)} %get-tuple-element.77), calls=%async_computation | async-start | bytes 262144 | tf_op jit(solution)/shard_map/all_to_all | solution.py:463
  32.1 0.6 gather_fusion
  32.8 1.1 collective-permute-start.5
  33.9 2.4 %collective-permute-start.6 = (bf16[64,1024]{1,0:T(8,128)(2,1)}, bf16[64,1024]{1,0:T(8,128)(2,1)S(1)}, u32[]{:S(2)}, u32[]{:S(2)}) collective-permute-start(bf16[64,1024]{1,0:T(8,128)(2,1)} %get-tuple-element.72), channel_id=1, source_target_pairs={{0,96},{32,64},{64,160},{96,128},{128,224},{160,192},{192,32},{224... | collective-permute-start | bytes 393224 | tf_op jit(solution)/shard_map/ppermute | solution.py:394
  36.3 5.9 %all-to-all-done.sums = f32[32,8,128]{2,1,0:T(8,128)S(1)} async-done(((f32[32,8,128]{2,1,0:T(8,128)}), f32[32,8,128]{2,1,0:T(8,128)S(1)}, u32[]{:S(2)}, u32[]{:S(2)}) %all-to-all-start) | async-done | bytes 131104 | tf_op jit(solution)/shard_map/all_to_all | solution.py:463
  42.2 1.6 %copy-done.2 = f32[8,64,1024]{2,1,0:T(8,128)S(1)} copy-done((f32[8,64,1024]{2,1,0:T(8,128)S(1)}, f32[8,64,1024]{2,1,0:T(8,128)}, u32[]{:S(2)}) %copy-start.2) | copy-done | bytes 2097176
  43.8 0.6 correction.1
  44.5 1.2 collective-permute-start.10
  45.7 2.4 %collective-permute-start.11 = (bf16[64,1024]{1,0:T(8,128)(2,1)S(1)}, bf16[64,1024]{1,0:T(8,128)(2,1)S(1)}, u32[]{:S(2)}, u32[]{:S(2)}) collective-permute-start(bf16[64,1024]{1,0:T(8,128)(2,1)S(1)} %get-tuple-element.82), channel_id=1, source_target_pairs={{0,128},{32,160},{64,192},{96,224},{128,0},{160,32},{192,64},{224,... | collective-permute-start | bytes 393224 | tf_op jit(solution)/shard_map/ppermute | solution.py:394
  48.2 1.2 collective-permute-start.12
  49.4 1.8 %collective-permute-start.13 = (bf16[64,1024]{1,0:T(8,128)(2,1)S(1)}, bf16[64,1024]{1,0:T(8,128)(2,1)S(1)}, u32[]{:S(2)}, u32[]{:S(2)}) collective-permute-start(bf16[64,1024]{1,0:T(8,128)(2,1)S(1)} %get-tuple-element.84), channel_id=1, source_target_pairs={{0,96},{32,64},{64,160},{96,128},{128,224},{160,192},{192,32},{224... | collective-permute-start | bytes 393224 | tf_op jit(solution)/shard_map/ppermute | solution.py:394
  51.4 2.1 %collective-permute-done.10.refs_10_ = bf16[64,1024]{1,0:T(8,128)(2,1)S(1)} collective-permute-done((bf16[64,1024]{1,0:T(8,128)(2,1)S(1)}, bf16[64,1024]{1,0:T(8,128)(2,1)S(1)}, u32[]{:S(2)}, u32[]{:S(2)}) %collective-permute-start.10) | collective-permute-done | bytes 131104 | tf_op jit(solution)/shard_map/ppermute | solution.py:394
  53.6 1.1 collective-permute-start.15
  54.7 1.1 collective-permute-done.11.refs_11_
  55.9 4.3 %collective-permute-done.12.refs_12_ = bf16[64,1024]{1,0:T(8,128)(2,1)S(1)} collective-permute-done((bf16[64,1024]{1,0:T(8,128)(2,1)S(1)}, bf16[64,1024]{1,0:T(8,128)(2,1)S(1)}, u32[]{:S(2)}, u32[]{:S(2)}) %collective-permute-start.12) | collective-permute-done | bytes 131104 | tf_op jit(solution)/shard_map/ppermute | solution.py:394
  60.3 1.9 %collective-permute-done.14.refs_14_ = bf16[64,1024]{1,0:T(8,128)(2,1)S(1)} collective-permute-done((bf16[64,1024]{1,0:T(8,128)(2,1)S(1)}, bf16[64,1024]{1,0:T(8,128)(2,1)S(1)}, u32[]{:S(2)}, u32[]{:S(2)}) %collective-permute-start.14) | collective-permute-done | bytes 131104 | tf_op jit(solution)/shard_map/ppermute | solution.py:394
  62.2 1.8 %right_side.1 = (f32[304,1024]{1,0:T(8,128)S(1)}, bf16[512,1024]{1,0:T(8,128)(2,1)S(1)}, bf16[304,128]{1,0:T(8,128)(2,1)S(1)}, bf16[304,128]{1,0:T(8,128)(2,1)S(1)}, bf16[16,304]{1,0:T(8,128)(2,1)S(1)}) custom-call(bf16[64,1024]{1,0:T(8,128)(2,1)S(1)} %copy-done.5, bf16[64,1024]{1,0:T(8,128)(2,1)S(1)} %collective-permute-done.2.refs_1_, ...), custom_call_target="tpu_custom_call" | custom-call | tf_op jit(solution)/shard_map/right_side/pallas_call | solution.py:30
  64.1 1.6 %collective-permute-start.19 = (bf16[16,304]{1,0:T(8,128)(2,1)S(1)}, bf16[16,304]{1,0:T(8,128)(2,1)S(1)}, u32[]{:S(2)}, u32[]{:S(2)}) collective-permute-start(bf16[16,304]{1,0:T(8,128)(2,1)S(1)} %get-tuple-element.92), channel_id=1, source_target_pairs={{0,224},{32,0},{64,32},{96,64},{128,96},{160,128},{192,160},{224,1... | collective-permute-start | bytes 29192 | tf_op jit(solution)/shard_map/ppermute | solution.py:394
  65.7 1.2 collective-permute-start.16
  66.9 4.2 %collective-permute-start.17 = (bf16[304,128]{1,0:T(8,128)(2,1)S(1)}, bf16[304,128]{1,0:T(8,128)(2,1)S(1)}, u32[]{:S(2)}, u32[]{:S(2)}) collective-permute-start(bf16[304,128]{1,0:T(8,128)(2,1)S(1)} %get-tuple-element.91), channel_id=1, source_target_pairs={{0,31},{1,0},{2,1},{3,2},{4,3},{5,4},{6,5},{7,6},{8,7},{9,8},{10,9... | collective-permute-start | bytes 233480 | tf_op jit(solution)/shard_map/ppermute | solution.py:394
  71.3 4.4 %apply0.1 = (f32[304,1024]{1,0:T(8,128)S(1)}, f32[3,8,128]{2,1,0:T(8,128)S(1)}) custom-call(f32[304,1024]{1,0:T(8,128)S(1)} %get-tuple-element.87.refs_0_.refs_4_.zero, bf16[512,1024]{1,0:T(8,128)(2,1)S(1)} %get-tuple-element.88.refs_1_, bf16[512,304]{1,0:T(8,128)(2,1)S(1)} %subtract_convert_fusion.refs_2_, ...), custom_call_target="tpu_custom_call" | custom-call | tf_op jit(solution)/shard_map/apply0/pallas_call | solution.py:30
  75.8 0.7 add_halo1.1
  76.5 5.4 %collective-permute-start.21 = (bf16[304,128]{1,0:T(8,128)(2,1)S(1)}, bf16[304,128]{1,0:T(8,128)(2,1)S(1)}, u32[]{:S(2)}, u32[]{:S(2)}) collective-permute-start(bf16[304,128]{1,0:T(8,128)(2,1)S(1)} %get-tuple-element.96), channel_id=1, source_target_pairs={{0,31},{1,0},{2,1},{3,2},{4,3},{5,4},{6,5},{7,6},{8,7},{9,8},{10,9... | collective-permute-start | bytes 233480 | tf_op jit(solution)/shard_map/ppermute | solution.py:394
  81.8 1.7 %collective-permute-start.23 = (bf16[16,304]{1,0:T(8,128)(2,1)S(1)}, bf16[16,304]{1,0:T(8,128)(2,1)S(1)}, u32[]{:S(2)}, u32[]{:S(2)}) collective-permute-start(bf16[16,304]{1,0:T(8,128)(2,1)S(1)} %get-tuple-element.97), channel_id=1, source_target_pairs={{0,224},{32,0},{64,32},{96,64},{128,96},{160,128},{192,160},{224,1... | collective-permute-start | bytes 29192 | tf_op jit(solution)/shard_map/ppermute | solution.py:394
  83.6 4.5 %apply1.1 = (f32[304,1024]{1,0:T(8,128)S(1)}, f32[3,8,128]{2,1,0:T(8,128)S(1)}) custom-call(f32[304,1024]{1,0:T(8,128)S(1)} %get-tuple-element.93.refs_0_.refs_4_.one, bf16[512,1024]{1,0:T(8,128)(2,1)S(1)} %get-tuple-element.88.refs_1_, bf16[512,304]{1,0:T(8,128)(2,1)S(1)} %subtract_convert_fusion.refs_2_, ...), custom_call_target="tpu_custom_call" | custom-call | tf_op jit(solution)/shard_map/apply1/pallas_call | solution.py:30
  88.1 1.1 add_halo2.1
  89.2 1.2 collective-permute-start.25
  90.4 4.3 %apply2.1.two = f32[3,8,128]{2,1,0:T(8,128)S(1)} custom-call(f32[304,1024]{1,0:T(8,128)S(1)} %get-tuple-element.98.refs_0_.field.two, bf16[512,1024]{1,0:T(8,128)(2,1)S(1)} %get-tuple-element.88.refs_1_, bf16[512,304]{1,0:T(8,128)(2,1)S(1)} %subtract_convert_fusion.refs_2_, bf16[304,512]{1,0:T(8,128)(2,1)S(1)} %subtract_convert_fusion.1.refs_16_.refs_3_, ...), custom_call_target="tpu_custom_call" | custom-call | tf_op jit(solution)/shard_map/apply2/pallas_call | solution.py:30
  94.7 2.9 %collective-permute-done.24.above = bf16[304,128]{1,0:T(8,128)(2,1)S(1)} collective-permute-done((bf16[304,128]{1,0:T(8,128)(2,1)S(1)}, bf16[304,128]{1,0:T(8,128)(2,1)S(1)}, u32[]{:S(2)}, u32[]{:S(2)}) %collective-permute-start.24) | collective-permute-done | bytes 77856 | tf_op jit(solution)/shard_map/ppermute | solution.py:394
  98.3 1.1 collective-permute-done.26
  99.5 3.4 %collective-permute-done.27 = f32[8,128]{1,0:T(8,128)S(1)} collective-permute-done((f32[8,128]{1,0:T(8,128)S(1)}, f32[8,128]{1,0:T(8,128)S(1)}, u32[]{:S(2)}, u32[]{:S(2)}) %collective-permute-start.27) | collective-permute-done | bytes 4128 | tf_op jit(solution)/shard_map/ppermute | solution.py:394
  103.0 2.8 %collective-permute-start.28 = (f32[8,128]{1,0:T(8,128)S(1)}, f32[8,128]{1,0:T(8,128)S(1)}, u32[]{:S(2)}, u32[]{:S(2)}) collective-permute-start(f32[8,128]{1,0:T(8,128)S(1)} %add.70.one), channel_id=1, source_target_pairs={{0,128},{32,160},{64,192},{96,224},{128,0},{160,32},{192,64},{224,... | collective-permute-start | bytes 12296 | tf_op jit(solution)/shard_map/ppermute | solution.py:394
  105.8 2.3 %collective-permute-done.28.two = f32[8,128]{1,0:T(8,128)S(1)} collective-permute-done((f32[8,128]{1,0:T(8,128)S(1)}, f32[8,128]{1,0:T(8,128)S(1)}, u32[]{:S(2)}, u32[]{:S(2)}) %collective-permute-start.28) | collective-permute-done | bytes 4128 | tf_op jit(solution)/shard_map/ppermute | solution.py:394
  108.1 0.7 add_and_spread.1
  108.7 6.8 %all-to-all-start.1 = ((f32[32,8,128]{2,1,0:T(8,128)}), f32[32,8,128]{2,1,0:T(8,128)S(1)}, u32[]{:S(2)}, u32[]{:S(2)}) async-start(f32[32,8,128]{2,1,0:T(8,128)} %add_and_spread.1), calls=%async_computation.1 | async-start | bytes 262144 | tf_op jit(solution)/shard_map/all_to_all | solution.py:536
  116.0 9.9 %all-to-all-done.1.parts = f32[32,8,128]{2,1,0:T(8,128)S(1)} async-done(((f32[32,8,128]{2,1,0:T(8,128)}), f32[32,8,128]{2,1,0:T(8,128)S(1)}, u32[]{:S(2)}, u32[]{:S(2)}) %all-to-all-start.1) | async-done | bytes 131104 | tf_op jit(solution)/shard_map/all_to_all | solution.py:536
  125.9 1.3 copy-done.1
  127.2 2.0 %combine.1 = f32[2400,128]{1,0:T(8,128)} custom-call(f32[32,8,128]{2,1,0:T(8,128)S(1)} %all-to-all-done.1.parts, f32[304,1024]{1,0:T(8,128)S(1)} %get-tuple-element.87.refs_0_.refs_4_.zero, f32[304,1024]{1,0:T(8,128)S(1)} %get-tuple-element.93.refs_0_.refs_4_.one, f32[304,1024]{1,0:T(8,128)S(1)} %copy-done.1), custom_call_target="tpu_custom_call" | custom-call | tf_op jit(solution)/shard_map/combine/pallas_call | solution.py:30
  (63 shorter events, 3.3 us)
Async XLA Ops:
  0.6 1.2 copy-start.3
  1.9 1.2 copy-start.4
  3.1 9.6 %copy-start.8 = (s32[64,8]{0,1:T(8,128)S(1)}, s32[64,8]{0,1:T(8,128)}, u32[]{:S(2)}) copy-start(s32[64,8]{0,1:T(8,128)} %param.8) | copy-start | bytes 6148
  3.1 9.7 %copy-start.6 = (f32[8,1024]{1,0:T(8,128)S(1)}, f32[8,1024]{1,0:T(8,128)}, u32[]{:S(2)}) copy-start(f32[8,1024]{1,0:T(8,128)} %height.5) | copy-start | bytes 98308
  4.2 14.7 %collective-permute-start = (bf16[128,1024]{1,0:T(8,128)(2,1)S(1)}, bf16[128,1024]{1,0:T(8,128)(2,1)S(1)}, u32[]{:S(2)}, u32[]{:S(2)}) collective-permute-start(bf16[128,1024]{1,0:T(8,128)(2,1)S(1)} %get-tuple-element.55), channel_id=1, source_target_pairs={{0,1},{1,2},{2,3},{3,4},{4,5},{5,6},{6,7},{7,8},{8,9},{9,10},{10,1... | collective-permute-start | bytes 786440 | tf_op jit(solution)/shard_map/ppermute | solution.py:394
  6.2 12.7 %collective-permute-start.1 = (bf16[128,1024]{1,0:T(8,128)(2,1)S(1)}, bf16[128,1024]{1,0:T(8,128)(2,1)S(1)}, u32[]{:S(2)}, u32[]{:S(2)}) collective-permute-start(bf16[128,1024]{1,0:T(8,128)(2,1)S(1)} %get-tuple-element.56), channel_id=1, source_target_pairs={{0,31},{1,0},{2,1},{3,2},{4,3},{5,4},{6,5},{7,6},{8,7},{9,8},{10,9... | collective-permute-start | bytes 786440 | tf_op jit(solution)/shard_map/ppermute | solution.py:394
  18.9 13.1 %copy-start.9 = (s32[512,2]{0,1:T(2,128)S(1)}, s32[512,2]{0,1:T(2,128)}, u32[]{:S(2)}) copy-start(s32[512,2]{0,1:T(2,128)} %param.9) | copy-start | bytes 12292
  21.5 3.7 %collective-permute-start.8 = (bf16[64,1024]{1,0:T(8,128)(2,1)}, bf16[64,1024]{1,0:T(8,128)(2,1)S(1)}, u32[]{:S(2)}, u32[]{:S(2)}) collective-permute-start(bf16[64,1024]{1,0:T(8,128)(2,1)} %get-tuple-element.75), channel_id=1, source_target_pairs={{0,32},{32,0},{64,96},{96,64},{128,160},{160,128},{192,224},{224,1... | collective-permute-start | bytes 393224 | tf_op jit(solution)/shard_map/ppermute | solution.py:394
  21.7 22.7 %collective-permute-start.2 = (bf16[64,1024]{1,0:T(8,128)(2,1)}, bf16[64,1024]{1,0:T(8,128)(2,1)S(1)}, u32[]{:S(2)}, u32[]{:S(2)}) collective-permute-start(bf16[64,1024]{1,0:T(8,128)(2,1)} %get-tuple-element.68), channel_id=1, source_target_pairs={{0,64},{32,96},{64,128},{96,160},{128,192},{160,224},{192,0},{224,... | collective-permute-start | bytes 393224 | tf_op jit(solution)/shard_map/ppermute | solution.py:394
  22.2 22.3 %collective-permute-start.3 = (bf16[64,1024]{1,0:T(8,128)(2,1)}, bf16[64,1024]{1,0:T(8,128)(2,1)S(1)}, u32[]{:S(2)}, u32[]{:S(2)}) collective-permute-start(bf16[64,1024]{1,0:T(8,128)(2,1)} %get-tuple-element.69), channel_id=1, source_target_pairs={{0,192},{32,224},{64,0},{96,32},{128,64},{160,96},{192,128},{224,1... | collective-permute-start | bytes 393224 | tf_op jit(solution)/shard_map/ppermute | solution.py:394
  23.7 22.0 %collective-permute-start.4 = (bf16[64,1024]{1,0:T(8,128)(2,1)}, bf16[64,1024]{1,0:T(8,128)(2,1)S(1)}, u32[]{:S(2)}, u32[]{:S(2)}) collective-permute-start(bf16[64,1024]{1,0:T(8,128)(2,1)} %get-tuple-element.70), channel_id=1, source_target_pairs={{0,128},{32,160},{64,192},{96,224},{128,0},{160,32},{192,64},{224,... | collective-permute-start | bytes 393224 | tf_op jit(solution)/shard_map/ppermute | solution.py:394
  25.1 17.1 %all-to-all-start = ((f32[32,8,128]{2,1,0:T(8,128)}), f32[32,8,128]{2,1,0:T(8,128)S(1)}, u32[]{:S(2)}, u32[]{:S(2)}) async-start(f32[32,8,128]{2,1,0:T(8,128)} %get-tuple-element.77), calls=%async_computation | async-start | bytes 262144 | tf_op jit(solution)/shard_map/all_to_all | solution.py:463
  32.1 12.3 %copy-start.7 = (bf16[64,1024]{1,0:T(8,128)(2,1)S(1)}, bf16[64,1024]{1,0:T(8,128)(2,1)}, u32[]{:S(2)}) copy-start(bf16[64,1024]{1,0:T(8,128)(2,1)} %get-tuple-element.73) | copy-start | bytes 393220
  32.8 15.4 %collective-permute-start.5 = (bf16[64,1024]{1,0:T(8,128)(2,1)}, bf16[64,1024]{1,0:T(8,128)(2,1)S(1)}, u32[]{:S(2)}, u32[]{:S(2)}) collective-permute-start(bf16[64,1024]{1,0:T(8,128)(2,1)} %get-tuple-element.71), channel_id=1, source_target_pairs={{0,160},{32,128},{64,224},{96,192},{128,32},{160,0},{192,96},{224,... | collective-permute-start | bytes 393224 | tf_op jit(solution)/shard_map/ppermute | solution.py:394
  33.9 15.5 %collective-permute-start.6 = (bf16[64,1024]{1,0:T(8,128)(2,1)}, bf16[64,1024]{1,0:T(8,128)(2,1)S(1)}, u32[]{:S(2)}, u32[]{:S(2)}) collective-permute-start(bf16[64,1024]{1,0:T(8,128)(2,1)} %get-tuple-element.72), channel_id=1, source_target_pairs={{0,96},{32,64},{64,160},{96,128},{128,224},{160,192},{192,32},{224... | collective-permute-start | bytes 393224 | tf_op jit(solution)/shard_map/ppermute | solution.py:394
  42.2 1.6 %copy-start.2 = (f32[8,64,1024]{2,1,0:T(8,128)S(1)}, f32[8,64,1024]{2,1,0:T(8,128)}, u32[]{:S(2)}) copy-start(f32[8,64,1024]{2,1,0:T(8,128)} %get-tuple-element.78.smooth) | copy-start | bytes 6291460
  43.8 18.3 %copy-start.5 = (bf16[64,1024]{1,0:T(8,128)(2,1)S(1)}, bf16[64,1024]{1,0:T(8,128)(2,1)}, u32[]{:S(2)}) copy-start(bf16[64,1024]{1,0:T(8,128)(2,1)} %get-tuple-element.67.refs_0_) | copy-start | bytes 393220
  44.4 7.0 %collective-permute-start.7 = (bf16[64,1024]{1,0:T(8,128)(2,1)S(1)}, bf16[64,1024]{1,0:T(8,128)(2,1)S(1)}, u32[]{:S(2)}, u32[]{:S(2)}) collective-permute-start(bf16[64,1024]{1,0:T(8,128)(2,1)S(1)} %copy-done.7), channel_id=1, source_target_pairs={{0,224},{32,192},{64,32},{96,0},{128,96},{160,64},{192,160},{224,1... | collective-permute-start | bytes 393224 | tf_op jit(solution)/shard_map/ppermute | solution.py:394
  44.5 9.0 %collective-permute-start.10 = (bf16[64,1024]{1,0:T(8,128)(2,1)S(1)}, bf16[64,1024]{1,0:T(8,128)(2,1)S(1)}, u32[]{:S(2)}, u32[]{:S(2)}) collective-permute-start(bf16[64,1024]{1,0:T(8,128)(2,1)S(1)} %get-tuple-element.81), channel_id=1, source_target_pairs={{0,192},{32,224},{64,0},{96,32},{128,64},{160,96},{192,128},{224,1... | collective-permute-start | bytes 393224 | tf_op jit(solution)/shard_map/ppermute | solution.py:394
  45.7 10.0 %collective-permute-start.11 = (bf16[64,1024]{1,0:T(8,128)(2,1)S(1)}, bf16[64,1024]{1,0:T(8,128)(2,1)S(1)}, u32[]{:S(2)}, u32[]{:S(2)}) collective-permute-start(bf16[64,1024]{1,0:T(8,128)(2,1)S(1)} %get-tuple-element.82), channel_id=1, source_target_pairs={{0,128},{32,160},{64,192},{96,224},{128,0},{160,32},{192,64},{224,... | collective-permute-start | bytes 393224 | tf_op jit(solution)/shard_map/ppermute | solution.py:394
  48.2 12.1 %collective-permute-start.12 = (bf16[64,1024]{1,0:T(8,128)(2,1)S(1)}, bf16[64,1024]{1,0:T(8,128)(2,1)S(1)}, u32[]{:S(2)}, u32[]{:S(2)}) collective-permute-start(bf16[64,1024]{1,0:T(8,128)(2,1)S(1)} %get-tuple-element.83), channel_id=1, source_target_pairs={{0,160},{32,128},{64,224},{96,192},{128,32},{160,0},{192,96},{224,... | collective-permute-start | bytes 393224 | tf_op jit(solution)/shard_map/ppermute | solution.py:394
  49.4 10.9 %collective-permute-start.13 = (bf16[64,1024]{1,0:T(8,128)(2,1)S(1)}, bf16[64,1024]{1,0:T(8,128)(2,1)S(1)}, u32[]{:S(2)}, u32[]{:S(2)}) collective-permute-start(bf16[64,1024]{1,0:T(8,128)(2,1)S(1)} %get-tuple-element.84), channel_id=1, source_target_pairs={{0,96},{32,64},{64,160},{96,128},{128,224},{160,192},{192,32},{224... | collective-permute-start | bytes 393224 | tf_op jit(solution)/shard_map/ppermute | solution.py:394
  51.4 10.7 %collective-permute-start.14 = (bf16[64,1024]{1,0:T(8,128)(2,1)S(1)}, bf16[64,1024]{1,0:T(8,128)(2,1)S(1)}, u32[]{:S(2)}, u32[]{:S(2)}) collective-permute-start(bf16[64,1024]{1,0:T(8,128)(2,1)S(1)} %get-tuple-element.85), channel_id=1, source_target_pairs={{0,224},{32,192},{64,32},{96,0},{128,96},{160,64},{192,160},{224,1... | collective-permute-start | bytes 393224 | tf_op jit(solution)/shard_map/ppermute | solution.py:394
  53.6 8.6 %collective-permute-start.15 = (bf16[64,1024]{1,0:T(8,128)(2,1)S(1)}, bf16[64,1024]{1,0:T(8,128)(2,1)S(1)}, u32[]{:S(2)}, u32[]{:S(2)}) collective-permute-start(bf16[64,1024]{1,0:T(8,128)(2,1)S(1)} %get-tuple-element.86), channel_id=1, source_target_pairs={{0,32},{32,0},{64,96},{96,64},{128,160},{160,128},{192,224},{224,1... | collective-permute-start | bytes 393224 | tf_op jit(solution)/shard_map/ppermute | solution.py:394
  55.8 6.4 %collective-permute-start.9 = (bf16[64,1024]{1,0:T(8,128)(2,1)S(1)}, bf16[64,1024]{1,0:T(8,128)(2,1)S(1)}, u32[]{:S(2)}, u32[]{:S(2)}) collective-permute-start(bf16[64,1024]{1,0:T(8,128)(2,1)S(1)} %get-tuple-element.80), channel_id=1, source_target_pairs={{0,64},{32,96},{64,128},{96,160},{128,192},{160,224},{192,0},{224,... | collective-permute-start | bytes 393224 | tf_op jit(solution)/shard_map/ppermute | solution.py:394
  63.9 11.8 %collective-permute-start.18 = (bf16[16,304]{1,0:T(8,128)(2,1)S(1)}, bf16[16,304]{1,0:T(8,128)(2,1)S(1)}, u32[]{:S(2)}, u32[]{:S(2)}) collective-permute-start(bf16[16,304]{1,0:T(8,128)(2,1)S(1)} %get-tuple-element.92), channel_id=1, source_target_pairs={{0,32},{32,64},{64,96},{96,128},{128,160},{160,192},{192,224},{224... | collective-permute-start | bytes 29192 | tf_op jit(solution)/shard_map/ppermute | solution.py:394
  64.1 11.6 %collective-permute-start.19 = (bf16[16,304]{1,0:T(8,128)(2,1)S(1)}, bf16[16,304]{1,0:T(8,128)(2,1)S(1)}, u32[]{:S(2)}, u32[]{:S(2)}) collective-permute-start(bf16[16,304]{1,0:T(8,128)(2,1)S(1)} %get-tuple-element.92), channel_id=1, source_target_pairs={{0,224},{32,0},{64,32},{96,64},{128,96},{160,128},{192,160},{224,1... | collective-permute-start | bytes 29192 | tf_op jit(solution)/shard_map/ppermute | solution.py:394
  65.7 10.0 %collective-permute-start.16 = (bf16[304,128]{1,0:T(8,128)(2,1)S(1)}, bf16[304,128]{1,0:T(8,128)(2,1)S(1)}, u32[]{:S(2)}, u32[]{:S(2)}) collective-permute-start(bf16[304,128]{1,0:T(8,128)(2,1)S(1)} %get-tuple-element.90), channel_id=1, source_target_pairs={{0,1},{1,2},{2,3},{3,4},{4,5},{5,6},{6,7},{7,8},{8,9},{9,10},{10,1... | collective-permute-start | bytes 233480 | tf_op jit(solution)/shard_map/ppermute | solution.py:394
  66.9 8.8 %collective-permute-start.17 = (bf16[304,128]{1,0:T(8,128)(2,1)S(1)}, bf16[304,128]{1,0:T(8,128)(2,1)S(1)}, u32[]{:S(2)}, u32[]{:S(2)}) collective-permute-start(bf16[304,128]{1,0:T(8,128)(2,1)S(1)} %get-tuple-element.91), channel_id=1, source_target_pairs={{0,31},{1,0},{2,1},{3,2},{4,3},{5,4},{6,5},{7,6},{8,7},{9,8},{10,9... | collective-permute-start | bytes 233480 | tf_op jit(solution)/shard_map/ppermute | solution.py:394
  76.5 11.6 %collective-permute-start.20 = (bf16[304,128]{1,0:T(8,128)(2,1)S(1)}, bf16[304,128]{1,0:T(8,128)(2,1)S(1)}, u32[]{:S(2)}, u32[]{:S(2)}) collective-permute-start(bf16[304,128]{1,0:T(8,128)(2,1)S(1)} %get-tuple-element.95), channel_id=1, source_target_pairs={{0,1},{1,2},{2,3},{3,4},{4,5},{5,6},{6,7},{7,8},{8,9},{9,10},{10,1... | collective-permute-start | bytes 233480 | tf_op jit(solution)/shard_map/ppermute | solution.py:394
  76.5 11.6 %collective-permute-start.21 = (bf16[304,128]{1,0:T(8,128)(2,1)S(1)}, bf16[304,128]{1,0:T(8,128)(2,1)S(1)}, u32[]{:S(2)}, u32[]{:S(2)}) collective-permute-start(bf16[304,128]{1,0:T(8,128)(2,1)S(1)} %get-tuple-element.96), channel_id=1, source_target_pairs={{0,31},{1,0},{2,1},{3,2},{4,3},{5,4},{6,5},{7,6},{8,7},{9,8},{10,9... | collective-permute-start | bytes 233480 | tf_op jit(solution)/shard_map/ppermute | solution.py:394
  81.8 6.2 %collective-permute-start.22 = (bf16[16,304]{1,0:T(8,128)(2,1)S(1)}, bf16[16,304]{1,0:T(8,128)(2,1)S(1)}, u32[]{:S(2)}, u32[]{:S(2)}) collective-permute-start(bf16[16,304]{1,0:T(8,128)(2,1)S(1)} %get-tuple-element.97), channel_id=1, source_target_pairs={{0,32},{32,64},{64,96},{96,128},{128,160},{160,192},{192,224},{224... | collective-permute-start | bytes 29192 | tf_op jit(solution)/shard_map/ppermute | solution.py:394
  81.8 6.2 %collective-permute-start.23 = (bf16[16,304]{1,0:T(8,128)(2,1)S(1)}, bf16[16,304]{1,0:T(8,128)(2,1)S(1)}, u32[]{:S(2)}, u32[]{:S(2)}) collective-permute-start(bf16[16,304]{1,0:T(8,128)(2,1)S(1)} %get-tuple-element.97), channel_id=1, source_target_pairs={{0,224},{32,0},{64,32},{96,64},{128,96},{160,128},{192,160},{224,1... | collective-permute-start | bytes 29192 | tf_op jit(solution)/shard_map/ppermute | solution.py:394
  89.2 8.3 %copy-start = (f32[304,1024]{1,0:T(8,128)}, f32[304,1024]{1,0:T(8,128)S(1)}, u32[]{:S(2)}) copy-start(f32[304,1024]{1,0:T(8,128)S(1)} %get-tuple-element.98.refs_0_.field.two) | copy-start | bytes 3735556
  89.2 8.3 %collective-permute-start.24 = (bf16[304,128]{1,0:T(8,128)(2,1)S(1)}, bf16[304,128]{1,0:T(8,128)(2,1)S(1)}, u32[]{:S(2)}, u32[]{:S(2)}) collective-permute-start(bf16[304,128]{1,0:T(8,128)(2,1)S(1)} %get-tuple-element.99), channel_id=1, source_target_pairs={{0,1},{1,2},{2,3},{3,4},{4,5},{5,6},{6,7},{7,8},{8,9},{9,10},{10,1... | collective-permute-start | bytes 233480 | tf_op jit(solution)/shard_map/ppermute | solution.py:394
  89.2 5.5 %collective-permute-start.25 = (bf16[16,304]{1,0:T(8,128)(2,1)S(1)}, bf16[16,304]{1,0:T(8,128)(2,1)S(1)}, u32[]{:S(2)}, u32[]{:S(2)}) collective-permute-start(bf16[16,304]{1,0:T(8,128)(2,1)S(1)} %get-tuple-element.100), channel_id=1, source_target_pairs={{0,32},{32,64},{64,96},{96,128},{128,160},{160,192},{192,224},{224... | collective-permute-start | bytes 29192 | tf_op jit(solution)/shard_map/ppermute | solution.py:394
  98.1 1.3 collective-permute-start.26
  99.4 3.6 %collective-permute-start.27 = (f32[8,128]{1,0:T(8,128)S(1)}, f32[8,128]{1,0:T(8,128)S(1)}, u32[]{:S(2)}, u32[]{:S(2)}) collective-permute-start(f32[8,128]{1,0:T(8,128)S(1)} %add.69), channel_id=1, source_target_pairs={{0,64},{32,96},{64,0},{96,32},{128,192},{160,224},{192,128},{224,1... | collective-permute-start | bytes 12296 | tf_op jit(solution)/shard_map/ppermute | solution.py:394
  103.0 5.1 %collective-permute-start.28 = (f32[8,128]{1,0:T(8,128)S(1)}, f32[8,128]{1,0:T(8,128)S(1)}, u32[]{:S(2)}, u32[]{:S(2)}) collective-permute-start(f32[8,128]{1,0:T(8,128)S(1)} %add.70.one), channel_id=1, source_target_pairs={{0,128},{32,160},{64,192},{96,224},{128,0},{160,32},{192,64},{224,... | collective-permute-start | bytes 12296 | tf_op jit(solution)/shard_map/ppermute | solution.py:394
  108.7 17.2 %all-to-all-start.1 = ((f32[32,8,128]{2,1,0:T(8,128)}), f32[32,8,128]{2,1,0:T(8,128)S(1)}, u32[]{:S(2)}, u32[]{:S(2)}) async-start(f32[32,8,128]{2,1,0:T(8,128)} %add_and_spread.1), calls=%async_computation.1 | async-start | bytes 262144 | tf_op jit(solution)/shard_map/all_to_all | solution.py:536
  125.9 1.3 %copy-start.1 = (f32[304,1024]{1,0:T(8,128)S(1)}, f32[304,1024]{1,0:T(8,128)}, u32[]{:S(2)}) copy-start(f32[304,1024]{1,0:T(8,128)} %copy-done) | copy-start | bytes 3735556

commit v5 on v4

--- a/solution.py
+++ b/solution.py
@@ -48,10 +48,21 @@
     return high, (values - high.astype(F32)).astype(BF16)
 
 
-def rows_first(phase, coher, phase_t, coher_t, first, last, wide):
+def rows_first(phase, coher, phase_t, coher_t, first, last, phase_in, coher_in, wide, sems):
+    pairs = ((phase, phase_in, phase_t), (coher, coher_in, coher_t))
+
+    def fetch(part, block):
+        ifgs, _ = block_of(block)
+        return pltpu.make_async_copy(pairs[part][0].at[ifgs], pairs[part][1].at[ifgs], sems.at[part, block])
+
+    for block in range(4):
+        for part in range(2):
+            fetch(part, block).start()
+
     def group(block, _):
-        ifgs = pl.ds(pl.multiple_of(block * 16, 16), 16)
-        for part, (source, target) in enumerate(((phase, phase_t), (coher, coher_t))):
+        ifgs, _ = block_of(block)
+        for part, (_, source, target) in enumerate(pairs):
+            fetch(part, block).wait()
             for tile in range(8):
                 lanes = pl.ds(tile * 128, 128)
                 wide[part, tile] = source[ifgs, :, lanes].astype(F32).reshape(128, 128)
@@ -89,6 +100,10 @@
     return other(lax.axis_index("ifg"), *OFFSETS[step])
 
 
+def pieces_of(outs):
+    return [*outs[:3], outs[3].at[0], outs[3].at[1], *outs[4:]]
+
+
 def smooth_row(rows, lane, mask, terrain):
     denom = shifted_sum(rows[0][0] + rows[1][0] + rows[2][0], lane, 1023)
     numer = shifted_sum(rows[0][1] + rows[1][1] + rows[2][1], lane, 1023)
@@ -107,7 +122,7 @@
 
 
 def inner_rows(phase_t, coher_t, mask, height, smooth_out, totals, *rest):
-    outs, weights, smooth, sems = rest[:8], rest[8], rest[9], rest[10]
+    outs, weights, smooth, sems = pieces_of(rest[:7]), *rest[7:]
     lane = lax.broadcasted_iota(jnp.int32, (16, 1024), 1)
 
     def copies(block):
@@ -149,8 +164,8 @@
 
 
 def border_rows(phase_t, coher_t, above, below, mask, height, totals, *rest):
-    smooth_out, sums, outs = rest[9], rest[10], rest[11:19]
-    weights, smooth, added, sems = rest[19:]
+    smooth_out, sums, outs = rest[8], rest[9], pieces_of(rest[10:17])
+    weights, smooth, added, sems = rest[17:]
     lane = lax.broadcasted_iota(jnp.int32, (16, 1024), 1)
     my_row = lax.axis_index("rows")
     valid = (my_row > 0, my_row < lax.axis_size("rows") - 1)
@@ -193,7 +208,7 @@
 
 
 def correction(sums, smooth, height, slope_row, *rest):
-    outs, blocks = rest[:8], rest[8]
+    outs, blocks = pieces_of(rest[:7]), rest[7]
     total = sums[0]
     for index in range(1, sums.shape[0]):
         total += sums[index]
@@ -259,7 +274,7 @@
 def local_image(field, weights, design, design_t, chunk):
     lanes = pl.ds(pl.multiple_of(chunk * 256, 256), 256)
     high, low = split(field[:, lanes])
-    scaled = (dot(design[...], high) + dot(design[...], low)) * weights[:, lanes].astype(F32)
+    scaled = dot(design[...], jnp.concatenate([high, low], axis=0)) * weights[:, lanes].astype(F32)
     high, low = split(scaled)
     back = dot(design_t[...], high) + dot(design_t[...], low)
     lane = lax.broadcasted_iota(jnp.int32, (DP, 128), 1)
@@ -355,7 +370,7 @@
     out[...] = jnp.concatenate(sums + [jnp.zeros((2, 128), F32)], axis=0)
 
 
-def add_and_spread(one, two, out):
+def add_and_spread(one, two, basis, out):
     out[...] = jnp.broadcast_to((one[...] + two[...])[None], out.shape)
 
 
@@ -404,15 +419,20 @@
     phase_t, coher_t, first, last = call(
         rows_first,
         (stacked, stacked, edge, edge),
-        phase,
-        coherence,
-        scratch=(pltpu.VMEM((2, 8, 128, 128), F32),),
+        pltpu.with_memory_space_constraint(phase, pltpu.HBM),
+        pltpu.with_memory_space_constraint(coherence, pltpu.HBM),
+        specs=[pltpu.HBM] * 2,
+        scratch=(
+            pltpu.VMEM((64, 8, 1024), BF16),
+            pltpu.VMEM((64, 8, 1024), BF16),
+            pltpu.VMEM((2, 8, 128, 128), F32),
+            pltpu.SemaphoreType.DMA((2, 4)),
+        ),
         name="rows_first",
     )
     above, below = forward(last, "rows"), backward(first, "rows")
-    block = sds((64, 1024), BF16)
     mask = gap_mask.astype(F32)
-    pieces = [in_hbm((64, 1024), BF16)] * 8
+    pieces = [in_hbm((2, 64, 1024) if step == 3 else (64, 1024), BF16) for step in range(7)]
     smooth, totals, *weight_parts = call(
         inner_rows,
         [in_hbm((8, 64, 1024), F32), sds((128, 128), F32)] + pieces,
@@ -420,7 +440,7 @@
         coher_t,
         mask,
         height,
-        out_specs=[pltpu.HBM, pltpu.VMEM] + [pltpu.HBM] * 8,
+        out_specs=[pltpu.HBM, pltpu.VMEM] + [pltpu.HBM] * 7,
         scratch=(
             pltpu.VMEM((8, 64, 768), BF16),
             pltpu.VMEM((6, 64, 1024), F32),
@@ -440,42 +460,57 @@
         totals,
         smooth,
         *weight_parts,
-        specs=[pltpu.VMEM] * 7 + [pltpu.HBM] * 9,
-        out_specs=[pltpu.HBM, pltpu.VMEM] + [pltpu.HBM] * 8,
+        specs=[pltpu.VMEM] * 7 + [pltpu.HBM] * 8,
+        out_specs=[pltpu.HBM, pltpu.VMEM] + [pltpu.HBM] * 7,
         scratch=(
             pltpu.VMEM((2, 8, 64, 128), BF16),
             pltpu.VMEM((2, 64, 1024), F32),
             pltpu.VMEM((128, 128), F32),
             pltpu.SemaphoreType.DMA((2, 9)),
         ),
-        aliases={7: 0, **{8 + step: 2 + step for step in range(8)}},
+        aliases={7: 0, **{8 + step: 2 + step for step in range(7)}},
         name="border_rows",
     )
 
     def exchange(parts):
-        return [parts[0]] + [
-            permute(part, "ifg", lambda i: other(i, *offset))
-            for part, offset in zip(parts[1:], OFFSETS[1:])
-        ]
+        def far(i):
+            return other(i, 3, 0) if i & 1 else other(i, 2, 0)
+
+        def near(i, core):
+            return other(i, 3, core) if i & 1 else other(i, 0, core)
+
+        def offset(values, chips, core):
+            return permute(values, "ifg", lambda i: other(i, chips, core))
+
+        own, up, down, twice, up_other, down_other, pair = parts
+        twice = permute(twice, "ifg", far)
+        up, down = offset(up, 1, 0), offset(down, 3, 0)
+        up_other, down_other = offset(up_other, 1, 1), offset(down_other, 3, 1)
+        pair = offset(pair, 0, 1)
+        twice, twice_other = (permute(twice[core], "ifg", lambda i: near(i, core)) for core in (0, 1))
+        return [own, up, down, twice, twice_other, up_other, down_other, pair]
 
     weight_parts = exchange(weight_parts)
     sums, weight_parts[7] = lax.optimization_barrier((sums, weight_parts[7]))
     sums = lax.all_to_all(sums, "rows", 0, 0, tiled=True)
+    sums, weight_parts = lax.optimization_barrier((sums, weight_parts))
     slope_row, *corrected_parts = call(
         correction,
-        [sds((8, 128), F32)] + [block] * 8,
+        [sds((8, 128), F32)] + [sds(piece.shape, BF16) for piece in pieces],
         sums,
         smooth,
         height,
         scratch=(pltpu.VMEM((8, 64, 1024), BF16),),
         name="correction",
     )
+    slope, corrected_parts[0] = lax.optimization_barrier((slope_row[0, :64], corrected_parts[0]))
     corrected_parts = exchange(corrected_parts)
     sources = jnp.stack([other(me, 4 - chips, core) for chips, core in OFFSETS])
     pairs = date_pairs.reshape(n_ifg, -1, 2)[sources].reshape(-1, 2)
     dates = jnp.arange(DP, dtype=jnp.int32)
     design = ((dates[None] == pairs[:, 1:2]).astype(F32) - (dates[None] == pairs[:, 0:1]).astype(F32)).astype(BF16)
     design_t = design.T
+    design = jnp.concatenate([design, design], axis=1)
 
     field = sds((DP, 1024), F32)
     edges = (sds((DP, 128), BF16), sds((DP, 128), BF16), sds((16, DP), BF16))
@@ -531,11 +566,12 @@
         sds((n_rows, 8, 128), F32),
         part,
         permute(part, "ifg", lambda i: i ^ 4),
+        k0,
         name="add_and_spread",
     )
     parts = lax.all_to_all(parts, "rows", 0, 0, tiled=True)
     displacement = call(combine, sds((DATES * 8, 128), F32), parts, k0, k1, k2, name="combine")
-    return displacement.reshape(DATES, 8, 128), slope_row[0, :64]
+    return displacement.reshape(DATES, 8, 128), slope
 
 
 def solution(mesh):

time: 130 us -> 129 us (level)
  blocking collectives: 0 us -> 15.9 us
  starting transfers between devices: 55.6 us -> 48.5 us
  waiting for transfers between devices: 38 us -> 33.1 us
  local copies, waits for them, and re-layouts: 6.8 us -> 3.09 us
    all_to_all x0 -> x1, blocking collectives: none -> 15.9 us  [per_device(): parts = lax.all_to_all(parts, 'rows', 0, 0, tiled=True)]
    all_to_all x1 -> x0, waiting for transfers between devices: 9.89 us -> none  [per_device(): parts = lax.all_to_all(parts, 'rows', 0, 0, tiled=True)]
    all_to_all x1 -> x0, starting transfers between devices: 6.78 us -> none  [per_device(): parts = lax.all_to_all(parts, 'rows', 0, 0, tiled=True)]
    unnamed x21 -> x11, local copies, waits for them, and re-layouts: 5.43 us -> 1.69 us
    ppermute x29 -> x31, waiting for transfers between devices: 22.2 us -> 25.3 us  [permute(): lax.ppermute(values, axis, [(i, target(i)) for i in range(lax.axis_size(a...]
    all_to_all x1, waiting for transfers between devices: 5.93 us -> 7.78 us  [per_device(): sums = lax.all_to_all(sums, 'rows', 0, 0, tiled=True)]
    ppermute x29 -> x31, starting transfers between devices: 42 us -> 41.7 us  [permute(): lax.ppermute(values, axis, [(i, target(i)) for i in range(lax.axis_size(a...]
  transfers between devices with their start and end apart: 31 -> 32, of which waited for: 12 -> 11; matrix products, arithmetic and copies ran while one was open for 1% -> 2% of each run, Pallas kernels for 13% -> 12%
where the time goes in v5:
time: 129 us
  starting transfers between devices  48.5 us (38%)
  waiting for transfers between devices  33.1 us (26%)
  Pallas kernels  26.6 us (21%)
  blocking collectives  15.9 us (12%)
  local copies, waits for them, and re-layouts  3.09 us (2%)
    ppermute x31, starting transfers between devices, permute(): lax.ppermute(values, axis, [(i, target(i)) for i in range(lax.axis_size(a...  41.7 us
    pallas_call x13, Pallas kernels, call(): pl.pallas_call(body, out_shape=outs, in_specs=[pl.BlockSpec(memory_space=...  26.6 us
    ppermute x31, waiting for transfers between devices, permute(): lax.ppermute(values, axis, [(i, target(i)) for i in range(lax.axis_size(a...  25.3 us
    all_to_all x1, blocking collectives, per_device(): parts = lax.all_to_all(parts, 'rows', 0, 0, tiled=True)  15.9 us
    all_to_all x1, waiting for transfers between devices, per_device(): sums = lax.all_to_all(sums, 'rows', 0, 0, tiled=True)  7.78 us
    all_to_all x1, starting transfers between devices, per_device(): sums = lax.all_to_all(sums, 'rows', 0, 0, tiled=True)  6.81 us
  transfers between devices with their start and end apart: 32, of which 11 were waited for; matrix products, arithmetic and copies ran while one was open for 2% of the time, Pallas kernels for 12%

profile of v5, /device:TPU:6, one launch (start us, length us, event | category | flops | bytes accessed | tf_op | source)
XLA Modules:
  0.0 128.8 jit_solution(10289924816797884724)
XLA Ops:
  0.7 2.1 %rows_first.1 = (bf16[8,64,1024]{2,1,0:T(8,128)(2,1)S(1)}, bf16[8,64,1024]{2,1,0:T(8,128)(2,1)S(1)}, bf16[128,1024]{1,0:T(8,128)(2,1)S(1)}, bf16[128,1024]{1,0:T(8,128)(2,1)S(1)}) custom-call(bf16[64,8,1024]{2,1,0:T(8,128)(2,1)} %phase.1, bf16[64,8,1024]{2,1,0:T(8,128)(2,1)} %coher.1), custom_call_target="tpu_custom_call" | custom-call | tf_op jit(solution)/shard_map/rows_first/pallas_call | solution.py:30
  2.8 2.0 %collective-permute-start = (bf16[128,1024]{1,0:T(8,128)(2,1)S(1)}, bf16[128,1024]{1,0:T(8,128)(2,1)S(1)}, u32[]{:S(2)}, u32[]{:S(2)}) collective-permute-start(bf16[128,1024]{1,0:T(8,128)(2,1)S(1)} %get-tuple-element.63), channel_id=1, source_target_pairs={{0,1},{1,2},{2,3},{3,4},{4,5},{5,6},{6,7},{7,8},{8,9},{9,10},{10,1... | collective-permute-start | bytes 786440 | tf_op jit(solution)/shard_map/ppermute | solution.py:409
  4.8 6.5 %collective-permute-start.1 = (bf16[128,1024]{1,0:T(8,128)(2,1)S(1)}, bf16[128,1024]{1,0:T(8,128)(2,1)S(1)}, u32[]{:S(2)}, u32[]{:S(2)}) collective-permute-start(bf16[128,1024]{1,0:T(8,128)(2,1)S(1)} %get-tuple-element.64), channel_id=1, source_target_pairs={{0,31},{1,0},{2,1},{3,2},{4,3},{5,4},{6,5},{7,6},{8,7},{9,8},{10,9... | collective-permute-start | bytes 786440 | tf_op jit(solution)/shard_map/ppermute | solution.py:409
  11.4 3.3 %inner_rows.1 = (f32[8,64,1024]{2,1,0:T(8,128)}, f32[128,128]{1,0:T(8,128)S(1)}, bf16[64,1024]{1,0:T(8,128)(2,1)}, bf16[64,1024]{1,0:T(8,128)(2,1)}, bf16[64,102...) custom-call(bf16[8,64,1024]{2,1,0:T(8,128)(2,1)S(1)} %get-tuple-elem, ...), custom_call_target="tpu_custom_call" | custom-call | tf_op jit(solution)/shard_map/inner_rows/pallas_call | solution.py:30
  14.8 2.7 %collective-permute-done.above = bf16[128,1024]{1,0:T(8,128)(2,1)S(1)} collective-permute-done((bf16[128,1024]{1,0:T(8,128)(2,1)S(1)}, bf16[128,1024]{1,0:T(8,128)(2,1)S(1)}, u32[]{:S(2)}, u32[]{:S(2)}) %collective-permute-start) | collective-permute-done | bytes 262176 | tf_op jit(solution)/shard_map/ppermute | solution.py:409
  17.5 2.6 %border_rows.1 = (f32[8,64,1024]{2,1,0:T(8,128)}, f32[32,8,128]{2,1,0:T(8,128)}, bf16[64,1024]{1,0:T(8,128)(2,1)}, bf16[64,1024]{1,0:T(8,128)(2,1)}, bf16[64,102...) custom-call(bf16[8,64,1024]{2,1,0:T(8,128)(2,1)S(1)} %get-tuple-elem, ...), custom_call_target="tpu_custom_call", output_to_operand_aliasing={{0}: (7, {}), {2}: (8, {}), {3}: (9, {}), {4}: (10, {}), {5... | custom-call | tf_op jit(solution)/shard_map/border_rows/pallas_call | solution.py:30
  20.2 1.5 %collective-permute-start.5 = (bf16[2,64,1024]{2,1,0:T(8,128)(2,1)}, bf16[2,64,1024]{2,1,0:T(8,128)(2,1)S(1)}, u32[]{:S(2)}, u32[]{:S(2)}) collective-permute-start(bf16[2,64,1024]{2,1,0:T(8,128)(2,1)} %get-tuple-element.80), channel_id=1, source_target_pairs={{0,128},{32,224},{64,192},{96,32},{128,0},{160,96},{192,64},{224,1... | collective-permute-start | bytes 786440 | tf_op jit(solution)/shard_map/ppermute | solution.py:409
  21.8 0.6 gather_fusion
  22.4 2.1 %collective-permute-start.3 = (bf16[64,1024]{1,0:T(8,128)(2,1)}, bf16[64,1024]{1,0:T(8,128)(2,1)S(1)}, u32[]{:S(2)}, u32[]{:S(2)}) collective-permute-start(bf16[64,1024]{1,0:T(8,128)(2,1)} %get-tuple-element.78), channel_id=1, source_target_pairs={{0,64},{32,96},{64,128},{96,160},{128,192},{160,224},{192,0},{224,... | collective-permute-start | bytes 393224 | tf_op jit(solution)/shard_map/ppermute | solution.py:409
  24.5 2.2 %collective-permute-start.8 = (bf16[64,1024]{1,0:T(8,128)(2,1)}, bf16[64,1024]{1,0:T(8,128)(2,1)S(1)}, u32[]{:S(2)}, u32[]{:S(2)}) collective-permute-start(bf16[64,1024]{1,0:T(8,128)(2,1)} %get-tuple-element.81), channel_id=1, source_target_pairs={{0,96},{32,64},{64,160},{96,128},{128,224},{160,192},{192,32},{224... | collective-permute-start | bytes 393224 | tf_op jit(solution)/shard_map/ppermute | solution.py:409
  26.7 6.8 %all-to-all-start = ((f32[32,8,128]{2,1,0:T(8,128)}), f32[32,8,128]{2,1,0:T(8,128)S(1)}, u32[]{:S(2)}, u32[]{:S(2)}) async-start(f32[32,8,128]{2,1,0:T(8,128)} %get-tuple-element.76), calls=%async_computation | async-start | bytes 262144 | tf_op jit(solution)/shard_map/all_to_all | solution.py:495
  33.5 0.7 collective-permute-start.6
  34.2 2.2 %collective-permute-start.7 = (bf16[64,1024]{1,0:T(8,128)(2,1)S(1)}, bf16[64,1024]{1,0:T(8,128)(2,1)S(1)}, u32[]{:S(2)}, u32[]{:S(2)}) collective-permute-start(bf16[64,1024]{1,0:T(8,128)(2,1)S(1)} %get-tuple-element.122), channel_id=1, source_target_pairs={{0,32},{32,192},{64,96},{96,0},{128,160},{160,64},{192,224},{224,1... | collective-permute-start | bytes 393224 | tf_op jit(solution)/shard_map/ppermute | solution.py:409
  36.5 7.8 %all-to-all-done.sums = f32[32,8,128]{2,1,0:T(8,128)S(1)} async-done(((f32[32,8,128]{2,1,0:T(8,128)}), f32[32,8,128]{2,1,0:T(8,128)S(1)}, u32[]{:S(2)}, u32[]{:S(2)}) %all-to-all-start) | async-done | bytes 131104 | tf_op jit(solution)/shard_map/all_to_all | solution.py:495
  44.3 1.6 %copy-done = f32[8,64,1024]{2,1,0:T(8,128)S(1)} copy-done((f32[8,64,1024]{2,1,0:T(8,128)S(1)}, f32[8,64,1024]{2,1,0:T(8,128)}, u32[]{:S(2)}) %copy-start) | copy-done | bytes 2097176
  45.9 0.6 correction.1
  46.5 1.9 %collective-permute-start.12 = (bf16[2,64,1024]{2,1,0:T(8,128)(2,1)S(1)}, bf16[2,64,1024]{2,1,0:T(8,128)(2,1)S(1)}, u32[]{:S(2)}, u32[]{:S(2)}) collective-permute-start(bf16[2,64,1024]{2,1,0:T(8,128)(2,1)S(1)} %get-tuple-element.99), channel_id=1, source_target_pairs={{0,128},{32,224},{64,192},{96,32},{128,0},{160,96},{192,64},{224,1... | collective-permute-start | bytes 786440 | tf_op jit(solution)/shard_map/ppermute | solution.py:409
  48.7 2.0 %collective-permute-start.10 = (bf16[64,1024]{1,0:T(8,128)(2,1)S(1)}, bf16[64,1024]{1,0:T(8,128)(2,1)S(1)}, u32[]{:S(2)}, u32[]{:S(2)}) collective-permute-start(bf16[64,1024]{1,0:T(8,128)(2,1)S(1)} %get-tuple-element.97), channel_id=1, source_target_pairs={{0,64},{32,96},{64,128},{96,160},{128,192},{160,224},{192,0},{224,... | collective-permute-start | bytes 393224 | tf_op jit(solution)/shard_map/ppermute | solution.py:409
  50.7 0.9 collective-permute-start.11
  51.6 0.8 collective-permute-start.15
  52.3 1.0 collective-permute-start.16
  53.3 3.9 %collective-permute-done.12 = bf16[2,64,1024]{2,1,0:T(8,128)(2,1)S(1)} collective-permute-done((bf16[2,64,1024]{2,1,0:T(8,128)(2,1)S(1)}, bf16[2,64,1024]{2,1,0:T(8,128)(2,1)S(1)}, u32[]{:S(2)}, u32[]{:S(2)}) %collective-permute-start.12) | collective-permute-done | bytes 262176 | tf_op jit(solution)/shard_map/ppermute | solution.py:409
  57.3 0.9 collective-permute-done.10.refs_9_
  58.2 0.7 collective-permute-start.13
  58.9 0.3 collective-permute-done.11.refs_10_
  59.2 0.6 collective-permute-start.14
  59.8 0.5 slice_bitcast_fusion.4
  60.3 1.0 collective-permute-done.16.refs_14_
  61.3 5.0 %collective-permute-done.14.refs_12_ = bf16[64,1024]{1,0:T(8,128)(2,1)S(1)} collective-permute-done((bf16[64,1024]{1,0:T(8,128)(2,1)S(1)}, bf16[64,1024]{1,0:T(8,128)(2,1)S(1)}, u32[]{:S(2)}, u32[]{:S(2)}) %collective-permute-start.14) | collective-permute-done | bytes 131104 | tf_op jit(solution)/shard_map/ppermute | solution.py:409
  66.3 1.8 %right_side.1 = (f32[304,1024]{1,0:T(8,128)S(1)}, bf16[512,1024]{1,0:T(8,128)(2,1)S(1)}, bf16[304,128]{1,0:T(8,128)(2,1)S(1)}, bf16[304,128]{1,0:T(8,128)(2,1)S(1)}, bf16[16,304]{1,0:T(8,128)(2,1)S(1)}) custom-call(bf16[64,1024]{1,0:T(8,128)(2,1)S(1)} %copy-done.1, bf16[64,1024]{1,0:T(8,128)(2,1)S(1)} %collective-permute-done.3.refs_1_, ...), custom_call_target="tpu_custom_call" | custom-call | tf_op jit(solution)/shard_map/right_side/pallas_call | solution.py:30
  68.1 1.7 %collective-permute-start.21 = (bf16[16,304]{1,0:T(8,128)(2,1)S(1)}, bf16[16,304]{1,0:T(8,128)(2,1)S(1)}, u32[]{:S(2)}, u32[]{:S(2)}) collective-permute-start(bf16[16,304]{1,0:T(8,128)(2,1)S(1)} %get-tuple-element.108), channel_id=1, source_target_pairs={{0,224},{32,0},{64,32},{96,64},{128,96},{160,128},{192,160},{224,1... | collective-permute-start | bytes 29192 | tf_op jit(solution)/shard_map/ppermute | solution.py:409
  69.9 1.9 %collective-permute-start.18 = (bf16[304,128]{1,0:T(8,128)(2,1)S(1)}, bf16[304,128]{1,0:T(8,128)(2,1)S(1)}, u32[]{:S(2)}, u32[]{:S(2)}) collective-permute-start(bf16[304,128]{1,0:T(8,128)(2,1)S(1)} %get-tuple-element.106), channel_id=1, source_target_pairs={{0,1},{1,2},{2,3},{3,4},{4,5},{5,6},{6,7},{7,8},{8,9},{9,10},{10,1... | collective-permute-start | bytes 233480 | tf_op jit(solution)/shard_map/ppermute | solution.py:409
  71.7 3.5 %collective-permute-start.19 = (bf16[304,128]{1,0:T(8,128)(2,1)S(1)}, bf16[304,128]{1,0:T(8,128)(2,1)S(1)}, u32[]{:S(2)}, u32[]{:S(2)}) collective-permute-start(bf16[304,128]{1,0:T(8,128)(2,1)S(1)} %get-tuple-element.107), channel_id=1, source_target_pairs={{0,31},{1,0},{2,1},{3,2},{4,3},{5,4},{6,5},{7,6},{8,7},{9,8},{10,9... | collective-permute-start | bytes 233480 | tf_op jit(solution)/shard_map/ppermute | solution.py:409
  75.5 4.0 %apply0.1 = (f32[304,1024]{1,0:T(8,128)S(1)}, f32[3,8,128]{2,1,0:T(8,128)S(1)}) custom-call(f32[304,1024]{1,0:T(8,128)S(1)} %get-tuple-element.103.refs_0_.refs_4_.basis.zero, bf16[512,1024]{1,0:T(8,128)(2,1)S(1)} %get-tuple-element.104.refs_1_, bf16[512,608]{1,0:T(8,128)(2,1)S(1)} %pad_maximum_fusion.refs_2_, ...), custom_call_target="tpu_custom_call" | custom-call | tf_op jit(solution)/shard_map/apply0/pallas_call | solution.py:30
  79.5 0.7 add_halo1.1
  80.2 5.4 %collective-permute-start.23 = (bf16[304,128]{1,0:T(8,128)(2,1)S(1)}, bf16[304,128]{1,0:T(8,128)(2,1)S(1)}, u32[]{:S(2)}, u32[]{:S(2)}) collective-permute-start(bf16[304,128]{1,0:T(8,128)(2,1)S(1)} %get-tuple-element.112), channel_id=1, source_target_pairs={{0,31},{1,0},{2,1},{3,2},{4,3},{5,4},{6,5},{7,6},{8,7},{9,8},{10,9... | collective-permute-start | bytes 233480 | tf_op jit(solution)/shard_map/ppermute | solution.py:409
  85.6 1.7 %collective-permute-start.25 = (bf16[16,304]{1,0:T(8,128)(2,1)S(1)}, bf16[16,304]{1,0:T(8,128)(2,1)S(1)}, u32[]{:S(2)}, u32[]{:S(2)}) collective-permute-start(bf16[16,304]{1,0:T(8,128)(2,1)S(1)} %get-tuple-element.113), channel_id=1, source_target_pairs={{0,224},{32,0},{64,32},{96,64},{128,96},{160,128},{192,160},{224,1... | collective-permute-start | bytes 29192 | tf_op jit(solution)/shard_map/ppermute | solution.py:409
  87.3 4.0 %apply1.1 = (f32[304,1024]{1,0:T(8,128)S(1)}, f32[3,8,128]{2,1,0:T(8,128)S(1)}) custom-call(f32[304,1024]{1,0:T(8,128)S(1)} %get-tuple-element.109.refs_0_.refs_4_.one, bf16[512,1024]{1,0:T(8,128)(2,1)S(1)} %get-tuple-element.104.refs_1_, bf16[512,608]{1,0:T(8,128)(2,1)S(1)} %pad_maximum_fusion.refs_2_, ...), custom_call_target="tpu_custom_call" | custom-call | tf_op jit(solution)/shard_map/apply1/pallas_call | solution.py:30
  91.4 1.1 add_halo2.1
  92.8 3.9 %apply2.1.two = f32[3,8,128]{2,1,0:T(8,128)S(1)} custom-call(f32[304,1024]{1,0:T(8,128)S(1)} %get-tuple-element.114.refs_0_.field.two, bf16[512,1024]{1,0:T(8,128)(2,1)S(1)} %get-tuple-element.104.refs_1_, bf16[512,608]{1,0:T(8,128)(2,1)S(1)} %pad_maximum_fusion.refs_2_, bf16[304,512]{1,0:T(8,128)(2,1)S(1)} %subtract_convert_fusion.1.refs_16_.refs_3_, ...), custom_call_target="tpu_custom_call" | custom-call | tf_op jit(solution)/shard_map/apply2/pallas_call | solution.py:30
  96.7 3.7 %collective-permute-done.26.above = bf16[304,128]{1,0:T(8,128)(2,1)S(1)} collective-permute-done((bf16[304,128]{1,0:T(8,128)(2,1)S(1)}, bf16[304,128]{1,0:T(8,128)(2,1)S(1)}, u32[]{:S(2)}, u32[]{:S(2)}) %collective-permute-start.26) | collective-permute-done | bytes 77856 | tf_op jit(solution)/shard_map/ppermute | solution.py:409
  100.4 0.5 all_moments.1
  101.0 1.2 collective-permute-done.28
  102.2 3.6 %collective-permute-done.29 = f32[8,128]{1,0:T(8,128)S(1)} collective-permute-done((f32[8,128]{1,0:T(8,128)S(1)}, f32[8,128]{1,0:T(8,128)S(1)}, u32[]{:S(2)}, u32[]{:S(2)}) %collective-permute-start.29) | collective-permute-done | bytes 4128 | tf_op jit(solution)/shard_map/ppermute | solution.py:409
  105.8 2.2 %collective-permute-start.30 = (f32[8,128]{1,0:T(8,128)S(1)}, f32[8,128]{1,0:T(8,128)S(1)}, u32[]{:S(2)}, u32[]{:S(2)}) collective-permute-start(f32[8,128]{1,0:T(8,128)S(1)} %add.70.one), channel_id=1, source_target_pairs={{0,128},{32,160},{64,192},{96,224},{128,0},{160,32},{192,64},{224,... | collective-permute-start | bytes 12296 | tf_op jit(solution)/shard_map/ppermute | solution.py:409
  108.0 2.9 %collective-permute-done.30.two = f32[8,128]{1,0:T(8,128)S(1)} collective-permute-done((f32[8,128]{1,0:T(8,128)S(1)}, f32[8,128]{1,0:T(8,128)S(1)}, u32[]{:S(2)}, u32[]{:S(2)}) %collective-permute-start.30) | collective-permute-done | bytes 4128 | tf_op jit(solution)/shard_map/ppermute | solution.py:409
  110.9 15.9 %all_to_all.10.parts = f32[32,8,128]{2,1,0:T(8,128)S(1)} all-to-all(f32[32,8,128]{2,1,0:T(8,128)S(1)} %add_and_spread.1), channel_id=1, replica_groups=mesh['ifg'=8,'rows'=32] {'rows'}, dimensions={0} | all-to-all | bytes 262144 | tf_op jit(solution)/shard_map/all_to_all | solution.py:572
  126.8 2.0 %combine.1 = f32[2400,128]{1,0:T(8,128)} custom-call(f32[32,8,128]{2,1,0:T(8,128)S(1)} %all_to_all.10.parts, f32[304,1024]{1,0:T(8,128)S(1)} %get-tuple-element.103.refs_0_.refs_4_.basis.zero, f32[304,1024]{1,0:T(8,128)S(1)} %get-tuple-element.109.refs_0_.refs_4_.one, f32[304,1024]{1,0:T(8,128)S(1)} %get-tuple-element.114.refs_0_.field.two), custom_call_target="tpu_custom_call" | custom-call | tf_op jit(solution)/shard_map/combine/pallas_call | solution.py:30
  (59 shorter events, 1.6 us)
Async XLA Ops:
  0.6 10.7 %copy-start.3 = (s32[64,8]{0,1:T(8,128)S(1)}, s32[64,8]{0,1:T(8,128)}, u32[]{:S(2)}) copy-start(s32[64,8]{0,1:T(8,128)} %param.8) | copy-start | bytes 6148
  0.6 10.7 %copy-start.2 = (f32[8,1024]{1,0:T(8,128)S(1)}, f32[8,1024]{1,0:T(8,128)}, u32[]{:S(2)}) copy-start(f32[8,1024]{1,0:T(8,128)} %height.5) | copy-start | bytes 98308
  2.8 14.7 %collective-permute-start = (bf16[128,1024]{1,0:T(8,128)(2,1)S(1)}, bf16[128,1024]{1,0:T(8,128)(2,1)S(1)}, u32[]{:S(2)}, u32[]{:S(2)}) collective-permute-start(bf16[128,1024]{1,0:T(8,128)(2,1)S(1)} %get-tuple-element.63), channel_id=1, source_target_pairs={{0,1},{1,2},{2,3},{3,4},{4,5},{5,6},{6,7},{7,8},{8,9},{9,10},{10,1... | collective-permute-start | bytes 786440 | tf_op jit(solution)/shard_map/ppermute | solution.py:409
  4.8 12.7 %collective-permute-start.1 = (bf16[128,1024]{1,0:T(8,128)(2,1)S(1)}, bf16[128,1024]{1,0:T(8,128)(2,1)S(1)}, u32[]{:S(2)}, u32[]{:S(2)}) collective-permute-start(bf16[128,1024]{1,0:T(8,128)(2,1)S(1)} %get-tuple-element.64), channel_id=1, source_target_pairs={{0,31},{1,0},{2,1},{3,2},{4,3},{5,4},{6,5},{7,6},{8,7},{9,8},{10,9... | collective-permute-start | bytes 786440 | tf_op jit(solution)/shard_map/ppermute | solution.py:409
  17.5 4.2 %copy-start.4 = (s32[512,2]{0,1:T(2,128)S(1)}, s32[512,2]{0,1:T(2,128)}, u32[]{:S(2)}) copy-start(s32[512,2]{0,1:T(2,128)} %param.9) | copy-start | bytes 12292
  20.1 6.6 %collective-permute-start.2 = (bf16[64,1024]{1,0:T(8,128)(2,1)}, bf16[64,1024]{1,0:T(8,128)(2,1)S(1)}, u32[]{:S(2)}, u32[]{:S(2)}) collective-permute-start(bf16[64,1024]{1,0:T(8,128)(2,1)} %get-tuple-element.75), channel_id=1, source_target_pairs={{0,32},{32,0},{64,96},{96,64},{128,160},{160,128},{192,224},{224,1... | collective-permute-start | bytes 393224 | tf_op jit(solution)/shard_map/ppermute | solution.py:409
  20.2 13.3 %collective-permute-start.5 = (bf16[2,64,1024]{2,1,0:T(8,128)(2,1)}, bf16[2,64,1024]{2,1,0:T(8,128)(2,1)S(1)}, u32[]{:S(2)}, u32[]{:S(2)}) collective-permute-start(bf16[2,64,1024]{2,1,0:T(8,128)(2,1)} %get-tuple-element.80), channel_id=1, source_target_pairs={{0,128},{32,224},{64,192},{96,32},{128,0},{160,96},{192,64},{224,1... | collective-permute-start | bytes 786440 | tf_op jit(solution)/shard_map/ppermute | solution.py:409
  22.4 11.8 %collective-permute-start.3 = (bf16[64,1024]{1,0:T(8,128)(2,1)}, bf16[64,1024]{1,0:T(8,128)(2,1)S(1)}, u32[]{:S(2)}, u32[]{:S(2)}) collective-permute-start(bf16[64,1024]{1,0:T(8,128)(2,1)} %get-tuple-element.78), channel_id=1, source_target_pairs={{0,64},{32,96},{64,128},{96,160},{128,192},{160,224},{192,0},{224,... | collective-permute-start | bytes 393224 | tf_op jit(solution)/shard_map/ppermute | solution.py:409
  24.5 12.0 %collective-permute-start.4 = (bf16[64,1024]{1,0:T(8,128)(2,1)}, bf16[64,1024]{1,0:T(8,128)(2,1)S(1)}, u32[]{:S(2)}, u32[]{:S(2)}) collective-permute-start(bf16[64,1024]{1,0:T(8,128)(2,1)} %get-tuple-element.79), channel_id=1, source_target_pairs={{0,192},{32,224},{64,0},{96,32},{128,64},{160,96},{192,128},{224,1... | collective-permute-start | bytes 393224 | tf_op jit(solution)/shard_map/ppermute | solution.py:409
  24.5 12.0 %collective-permute-start.8 = (bf16[64,1024]{1,0:T(8,128)(2,1)}, bf16[64,1024]{1,0:T(8,128)(2,1)S(1)}, u32[]{:S(2)}, u32[]{:S(2)}) collective-permute-start(bf16[64,1024]{1,0:T(8,128)(2,1)} %get-tuple-element.81), channel_id=1, source_target_pairs={{0,96},{32,64},{64,160},{96,128},{128,224},{160,192},{192,32},{224... | collective-permute-start | bytes 393224 | tf_op jit(solution)/shard_map/ppermute | solution.py:409
  26.7 9.8 %collective-permute-start.9 = (bf16[64,1024]{1,0:T(8,128)(2,1)}, bf16[64,1024]{1,0:T(8,128)(2,1)S(1)}, u32[]{:S(2)}, u32[]{:S(2)}) collective-permute-start(bf16[64,1024]{1,0:T(8,128)(2,1)} %get-tuple-element.82), channel_id=1, source_target_pairs={{0,224},{32,192},{64,32},{96,0},{128,96},{160,64},{192,160},{224,1... | collective-permute-start | bytes 393224 | tf_op jit(solution)/shard_map/ppermute | solution.py:409
  26.7 17.6 %all-to-all-start = ((f32[32,8,128]{2,1,0:T(8,128)}), f32[32,8,128]{2,1,0:T(8,128)S(1)}, u32[]{:S(2)}, u32[]{:S(2)}) async-start(f32[32,8,128]{2,1,0:T(8,128)} %get-tuple-element.76), calls=%async_computation | async-start | bytes 262144 | tf_op jit(solution)/shard_map/all_to_all | solution.py:495
  33.5 10.7 %collective-permute-start.6 = (bf16[64,1024]{1,0:T(8,128)(2,1)S(1)}, bf16[64,1024]{1,0:T(8,128)(2,1)S(1)}, u32[]{:S(2)}, u32[]{:S(2)}) collective-permute-start(bf16[64,1024]{1,0:T(8,128)(2,1)S(1)} %get-tuple-element.123), channel_id=1, source_target_pairs={{0,0},{32,224},{64,64},{96,32},{128,128},{160,96},{192,192},{224,1... | collective-permute-start | bytes 393224 | tf_op jit(solution)/shard_map/ppermute | solution.py:409
  34.2 10.1 %collective-permute-start.7 = (bf16[64,1024]{1,0:T(8,128)(2,1)S(1)}, bf16[64,1024]{1,0:T(8,128)(2,1)S(1)}, u32[]{:S(2)}, u32[]{:S(2)}) collective-permute-start(bf16[64,1024]{1,0:T(8,128)(2,1)S(1)} %get-tuple-element.122), channel_id=1, source_target_pairs={{0,32},{32,192},{64,96},{96,0},{128,160},{160,64},{192,224},{224,1... | collective-permute-start | bytes 393224 | tf_op jit(solution)/shard_map/ppermute | solution.py:409
  44.3 1.6 %copy-start = (f32[8,64,1024]{2,1,0:T(8,128)S(1)}, f32[8,64,1024]{2,1,0:T(8,128)}, u32[]{:S(2)}) copy-start(f32[8,64,1024]{2,1,0:T(8,128)} %get-tuple-element.93.smooth) | copy-start | bytes 6291460
  45.9 20.4 %copy-start.1 = (bf16[64,1024]{1,0:T(8,128)(2,1)S(1)}, bf16[64,1024]{1,0:T(8,128)(2,1)}, u32[]{:S(2)}) copy-start(bf16[64,1024]{1,0:T(8,128)(2,1)} %get-tuple-element.84.refs_0_) | copy-start | bytes 393220
  46.5 10.8 %collective-permute-start.12 = (bf16[2,64,1024]{2,1,0:T(8,128)(2,1)S(1)}, bf16[2,64,1024]{2,1,0:T(8,128)(2,1)S(1)}, u32[]{:S(2)}, u32[]{:S(2)}) collective-permute-start(bf16[2,64,1024]{2,1,0:T(8,128)(2,1)S(1)} %get-tuple-element.99), channel_id=1, source_target_pairs={{0,128},{32,224},{64,192},{96,32},{128,0},{160,96},{192,64},{224,1... | collective-permute-start | bytes 786440 | tf_op jit(solution)/shard_map/ppermute | solution.py:409
  48.7 9.5 %collective-permute-start.10 = (bf16[64,1024]{1,0:T(8,128)(2,1)S(1)}, bf16[64,1024]{1,0:T(8,128)(2,1)S(1)}, u32[]{:S(2)}, u32[]{:S(2)}) collective-permute-start(bf16[64,1024]{1,0:T(8,128)(2,1)S(1)} %get-tuple-element.97), channel_id=1, source_target_pairs={{0,64},{32,96},{64,128},{96,160},{128,192},{160,224},{192,0},{224,... | collective-permute-start | bytes 393224 | tf_op jit(solution)/shard_map/ppermute | solution.py:409
  50.7 8.6 %collective-permute-start.11 = (bf16[64,1024]{1,0:T(8,128)(2,1)S(1)}, bf16[64,1024]{1,0:T(8,128)(2,1)S(1)}, u32[]{:S(2)}, u32[]{:S(2)}) collective-permute-start(bf16[64,1024]{1,0:T(8,128)(2,1)S(1)} %get-tuple-element.98), channel_id=1, source_target_pairs={{0,192},{32,224},{64,0},{96,32},{128,64},{160,96},{192,128},{224,1... | collective-permute-start | bytes 393224 | tf_op jit(solution)/shard_map/ppermute | solution.py:409
  51.6 8.8 %collective-permute-start.15 = (bf16[64,1024]{1,0:T(8,128)(2,1)S(1)}, bf16[64,1024]{1,0:T(8,128)(2,1)S(1)}, u32[]{:S(2)}, u32[]{:S(2)}) collective-permute-start(bf16[64,1024]{1,0:T(8,128)(2,1)S(1)} %get-tuple-element.100), channel_id=1, source_target_pairs={{0,96},{32,64},{64,160},{96,128},{128,224},{160,192},{192,32},{224... | collective-permute-start | bytes 393224 | tf_op jit(solution)/shard_map/ppermute | solution.py:409
  52.3 9.0 %collective-permute-start.16 = (bf16[64,1024]{1,0:T(8,128)(2,1)S(1)}, bf16[64,1024]{1,0:T(8,128)(2,1)S(1)}, u32[]{:S(2)}, u32[]{:S(2)}) collective-permute-start(bf16[64,1024]{1,0:T(8,128)(2,1)S(1)} %get-tuple-element.101), channel_id=1, source_target_pairs={{0,224},{32,192},{64,32},{96,0},{128,96},{160,64},{192,160},{224,1... | collective-permute-start | bytes 393224 | tf_op jit(solution)/shard_map/ppermute | solution.py:409
  57.3 4.1 %collective-permute-start.17 = (bf16[64,1024]{1,0:T(8,128)(2,1)S(1)}, bf16[64,1024]{1,0:T(8,128)(2,1)S(1)}, u32[]{:S(2)}, u32[]{:S(2)}) collective-permute-start(bf16[64,1024]{1,0:T(8,128)(2,1)S(1)} %get-tuple-element.102), channel_id=1, source_target_pairs={{0,32},{32,0},{64,96},{96,64},{128,160},{160,128},{192,224},{224,1... | collective-permute-start | bytes 393224 | tf_op jit(solution)/shard_map/ppermute | solution.py:409
  58.2 3.1 %collective-permute-start.13 = (bf16[64,1024]{1,0:T(8,128)(2,1)S(1)}, bf16[64,1024]{1,0:T(8,128)(2,1)S(1)}, u32[]{:S(2)}, u32[]{:S(2)}) collective-permute-start(bf16[64,1024]{1,0:T(8,128)(2,1)S(1)} %get-tuple-element.121), channel_id=1, source_target_pairs={{0,0},{32,224},{64,64},{96,32},{128,128},{160,96},{192,192},{224,1... | collective-permute-start | bytes 393224 | tf_op jit(solution)/shard_map/ppermute | solution.py:409
  59.2 7.1 %collective-permute-start.14 = (bf16[64,1024]{1,0:T(8,128)(2,1)S(1)}, bf16[64,1024]{1,0:T(8,128)(2,1)S(1)}, u32[]{:S(2)}, u32[]{:S(2)}) collective-permute-start(bf16[64,1024]{1,0:T(8,128)(2,1)S(1)} %get-tuple-element.120), channel_id=1, source_target_pairs={{0,32},{32,192},{64,96},{96,0},{128,160},{160,64},{192,224},{224,1... | collective-permute-start | bytes 393224 | tf_op jit(solution)/shard_map/ppermute | solution.py:409
  68.1 11.4 %collective-permute-start.20 = (bf16[16,304]{1,0:T(8,128)(2,1)S(1)}, bf16[16,304]{1,0:T(8,128)(2,1)S(1)}, u32[]{:S(2)}, u32[]{:S(2)}) collective-permute-start(bf16[16,304]{1,0:T(8,128)(2,1)S(1)} %get-tuple-element.108), channel_id=1, source_target_pairs={{0,32},{32,64},{64,96},{96,128},{128,160},{160,192},{192,224},{224... | collective-permute-start | bytes 29192 | tf_op jit(solution)/shard_map/ppermute | solution.py:409
  68.1 11.4 %collective-permute-start.21 = (bf16[16,304]{1,0:T(8,128)(2,1)S(1)}, bf16[16,304]{1,0:T(8,128)(2,1)S(1)}, u32[]{:S(2)}, u32[]{:S(2)}) collective-permute-start(bf16[16,304]{1,0:T(8,128)(2,1)S(1)} %get-tuple-element.108), channel_id=1, source_target_pairs={{0,224},{32,0},{64,32},{96,64},{128,96},{160,128},{192,160},{224,1... | collective-permute-start | bytes 29192 | tf_op jit(solution)/shard_map/ppermute | solution.py:409
  69.9 9.6 %collective-permute-start.18 = (bf16[304,128]{1,0:T(8,128)(2,1)S(1)}, bf16[304,128]{1,0:T(8,128)(2,1)S(1)}, u32[]{:S(2)}, u32[]{:S(2)}) collective-permute-start(bf16[304,128]{1,0:T(8,128)(2,1)S(1)} %get-tuple-element.106), channel_id=1, source_target_pairs={{0,1},{1,2},{2,3},{3,4},{4,5},{5,6},{6,7},{7,8},{8,9},{9,10},{10,1... | collective-permute-start | bytes 233480 | tf_op jit(solution)/shard_map/ppermute | solution.py:409
  71.7 7.8 %collective-permute-start.19 = (bf16[304,128]{1,0:T(8,128)(2,1)S(1)}, bf16[304,128]{1,0:T(8,128)(2,1)S(1)}, u32[]{:S(2)}, u32[]{:S(2)}) collective-permute-start(bf16[304,128]{1,0:T(8,128)(2,1)S(1)} %get-tuple-element.107), channel_id=1, source_target_pairs={{0,31},{1,0},{2,1},{3,2},{4,3},{5,4},{6,5},{7,6},{8,7},{9,8},{10,9... | collective-permute-start | bytes 233480 | tf_op jit(solution)/shard_map/ppermute | solution.py:409
  80.2 11.2 %collective-permute-start.22 = (bf16[304,128]{1,0:T(8,128)(2,1)S(1)}, bf16[304,128]{1,0:T(8,128)(2,1)S(1)}, u32[]{:S(2)}, u32[]{:S(2)}) collective-permute-start(bf16[304,128]{1,0:T(8,128)(2,1)S(1)} %get-tuple-element.111), channel_id=1, source_target_pairs={{0,1},{1,2},{2,3},{3,4},{4,5},{5,6},{6,7},{7,8},{8,9},{9,10},{10,1... | collective-permute-start | bytes 233480 | tf_op jit(solution)/shard_map/ppermute | solution.py:409
  80.2 11.2 %collective-permute-start.23 = (bf16[304,128]{1,0:T(8,128)(2,1)S(1)}, bf16[304,128]{1,0:T(8,128)(2,1)S(1)}, u32[]{:S(2)}, u32[]{:S(2)}) collective-permute-start(bf16[304,128]{1,0:T(8,128)(2,1)S(1)} %get-tuple-element.112), channel_id=1, source_target_pairs={{0,31},{1,0},{2,1},{3,2},{4,3},{5,4},{6,5},{7,6},{8,7},{9,8},{10,9... | collective-permute-start | bytes 233480 | tf_op jit(solution)/shard_map/ppermute | solution.py:409
  85.6 5.8 %collective-permute-start.24 = (bf16[16,304]{1,0:T(8,128)(2,1)S(1)}, bf16[16,304]{1,0:T(8,128)(2,1)S(1)}, u32[]{:S(2)}, u32[]{:S(2)}) collective-permute-start(bf16[16,304]{1,0:T(8,128)(2,1)S(1)} %get-tuple-element.113), channel_id=1, source_target_pairs={{0,32},{32,64},{64,96},{96,128},{128,160},{160,192},{192,224},{224... | collective-permute-start | bytes 29192 | tf_op jit(solution)/shard_map/ppermute | solution.py:409
  85.6 5.8 %collective-permute-start.25 = (bf16[16,304]{1,0:T(8,128)(2,1)S(1)}, bf16[16,304]{1,0:T(8,128)(2,1)S(1)}, u32[]{:S(2)}, u32[]{:S(2)}) collective-permute-start(bf16[16,304]{1,0:T(8,128)(2,1)S(1)} %get-tuple-element.113), channel_id=1, source_target_pairs={{0,224},{32,0},{64,32},{96,64},{128,96},{160,128},{192,160},{224,1... | collective-permute-start | bytes 29192 | tf_op jit(solution)/shard_map/ppermute | solution.py:409
  92.6 7.8 %collective-permute-start.26 = (bf16[304,128]{1,0:T(8,128)(2,1)S(1)}, bf16[304,128]{1,0:T(8,128)(2,1)S(1)}, u32[]{:S(2)}, u32[]{:S(2)}) collective-permute-start(bf16[304,128]{1,0:T(8,128)(2,1)S(1)} %get-tuple-element.115), channel_id=1, source_target_pairs={{0,1},{1,2},{2,3},{3,4},{4,5},{5,6},{6,7},{7,8},{8,9},{9,10},{10,1... | collective-permute-start | bytes 233480 | tf_op jit(solution)/shard_map/ppermute | solution.py:409
  92.6 4.1 %collective-permute-start.27 = (bf16[16,304]{1,0:T(8,128)(2,1)S(1)}, bf16[16,304]{1,0:T(8,128)(2,1)S(1)}, u32[]{:S(2)}, u32[]{:S(2)}) collective-permute-start(bf16[16,304]{1,0:T(8,128)(2,1)S(1)} %get-tuple-element.116), channel_id=1, source_target_pairs={{0,32},{32,64},{64,96},{96,128},{128,160},{160,192},{192,224},{224... | collective-permute-start | bytes 29192 | tf_op jit(solution)/shard_map/ppermute | solution.py:409
  100.9 1.3 collective-permute-start.28
  102.2 3.6 %collective-permute-start.29 = (f32[8,128]{1,0:T(8,128)S(1)}, f32[8,128]{1,0:T(8,128)S(1)}, u32[]{:S(2)}, u32[]{:S(2)}) collective-permute-start(f32[8,128]{1,0:T(8,128)S(1)} %add.69), channel_id=1, source_target_pairs={{0,64},{32,96},{64,0},{96,32},{128,192},{160,224},{192,128},{224,1... | collective-permute-start | bytes 12296 | tf_op jit(solution)/shard_map/ppermute | solution.py:409
  105.8 5.1 %collective-permute-start.30 = (f32[8,128]{1,0:T(8,128)S(1)}, f32[8,128]{1,0:T(8,128)S(1)}, u32[]{:S(2)}, u32[]{:S(2)}) collective-permute-start(f32[8,128]{1,0:T(8,128)S(1)} %add.70.one), channel_id=1, source_target_pairs={{0,128},{32,160},{64,192},{96,224},{128,0},{160,32},{192,64},{224,... | collective-permute-start | bytes 12296 | tf_op jit(solution)/shard_map/ppermute | solution.py:409

commit v6 on v5

--- a/solution.py
+++ b/solution.py
@@ -100,10 +100,6 @@
     return other(lax.axis_index("ifg"), *OFFSETS[step])
 
 
-def pieces_of(outs):
-    return [*outs[:3], outs[3].at[0], outs[3].at[1], *outs[4:]]
-
-
 def smooth_row(rows, lane, mask, terrain):
     denom = shifted_sum(rows[0][0] + rows[1][0] + rows[2][0], lane, 1023)
     numer = shifted_sum(rows[0][1] + rows[1][1] + rows[2][1], lane, 1023)
@@ -122,7 +118,7 @@
 
 
 def inner_rows(phase_t, coher_t, mask, height, smooth_out, totals, *rest):
-    outs, weights, smooth, sems = pieces_of(rest[:7]), *rest[7:]
+    outs, weights, smooth, sems = rest[:8], *rest[8:]
     lane = lax.broadcasted_iota(jnp.int32, (16, 1024), 1)
 
     def copies(block):
@@ -164,8 +160,8 @@
 
 
 def border_rows(phase_t, coher_t, above, below, mask, height, totals, *rest):
-    smooth_out, sums, outs = rest[8], rest[9], pieces_of(rest[10:17])
-    weights, smooth, added, sems = rest[17:]
+    smooth_out, sums, outs = rest[9], rest[10], rest[11:19]
+    weights, smooth, added, sems = rest[19:]
     lane = lax.broadcasted_iota(jnp.int32, (16, 1024), 1)
     my_row = lax.axis_index("rows")
     valid = (my_row > 0, my_row < lax.axis_size("rows") - 1)
@@ -207,13 +203,24 @@
         copy.wait()
 
 
+def stage(source, out, sems):
+    copies = [
+        pltpu.make_async_copy(source.at[pl.ds(part * 2, 2)], out.at[pl.ds(part * 2, 2)], sems.at[part])
+        for part in range(4)
+    ]
+    for copy in copies:
+        copy.start()
+    for copy in copies:
+        copy.wait()
+
+
 def correction(sums, smooth, height, slope_row, *rest):
-    outs, blocks = pieces_of(rest[:7]), rest[7]
+    outs, blocks = rest[:8], rest[8]
     total = sums[0]
     for index in range(1, sums.shape[0]):
         total += sums[index]
     slope_row[...] = total / pltpu.roll(total, 64, 1)
-    column = jnp.broadcast_to(total[0:1, :], (128, 128)).T
+    column = jnp.broadcast_to(total, (128, 128)).T
     slope = column[:64, :] / column[64:, :]
 
     def one_tile(tile, _):
@@ -320,7 +327,7 @@
         return square, cross, ahead
 
     zero = jnp.zeros((8, 128), F32)
-    totals = lax.fori_loop(0, 4, one_chunk, (zero, zero, zero))
+    totals = lax.fori_loop(0, 4, one_chunk, (zero, zero, zero), unroll=True)
     for index in range(3):
         moments[index] = totals[index]
 
@@ -366,20 +373,23 @@
             halo += keep(flags[0], above[...])
         ahead -= (2.0 * SMOOTHING_WEIGHT) * fold(field[:, pl.ds(row * 128, 128)] * halo)
     rows = [zero[0], one[1], one[0], two[1], two[0], ahead]
-    sums = [jnp.sum(values, axis=0, keepdims=True) for values in rows]
-    out[...] = jnp.concatenate(sums + [jnp.zeros((2, 128), F32)], axis=0)
+    lane = lax.broadcasted_iota(jnp.int32, (1, 128), 1)
+    total = jnp.zeros((1, 128), F32)
+    for index, values in enumerate(rows):
+        line = jnp.sum(values, axis=0, keepdims=True)
+        total += jnp.where(lane == index, jnp.sum(line, axis=1, keepdims=True), 0.0)
+    out[...] = total
 
 
 def add_and_spread(one, two, basis, out):
     out[...] = jnp.broadcast_to((one[...] + two[...])[None], out.shape)
 
 
-def combine(parts, zero, one, two, out):
+def combine(parts, zero, one, two, out, field, sems):
     total = parts[0]
     for index in range(1, parts.shape[0]):
         total += parts[index]
-    sums = jnp.sum(total, axis=1, keepdims=True)
-    m0, m1, m2, m3, m4, m5 = (jnp.broadcast_to(sums[i : i + 1, :], (1, 128)) for i in range(6))
+    m0, m1, m2, m3, m4, m5 = (jnp.broadcast_to(total[:, i : i + 1], (1, 128)) for i in range(6))
     t00, t01, t11 = m1 + SHIFT * m0, m2 + SHIFT * m1, m3 + SHIFT * m2
     t12, t22 = m4 + SHIFT * m3, m5 + SHIFT * m4
     l10, l20 = t01 / t00, t11 / t00
@@ -395,10 +405,19 @@
     c2 = jnp.where(keep_last, y2 / jnp.where(keep_last, last, 1.0), 0.0)
     c1 = jnp.where(keep, y1 / safe, 0.0) - l21 * c2
     c0 = m0 / t00 - l10 * c1 - l20 * c2
-    for row in range(8):
-        lanes = pl.ds(row * 128, 128)
-        value = c0 * zero[:, lanes] + c1 * one[:, lanes] + c2 * two[:, lanes]
-        out[pl.ds(row, DATES, stride=8), :] = value[:DATES, :]
+    copies = []
+    for part in range(4):
+        count = min(80, DATES - part * 80)
+        dates = pl.ds(part * 80, (count + 7) // 8 * 8)
+        for row in range(8):
+            lanes = pl.ds(row * 128, 128)
+            value = c0 * zero[dates, lanes] + c1 * one[dates, lanes] + c2 * two[dates, lanes]
+            field[pl.ds(part * 640 + row, count, stride=8), :] = value[:count, :]
+        lines = pl.ds(part * 640, count * 8)
+        copies.append(pltpu.make_async_copy(field.at[lines], out.at[lines], sems.at[part]))
+        copies[-1].start()
+    for copy in copies:
+        copy.wait()
 
 
 def per_device(phase, coherence, height, gap_mask, date_pairs):
@@ -432,7 +451,7 @@
     )
     above, below = forward(last, "rows"), backward(first, "rows")
     mask = gap_mask.astype(F32)
-    pieces = [in_hbm((2, 64, 1024) if step == 3 else (64, 1024), BF16) for step in range(7)]
+    pieces = [in_hbm((64, 1024), BF16)] * 8
     smooth, totals, *weight_parts = call(
         inner_rows,
         [in_hbm((8, 64, 1024), F32), sds((128, 128), F32)] + pieces,
@@ -440,7 +459,7 @@
         coher_t,
         mask,
         height,
-        out_specs=[pltpu.HBM, pltpu.VMEM] + [pltpu.HBM] * 7,
+        out_specs=[pltpu.HBM, pltpu.VMEM] + [pltpu.HBM] * 8,
         scratch=(
             pltpu.VMEM((8, 64, 768), BF16),
             pltpu.VMEM((6, 64, 1024), F32),
@@ -450,7 +469,7 @@
     )
     smooth, sums, *weight_parts = call(
         border_rows,
-        [in_hbm((8, 64, 1024), F32), sds((n_rows, 8, 128), F32)] + pieces,
+        [in_hbm((8, 64, 1024), F32), sds((n_rows, 1, 128), F32)] + pieces,
         phase_t,
         coher_t,
         above,
@@ -460,43 +479,38 @@
         totals,
         smooth,
         *weight_parts,
-        specs=[pltpu.VMEM] * 7 + [pltpu.HBM] * 8,
-        out_specs=[pltpu.HBM, pltpu.VMEM] + [pltpu.HBM] * 7,
+        specs=[pltpu.VMEM] * 7 + [pltpu.HBM] * 9,
+        out_specs=[pltpu.HBM, pltpu.VMEM] + [pltpu.HBM] * 8,
         scratch=(
             pltpu.VMEM((2, 8, 64, 128), BF16),
             pltpu.VMEM((2, 64, 1024), F32),
             pltpu.VMEM((128, 128), F32),
             pltpu.SemaphoreType.DMA((2, 9)),
         ),
-        aliases={7: 0, **{8 + step: 2 + step for step in range(7)}},
+        aliases={7: 0, **{8 + step: 2 + step for step in range(8)}},
         name="border_rows",
     )
 
     def exchange(parts):
-        def far(i):
-            return other(i, 3, 0) if i & 1 else other(i, 2, 0)
-
-        def near(i, core):
-            return other(i, 3, core) if i & 1 else other(i, 0, core)
-
-        def offset(values, chips, core):
-            return permute(values, "ifg", lambda i: other(i, chips, core))
-
-        own, up, down, twice, up_other, down_other, pair = parts
-        twice = permute(twice, "ifg", far)
-        up, down = offset(up, 1, 0), offset(down, 3, 0)
-        up_other, down_other = offset(up_other, 1, 1), offset(down_other, 3, 1)
-        pair = offset(pair, 0, 1)
-        twice, twice_other = (permute(twice[core], "ifg", lambda i: near(i, core)) for core in (0, 1))
-        return [own, up, down, twice, twice_other, up_other, down_other, pair]
+        return [parts[0]] + [
+            permute(part, "ifg", lambda i: other(i, *offset))
+            for part, offset in zip(parts[1:], OFFSETS[1:])
+        ]
 
     weight_parts = exchange(weight_parts)
     sums, weight_parts[7] = lax.optimization_barrier((sums, weight_parts[7]))
     sums = lax.all_to_all(sums, "rows", 0, 0, tiled=True)
-    sums, weight_parts = lax.optimization_barrier((sums, weight_parts))
+    smooth = call(
+        stage,
+        sds((8, 64, 1024), F32),
+        pltpu.with_memory_space_constraint(smooth, pltpu.HBM),
+        specs=[pltpu.HBM],
+        scratch=(pltpu.SemaphoreType.DMA((4,)),),
+        name="stage",
+    )
     slope_row, *corrected_parts = call(
         correction,
-        [sds((8, 128), F32)] + [sds(piece.shape, BF16) for piece in pieces],
+        [sds((1, 128), F32)] + [sds((64, 1024), BF16)] * 8,
         sums,
         smooth,
         height,
@@ -550,7 +564,7 @@
     (mom2,) = local(True, False, "apply2", k2, weights, design, design_t, k1)
     part = call(
         all_moments,
-        sds((8, 128), F32),
+        sds((1, 128), F32),
         k2,
         above,
         left,
@@ -563,14 +577,24 @@
         part = part + permute(part, "ifg", lambda i: i ^ step)
     parts = call(
         add_and_spread,
-        sds((n_rows, 8, 128), F32),
+        sds((n_rows, 1, 128), F32),
         part,
         permute(part, "ifg", lambda i: i ^ 4),
         k0,
         name="add_and_spread",
     )
     parts = lax.all_to_all(parts, "rows", 0, 0, tiled=True)
-    displacement = call(combine, sds((DATES * 8, 128), F32), parts, k0, k1, k2, name="combine")
+    displacement = call(
+        combine,
+        sds((DATES * 8, 128), F32),
+        parts,
+        k0,
+        k1,
+        k2,
+        out_specs=[pltpu.HBM],
+        scratch=(pltpu.VMEM((DATES * 8, 128), F32), pltpu.SemaphoreType.DMA((4,))),
+        name="combine",
+    )
     return displacement.reshape(DATES, 8, 128), slope
 
 

time: 129 us -> 120 us (0.930)
  waiting for transfers between devices: 33.1 us -> 24.2 us
  starting transfers between devices: 48.5 us -> 50.5 us
    ppermute x31 -> x29, waiting for transfers between devices: 25.3 us -> 19.8 us  [permute(): lax.ppermute(values, axis, [(i, target(i)) for i in range(lax.axis_size(a...]
    all_to_all x1, waiting for transfers between devices: 7.78 us -> 4.38 us  [per_device(): sums = lax.all_to_all(sums, 'rows', 0, 0, tiled=True)]
    ppermute x31 -> x29, starting transfers between devices: 41.7 us -> 43.7 us  [permute(): lax.ppermute(values, axis, [(i, target(i)) for i in range(lax.axis_size(a...]
    pallas_call x13 -> x14, Pallas kernels: 26.6 us -> 25.8 us  [call(): pl.pallas_call(body, out_shape=outs, in_specs=[pl.BlockSpec(memory_space=...]
  transfers between devices with their start and end apart: 32 -> 30, of which waited for: 11 -> 11; matrix products, arithmetic and copies ran while one was open for 2% -> 2% of each run, Pallas kernels for 12% -> 13%
where the time goes in v6:
time: 120 us
  starting transfers between devices  50.5 us (42%)
  Pallas kernels  25.8 us (22%)
  waiting for transfers between devices  24.2 us (20%)
  blocking collectives  15.6 us (13%)
  local copies, waits for them, and re-layouts  1.8 us (2%)
    ppermute x29, starting transfers between devices, permute(): lax.ppermute(values, axis, [(i, target(i)) for i in range(lax.axis_size(a...  43.7 us
    pallas_call x14, Pallas kernels, call(): pl.pallas_call(body, out_shape=outs, in_specs=[pl.BlockSpec(memory_space=...  25.8 us
    ppermute x29, waiting for transfers between devices, permute(): lax.ppermute(values, axis, [(i, target(i)) for i in range(lax.axis_size(a...  19.8 us
    all_to_all x1, blocking collectives, per_device(): parts = lax.all_to_all(parts, 'rows', 0, 0, tiled=True)  15.6 us
    all_to_all x1, starting transfers between devices, per_device(): sums = lax.all_to_all(sums, 'rows', 0, 0, tiled=True)  6.81 us
    all_to_all x1, waiting for transfers between devices, per_device(): sums = lax.all_to_all(sums, 'rows', 0, 0, tiled=True)  4.38 us
  transfers between devices with their start and end apart: 30, of which 11 were waited for; matrix products, arithmetic and copies ran while one was open for 2% of the time, Pallas kernels for 13%

profile of v6, /device:TPU:6, one launch (start us, length us, event | category | flops | bytes accessed | tf_op | source)
XLA Modules:
  0.0 119.6 jit_solution(4255573201618079048)
XLA Ops:
  0.7 2.2 %rows_first.1 = (bf16[8,64,1024]{2,1,0:T(8,128)(2,1)S(1)}, bf16[8,64,1024]{2,1,0:T(8,128)(2,1)S(1)}, bf16[128,1024]{1,0:T(8,128)(2,1)S(1)}, bf16[128,1024]{1,0:T(8,128)(2,1)S(1)}) custom-call(bf16[64,8,1024]{2,1,0:T(8,128)(2,1)} %phase.1, bf16[64,8,1024]{2,1,0:T(8,128)(2,1)} %coher.1), custom_call_target="tpu_custom_call" | custom-call | tf_op jit(solution)/shard_map/rows_first/pallas_call | solution.py:30
  2.8 2.0 %collective-permute-start = (bf16[128,1024]{1,0:T(8,128)(2,1)S(1)}, bf16[128,1024]{1,0:T(8,128)(2,1)S(1)}, u32[]{:S(2)}, u32[]{:S(2)}) collective-permute-start(bf16[128,1024]{1,0:T(8,128)(2,1)S(1)} %get-tuple-element.57), channel_id=1, source_target_pairs={{0,1},{1,2},{2,3},{3,4},{4,5},{5,6},{6,7},{7,8},{8,9},{9,10},{10,1... | collective-permute-start | bytes 786440 | tf_op jit(solution)/shard_map/ppermute | solution.py:428
  4.8 6.5 %collective-permute-start.1 = (bf16[128,1024]{1,0:T(8,128)(2,1)S(1)}, bf16[128,1024]{1,0:T(8,128)(2,1)S(1)}, u32[]{:S(2)}, u32[]{:S(2)}) collective-permute-start(bf16[128,1024]{1,0:T(8,128)(2,1)S(1)} %get-tuple-element.58), channel_id=1, source_target_pairs={{0,31},{1,0},{2,1},{3,2},{4,3},{5,4},{6,5},{7,6},{8,7},{9,8},{10,9... | collective-permute-start | bytes 786440 | tf_op jit(solution)/shard_map/ppermute | solution.py:428
  11.6 0.6 gather_fusion
  12.3 3.3 %inner_rows.1 = (f32[8,64,1024]{2,1,0:T(8,128)}, f32[128,128]{1,0:T(8,128)S(1)}, bf16[64,1024]{1,0:T(8,128)(2,1)}, bf16[64,1024]{1,0:T(8,128)(2,1)}, bf16[64,102...) custom-call(bf16[8,64,1024]{2,1,0:T(8,128)(2,1)S(1)} %get-tuple-elem, ...), custom_call_target="tpu_custom_call" | custom-call | tf_op jit(solution)/shard_map/inner_rows/pallas_call | solution.py:30
  15.6 1.9 %collective-permute-done.above = bf16[128,1024]{1,0:T(8,128)(2,1)S(1)} collective-permute-done((bf16[128,1024]{1,0:T(8,128)(2,1)S(1)}, bf16[128,1024]{1,0:T(8,128)(2,1)S(1)}, u32[]{:S(2)}, u32[]{:S(2)}) %collective-permute-start) | collective-permute-done | bytes 262176 | tf_op jit(solution)/shard_map/ppermute | solution.py:428
  17.5 2.5 %border_rows.1 = (f32[8,64,1024]{2,1,0:T(8,128)}, f32[32,1,128]{2,1,0:T(1,128)}, bf16[64,1024]{1,0:T(8,128)(2,1)}, bf16[64,1024]{1,0:T(8,128)(2,1)}, bf16[64,102...) custom-call(bf16[8,64,1024]{2,1,0:T(8,128)(2,1)S(1)} %get-tuple-elem, ...), custom_call_target="tpu_custom_call", output_to_operand_aliasing={{0}: (7, {}), {2}: (8, {}), {3}: (9, {}), {4}: (10, {}), {5... | custom-call | tf_op jit(solution)/shard_map/border_rows/pallas_call | solution.py:30
  20.2 0.6 collective-permute-start.2
  20.7 1.5 %collective-permute-start.3 = (bf16[64,1024]{1,0:T(8,128)(2,1)}, bf16[64,1024]{1,0:T(8,128)(2,1)S(1)}, u32[]{:S(2)}, u32[]{:S(2)}) collective-permute-start(bf16[64,1024]{1,0:T(8,128)(2,1)} %get-tuple-element.71), channel_id=1, source_target_pairs={{0,192},{32,224},{64,0},{96,32},{128,64},{160,96},{192,128},{224,1... | collective-permute-start | bytes 393224 | tf_op jit(solution)/shard_map/ppermute | solution.py:428
  22.3 1.4 %collective-permute-start.4 = (bf16[64,1024]{1,0:T(8,128)(2,1)}, bf16[64,1024]{1,0:T(8,128)(2,1)S(1)}, u32[]{:S(2)}, u32[]{:S(2)}) collective-permute-start(bf16[64,1024]{1,0:T(8,128)(2,1)} %get-tuple-element.72), channel_id=1, source_target_pairs={{0,128},{32,160},{64,192},{96,224},{128,0},{160,32},{192,64},{224,... | collective-permute-start | bytes 393224 | tf_op jit(solution)/shard_map/ppermute | solution.py:428
  23.7 6.8 %all-to-all-start = ((f32[32,1,128]{2,1,0:T(1,128)}), f32[32,1,128]{2,1,0:T(1,128)S(1)}, u32[]{:S(2)}, u32[]{:S(2)}) async-start(f32[32,1,128]{2,1,0:T(1,128)} %get-tuple-element.79), calls=%async_computation | async-start | bytes 32768 | tf_op jit(solution)/shard_map/all_to_all | solution.py:502
  30.7 1.6 %stage.1.smooth = f32[8,64,1024]{2,1,0:T(8,128)S(1)} custom-call(f32[8,64,1024]{2,1,0:T(8,128)} %get-tuple-element.80.source), custom_call_target="tpu_custom_call" | custom-call | tf_op jit(solution)/shard_map/stage/pallas_call | solution.py:30
  32.3 1.1 collective-permute-start.5
  33.4 2.5 %collective-permute-start.6 = (bf16[64,1024]{1,0:T(8,128)(2,1)}, bf16[64,1024]{1,0:T(8,128)(2,1)S(1)}, u32[]{:S(2)}, u32[]{:S(2)}) collective-permute-start(bf16[64,1024]{1,0:T(8,128)(2,1)} %get-tuple-element.74), channel_id=1, source_target_pairs={{0,96},{32,64},{64,160},{96,128},{128,224},{160,192},{192,32},{224... | collective-permute-start | bytes 393224 | tf_op jit(solution)/shard_map/ppermute | solution.py:428
  35.9 4.4 %all-to-all-done.sums = f32[32,1,128]{2,1,0:T(1,128)S(1)} async-done(((f32[32,1,128]{2,1,0:T(1,128)}), f32[32,1,128]{2,1,0:T(1,128)S(1)}, u32[]{:S(2)}, u32[]{:S(2)}) %all-to-all-start) | async-done | bytes 16416 | tf_op jit(solution)/shard_map/all_to_all | solution.py:502
  40.3 0.6 correction.1
  40.9 0.3 copy-done.2
  41.2 1.2 collective-permute-start.10
  42.4 2.4 %collective-permute-start.11 = (bf16[64,1024]{1,0:T(8,128)(2,1)S(1)}, bf16[64,1024]{1,0:T(8,128)(2,1)S(1)}, u32[]{:S(2)}, u32[]{:S(2)}) collective-permute-start(bf16[64,1024]{1,0:T(8,128)(2,1)S(1)} %get-tuple-element.86), channel_id=1, source_target_pairs={{0,128},{32,160},{64,192},{96,224},{128,0},{160,32},{192,64},{224,... | collective-permute-start | bytes 393224 | tf_op jit(solution)/shard_map/ppermute | solution.py:428
  45.0 1.3 %collective-permute-start.12 = (bf16[64,1024]{1,0:T(8,128)(2,1)S(1)}, bf16[64,1024]{1,0:T(8,128)(2,1)S(1)}, u32[]{:S(2)}, u32[]{:S(2)}) collective-permute-start(bf16[64,1024]{1,0:T(8,128)(2,1)S(1)} %get-tuple-element.87), channel_id=1, source_target_pairs={{0,160},{32,128},{64,224},{96,192},{128,32},{160,0},{192,96},{224,... | collective-permute-start | bytes 393224 | tf_op jit(solution)/shard_map/ppermute | solution.py:428
  46.2 1.7 %collective-permute-start.13 = (bf16[64,1024]{1,0:T(8,128)(2,1)S(1)}, bf16[64,1024]{1,0:T(8,128)(2,1)S(1)}, u32[]{:S(2)}, u32[]{:S(2)}) collective-permute-start(bf16[64,1024]{1,0:T(8,128)(2,1)S(1)} %get-tuple-element.88), channel_id=1, source_target_pairs={{0,96},{32,64},{64,160},{96,128},{128,224},{160,192},{192,32},{224... | collective-permute-start | bytes 393224 | tf_op jit(solution)/shard_map/ppermute | solution.py:428
  48.1 2.1 %collective-permute-done.10.refs_10_ = bf16[64,1024]{1,0:T(8,128)(2,1)S(1)} collective-permute-done((bf16[64,1024]{1,0:T(8,128)(2,1)S(1)}, bf16[64,1024]{1,0:T(8,128)(2,1)S(1)}, u32[]{:S(2)}, u32[]{:S(2)}) %collective-permute-start.10) | collective-permute-done | bytes 131104 | tf_op jit(solution)/shard_map/ppermute | solution.py:428
  50.3 1.1 collective-permute-start.15
  51.4 1.1 collective-permute-done.11.refs_11_
  52.5 0.5 slice_bitcast_fusion
  53.0 4.0 %collective-permute-done.12.refs_12_ = bf16[64,1024]{1,0:T(8,128)(2,1)S(1)} collective-permute-done((bf16[64,1024]{1,0:T(8,128)(2,1)S(1)}, bf16[64,1024]{1,0:T(8,128)(2,1)S(1)}, u32[]{:S(2)}, u32[]{:S(2)}) %collective-permute-start.12) | collective-permute-done | bytes 131104 | tf_op jit(solution)/shard_map/ppermute | solution.py:428
  57.0 1.9 %collective-permute-done.14.refs_14_ = bf16[64,1024]{1,0:T(8,128)(2,1)S(1)} collective-permute-done((bf16[64,1024]{1,0:T(8,128)(2,1)S(1)}, bf16[64,1024]{1,0:T(8,128)(2,1)S(1)}, u32[]{:S(2)}, u32[]{:S(2)}) %collective-permute-start.14) | collective-permute-done | bytes 131104 | tf_op jit(solution)/shard_map/ppermute | solution.py:428
  58.9 1.8 %right_side.1 = (f32[304,1024]{1,0:T(8,128)S(1)}, bf16[512,1024]{1,0:T(8,128)(2,1)S(1)}, bf16[304,128]{1,0:T(8,128)(2,1)S(1)}, bf16[304,128]{1,0:T(8,128)(2,1)S(1)}, bf16[16,304]{1,0:T(8,128)(2,1)S(1)}) custom-call(bf16[64,1024]{1,0:T(8,128)(2,1)S(1)} %copy-done, bf16[64,1024]{1,0:T(8,128)(2,1)S(1)} %collective-permute-done.2.refs_1_, ...), custom_call_target="tpu_custom_call" | custom-call | tf_op jit(solution)/shard_map/right_side/pallas_call | solution.py:30
  60.8 1.6 %collective-permute-start.19 = (bf16[16,304]{1,0:T(8,128)(2,1)S(1)}, bf16[16,304]{1,0:T(8,128)(2,1)S(1)}, u32[]{:S(2)}, u32[]{:S(2)}) collective-permute-start(bf16[16,304]{1,0:T(8,128)(2,1)S(1)} %get-tuple-element.96), channel_id=1, source_target_pairs={{0,224},{32,0},{64,32},{96,64},{128,96},{160,128},{192,160},{224,1... | collective-permute-start | bytes 29192 | tf_op jit(solution)/shard_map/ppermute | solution.py:428
  62.4 0.6 collective-permute-start.16
  63.0 4.7 %collective-permute-start.17 = (bf16[304,128]{1,0:T(8,128)(2,1)S(1)}, bf16[304,128]{1,0:T(8,128)(2,1)S(1)}, u32[]{:S(2)}, u32[]{:S(2)}) collective-permute-start(bf16[304,128]{1,0:T(8,128)(2,1)S(1)} %get-tuple-element.95), channel_id=1, source_target_pairs={{0,31},{1,0},{2,1},{3,2},{4,3},{5,4},{6,5},{7,6},{8,7},{9,8},{10,9... | collective-permute-start | bytes 233480 | tf_op jit(solution)/shard_map/ppermute | solution.py:428
  68.0 3.4 %apply0.1 = (f32[304,1024]{1,0:T(8,128)S(1)}, f32[3,8,128]{2,1,0:T(8,128)S(1)}) custom-call(f32[304,1024]{1,0:T(8,128)S(1)} %get-tuple-element.91.refs_0_.refs_4_.basis.zero, bf16[512,1024]{1,0:T(8,128)(2,1)S(1)} %get-tuple-element.92.refs_1_, bf16[512,608]{1,0:T(8,128)(2,1)S(1)} %pad_maximum_fusion.refs_2_, ...), custom_call_target="tpu_custom_call" | custom-call | tf_op jit(solution)/shard_map/apply0/pallas_call | solution.py:30
  71.4 0.7 add_halo1.1
  72.1 5.4 %collective-permute-start.21 = (bf16[304,128]{1,0:T(8,128)(2,1)S(1)}, bf16[304,128]{1,0:T(8,128)(2,1)S(1)}, u32[]{:S(2)}, u32[]{:S(2)}) collective-permute-start(bf16[304,128]{1,0:T(8,128)(2,1)S(1)} %get-tuple-element.100), channel_id=1, source_target_pairs={{0,31},{1,0},{2,1},{3,2},{4,3},{5,4},{6,5},{7,6},{8,7},{9,8},{10,9... | collective-permute-start | bytes 233480 | tf_op jit(solution)/shard_map/ppermute | solution.py:428
  77.5 1.7 %collective-permute-start.23 = (bf16[16,304]{1,0:T(8,128)(2,1)S(1)}, bf16[16,304]{1,0:T(8,128)(2,1)S(1)}, u32[]{:S(2)}, u32[]{:S(2)}) collective-permute-start(bf16[16,304]{1,0:T(8,128)(2,1)S(1)} %get-tuple-element.101), channel_id=1, source_target_pairs={{0,224},{32,0},{64,32},{96,64},{128,96},{160,128},{192,160},{224,1... | collective-permute-start | bytes 29192 | tf_op jit(solution)/shard_map/ppermute | solution.py:428
  79.2 3.4 %apply1.1 = (f32[304,1024]{1,0:T(8,128)S(1)}, f32[3,8,128]{2,1,0:T(8,128)S(1)}) custom-call(f32[304,1024]{1,0:T(8,128)S(1)} %get-tuple-element.97.refs_0_.refs_4_.one, bf16[512,1024]{1,0:T(8,128)(2,1)S(1)} %get-tuple-element.92.refs_1_, bf16[512,608]{1,0:T(8,128)(2,1)S(1)} %pad_maximum_fusion.refs_2_, ...), custom_call_target="tpu_custom_call" | custom-call | tf_op jit(solution)/shard_map/apply1/pallas_call | solution.py:30
  82.7 1.1 add_halo2.1
  83.8 2.1 %collective-permute-start.25 = (bf16[16,304]{1,0:T(8,128)(2,1)S(1)}, bf16[16,304]{1,0:T(8,128)(2,1)S(1)}, u32[]{:S(2)}, u32[]{:S(2)}) collective-permute-start(bf16[16,304]{1,0:T(8,128)(2,1)S(1)} %get-tuple-element.104), channel_id=1, source_target_pairs={{0,32},{32,64},{64,96},{96,128},{128,160},{160,192},{192,224},{224... | collective-permute-start | bytes 29192 | tf_op jit(solution)/shard_map/ppermute | solution.py:428
  85.9 3.5 %apply2.1.two = f32[3,8,128]{2,1,0:T(8,128)S(1)} custom-call(f32[304,1024]{1,0:T(8,128)S(1)} %get-tuple-element.102.refs_0_.field.two, bf16[512,1024]{1,0:T(8,128)(2,1)S(1)} %get-tuple-element.92.refs_1_, bf16[512,608]{1,0:T(8,128)(2,1)S(1)} %pad_maximum_fusion.refs_2_, bf16[304,512]{1,0:T(8,128)(2,1)S(1)} %subtract_convert_fusion.1.refs_16_.refs_3_, ...), custom_call_target="tpu_custom_call" | custom-call | tf_op jit(solution)/shard_map/apply2/pallas_call | solution.py:30
  89.4 2.1 %collective-permute-done.24.above = bf16[304,128]{1,0:T(8,128)(2,1)S(1)} collective-permute-done((bf16[304,128]{1,0:T(8,128)(2,1)S(1)}, bf16[304,128]{1,0:T(8,128)(2,1)S(1)}, u32[]{:S(2)}, u32[]{:S(2)}) %collective-permute-start.24) | collective-permute-done | bytes 77856 | tf_op jit(solution)/shard_map/ppermute | solution.py:428
  91.6 0.6 all_moments.1
  92.1 1.0 collective-permute-start.26
  93.1 0.8 collective-permute-done.26
  94.0 3.4 %collective-permute-done.27 = f32[1,128]{1,0:T(1,128)S(1)} collective-permute-done((f32[1,128]{1,0:T(1,128)S(1)}, f32[1,128]{1,0:T(1,128)S(1)}, u32[]{:S(2)}, u32[]{:S(2)}) %collective-permute-start.27) | collective-permute-done | bytes 544 | tf_op jit(solution)/shard_map/ppermute | solution.py:428
  97.5 2.8 %collective-permute-start.28 = (f32[1,128]{1,0:T(1,128)S(1)}, f32[1,128]{1,0:T(1,128)S(1)}, u32[]{:S(2)}, u32[]{:S(2)}) collective-permute-start(f32[1,128]{1,0:T(1,128)S(1)} %add.70.one), channel_id=1, source_target_pairs={{0,128},{32,160},{64,192},{96,224},{128,0},{160,32},{192,64},{224,... | collective-permute-start | bytes 1544 | tf_op jit(solution)/shard_map/ppermute | solution.py:428
  100.3 2.2 %collective-permute-done.28.two = f32[1,128]{1,0:T(1,128)S(1)} collective-permute-done((f32[1,128]{1,0:T(1,128)S(1)}, f32[1,128]{1,0:T(1,128)S(1)}, u32[]{:S(2)}, u32[]{:S(2)}) %collective-permute-start.28) | collective-permute-done | bytes 544 | tf_op jit(solution)/shard_map/ppermute | solution.py:428
  102.6 15.6 %all_to_all.10.parts = f32[32,1,128]{2,1,0:T(1,128)S(1)} all-to-all(f32[32,1,128]{2,1,0:T(1,128)S(1)} %add_and_spread.1), channel_id=1, replica_groups=mesh['ifg'=8,'rows'=32] {'rows'}, dimensions={0} | all-to-all | bytes 32768 | tf_op jit(solution)/shard_map/all_to_all | solution.py:586
  118.1 1.3 %combine.1 = f32[2400,128]{1,0:T(8,128)} custom-call(f32[32,1,128]{2,1,0:T(1,128)S(1)} %all_to_all.10.parts, f32[304,1024]{1,0:T(8,128)S(1)} %get-tuple-element.91.refs_0_.refs_4_.basis.zero, f32[304,1024]{1,0:T(8,128)S(1)} %get-tuple-element.97.refs_0_.refs_4_.one, f32[304,1024]{1,0:T(8,128)S(1)} %get-tuple-element.102.refs_0_.field.two), custom_call_target="tpu_custom_call" | custom-call | tf_op jit(solution)/shard_map/combine/pallas_call | solution.py:30
  (54 shorter events, 1.6 us)
Async XLA Ops:
  0.6 10.7 %copy-start.3 = (s32[64,8]{0,1:T(8,128)S(1)}, s32[64,8]{0,1:T(8,128)}, u32[]{:S(2)}) copy-start(s32[64,8]{0,1:T(8,128)} %param.8) | copy-start | bytes 6148
  0.6 10.8 %copy-start.4 = (s32[512,2]{0,1:T(2,128)S(1)}, s32[512,2]{0,1:T(2,128)}, u32[]{:S(2)}) copy-start(s32[512,2]{0,1:T(2,128)} %param.9) | copy-start | bytes 12292
  0.7 11.6 %copy-start.1 = (f32[8,1024]{1,0:T(8,128)S(1)}, f32[8,1024]{1,0:T(8,128)}, u32[]{:S(2)}) copy-start(f32[8,1024]{1,0:T(8,128)} %height.5) | copy-start | bytes 98308
  2.8 14.7 %collective-permute-start = (bf16[128,1024]{1,0:T(8,128)(2,1)S(1)}, bf16[128,1024]{1,0:T(8,128)(2,1)S(1)}, u32[]{:S(2)}, u32[]{:S(2)}) collective-permute-start(bf16[128,1024]{1,0:T(8,128)(2,1)S(1)} %get-tuple-element.57), channel_id=1, source_target_pairs={{0,1},{1,2},{2,3},{3,4},{4,5},{5,6},{6,7},{7,8},{8,9},{9,10},{10,1... | collective-permute-start | bytes 786440 | tf_op jit(solution)/shard_map/ppermute | solution.py:428
  4.8 12.7 %collective-permute-start.1 = (bf16[128,1024]{1,0:T(8,128)(2,1)S(1)}, bf16[128,1024]{1,0:T(8,128)(2,1)S(1)}, u32[]{:S(2)}, u32[]{:S(2)}) collective-permute-start(bf16[128,1024]{1,0:T(8,128)(2,1)S(1)} %get-tuple-element.58), channel_id=1, source_target_pairs={{0,31},{1,0},{2,1},{3,2},{4,3},{5,4},{6,5},{7,6},{8,7},{9,8},{10,9... | collective-permute-start | bytes 786440 | tf_op jit(solution)/shard_map/ppermute | solution.py:428
  20.1 3.6 %collective-permute-start.8 = (bf16[64,1024]{1,0:T(8,128)(2,1)}, bf16[64,1024]{1,0:T(8,128)(2,1)S(1)}, u32[]{:S(2)}, u32[]{:S(2)}) collective-permute-start(bf16[64,1024]{1,0:T(8,128)(2,1)} %get-tuple-element.77), channel_id=1, source_target_pairs={{0,32},{32,0},{64,96},{96,64},{128,160},{160,128},{192,224},{224,1... | collective-permute-start | bytes 393224 | tf_op jit(solution)/shard_map/ppermute | solution.py:428
  20.2 20.7 %collective-permute-start.2 = (bf16[64,1024]{1,0:T(8,128)(2,1)}, bf16[64,1024]{1,0:T(8,128)(2,1)S(1)}, u32[]{:S(2)}, u32[]{:S(2)}) collective-permute-start(bf16[64,1024]{1,0:T(8,128)(2,1)} %get-tuple-element.70), channel_id=1, source_target_pairs={{0,64},{32,96},{64,128},{96,160},{128,192},{160,224},{192,0},{224,... | collective-permute-start | bytes 393224 | tf_op jit(solution)/shard_map/ppermute | solution.py:428
  20.7 20.5 %collective-permute-start.3 = (bf16[64,1024]{1,0:T(8,128)(2,1)}, bf16[64,1024]{1,0:T(8,128)(2,1)S(1)}, u32[]{:S(2)}, u32[]{:S(2)}) collective-permute-start(bf16[64,1024]{1,0:T(8,128)(2,1)} %get-tuple-element.71), channel_id=1, source_target_pairs={{0,192},{32,224},{64,0},{96,32},{128,64},{160,96},{192,128},{224,1... | collective-permute-start | bytes 393224 | tf_op jit(solution)/shard_map/ppermute | solution.py:428
  22.3 20.1 %collective-permute-start.4 = (bf16[64,1024]{1,0:T(8,128)(2,1)}, bf16[64,1024]{1,0:T(8,128)(2,1)S(1)}, u32[]{:S(2)}, u32[]{:S(2)}) collective-permute-start(bf16[64,1024]{1,0:T(8,128)(2,1)} %get-tuple-element.72), channel_id=1, source_target_pairs={{0,128},{32,160},{64,192},{96,224},{128,0},{160,32},{192,64},{224,... | collective-permute-start | bytes 393224 | tf_op jit(solution)/shard_map/ppermute | solution.py:428
  23.7 16.6 %all-to-all-start = ((f32[32,1,128]{2,1,0:T(1,128)}), f32[32,1,128]{2,1,0:T(1,128)S(1)}, u32[]{:S(2)}, u32[]{:S(2)}) async-start(f32[32,1,128]{2,1,0:T(1,128)} %get-tuple-element.79), calls=%async_computation | async-start | bytes 32768 | tf_op jit(solution)/shard_map/all_to_all | solution.py:502
  32.3 26.6 %copy-start = (bf16[64,1024]{1,0:T(8,128)(2,1)S(1)}, bf16[64,1024]{1,0:T(8,128)(2,1)}, u32[]{:S(2)}) copy-start(bf16[64,1024]{1,0:T(8,128)(2,1)} %get-tuple-element.69.refs_0_) | copy-start | bytes 393220
  32.3 12.7 %collective-permute-start.5 = (bf16[64,1024]{1,0:T(8,128)(2,1)}, bf16[64,1024]{1,0:T(8,128)(2,1)S(1)}, u32[]{:S(2)}, u32[]{:S(2)}) collective-permute-start(bf16[64,1024]{1,0:T(8,128)(2,1)} %get-tuple-element.73), channel_id=1, source_target_pairs={{0,160},{32,128},{64,224},{96,192},{128,32},{160,0},{192,96},{224,... | collective-permute-start | bytes 393224 | tf_op jit(solution)/shard_map/ppermute | solution.py:428
  33.4 12.8 %collective-permute-start.6 = (bf16[64,1024]{1,0:T(8,128)(2,1)}, bf16[64,1024]{1,0:T(8,128)(2,1)S(1)}, u32[]{:S(2)}, u32[]{:S(2)}) collective-permute-start(bf16[64,1024]{1,0:T(8,128)(2,1)} %get-tuple-element.74), channel_id=1, source_target_pairs={{0,96},{32,64},{64,160},{96,128},{128,224},{160,192},{192,32},{224... | collective-permute-start | bytes 393224 | tf_op jit(solution)/shard_map/ppermute | solution.py:428
  40.3 0.9 copy-start.2
  41.2 6.9 %collective-permute-start.7 = (bf16[64,1024]{1,0:T(8,128)(2,1)S(1)}, bf16[64,1024]{1,0:T(8,128)(2,1)S(1)}, u32[]{:S(2)}, u32[]{:S(2)}) collective-permute-start(bf16[64,1024]{1,0:T(8,128)(2,1)S(1)} %copy-done.2), channel_id=1, source_target_pairs={{0,224},{32,192},{64,32},{96,0},{128,96},{160,64},{192,160},{224,1... | collective-permute-start | bytes 393224 | tf_op jit(solution)/shard_map/ppermute | solution.py:428
  41.2 9.1 %collective-permute-start.10 = (bf16[64,1024]{1,0:T(8,128)(2,1)S(1)}, bf16[64,1024]{1,0:T(8,128)(2,1)S(1)}, u32[]{:S(2)}, u32[]{:S(2)}) collective-permute-start(bf16[64,1024]{1,0:T(8,128)(2,1)S(1)} %get-tuple-element.85), channel_id=1, source_target_pairs={{0,192},{32,224},{64,0},{96,32},{128,64},{160,96},{192,128},{224,1... | collective-permute-start | bytes 393224 | tf_op jit(solution)/shard_map/ppermute | solution.py:428
  42.4 10.1 %collective-permute-start.11 = (bf16[64,1024]{1,0:T(8,128)(2,1)S(1)}, bf16[64,1024]{1,0:T(8,128)(2,1)S(1)}, u32[]{:S(2)}, u32[]{:S(2)}) collective-permute-start(bf16[64,1024]{1,0:T(8,128)(2,1)S(1)} %get-tuple-element.86), channel_id=1, source_target_pairs={{0,128},{32,160},{64,192},{96,224},{128,0},{160,32},{192,64},{224,... | collective-permute-start | bytes 393224 | tf_op jit(solution)/shard_map/ppermute | solution.py:428
  45.0 12.0 %collective-permute-start.12 = (bf16[64,1024]{1,0:T(8,128)(2,1)S(1)}, bf16[64,1024]{1,0:T(8,128)(2,1)S(1)}, u32[]{:S(2)}, u32[]{:S(2)}) collective-permute-start(bf16[64,1024]{1,0:T(8,128)(2,1)S(1)} %get-tuple-element.87), channel_id=1, source_target_pairs={{0,160},{32,128},{64,224},{96,192},{128,32},{160,0},{192,96},{224,... | collective-permute-start | bytes 393224 | tf_op jit(solution)/shard_map/ppermute | solution.py:428
  46.2 10.7 %collective-permute-start.13 = (bf16[64,1024]{1,0:T(8,128)(2,1)S(1)}, bf16[64,1024]{1,0:T(8,128)(2,1)S(1)}, u32[]{:S(2)}, u32[]{:S(2)}) collective-permute-start(bf16[64,1024]{1,0:T(8,128)(2,1)S(1)} %get-tuple-element.88), channel_id=1, source_target_pairs={{0,96},{32,64},{64,160},{96,128},{128,224},{160,192},{192,32},{224... | collective-permute-start | bytes 393224 | tf_op jit(solution)/shard_map/ppermute | solution.py:428
  48.1 10.7 %collective-permute-start.14 = (bf16[64,1024]{1,0:T(8,128)(2,1)S(1)}, bf16[64,1024]{1,0:T(8,128)(2,1)S(1)}, u32[]{:S(2)}, u32[]{:S(2)}) collective-permute-start(bf16[64,1024]{1,0:T(8,128)(2,1)S(1)} %get-tuple-element.89), channel_id=1, source_target_pairs={{0,224},{32,192},{64,32},{96,0},{128,96},{160,64},{192,160},{224,1... | collective-permute-start | bytes 393224 | tf_op jit(solution)/shard_map/ppermute | solution.py:428
  50.3 8.6 %collective-permute-start.15 = (bf16[64,1024]{1,0:T(8,128)(2,1)S(1)}, bf16[64,1024]{1,0:T(8,128)(2,1)S(1)}, u32[]{:S(2)}, u32[]{:S(2)}) collective-permute-start(bf16[64,1024]{1,0:T(8,128)(2,1)S(1)} %get-tuple-element.90), channel_id=1, source_target_pairs={{0,32},{32,0},{64,96},{96,64},{128,160},{160,128},{192,224},{224,1... | collective-permute-start | bytes 393224 | tf_op jit(solution)/shard_map/ppermute | solution.py:428
  52.5 6.4 %collective-permute-start.9 = (bf16[64,1024]{1,0:T(8,128)(2,1)S(1)}, bf16[64,1024]{1,0:T(8,128)(2,1)S(1)}, u32[]{:S(2)}, u32[]{:S(2)}) collective-permute-start(bf16[64,1024]{1,0:T(8,128)(2,1)S(1)} %get-tuple-element.84), channel_id=1, source_target_pairs={{0,64},{32,96},{64,128},{96,160},{128,192},{160,224},{192,0},{224,... | collective-permute-start | bytes 393224 | tf_op jit(solution)/shard_map/ppermute | solution.py:428
  60.6 10.8 %collective-permute-start.18 = (bf16[16,304]{1,0:T(8,128)(2,1)S(1)}, bf16[16,304]{1,0:T(8,128)(2,1)S(1)}, u32[]{:S(2)}, u32[]{:S(2)}) collective-permute-start(bf16[16,304]{1,0:T(8,128)(2,1)S(1)} %get-tuple-element.96), channel_id=1, source_target_pairs={{0,32},{32,64},{64,96},{96,128},{128,160},{160,192},{192,224},{224... | collective-permute-start | bytes 29192 | tf_op jit(solution)/shard_map/ppermute | solution.py:428
  60.8 10.6 %collective-permute-start.19 = (bf16[16,304]{1,0:T(8,128)(2,1)S(1)}, bf16[16,304]{1,0:T(8,128)(2,1)S(1)}, u32[]{:S(2)}, u32[]{:S(2)}) collective-permute-start(bf16[16,304]{1,0:T(8,128)(2,1)S(1)} %get-tuple-element.96), channel_id=1, source_target_pairs={{0,224},{32,0},{64,32},{96,64},{128,96},{160,128},{192,160},{224,1... | collective-permute-start | bytes 29192 | tf_op jit(solution)/shard_map/ppermute | solution.py:428
  62.4 9.0 %collective-permute-start.16 = (bf16[304,128]{1,0:T(8,128)(2,1)S(1)}, bf16[304,128]{1,0:T(8,128)(2,1)S(1)}, u32[]{:S(2)}, u32[]{:S(2)}) collective-permute-start(bf16[304,128]{1,0:T(8,128)(2,1)S(1)} %get-tuple-element.94), channel_id=1, source_target_pairs={{0,1},{1,2},{2,3},{3,4},{4,5},{5,6},{6,7},{7,8},{8,9},{9,10},{10,1... | collective-permute-start | bytes 233480 | tf_op jit(solution)/shard_map/ppermute | solution.py:428
  63.0 8.4 %collective-permute-start.17 = (bf16[304,128]{1,0:T(8,128)(2,1)S(1)}, bf16[304,128]{1,0:T(8,128)(2,1)S(1)}, u32[]{:S(2)}, u32[]{:S(2)}) collective-permute-start(bf16[304,128]{1,0:T(8,128)(2,1)S(1)} %get-tuple-element.95), channel_id=1, source_target_pairs={{0,31},{1,0},{2,1},{3,2},{4,3},{5,4},{6,5},{7,6},{8,7},{9,8},{10,9... | collective-permute-start | bytes 233480 | tf_op jit(solution)/shard_map/ppermute | solution.py:428
  72.1 10.5 %collective-permute-start.20 = (bf16[304,128]{1,0:T(8,128)(2,1)S(1)}, bf16[304,128]{1,0:T(8,128)(2,1)S(1)}, u32[]{:S(2)}, u32[]{:S(2)}) collective-permute-start(bf16[304,128]{1,0:T(8,128)(2,1)S(1)} %get-tuple-element.99), channel_id=1, source_target_pairs={{0,1},{1,2},{2,3},{3,4},{4,5},{5,6},{6,7},{7,8},{8,9},{9,10},{10,1... | collective-permute-start | bytes 233480 | tf_op jit(solution)/shard_map/ppermute | solution.py:428
  72.1 10.5 %collective-permute-start.21 = (bf16[304,128]{1,0:T(8,128)(2,1)S(1)}, bf16[304,128]{1,0:T(8,128)(2,1)S(1)}, u32[]{:S(2)}, u32[]{:S(2)}) collective-permute-start(bf16[304,128]{1,0:T(8,128)(2,1)S(1)} %get-tuple-element.100), channel_id=1, source_target_pairs={{0,31},{1,0},{2,1},{3,2},{4,3},{5,4},{6,5},{7,6},{8,7},{9,8},{10,9... | collective-permute-start | bytes 233480 | tf_op jit(solution)/shard_map/ppermute | solution.py:428
  77.5 5.2 %collective-permute-start.22 = (bf16[16,304]{1,0:T(8,128)(2,1)S(1)}, bf16[16,304]{1,0:T(8,128)(2,1)S(1)}, u32[]{:S(2)}, u32[]{:S(2)}) collective-permute-start(bf16[16,304]{1,0:T(8,128)(2,1)S(1)} %get-tuple-element.101), channel_id=1, source_target_pairs={{0,32},{32,64},{64,96},{96,128},{128,160},{160,192},{192,224},{224... | collective-permute-start | bytes 29192 | tf_op jit(solution)/shard_map/ppermute | solution.py:428
  77.5 5.2 %collective-permute-start.23 = (bf16[16,304]{1,0:T(8,128)(2,1)S(1)}, bf16[16,304]{1,0:T(8,128)(2,1)S(1)}, u32[]{:S(2)}, u32[]{:S(2)}) collective-permute-start(bf16[16,304]{1,0:T(8,128)(2,1)S(1)} %get-tuple-element.101), channel_id=1, source_target_pairs={{0,224},{32,0},{64,32},{96,64},{128,96},{160,128},{192,160},{224,1... | collective-permute-start | bytes 29192 | tf_op jit(solution)/shard_map/ppermute | solution.py:428
  83.8 7.7 %collective-permute-start.24 = (bf16[304,128]{1,0:T(8,128)(2,1)S(1)}, bf16[304,128]{1,0:T(8,128)(2,1)S(1)}, u32[]{:S(2)}, u32[]{:S(2)}) collective-permute-start(bf16[304,128]{1,0:T(8,128)(2,1)S(1)} %get-tuple-element.103), channel_id=1, source_target_pairs={{0,1},{1,2},{2,3},{3,4},{4,5},{5,6},{6,7},{7,8},{8,9},{9,10},{10,1... | collective-permute-start | bytes 233480 | tf_op jit(solution)/shard_map/ppermute | solution.py:428
  83.8 5.6 %collective-permute-start.25 = (bf16[16,304]{1,0:T(8,128)(2,1)S(1)}, bf16[16,304]{1,0:T(8,128)(2,1)S(1)}, u32[]{:S(2)}, u32[]{:S(2)}) collective-permute-start(bf16[16,304]{1,0:T(8,128)(2,1)S(1)} %get-tuple-element.104), channel_id=1, source_target_pairs={{0,32},{32,64},{64,96},{96,128},{128,160},{160,192},{192,224},{224... | collective-permute-start | bytes 29192 | tf_op jit(solution)/shard_map/ppermute | solution.py:428
  92.1 1.8 %collective-permute-start.26 = (f32[1,128]{1,0:T(1,128)S(1)}, f32[1,128]{1,0:T(1,128)S(1)}, u32[]{:S(2)}, u32[]{:S(2)}) collective-permute-start(f32[1,128]{1,0:T(1,128)S(1)} %all_moments.1), channel_id=1, source_target_pairs={{0,32},{32,0},{64,96},{96,64},{128,160},{160,128},{192,224},{224,1... | collective-permute-start | bytes 1544 | tf_op jit(solution)/shard_map/ppermute | solution.py:428
  94.0 3.5 %collective-permute-start.27 = (f32[1,128]{1,0:T(1,128)S(1)}, f32[1,128]{1,0:T(1,128)S(1)}, u32[]{:S(2)}, u32[]{:S(2)}) collective-permute-start(f32[1,128]{1,0:T(1,128)S(1)} %add.69), channel_id=1, source_target_pairs={{0,64},{32,96},{64,0},{96,32},{128,192},{160,224},{192,128},{224,1... | collective-permute-start | bytes 1544 | tf_op jit(solution)/shard_map/ppermute | solution.py:428
  97.5 5.0 %collective-permute-start.28 = (f32[1,128]{1,0:T(1,128)S(1)}, f32[1,128]{1,0:T(1,128)S(1)}, u32[]{:S(2)}, u32[]{:S(2)}) collective-permute-start(f32[1,128]{1,0:T(1,128)S(1)} %add.70.one), channel_id=1, source_target_pairs={{0,128},{32,160},{64,192},{96,224},{128,0},{160,32},{192,64},{224,... | collective-permute-start | bytes 1544 | tf_op jit(solution)/shard_map/ppermute | solution.py:428

commit v7 on v6

--- a/solution.py
+++ b/solution.py
@@ -100,6 +100,11 @@
     return other(lax.axis_index("ifg"), *OFFSETS[step])
 
 
+def pieces_of(outs):
+    own, up, down, twice, pair = outs
+    return [own, up.at[0], down.at[0], twice.at[0], twice.at[1], up.at[1], down.at[1], pair]
+
+
 def smooth_row(rows, lane, mask, terrain):
     denom = shifted_sum(rows[0][0] + rows[1][0] + rows[2][0], lane, 1023)
     numer = shifted_sum(rows[0][1] + rows[1][1] + rows[2][1], lane, 1023)
@@ -118,7 +123,7 @@
 
 
 def inner_rows(phase_t, coher_t, mask, height, smooth_out, totals, *rest):
-    outs, weights, smooth, sems = rest[:8], *rest[8:]
+    outs, weights, smooth, sems = pieces_of(rest[:5]), *rest[5:]
     lane = lax.broadcasted_iota(jnp.int32, (16, 1024), 1)
 
     def copies(block):
@@ -160,8 +165,8 @@
 
 
 def border_rows(phase_t, coher_t, above, below, mask, height, totals, *rest):
-    smooth_out, sums, outs = rest[9], rest[10], rest[11:19]
-    weights, smooth, added, sems = rest[19:]
+    smooth_out, sums, outs = rest[6], rest[7], pieces_of(rest[8:13])
+    weights, smooth, added, sems = rest[13:]
     lane = lax.broadcasted_iota(jnp.int32, (16, 1024), 1)
     my_row = lax.axis_index("rows")
     valid = (my_row > 0, my_row < lax.axis_size("rows") - 1)
@@ -198,7 +203,7 @@
             )
     for copy in copies:
         copy.start()
-    sums[...] = jnp.broadcast_to(jnp.sum(added[...].T, axis=0)[None, None, :], sums.shape)
+    sums[...] = jnp.broadcast_to(jnp.sum(added[...].T, axis=0, keepdims=True), sums.shape)
     for copy in copies:
         copy.wait()
 
@@ -242,8 +247,9 @@
     return (pixel == wanted).astype(BF16)
 
 
-def write_edges(field, first, last, columns):
-    first[...] = field[:, pl.ds(0, 128)].astype(BF16)
+def write_edges(field, last, columns, first=None):
+    if first is not None:
+        first[...] = field[:, pl.ds(0, 128)].astype(BF16)
     last[...] = field[:, pl.ds(896, 128)].astype(BF16)
     picked = lax.dot_general(
         column_selector(), field[...].astype(BF16), (((1,), (1,)), ((), ())), preferred_element_type=F32
@@ -252,8 +258,10 @@
 
 
 def right_side(*refs):
-    weight_parts, corrected_parts = refs[:8], refs[8:16]
-    design_t, field, weights, first, last, columns = refs[16:]
+    own, up, down, twice, swap = refs[:5]
+    weight_parts = [own, up.at[0], down.at[0], twice.at[0]] + [swap.at[part] for part in range(4)]
+    corrected_parts = refs[5:13]
+    design_t, field, weights, *edges = refs[13:]
     for part in range(8):
         weights[pl.ds(part * 64, 64), :] = weight_parts[part][...]
 
@@ -271,7 +279,7 @@
         return 0
 
     lax.fori_loop(0, 4, one_chunk, 0)
-    write_edges(field, first, last, columns)
+    write_edges(field, *edges)
 
 
 def row_lanes(row):
@@ -349,7 +357,7 @@
     return row > 0, row < lax.axis_size("rows") - 1, col > 0, col < lax.axis_size("ifg") - 1
 
 
-def add_halo(image, above, below, left, right, field, first, last, columns):
+def add_halo(image, above, below, left, right, field, *edges):
     flags = inside()
     sides = jnp.concatenate([keep(flags[2], left[8:16, :]), keep(flags[3], right[0:8, :])], axis=0).astype(BF16)
     for row in range(8):
@@ -360,7 +368,7 @@
         if row == 7:
             halo += keep(flags[1], below[...])
         field[:, lanes] = image[:, lanes] - SMOOTHING_WEIGHT * halo
-    write_edges(field, first, last, columns)
+    write_edges(field, *edges)
 
 
 def all_moments(field, above, left, zero, one, two, out):
@@ -381,7 +389,8 @@
     out[...] = total
 
 
-def add_and_spread(one, two, basis, out):
+def add_and_spread(one, two, *rest):
+    out = rest[-1]
     out[...] = jnp.broadcast_to((one[...] + two[...])[None], out.shape)
 
 
@@ -451,7 +460,8 @@
     )
     above, below = forward(last, "rows"), backward(first, "rows")
     mask = gap_mask.astype(F32)
-    pieces = [in_hbm((64, 1024), BF16)] * 8
+    single, double = in_hbm((64, 1024), BF16), in_hbm((2, 64, 1024), BF16)
+    pieces = [single, double, double, double, single]
     smooth, totals, *weight_parts = call(
         inner_rows,
         [in_hbm((8, 64, 1024), F32), sds((128, 128), F32)] + pieces,
@@ -459,7 +469,7 @@
         coher_t,
         mask,
         height,
-        out_specs=[pltpu.HBM, pltpu.VMEM] + [pltpu.HBM] * 8,
+        out_specs=[pltpu.HBM, pltpu.VMEM] + [pltpu.HBM] * 5,
         scratch=(
             pltpu.VMEM((8, 64, 768), BF16),
             pltpu.VMEM((6, 64, 1024), F32),
@@ -469,7 +479,7 @@
     )
     smooth, sums, *weight_parts = call(
         border_rows,
-        [in_hbm((8, 64, 1024), F32), sds((n_rows, 1, 128), F32)] + pieces,
+        [in_hbm((8, 64, 1024), F32), sds((1, 128), F32)] + pieces,
         phase_t,
         coher_t,
         above,
@@ -479,27 +489,38 @@
         totals,
         smooth,
         *weight_parts,
-        specs=[pltpu.VMEM] * 7 + [pltpu.HBM] * 9,
-        out_specs=[pltpu.HBM, pltpu.VMEM] + [pltpu.HBM] * 8,
+        specs=[pltpu.VMEM] * 7 + [pltpu.HBM] * 6,
+        out_specs=[pltpu.HBM, pltpu.VMEM] + [pltpu.HBM] * 5,
         scratch=(
             pltpu.VMEM((2, 8, 64, 128), BF16),
             pltpu.VMEM((2, 64, 1024), F32),
             pltpu.VMEM((128, 128), F32),
             pltpu.SemaphoreType.DMA((2, 9)),
         ),
-        aliases={7: 0, **{8 + step: 2 + step for step in range(8)}},
+        aliases={7: 0, **{8 + step: 2 + step for step in range(5)}},
         name="border_rows",
     )
 
-    def exchange(parts):
-        return [parts[0]] + [
-            permute(part, "ifg", lambda i: other(i, *offset))
-            for part, offset in zip(parts[1:], OFFSETS[1:])
-        ]
-
-    weight_parts = exchange(weight_parts)
-    sums, weight_parts[7] = lax.optimization_barrier((sums, weight_parts[7]))
-    sums = lax.all_to_all(sums, "rows", 0, 0, tiled=True)
+    def offset(values, chips, core):
+        return permute(values, "ifg", lambda i: other(i, chips, core))
+
+    groups = [[8 * y + 2 * z + half for y in range(4) for z in range(4)] for half in range(2)]
+
+    def gather_rows(values, *after):
+        spread = call(
+            add_and_spread,
+            sds((n_rows // 2, 1, 128), F32),
+            values,
+            permute(values, "rows", lambda i: i ^ 1),
+            *after,
+            name="add_and_spread",
+        )
+        return lax.all_to_all(spread, "rows", 0, 0, tiled=True, axis_index_groups=groups)
+
+    sums = gather_rows(sums)
+    own, up, down, twice, pair = weight_parts
+    twice, up, down = offset(twice, 2, 0), offset(up, 1, 0), offset(down, 3, 0)
+    swap = offset(jnp.stack([twice[1], up[1], down[1], pair]), 0, 1)
     smooth = call(
         stage,
         sds((8, 64, 1024), F32),
@@ -518,7 +539,9 @@
         name="correction",
     )
     slope, corrected_parts[0] = lax.optimization_barrier((slope_row[0, :64], corrected_parts[0]))
-    corrected_parts = exchange(corrected_parts)
+    corrected_parts = corrected_parts[:1] + [
+        offset(part, *where) for part, where in zip(corrected_parts[1:], OFFSETS[1:])
+    ]
     sources = jnp.stack([other(me, 4 - chips, core) for chips, core in OFFSETS])
     pairs = date_pairs.reshape(n_ifg, -1, 2)[sources].reshape(-1, 2)
     dates = jnp.arange(DP, dtype=jnp.int32)
@@ -527,18 +550,22 @@
     design = jnp.concatenate([design, design], axis=1)
 
     field = sds((DP, 1024), F32)
-    edges = (sds((DP, 128), BF16), sds((DP, 128), BF16), sds((16, DP), BF16))
+    edges = (sds((DP, 128), BF16), sds((16, DP), BF16), sds((DP, 128), BF16))
     moments = sds((3, 8, 128), F32)
-    k0, weights, first, last, columns = call(
+    k0, weights, *sides = call(
         right_side,
         (field, sds((512, 1024), BF16)) + edges,
-        *weight_parts,
+        own,
+        up,
+        down,
+        twice,
+        swap,
         *corrected_parts,
         design_t,
         name="right_side",
     )
 
-    def halos(first, last, columns):
+    def halos(last, columns, first):
         return (
             forward(last, "rows"),
             backward(first, "rows"),
@@ -551,15 +578,15 @@
         body = lambda *refs: apply_local(with_before, with_image, *refs)
         return call(body, outs, *args, name=name)
 
-    def joined(image, around, name):
-        return call(add_halo, (field,) + edges, image, *around, name=name)
-
-    around = halos(first, last, columns)
+    def joined(image, around, count, name):
+        return call(add_halo, (field,) + edges[:count], image, *around, name=name)
+
+    around = halos(*sides)
     image, mom0 = local(False, True, "apply0", k0, weights, design, design_t)
-    k1, first, last, columns = joined(image, around, "add_halo1")
-    around = halos(first, last, columns)
+    k1, *sides = joined(image, around, 3, "add_halo1")
+    around = halos(*sides)
     image, mom1 = local(True, True, "apply1", k1, weights, design, design_t, k0)
-    k2, first, last, columns = joined(image, around, "add_halo2")
+    k2, last, columns = joined(image, around, 2, "add_halo2")
     above, left = forward(last, "rows"), forward(columns, "ifg")
     (mom2,) = local(True, False, "apply2", k2, weights, design, design_t, k1)
     part = call(
@@ -573,17 +600,9 @@
         mom2,
         name="all_moments",
     )
-    for step in (1, 2):
+    for step in (1, 2, 4):
         part = part + permute(part, "ifg", lambda i: i ^ step)
-    parts = call(
-        add_and_spread,
-        sds((n_rows, 1, 128), F32),
-        part,
-        permute(part, "ifg", lambda i: i ^ 4),
-        k0,
-        name="add_and_spread",
-    )
-    parts = lax.all_to_all(parts, "rows", 0, 0, tiled=True)
+    parts = gather_rows(part, k0)
     displacement = call(
         combine,
         sds((DATES * 8, 128), F32),

time: 120 us -> 128 us (1.067)
  waiting for transfers between devices: 24.2 us -> 35.1 us
  starting transfers between devices: 50.5 us -> 46.5 us
  other arithmetic: 0.65 us -> 2.29 us
  blocking collectives: 15.6 us -> 14.2 us
    ppermute x29 -> x28, waiting for transfers between devices: 19.8 us -> 29.1 us  [permute(): lax.ppermute(values, axis, [(i, target(i)) for i in range(lax.axis_size(a...]
    ppermute x29 -> x28, starting transfers between devices: 43.7 us -> 40.5 us  [permute(): lax.ppermute(values, axis, [(i, target(i)) for i in range(lax.axis_size(a...]
    all_to_all x1, waiting for transfers between devices: 4.38 us -> 5.96 us  [gather_rows(): lax.all_to_all(spread, 'rows', 0, 0, tiled=True, axis_index_groups=groups)]
    all_to_all x1, blocking collectives: 15.6 us -> 14.2 us  [gather_rows(): lax.all_to_all(spread, 'rows', 0, 0, tiled=True, axis_index_groups=groups)]
    pallas_call x14 -> x15, Pallas kernels: 25.8 us -> 25.5 us  [call(): pl.pallas_call(body, out_shape=outs, in_specs=[pl.BlockSpec(memory_space=...]
  transfers between devices with their start and end apart: 30 -> 29, of which waited for: 11 -> 12; matrix products, arithmetic and copies ran while one was open for 2% -> 3% of each run, Pallas kernels for 13% -> 13%
where the time goes in v7:
time: 128 us; the launch traced here: 127 us
  starting transfers between devices  46.5 us (36%)
  waiting for transfers between devices  35.1 us (27%)
  Pallas kernels  25.5 us (20%)
  blocking collectives  14.2 us (11%)
  other arithmetic  2.29 us (2%)
  local copies, waits for them, and re-layouts  2.26 us (2%)
    ppermute x28, starting transfers between devices, permute(): lax.ppermute(values, axis, [(i, target(i)) for i in range(lax.axis_size(a...  40.5 us
    ppermute x28, waiting for transfers between devices, permute(): lax.ppermute(values, axis, [(i, target(i)) for i in range(lax.axis_size(a...  29.1 us
    pallas_call x15, Pallas kernels, call(): pl.pallas_call(body, out_shape=outs, in_specs=[pl.BlockSpec(memory_space=...  25.5 us
    all_to_all x1, blocking collectives, gather_rows(): lax.all_to_all(spread, 'rows', 0, 0, tiled=True, axis_index_groups=groups)  14.2 us
    all_to_all x1, starting transfers between devices, gather_rows(): lax.all_to_all(spread, 'rows', 0, 0, tiled=True, axis_index_groups=groups)  5.97 us
    all_to_all x1, waiting for transfers between devices, gather_rows(): lax.all_to_all(spread, 'rows', 0, 0, tiled=True, axis_index_groups=groups)  5.96 us
  transfers between devices with their start and end apart: 29, of which 12 were waited for; matrix products, arithmetic and copies ran while one was open for 3% of the time, Pallas kernels for 13%

profile of v7, /device:TPU:6, one launch (start us, length us, event | category | flops | bytes accessed | tf_op | source)
XLA Modules:
  0.0 126.9 jit_solution(13468613981846009324)
XLA Ops:
  0.7 2.1 %rows_first.1 = (bf16[8,64,1024]{2,1,0:T(8,128)(2,1)S(1)}, bf16[8,64,1024]{2,1,0:T(8,128)(2,1)S(1)}, bf16[128,1024]{1,0:T(8,128)(2,1)S(1)}, bf16[128,1024]{1,0:T(8,128)(2,1)S(1)}) custom-call(bf16[64,8,1024]{2,1,0:T(8,128)(2,1)} %phase.1, bf16[64,8,1024]{2,1,0:T(8,128)(2,1)} %coher.1), custom_call_target="tpu_custom_call" | custom-call | tf_op jit(solution)/shard_map/rows_first/pallas_call | solution.py:30
  2.8 2.0 %collective-permute-start = (bf16[128,1024]{1,0:T(8,128)(2,1)S(1)}, bf16[128,1024]{1,0:T(8,128)(2,1)S(1)}, u32[]{:S(2)}, u32[]{:S(2)}) collective-permute-start(bf16[128,1024]{1,0:T(8,128)(2,1)S(1)} %get-tuple-element.49), channel_id=1, source_target_pairs={{0,1},{1,2},{2,3},{3,4},{4,5},{5,6},{6,7},{7,8},{8,9},{9,10},{10,1... | collective-permute-start | bytes 786440 | tf_op jit(solution)/shard_map/ppermute | solution.py:437
  4.8 6.5 %collective-permute-start.1 = (bf16[128,1024]{1,0:T(8,128)(2,1)S(1)}, bf16[128,1024]{1,0:T(8,128)(2,1)S(1)}, u32[]{:S(2)}, u32[]{:S(2)}) collective-permute-start(bf16[128,1024]{1,0:T(8,128)(2,1)S(1)} %get-tuple-element.50), channel_id=1, source_target_pairs={{0,31},{1,0},{2,1},{3,2},{4,3},{5,4},{6,5},{7,6},{8,7},{9,8},{10,9... | collective-permute-start | bytes 786440 | tf_op jit(solution)/shard_map/ppermute | solution.py:437
  11.4 3.4 %inner_rows.1 = (f32[8,64,1024]{2,1,0:T(8,128)}, f32[128,128]{1,0:T(8,128)S(1)}, bf16[64,1024]{1,0:T(8,128)(2,1)}, bf16[2,64,1024]{2,1,0:T(8,128)(2,1)}, bf16[2,...) custom-call(bf16[8,64,1024]{2,1,0:T(8,128)(2,1)S(1)} %get-tuple-element.47.phase_t, ...), custom_call_target="tpu_custom_call" | custom-call | tf_op jit(solution)/shard_map/inner_rows/pallas_call | solution.py:30
  14.9 2.6 %collective-permute-done.above = bf16[128,1024]{1,0:T(8,128)(2,1)S(1)} collective-permute-done((bf16[128,1024]{1,0:T(8,128)(2,1)S(1)}, bf16[128,1024]{1,0:T(8,128)(2,1)S(1)}, u32[]{:S(2)}, u32[]{:S(2)}) %collective-permute-start) | collective-permute-done | bytes 262176 | tf_op jit(solution)/shard_map/ppermute | solution.py:437
  17.5 1.9 %border_rows.1 = (f32[8,64,1024]{2,1,0:T(8,128)}, f32[1,128]{1,0:T(1,128)S(1)}, bf16[64,1024]{1,0:T(8,128)(2,1)}, bf16[2,64,1024]{2,1,0:T(8,128)(2,1)}, bf16[2,6...) custom-call(bf16[8,64,1024]{2,1,0:T(8,128)(2,1)S(1)} %get-tuple-elem, ...), custom_call_target="tpu_custom_call", output_to_operand_aliasing={{0}: (7, {}), {2}: (8, {}), {3}: (9, {}), {4}: (10, {}), {5... | custom-call | tf_op jit(solution)/shard_map/border_rows/pallas_call | solution.py:30
  19.5 1.5 %collective-permute-start.4 = (bf16[2,64,1024]{2,1,0:T(8,128)(2,1)}, bf16[2,64,1024]{2,1,0:T(8,128)(2,1)S(1)}, u32[]{:S(2)}, u32[]{:S(2)}) collective-permute-start(bf16[2,64,1024]{2,1,0:T(8,128)(2,1)} %get-tuple-element.61), channel_id=1, source_target_pairs={{0,128},{32,160},{64,192},{96,224},{128,0},{160,32},{192,64},{224,... | collective-permute-start | bytes 786440 | tf_op jit(solution)/shard_map/ppermute | solution.py:437
  20.9 2.1 %collective-permute-start.2 = (bf16[2,64,1024]{2,1,0:T(8,128)(2,1)}, bf16[2,64,1024]{2,1,0:T(8,128)(2,1)S(1)}, u32[]{:S(2)}, u32[]{:S(2)}) collective-permute-start(bf16[2,64,1024]{2,1,0:T(8,128)(2,1)} %get-tuple-element.59), channel_id=1, source_target_pairs={{0,64},{32,96},{64,128},{96,160},{128,192},{160,224},{192,0},{224,... | collective-permute-start | bytes 786440 | tf_op jit(solution)/shard_map/ppermute | solution.py:437
  23.2 0.6 gather_fusion
  23.9 3.5 %collective-permute-done.6.two = f32[1,128]{1,0:T(1,128)S(1)} collective-permute-done((f32[1,128]{1,0:T(1,128)S(1)}, f32[1,128]{1,0:T(1,128)S(1)}, u32[]{:S(2)}, u32[]{:S(2)}) %collective-permute-start.6) | collective-permute-done | bytes 544 | tf_op jit(solution)/shard_map/ppermute | solution.py:437
  27.4 0.6 add_and_spread.2
  28.0 6.0 %all-to-all-start = ((f32[16,1,128]{2,1,0:T(1,128)}), f32[16,1,128]{2,1,0:T(1,128)S(1)}, u32[]{:S(2)}, u32[]{:S(2)}) async-start(f32[16,1,128]{2,1,0:T(1,128)} %add_and_spread.2), calls=%async_computation | async-start | bytes 16384 | tf_op jit(solution)/shard_map/all_to_all | solution.py:518
  34.0 0.4 collective-permute-done.3.refs_2_
  34.4 0.9 pad_maximum_fusion.1
  35.3 1.0 subtract_convert_fusion
  36.2 1.5 %stage.1.smooth = f32[8,64,1024]{2,1,0:T(8,128)S(1)} custom-call(f32[8,64,1024]{2,1,0:T(8,128)} %get-tuple-element.64.source), custom_call_target="tpu_custom_call" | custom-call | tf_op jit(solution)/shard_map/stage/pallas_call | solution.py:30
  37.8 6.0 %all-to-all-done.sums = f32[16,1,128]{2,1,0:T(1,128)S(1)} async-done(((f32[16,1,128]{2,1,0:T(1,128)}), f32[16,1,128]{2,1,0:T(1,128)S(1)}, u32[]{:S(2)}, u32[]{:S(2)}) %all-to-all-start) | async-done | bytes 8224 | tf_op jit(solution)/shard_map/all_to_all | solution.py:518
  43.8 0.8 copy-done.2
  44.5 0.5 correction.1
  45.2 2.4 %collective-permute-start.11 = (bf16[64,1024]{1,0:T(8,128)(2,1)S(1)}, bf16[64,1024]{1,0:T(8,128)(2,1)S(1)}, u32[]{:S(2)}, u32[]{:S(2)}) collective-permute-start(bf16[64,1024]{1,0:T(8,128)(2,1)S(1)} %get-tuple-element.72), channel_id=1, source_target_pairs={{0,96},{32,64},{64,160},{96,128},{128,224},{160,192},{192,32},{224... | collective-permute-start | bytes 393224 | tf_op jit(solution)/shard_map/ppermute | solution.py:437
  47.5 1.5 %collective-permute-start.12 = (bf16[64,1024]{1,0:T(8,128)(2,1)S(1)}, bf16[64,1024]{1,0:T(8,128)(2,1)S(1)}, u32[]{:S(2)}, u32[]{:S(2)}) collective-permute-start(bf16[64,1024]{1,0:T(8,128)(2,1)S(1)} %get-tuple-element.73), channel_id=1, source_target_pairs={{0,224},{32,192},{64,32},{96,0},{128,96},{160,64},{192,160},{224,1... | collective-permute-start | bytes 393224 | tf_op jit(solution)/shard_map/ppermute | solution.py:437
  49.3 2.2 %collective-permute-done.10.refs_9_ = bf16[64,1024]{1,0:T(8,128)(2,1)S(1)} collective-permute-done((bf16[64,1024]{1,0:T(8,128)(2,1)S(1)}, bf16[64,1024]{1,0:T(8,128)(2,1)S(1)}, u32[]{:S(2)}, u32[]{:S(2)}) %collective-permute-start.10) | collective-permute-done | bytes 131104 | tf_op jit(solution)/shard_map/ppermute | solution.py:437
  51.5 3.9 %collective-permute-start.7 = (bf16[64,1024]{1,0:T(8,128)(2,1)S(1)}, bf16[64,1024]{1,0:T(8,128)(2,1)S(1)}, u32[]{:S(2)}, u32[]{:S(2)}) collective-permute-start(bf16[64,1024]{1,0:T(8,128)(2,1)S(1)} %get-tuple-element.68), channel_id=1, source_target_pairs={{0,64},{32,96},{64,128},{96,160},{128,192},{160,224},{192,0},{224,... | collective-permute-start | bytes 393224 | tf_op jit(solution)/shard_map/ppermute | solution.py:437
  55.4 2.6 %collective-permute-start.9 = (bf16[64,1024]{1,0:T(8,128)(2,1)S(1)}, bf16[64,1024]{1,0:T(8,128)(2,1)S(1)}, u32[]{:S(2)}, u32[]{:S(2)}) collective-permute-start(bf16[64,1024]{1,0:T(8,128)(2,1)S(1)} %get-tuple-element.70), channel_id=1, source_target_pairs={{0,128},{32,160},{64,192},{96,224},{128,0},{160,32},{192,64},{224,... | collective-permute-start | bytes 393224 | tf_op jit(solution)/shard_map/ppermute | solution.py:437
  58.0 0.5 slice_bitcast_fusion
  58.5 0.8 collective-permute-done.7.refs_6_
  59.3 5.0 %collective-permute-done.8.refs_7_ = bf16[64,1024]{1,0:T(8,128)(2,1)S(1)} collective-permute-done((bf16[64,1024]{1,0:T(8,128)(2,1)S(1)}, bf16[64,1024]{1,0:T(8,128)(2,1)S(1)}, u32[]{:S(2)}, u32[]{:S(2)}) %collective-permute-start.8) | collective-permute-done | bytes 131104 | tf_op jit(solution)/shard_map/ppermute | solution.py:437
  64.3 1.8 %right_side.1 = (f32[304,1024]{1,0:T(8,128)S(1)}, bf16[512,1024]{1,0:T(8,128)(2,1)S(1)}, bf16[304,128]{1,0:T(8,128)(2,1)S(1)}, bf16[16,304]{1,0:T(8,128)(2,1)S(1)}, bf16[304,128]{1,0:T(8,128)(2,1)S(1)}) custom-call(bf16[64,1024]{1,0:T(8,128)(2,1)S(1)} %copy-done, bf16[2,64,1024]{2,1,0:T(8,128)(2,1)S(1)} %collective-permute-done.2.refs_1_, ...), custom_call_target="tpu_custom_call" | custom-call | tf_op jit(solution)/shard_map/right_side/pallas_call | solution.py:30
  66.1 1.7 %collective-permute-start.17 = (bf16[16,304]{1,0:T(8,128)(2,1)S(1)}, bf16[16,304]{1,0:T(8,128)(2,1)S(1)}, u32[]{:S(2)}, u32[]{:S(2)}) collective-permute-start(bf16[16,304]{1,0:T(8,128)(2,1)S(1)} %get-tuple-element.80), channel_id=1, source_target_pairs={{0,224},{32,0},{64,32},{96,64},{128,96},{160,128},{192,160},{224,1... | collective-permute-start | bytes 29192 | tf_op jit(solution)/shard_map/ppermute | solution.py:437
  67.9 2.0 %collective-permute-start.14 = (bf16[304,128]{1,0:T(8,128)(2,1)S(1)}, bf16[304,128]{1,0:T(8,128)(2,1)S(1)}, u32[]{:S(2)}, u32[]{:S(2)}) collective-permute-start(bf16[304,128]{1,0:T(8,128)(2,1)S(1)} %get-tuple-element.78), channel_id=1, source_target_pairs={{0,1},{1,2},{2,3},{3,4},{4,5},{5,6},{6,7},{7,8},{8,9},{9,10},{10,1... | collective-permute-start | bytes 233480 | tf_op jit(solution)/shard_map/ppermute | solution.py:437
  69.9 3.3 %collective-permute-start.15 = (bf16[304,128]{1,0:T(8,128)(2,1)S(1)}, bf16[304,128]{1,0:T(8,128)(2,1)S(1)}, u32[]{:S(2)}, u32[]{:S(2)}) collective-permute-start(bf16[304,128]{1,0:T(8,128)(2,1)S(1)} %get-tuple-element.79), channel_id=1, source_target_pairs={{0,31},{1,0},{2,1},{3,2},{4,3},{5,4},{6,5},{7,6},{8,7},{9,8},{10,9... | collective-permute-start | bytes 233480 | tf_op jit(solution)/shard_map/ppermute | solution.py:437
  73.5 3.4 %apply0.1 = (f32[304,1024]{1,0:T(8,128)S(1)}, f32[3,8,128]{2,1,0:T(8,128)S(1)}) custom-call(f32[304,1024]{1,0:T(8,128)S(1)} %get-tuple-element.75.refs_0_.refs_4_.rest_0_.zero, bf16[512,1024]{1,0:T(8,128)(2,1)S(1)} %get-tuple-element.76.refs_1_, bf16[512,608]{1,0:T(8,128)(2,1)S(1)} %pad_maximum_fusion.refs_2_, ...), custom_call_target="tpu_custom_call" | custom-call | tf_op jit(solution)/shard_map/apply0/pallas_call | solution.py:30
  76.9 0.7 add_halo1.1
  77.6 5.4 %collective-permute-start.19 = (bf16[304,128]{1,0:T(8,128)(2,1)S(1)}, bf16[304,128]{1,0:T(8,128)(2,1)S(1)}, u32[]{:S(2)}, u32[]{:S(2)}) collective-permute-start(bf16[304,128]{1,0:T(8,128)(2,1)S(1)} %get-tuple-element.84), channel_id=1, source_target_pairs={{0,31},{1,0},{2,1},{3,2},{4,3},{5,4},{6,5},{7,6},{8,7},{9,8},{10,9... | collective-permute-start | bytes 233480 | tf_op jit(solution)/shard_map/ppermute | solution.py:437
  83.0 1.7 %collective-permute-start.21 = (bf16[16,304]{1,0:T(8,128)(2,1)S(1)}, bf16[16,304]{1,0:T(8,128)(2,1)S(1)}, u32[]{:S(2)}, u32[]{:S(2)}) collective-permute-start(bf16[16,304]{1,0:T(8,128)(2,1)S(1)} %get-tuple-element.85), channel_id=1, source_target_pairs={{0,224},{32,0},{64,32},{96,64},{128,96},{160,128},{192,160},{224,1... | collective-permute-start | bytes 29192 | tf_op jit(solution)/shard_map/ppermute | solution.py:437
  84.7 3.4 %apply1.1 = (f32[304,1024]{1,0:T(8,128)S(1)}, f32[3,8,128]{2,1,0:T(8,128)S(1)}) custom-call(f32[304,1024]{1,0:T(8,128)S(1)} %get-tuple-element.81.refs_0_.refs_4_.one, bf16[512,1024]{1,0:T(8,128)(2,1)S(1)} %get-tuple-element.76.refs_1_, bf16[512,608]{1,0:T(8,128)(2,1)S(1)} %pad_maximum_fusion.refs_2_, ...), custom_call_target="tpu_custom_call" | custom-call | tf_op jit(solution)/shard_map/apply1/pallas_call | solution.py:30
  88.2 0.7 add_halo2.1
  89.1 1.3 %collective-permute-start.23 = (bf16[16,304]{1,0:T(8,128)(2,1)S(1)}, bf16[16,304]{1,0:T(8,128)(2,1)S(1)}, u32[]{:S(2)}, u32[]{:S(2)}) collective-permute-start(bf16[16,304]{1,0:T(8,128)(2,1)S(1)} %get-tuple-element.88), channel_id=1, source_target_pairs={{0,32},{32,64},{64,96},{96,128},{128,160},{160,192},{192,224},{224... | collective-permute-start | bytes 29192 | tf_op jit(solution)/shard_map/ppermute | solution.py:437
  90.4 3.5 %apply2.1.two = f32[3,8,128]{2,1,0:T(8,128)S(1)} custom-call(f32[304,1024]{1,0:T(8,128)S(1)} %get-tuple-element.86.refs_0_.field.two, bf16[512,1024]{1,0:T(8,128)(2,1)S(1)} %get-tuple-element.76.refs_1_, bf16[512,608]{1,0:T(8,128)(2,1)S(1)} %pad_maximum_fusion.refs_2_, bf16[304,512]{1,0:T(8,128)(2,1)S(1)} %subtract_convert_fusion.1.refs_13_.refs_3_, ...), custom_call_target="tpu_custom_call" | custom-call | tf_op jit(solution)/shard_map/apply2/pallas_call | solution.py:30
  93.9 3.5 %collective-permute-done.22.above = bf16[304,128]{1,0:T(8,128)(2,1)S(1)} collective-permute-done((bf16[304,128]{1,0:T(8,128)(2,1)S(1)}, bf16[304,128]{1,0:T(8,128)(2,1)S(1)}, u32[]{:S(2)}, u32[]{:S(2)}) %collective-permute-start.22) | collective-permute-done | bytes 77856 | tf_op jit(solution)/shard_map/ppermute | solution.py:437
  97.4 0.6 all_moments.1
  98.1 1.0 collective-permute-done.24
  99.1 3.5 %collective-permute-done.25 = f32[1,128]{1,0:T(1,128)S(1)} collective-permute-done((f32[1,128]{1,0:T(1,128)S(1)}, f32[1,128]{1,0:T(1,128)S(1)}, u32[]{:S(2)}, u32[]{:S(2)}) %collective-permute-start.25) | collective-permute-done | bytes 544 | tf_op jit(solution)/shard_map/ppermute | solution.py:437
  102.6 2.1 %collective-permute-start.26 = (f32[1,128]{1,0:T(1,128)S(1)}, f32[1,128]{1,0:T(1,128)S(1)}, u32[]{:S(2)}, u32[]{:S(2)}) collective-permute-start(f32[1,128]{1,0:T(1,128)S(1)} %add.73), channel_id=1, source_target_pairs={{0,128},{32,160},{64,192},{96,224},{128,0},{160,32},{192,64},{224,... | collective-permute-start | bytes 1544 | tf_op jit(solution)/shard_map/ppermute | solution.py:437
  104.8 2.9 %collective-permute-done.26 = f32[1,128]{1,0:T(1,128)S(1)} collective-permute-done((f32[1,128]{1,0:T(1,128)S(1)}, f32[1,128]{1,0:T(1,128)S(1)}, u32[]{:S(2)}, u32[]{:S(2)}) %collective-permute-start.26) | collective-permute-done | bytes 544 | tf_op jit(solution)/shard_map/ppermute | solution.py:437
  107.7 3.5 %collective-permute-done.27.two = f32[1,128]{1,0:T(1,128)S(1)} collective-permute-done((f32[1,128]{1,0:T(1,128)S(1)}, f32[1,128]{1,0:T(1,128)S(1)}, u32[]{:S(2)}, u32[]{:S(2)}) %collective-permute-start.27) | collective-permute-done | bytes 544 | tf_op jit(solution)/shard_map/ppermute | solution.py:437
  111.2 14.2 %all_to_all.10.parts = f32[16,1,128]{2,1,0:T(1,128)S(1)} all-to-all(f32[16,1,128]{2,1,0:T(1,128)S(1)} %add_and_spread.3), channel_id=1, replica_groups={{0,2,4,6,8,10,12,14,16,18,20,22,24,26,28,30},{1,3,5,7,9,11,13,15,17,19,..., dimensions={0} | all-to-all | bytes 16384 | tf_op jit(solution)/shard_map/all_to_all | solution.py:518
  125.4 1.3 %combine.1 = f32[2400,128]{1,0:T(8,128)} custom-call(f32[16,1,128]{2,1,0:T(1,128)S(1)} %all_to_all.10.parts, f32[304,1024]{1,0:T(8,128)S(1)} %get-tuple-element.75.refs_0_.refs_4_.rest_0_.zero, f32[304,1024]{1,0:T(8,128)S(1)} %get-tuple-element.81.refs_0_.refs_4_.one, f32[304,1024]{1,0:T(8,128)S(1)} %get-tuple-element.86.refs_0_.field.two), custom_call_target="tpu_custom_call" | custom-call | tf_op jit(solution)/shard_map/combine/pallas_call | solution.py:30
  (62 shorter events, 1.6 us)
Async XLA Ops:
  0.6 10.7 %copy-start.5 = (s32[64,8]{0,1:T(8,128)S(1)}, s32[64,8]{0,1:T(8,128)}, u32[]{:S(2)}) copy-start(s32[64,8]{0,1:T(8,128)} %param.8) | copy-start | bytes 6148
  0.6 10.7 %copy-start.1 = (f32[8,1024]{1,0:T(8,128)S(1)}, f32[8,1024]{1,0:T(8,128)}, u32[]{:S(2)}) copy-start(f32[8,1024]{1,0:T(8,128)} %height.5) | copy-start | bytes 98308
  2.8 14.7 %collective-permute-start = (bf16[128,1024]{1,0:T(8,128)(2,1)S(1)}, bf16[128,1024]{1,0:T(8,128)(2,1)S(1)}, u32[]{:S(2)}, u32[]{:S(2)}) collective-permute-start(bf16[128,1024]{1,0:T(8,128)(2,1)S(1)} %get-tuple-element.49), channel_id=1, source_target_pairs={{0,1},{1,2},{2,3},{3,4},{4,5},{5,6},{6,7},{7,8},{8,9},{9,10},{10,1... | collective-permute-start | bytes 786440 | tf_op jit(solution)/shard_map/ppermute | solution.py:437
  4.8 12.7 %collective-permute-start.1 = (bf16[128,1024]{1,0:T(8,128)(2,1)S(1)}, bf16[128,1024]{1,0:T(8,128)(2,1)S(1)}, u32[]{:S(2)}, u32[]{:S(2)}) collective-permute-start(bf16[128,1024]{1,0:T(8,128)(2,1)S(1)} %get-tuple-element.50), channel_id=1, source_target_pairs={{0,31},{1,0},{2,1},{3,2},{4,3},{5,4},{6,5},{7,6},{8,7},{9,8},{10,9... | collective-permute-start | bytes 786440 | tf_op jit(solution)/shard_map/ppermute | solution.py:437
  17.5 5.6 %copy-start.6 = (s32[512,2]{0,1:T(2,128)S(1)}, s32[512,2]{0,1:T(2,128)}, u32[]{:S(2)}) copy-start(s32[512,2]{0,1:T(2,128)} %param.9) | copy-start | bytes 12292
  19.4 14.9 %copy-start.4 = (bf16[64,1024]{1,0:T(8,128)(2,1)S(1)}, bf16[64,1024]{1,0:T(8,128)(2,1)}, u32[]{:S(2)}) copy-start(bf16[64,1024]{1,0:T(8,128)(2,1)} %get-tuple-element.62) | copy-start | bytes 393220
  19.5 14.5 %collective-permute-start.4 = (bf16[2,64,1024]{2,1,0:T(8,128)(2,1)}, bf16[2,64,1024]{2,1,0:T(8,128)(2,1)S(1)}, u32[]{:S(2)}, u32[]{:S(2)}) collective-permute-start(bf16[2,64,1024]{2,1,0:T(8,128)(2,1)} %get-tuple-element.61), channel_id=1, source_target_pairs={{0,128},{32,160},{64,192},{96,224},{128,0},{160,32},{192,64},{224,... | collective-permute-start | bytes 786440 | tf_op jit(solution)/shard_map/ppermute | solution.py:437
  20.9 13.0 %collective-permute-start.2 = (bf16[2,64,1024]{2,1,0:T(8,128)(2,1)}, bf16[2,64,1024]{2,1,0:T(8,128)(2,1)S(1)}, u32[]{:S(2)}, u32[]{:S(2)}) collective-permute-start(bf16[2,64,1024]{2,1,0:T(8,128)(2,1)} %get-tuple-element.59), channel_id=1, source_target_pairs={{0,64},{32,96},{64,128},{96,160},{128,192},{160,224},{192,0},{224,... | collective-permute-start | bytes 786440 | tf_op jit(solution)/shard_map/ppermute | solution.py:437
  23.0 11.3 %collective-permute-start.3 = (bf16[2,64,1024]{2,1,0:T(8,128)(2,1)}, bf16[2,64,1024]{2,1,0:T(8,128)(2,1)S(1)}, u32[]{:S(2)}, u32[]{:S(2)}) collective-permute-start(bf16[2,64,1024]{2,1,0:T(8,128)(2,1)} %get-tuple-element.60), channel_id=1, source_target_pairs={{0,192},{32,224},{64,0},{96,32},{128,64},{160,96},{192,128},{224,1... | collective-permute-start | bytes 786440 | tf_op jit(solution)/shard_map/ppermute | solution.py:437
  23.8 3.6 %collective-permute-start.6 = (f32[1,128]{1,0:T(1,128)S(1)}, f32[1,128]{1,0:T(1,128)S(1)}, u32[]{:S(2)}, u32[]{:S(2)}) collective-permute-start(f32[1,128]{1,0:T(1,128)S(1)} %get-tuple-element.63.one), channel_id=1, source_target_pairs={{0,1},{1,0},{2,3},{3,2},{4,5},{5,4},{6,7},{7,6},{8,9},{9,8},{10,11... | collective-permute-start | bytes 1544 | tf_op jit(solution)/shard_map/ppermute | solution.py:437
  28.0 15.8 %all-to-all-start = ((f32[16,1,128]{2,1,0:T(1,128)}), f32[16,1,128]{2,1,0:T(1,128)S(1)}, u32[]{:S(2)}, u32[]{:S(2)}) async-start(f32[16,1,128]{2,1,0:T(1,128)} %add_and_spread.2), calls=%async_computation | async-start | bytes 16384 | tf_op jit(solution)/shard_map/all_to_all | solution.py:518
  35.3 29.1 %collective-permute-start.5 = (bf16[4,64,1024]{2,1,0:T(8,128)(2,1)}, bf16[4,64,1024]{2,1,0:T(8,128)(2,1)S(1)}, u32[]{:S(2)}, u32[]{:S(2)}) collective-permute-start(bf16[4,64,1024]{2,1,0:T(8,128)(2,1)} %pad_maximum_fusion.1), channel_id=1, source_target_pairs={{0,32},{32,0},{64,96},{96,64},{128,160},{160,128},{192,224},{224,1... | collective-permute-start | bytes 1572872 | tf_op jit(solution)/shard_map/ppermute | solution.py:437
  37.8 26.5 %copy-start = (bf16[64,1024]{1,0:T(8,128)(2,1)S(1)}, bf16[64,1024]{1,0:T(8,128)(2,1)}, u32[]{:S(2)}) copy-start(bf16[64,1024]{1,0:T(8,128)(2,1)} %get-tuple-element.58.refs_0_) | copy-start | bytes 393220
  43.8 0.8 copy-start.2
  45.1 6.5 %collective-permute-start.10 = (bf16[64,1024]{1,0:T(8,128)(2,1)S(1)}, bf16[64,1024]{1,0:T(8,128)(2,1)S(1)}, u32[]{:S(2)}, u32[]{:S(2)}) collective-permute-start(bf16[64,1024]{1,0:T(8,128)(2,1)S(1)} %get-tuple-element.71), channel_id=1, source_target_pairs={{0,160},{32,128},{64,224},{96,192},{128,32},{160,0},{192,96},{224,... | collective-permute-start | bytes 393224 | tf_op jit(solution)/shard_map/ppermute | solution.py:437
  45.2 10.2 %collective-permute-start.11 = (bf16[64,1024]{1,0:T(8,128)(2,1)S(1)}, bf16[64,1024]{1,0:T(8,128)(2,1)S(1)}, u32[]{:S(2)}, u32[]{:S(2)}) collective-permute-start(bf16[64,1024]{1,0:T(8,128)(2,1)S(1)} %get-tuple-element.72), channel_id=1, source_target_pairs={{0,96},{32,64},{64,160},{96,128},{128,224},{160,192},{192,32},{224... | collective-permute-start | bytes 393224 | tf_op jit(solution)/shard_map/ppermute | solution.py:437
  47.5 7.9 %collective-permute-start.12 = (bf16[64,1024]{1,0:T(8,128)(2,1)S(1)}, bf16[64,1024]{1,0:T(8,128)(2,1)S(1)}, u32[]{:S(2)}, u32[]{:S(2)}) collective-permute-start(bf16[64,1024]{1,0:T(8,128)(2,1)S(1)} %get-tuple-element.73), channel_id=1, source_target_pairs={{0,224},{32,192},{64,32},{96,0},{128,96},{160,64},{192,160},{224,1... | collective-permute-start | bytes 393224 | tf_op jit(solution)/shard_map/ppermute | solution.py:437
  49.1 9.4 %collective-permute-start.13 = (bf16[64,1024]{1,0:T(8,128)(2,1)S(1)}, bf16[64,1024]{1,0:T(8,128)(2,1)S(1)}, u32[]{:S(2)}, u32[]{:S(2)}) collective-permute-start(bf16[64,1024]{1,0:T(8,128)(2,1)S(1)} %get-tuple-element.74), channel_id=1, source_target_pairs={{0,32},{32,0},{64,96},{96,64},{128,160},{160,128},{192,224},{224,1... | collective-permute-start | bytes 393224 | tf_op jit(solution)/shard_map/ppermute | solution.py:437
  51.5 7.8 %collective-permute-start.7 = (bf16[64,1024]{1,0:T(8,128)(2,1)S(1)}, bf16[64,1024]{1,0:T(8,128)(2,1)S(1)}, u32[]{:S(2)}, u32[]{:S(2)}) collective-permute-start(bf16[64,1024]{1,0:T(8,128)(2,1)S(1)} %get-tuple-element.68), channel_id=1, source_target_pairs={{0,64},{32,96},{64,128},{96,160},{128,192},{160,224},{192,0},{224,... | collective-permute-start | bytes 393224 | tf_op jit(solution)/shard_map/ppermute | solution.py:437
  55.4 8.9 %collective-permute-start.8 = (bf16[64,1024]{1,0:T(8,128)(2,1)S(1)}, bf16[64,1024]{1,0:T(8,128)(2,1)S(1)}, u32[]{:S(2)}, u32[]{:S(2)}) collective-permute-start(bf16[64,1024]{1,0:T(8,128)(2,1)S(1)} %get-tuple-element.69), channel_id=1, source_target_pairs={{0,192},{32,224},{64,0},{96,32},{128,64},{160,96},{192,128},{224,1... | collective-permute-start | bytes 393224 | tf_op jit(solution)/shard_map/ppermute | solution.py:437
  55.4 8.9 %collective-permute-start.9 = (bf16[64,1024]{1,0:T(8,128)(2,1)S(1)}, bf16[64,1024]{1,0:T(8,128)(2,1)S(1)}, u32[]{:S(2)}, u32[]{:S(2)}) collective-permute-start(bf16[64,1024]{1,0:T(8,128)(2,1)S(1)} %get-tuple-element.70), channel_id=1, source_target_pairs={{0,128},{32,160},{64,192},{96,224},{128,0},{160,32},{192,64},{224,... | collective-permute-start | bytes 393224 | tf_op jit(solution)/shard_map/ppermute | solution.py:437
  64.3 8.9 %copy-start.3 = (bf16[512,304]{1,0:T(8,128)(2,1)S(1)}, bf16[512,304]{1,0:T(8,128)(2,1)}, u32[]{:S(2)}) copy-start(bf16[512,304]{1,0:T(8,128)(2,1)} %subtract_convert_fusion) | copy-start | bytes 933892
  66.1 10.8 %collective-permute-start.16 = (bf16[16,304]{1,0:T(8,128)(2,1)S(1)}, bf16[16,304]{1,0:T(8,128)(2,1)S(1)}, u32[]{:S(2)}, u32[]{:S(2)}) collective-permute-start(bf16[16,304]{1,0:T(8,128)(2,1)S(1)} %get-tuple-element.80), channel_id=1, source_target_pairs={{0,32},{32,64},{64,96},{96,128},{128,160},{160,192},{192,224},{224... | collective-permute-start | bytes 29192 | tf_op jit(solution)/shard_map/ppermute | solution.py:437
  66.1 10.7 %collective-permute-start.17 = (bf16[16,304]{1,0:T(8,128)(2,1)S(1)}, bf16[16,304]{1,0:T(8,128)(2,1)S(1)}, u32[]{:S(2)}, u32[]{:S(2)}) collective-permute-start(bf16[16,304]{1,0:T(8,128)(2,1)S(1)} %get-tuple-element.80), channel_id=1, source_target_pairs={{0,224},{32,0},{64,32},{96,64},{128,96},{160,128},{192,160},{224,1... | collective-permute-start | bytes 29192 | tf_op jit(solution)/shard_map/ppermute | solution.py:437
  67.9 9.0 %collective-permute-start.14 = (bf16[304,128]{1,0:T(8,128)(2,1)S(1)}, bf16[304,128]{1,0:T(8,128)(2,1)S(1)}, u32[]{:S(2)}, u32[]{:S(2)}) collective-permute-start(bf16[304,128]{1,0:T(8,128)(2,1)S(1)} %get-tuple-element.78), channel_id=1, source_target_pairs={{0,1},{1,2},{2,3},{3,4},{4,5},{5,6},{6,7},{7,8},{8,9},{9,10},{10,1... | collective-permute-start | bytes 233480 | tf_op jit(solution)/shard_map/ppermute | solution.py:437
  69.9 7.0 %collective-permute-start.15 = (bf16[304,128]{1,0:T(8,128)(2,1)S(1)}, bf16[304,128]{1,0:T(8,128)(2,1)S(1)}, u32[]{:S(2)}, u32[]{:S(2)}) collective-permute-start(bf16[304,128]{1,0:T(8,128)(2,1)S(1)} %get-tuple-element.79), channel_id=1, source_target_pairs={{0,31},{1,0},{2,1},{3,2},{4,3},{5,4},{6,5},{7,6},{8,7},{9,8},{10,9... | collective-permute-start | bytes 233480 | tf_op jit(solution)/shard_map/ppermute | solution.py:437
  77.6 10.5 %collective-permute-start.18 = (bf16[304,128]{1,0:T(8,128)(2,1)S(1)}, bf16[304,128]{1,0:T(8,128)(2,1)S(1)}, u32[]{:S(2)}, u32[]{:S(2)}) collective-permute-start(bf16[304,128]{1,0:T(8,128)(2,1)S(1)} %get-tuple-element.83), channel_id=1, source_target_pairs={{0,1},{1,2},{2,3},{3,4},{4,5},{5,6},{6,7},{7,8},{8,9},{9,10},{10,1... | collective-permute-start | bytes 233480 | tf_op jit(solution)/shard_map/ppermute | solution.py:437
  77.6 10.5 %collective-permute-start.19 = (bf16[304,128]{1,0:T(8,128)(2,1)S(1)}, bf16[304,128]{1,0:T(8,128)(2,1)S(1)}, u32[]{:S(2)}, u32[]{:S(2)}) collective-permute-start(bf16[304,128]{1,0:T(8,128)(2,1)S(1)} %get-tuple-element.84), channel_id=1, source_target_pairs={{0,31},{1,0},{2,1},{3,2},{4,3},{5,4},{6,5},{7,6},{8,7},{9,8},{10,9... | collective-permute-start | bytes 233480 | tf_op jit(solution)/shard_map/ppermute | solution.py:437
  83.0 5.2 %collective-permute-start.20 = (bf16[16,304]{1,0:T(8,128)(2,1)S(1)}, bf16[16,304]{1,0:T(8,128)(2,1)S(1)}, u32[]{:S(2)}, u32[]{:S(2)}) collective-permute-start(bf16[16,304]{1,0:T(8,128)(2,1)S(1)} %get-tuple-element.85), channel_id=1, source_target_pairs={{0,32},{32,64},{64,96},{96,128},{128,160},{160,192},{192,224},{224... | collective-permute-start | bytes 29192 | tf_op jit(solution)/shard_map/ppermute | solution.py:437
  83.0 5.2 %collective-permute-start.21 = (bf16[16,304]{1,0:T(8,128)(2,1)S(1)}, bf16[16,304]{1,0:T(8,128)(2,1)S(1)}, u32[]{:S(2)}, u32[]{:S(2)}) collective-permute-start(bf16[16,304]{1,0:T(8,128)(2,1)S(1)} %get-tuple-element.85), channel_id=1, source_target_pairs={{0,224},{32,0},{64,32},{96,64},{128,96},{160,128},{192,160},{224,1... | collective-permute-start | bytes 29192 | tf_op jit(solution)/shard_map/ppermute | solution.py:437
  88.9 8.5 %collective-permute-start.22 = (bf16[304,128]{1,0:T(8,128)(2,1)S(1)}, bf16[304,128]{1,0:T(8,128)(2,1)S(1)}, u32[]{:S(2)}, u32[]{:S(2)}) collective-permute-start(bf16[304,128]{1,0:T(8,128)(2,1)S(1)} %get-tuple-element.87), channel_id=1, source_target_pairs={{0,1},{1,2},{2,3},{3,4},{4,5},{5,6},{6,7},{7,8},{8,9},{9,10},{10,1... | collective-permute-start | bytes 233480 | tf_op jit(solution)/shard_map/ppermute | solution.py:437
  89.1 4.7 %collective-permute-start.23 = (bf16[16,304]{1,0:T(8,128)(2,1)S(1)}, bf16[16,304]{1,0:T(8,128)(2,1)S(1)}, u32[]{:S(2)}, u32[]{:S(2)}) collective-permute-start(bf16[16,304]{1,0:T(8,128)(2,1)S(1)} %get-tuple-element.88), channel_id=1, source_target_pairs={{0,32},{32,64},{64,96},{96,128},{128,160},{160,192},{192,224},{224... | collective-permute-start | bytes 29192 | tf_op jit(solution)/shard_map/ppermute | solution.py:437
  98.0 1.1 collective-permute-start.24
  99.1 3.5 %collective-permute-start.25 = (f32[1,128]{1,0:T(1,128)S(1)}, f32[1,128]{1,0:T(1,128)S(1)}, u32[]{:S(2)}, u32[]{:S(2)}) collective-permute-start(f32[1,128]{1,0:T(1,128)S(1)} %add.72), channel_id=1, source_target_pairs={{0,64},{32,96},{64,0},{96,32},{128,192},{160,224},{192,128},{224,1... | collective-permute-start | bytes 1544 | tf_op jit(solution)/shard_map/ppermute | solution.py:437
  102.6 5.0 %collective-permute-start.26 = (f32[1,128]{1,0:T(1,128)S(1)}, f32[1,128]{1,0:T(1,128)S(1)}, u32[]{:S(2)}, u32[]{:S(2)}) collective-permute-start(f32[1,128]{1,0:T(1,128)S(1)} %add.73), channel_id=1, source_target_pairs={{0,128},{32,160},{64,192},{96,224},{128,0},{160,32},{192,64},{224,... | collective-permute-start | bytes 1544 | tf_op jit(solution)/shard_map/ppermute | solution.py:437
  107.7 3.5 %collective-permute-start.27 = (f32[1,128]{1,0:T(1,128)S(1)}, f32[1,128]{1,0:T(1,128)S(1)}, u32[]{:S(2)}, u32[]{:S(2)}) collective-permute-start(f32[1,128]{1,0:T(1,128)S(1)} %add.74.one), channel_id=1, source_target_pairs={{0,1},{1,0},{2,3},{3,2},{4,5},{5,4},{6,7},{7,6},{8,9},{9,8},{10,11... | collective-permute-start | bytes 1544 | tf_op jit(solution)/shard_map/ppermute | solution.py:437

commit v8 on v6

--- a/solution.py
+++ b/solution.py
@@ -89,7 +89,7 @@
     return total
 
 
-OFFSETS = ((0, 0), (1, 0), (3, 0), (2, 0), (2, 1), (1, 1), (3, 1), (0, 1))
+OFFSETS = ((0, 0), (0, 1), (2, 0), (2, 1), (1, 0), (1, 1), (3, 0), (3, 1))
 
 
 def other(index, chips, core):
@@ -242,8 +242,9 @@
     return (pixel == wanted).astype(BF16)
 
 
-def write_edges(field, first, last, columns):
-    first[...] = field[:, pl.ds(0, 128)].astype(BF16)
+def write_edges(field, last, columns, first=None):
+    if first is not None:
+        first[...] = field[:, pl.ds(0, 128)].astype(BF16)
     last[...] = field[:, pl.ds(896, 128)].astype(BF16)
     picked = lax.dot_general(
         column_selector(), field[...].astype(BF16), (((1,), (1,)), ((), ())), preferred_element_type=F32
@@ -253,7 +254,7 @@
 
 def right_side(*refs):
     weight_parts, corrected_parts = refs[:8], refs[8:16]
-    design_t, field, weights, first, last, columns = refs[16:]
+    design_t, field, weights, *edges = refs[16:]
     for part in range(8):
         weights[pl.ds(part * 64, 64), :] = weight_parts[part][...]
 
@@ -271,7 +272,7 @@
         return 0
 
     lax.fori_loop(0, 4, one_chunk, 0)
-    write_edges(field, first, last, columns)
+    write_edges(field, *edges)
 
 
 def row_lanes(row):
@@ -349,7 +350,7 @@
     return row > 0, row < lax.axis_size("rows") - 1, col > 0, col < lax.axis_size("ifg") - 1
 
 
-def add_halo(image, above, below, left, right, field, first, last, columns):
+def add_halo(image, above, below, left, right, field, *edges):
     flags = inside()
     sides = jnp.concatenate([keep(flags[2], left[8:16, :]), keep(flags[3], right[0:8, :])], axis=0).astype(BF16)
     for row in range(8):
@@ -360,7 +361,7 @@
         if row == 7:
             halo += keep(flags[1], below[...])
         field[:, lanes] = image[:, lanes] - SMOOTHING_WEIGHT * halo
-    write_edges(field, first, last, columns)
+    write_edges(field, *edges)
 
 
 def all_moments(field, above, left, zero, one, two, out):
@@ -498,8 +499,9 @@
         ]
 
     weight_parts = exchange(weight_parts)
-    sums, weight_parts[7] = lax.optimization_barrier((sums, weight_parts[7]))
+    sums, weight_parts[1] = lax.optimization_barrier((sums, weight_parts[1]))
     sums = lax.all_to_all(sums, "rows", 0, 0, tiled=True)
+    sums, *weight_parts[2:5] = lax.optimization_barrier((sums, *weight_parts[2:5]))
     smooth = call(
         stage,
         sds((8, 64, 1024), F32),
@@ -527,9 +529,9 @@
     design = jnp.concatenate([design, design], axis=1)
 
     field = sds((DP, 1024), F32)
-    edges = (sds((DP, 128), BF16), sds((DP, 128), BF16), sds((16, DP), BF16))
+    edges = (sds((DP, 128), BF16), sds((16, DP), BF16), sds((DP, 128), BF16))
     moments = sds((3, 8, 128), F32)
-    k0, weights, first, last, columns = call(
+    k0, weights, *sides = call(
         right_side,
         (field, sds((512, 1024), BF16)) + edges,
         *weight_parts,
@@ -538,7 +540,7 @@
         name="right_side",
     )
 
-    def halos(first, last, columns):
+    def halos(last, columns, first):
         return (
             forward(last, "rows"),
             backward(first, "rows"),
@@ -551,15 +553,15 @@
         body = lambda *refs: apply_local(with_before, with_image, *refs)
         return call(body, outs, *args, name=name)
 
-    def joined(image, around, name):
-        return call(add_halo, (field,) + edges, image, *around, name=name)
-
-    around = halos(first, last, columns)
+    def joined(image, around, count, name):
+        return call(add_halo, (field,) + edges[:count], image, *around, name=name)
+
+    around = halos(*sides)
     image, mom0 = local(False, True, "apply0", k0, weights, design, design_t)
-    k1, first, last, columns = joined(image, around, "add_halo1")
-    around = halos(first, last, columns)
+    k1, *sides = joined(image, around, 3, "add_halo1")
+    around = halos(*sides)
     image, mom1 = local(True, True, "apply1", k1, weights, design, design_t, k0)
-    k2, first, last, columns = joined(image, around, "add_halo2")
+    k2, last, columns = joined(image, around, 2, "add_halo2")
     above, left = forward(last, "rows"), forward(columns, "ifg")
     (mom2,) = local(True, False, "apply2", k2, weights, design, design_t, k1)
     part = call(

time: 120 us -> 118 us (0.983)
  transfers between devices with their start and end apart: 30 -> 30, of which waited for: 11 -> 9; matrix products, arithmetic and copies ran while one was open for 2% -> 2% of each run, Pallas kernels for 13% -> 13%
where the time goes in v8:
time: 118 us
  starting transfers between devices  50.1 us (42%)
  Pallas kernels  25.5 us (22%)
  waiting for transfers between devices  24.2 us (21%)
  blocking collectives  14.4 us (12%)
  local copies, waits for them, and re-layouts  1.47 us (1%)
  other arithmetic  1.4 us (1%)
    ppermute x29, starting transfers between devices, permute(): lax.ppermute(values, axis, [(i, target(i)) for i in range(lax.axis_size(a...  43.2 us
    pallas_call x14, Pallas kernels, call(): pl.pallas_call(body, out_shape=outs, in_specs=[pl.BlockSpec(memory_space=...  25.5 us
    ppermute x29, waiting for transfers between devices, permute(): lax.ppermute(values, axis, [(i, target(i)) for i in range(lax.axis_size(a...  20.1 us
    all_to_all x1, blocking collectives, per_device(): parts = lax.all_to_all(parts, 'rows', 0, 0, tiled=True)  14.4 us
    all_to_all x1, starting transfers between devices, per_device(): sums = lax.all_to_all(sums, 'rows', 0, 0, tiled=True)  6.81 us
    all_to_all x1, waiting for transfers between devices, per_device(): sums = lax.all_to_all(sums, 'rows', 0, 0, tiled=True)  4.09 us
  transfers between devices with their start and end apart: 30, of which 9 were waited for; matrix products, arithmetic and copies ran while one was open for 2% of the time, Pallas kernels for 13%

profile of v8, /device:TPU:6, one launch (start us, length us, event | category | flops | bytes accessed | tf_op | source)
XLA Modules:
  0.0 118.1 jit_solution(867297293527635124)
XLA Ops:
  0.7 2.2 %rows_first.1 = (bf16[8,64,1024]{2,1,0:T(8,128)(2,1)S(1)}, bf16[8,64,1024]{2,1,0:T(8,128)(2,1)S(1)}, bf16[128,1024]{1,0:T(8,128)(2,1)S(1)}, bf16[128,1024]{1,0:T(8,128)(2,1)S(1)}) custom-call(bf16[64,8,1024]{2,1,0:T(8,128)(2,1)} %phase.1, bf16[64,8,1024]{2,1,0:T(8,128)(2,1)} %coher.1), custom_call_target="tpu_custom_call" | custom-call | tf_op jit(solution)/shard_map/rows_first/pallas_call | solution.py:30
  2.8 2.0 %collective-permute-start = (bf16[128,1024]{1,0:T(8,128)(2,1)S(1)}, bf16[128,1024]{1,0:T(8,128)(2,1)S(1)}, u32[]{:S(2)}, u32[]{:S(2)}) collective-permute-start(bf16[128,1024]{1,0:T(8,128)(2,1)S(1)} %get-tuple-element.61), channel_id=1, source_target_pairs={{0,1},{1,2},{2,3},{3,4},{4,5},{5,6},{6,7},{7,8},{8,9},{9,10},{10,1... | collective-permute-start | bytes 786440 | tf_op jit(solution)/shard_map/ppermute | solution.py:429
  4.8 6.5 %collective-permute-start.1 = (bf16[128,1024]{1,0:T(8,128)(2,1)S(1)}, bf16[128,1024]{1,0:T(8,128)(2,1)S(1)}, u32[]{:S(2)}, u32[]{:S(2)}) collective-permute-start(bf16[128,1024]{1,0:T(8,128)(2,1)S(1)} %get-tuple-element.62), channel_id=1, source_target_pairs={{0,31},{1,0},{2,1},{3,2},{4,3},{5,4},{6,5},{7,6},{8,7},{9,8},{10,9... | collective-permute-start | bytes 786440 | tf_op jit(solution)/shard_map/ppermute | solution.py:429
  11.6 0.6 gather_fusion
  12.3 3.3 %inner_rows.1 = (f32[8,64,1024]{2,1,0:T(8,128)}, f32[128,128]{1,0:T(8,128)S(1)}, bf16[64,1024]{1,0:T(8,128)(2,1)}, bf16[64,1024]{1,0:T(8,128)(2,1)}, bf16[64,102...) custom-call(bf16[8,64,1024]{2,1,0:T(8,128)(2,1)S(1)} %get-tuple-elem, ...), custom_call_target="tpu_custom_call" | custom-call | tf_op jit(solution)/shard_map/inner_rows/pallas_call | solution.py:30
  15.6 1.9 %collective-permute-done.above = bf16[128,1024]{1,0:T(8,128)(2,1)S(1)} collective-permute-done((bf16[128,1024]{1,0:T(8,128)(2,1)S(1)}, bf16[128,1024]{1,0:T(8,128)(2,1)S(1)}, u32[]{:S(2)}, u32[]{:S(2)}) %collective-permute-start) | collective-permute-done | bytes 262176 | tf_op jit(solution)/shard_map/ppermute | solution.py:429
  17.5 2.5 %border_rows.1 = (f32[8,64,1024]{2,1,0:T(8,128)}, f32[32,1,128]{2,1,0:T(1,128)}, bf16[64,1024]{1,0:T(8,128)(2,1)}, bf16[64,1024]{1,0:T(8,128)(2,1)}, bf16[64,102...) custom-call(bf16[8,64,1024]{2,1,0:T(8,128)(2,1)S(1)} %get-tuple-elem, ...), custom_call_target="tpu_custom_call", output_to_operand_aliasing={{0}: (7, {}), {2}: (8, {}), {3}: (9, {}), {4}: (10, {}), {5... | custom-call | tf_op jit(solution)/shard_map/border_rows/pallas_call | solution.py:30
  20.2 1.5 %collective-permute-start.3 = (bf16[64,1024]{1,0:T(8,128)(2,1)}, bf16[64,1024]{1,0:T(8,128)(2,1)S(1)}, u32[]{:S(2)}, u32[]{:S(2)}) collective-permute-start(bf16[64,1024]{1,0:T(8,128)(2,1)} %get-tuple-element.78), channel_id=1, source_target_pairs={{0,128},{32,160},{64,192},{96,224},{128,0},{160,32},{192,64},{224,... | collective-permute-start | bytes 393224 | tf_op jit(solution)/shard_map/ppermute | solution.py:429
  21.7 1.9 %collective-permute-start.4 = (bf16[64,1024]{1,0:T(8,128)(2,1)}, bf16[64,1024]{1,0:T(8,128)(2,1)S(1)}, u32[]{:S(2)}, u32[]{:S(2)}) collective-permute-start(bf16[64,1024]{1,0:T(8,128)(2,1)} %get-tuple-element.79), channel_id=1, source_target_pairs={{0,160},{32,128},{64,224},{96,192},{128,32},{160,0},{192,96},{224,... | collective-permute-start | bytes 393224 | tf_op jit(solution)/shard_map/ppermute | solution.py:429
  23.5 0.5 collective-permute-start.5
  24.0 6.8 %all-to-all-start = ((f32[32,1,128]{2,1,0:T(1,128)}), f32[32,1,128]{2,1,0:T(1,128)S(1)}, u32[]{:S(2)}, u32[]{:S(2)}) async-start(f32[32,1,128]{2,1,0:T(1,128)} %get-tuple-element.77), calls=%async_computation | async-start | bytes 32768 | tf_op jit(solution)/shard_map/all_to_all | solution.py:503
  30.9 1.0 subtract_convert_fusion
  31.8 1.6 %stage.1.smooth = f32[8,64,1024]{2,1,0:T(8,128)S(1)} custom-call(f32[8,64,1024]{2,1,0:T(8,128)} %get-tuple-element.88.source), custom_call_target="tpu_custom_call" | custom-call | tf_op jit(solution)/shard_map/stage/pallas_call | solution.py:30
  33.4 1.0 collective-permute-start.6
  34.4 0.8 collective-permute-start.7
  35.2 1.4 %collective-permute-start.8 = (bf16[64,1024]{1,0:T(8,128)(2,1)}, bf16[64,1024]{1,0:T(8,128)(2,1)S(1)}, u32[]{:S(2)}, u32[]{:S(2)}) collective-permute-start(bf16[64,1024]{1,0:T(8,128)(2,1)} %get-tuple-element.86), channel_id=1, source_target_pairs={{0,224},{32,192},{64,32},{96,0},{128,96},{160,64},{192,160},{224,1... | collective-permute-start | bytes 393224 | tf_op jit(solution)/shard_map/ppermute | solution.py:429
  36.5 4.1 %all-to-all-done.sums = f32[32,1,128]{2,1,0:T(1,128)S(1)} async-done(((f32[32,1,128]{2,1,0:T(1,128)}), f32[32,1,128]{2,1,0:T(1,128)S(1)}, u32[]{:S(2)}, u32[]{:S(2)}) %all-to-all-start) | async-done | bytes 16416 | tf_op jit(solution)/shard_map/all_to_all | solution.py:503
  40.6 0.6 correction.1
  41.2 2.5 %collective-permute-start.10 = (bf16[64,1024]{1,0:T(8,128)(2,1)S(1)}, bf16[64,1024]{1,0:T(8,128)(2,1)S(1)}, u32[]{:S(2)}, u32[]{:S(2)}) collective-permute-start(bf16[64,1024]{1,0:T(8,128)(2,1)S(1)} %get-tuple-element.93), channel_id=1, source_target_pairs={{0,128},{32,160},{64,192},{96,224},{128,0},{160,32},{192,64},{224,... | collective-permute-start | bytes 393224 | tf_op jit(solution)/shard_map/ppermute | solution.py:429
  43.9 1.9 %collective-permute-start.12 = (bf16[64,1024]{1,0:T(8,128)(2,1)S(1)}, bf16[64,1024]{1,0:T(8,128)(2,1)S(1)}, u32[]{:S(2)}, u32[]{:S(2)}) collective-permute-start(bf16[64,1024]{1,0:T(8,128)(2,1)S(1)} %get-tuple-element.95), channel_id=1, source_target_pairs={{0,64},{32,96},{64,128},{96,160},{128,192},{160,224},{192,0},{224,... | collective-permute-start | bytes 393224 | tf_op jit(solution)/shard_map/ppermute | solution.py:429
  45.8 1.7 %collective-permute-start.13 = (bf16[64,1024]{1,0:T(8,128)(2,1)S(1)}, bf16[64,1024]{1,0:T(8,128)(2,1)S(1)}, u32[]{:S(2)}, u32[]{:S(2)}) collective-permute-start(bf16[64,1024]{1,0:T(8,128)(2,1)S(1)} %get-tuple-element.96), channel_id=1, source_target_pairs={{0,96},{32,64},{64,160},{96,128},{128,224},{160,192},{192,32},{224... | collective-permute-start | bytes 393224 | tf_op jit(solution)/shard_map/ppermute | solution.py:429
  47.5 0.5 collective-permute-start.14
  48.1 2.5 %collective-permute-done.11.refs_11_ = bf16[64,1024]{1,0:T(8,128)(2,1)S(1)} collective-permute-done((bf16[64,1024]{1,0:T(8,128)(2,1)S(1)}, bf16[64,1024]{1,0:T(8,128)(2,1)S(1)}, u32[]{:S(2)}, u32[]{:S(2)}) %collective-permute-start.11) | collective-permute-done | bytes 131104 | tf_op jit(solution)/shard_map/ppermute | solution.py:429
  50.7 0.5 slice_bitcast_fusion
  51.4 3.6 %collective-permute-done.13.refs_13_ = bf16[64,1024]{1,0:T(8,128)(2,1)S(1)} collective-permute-done((bf16[64,1024]{1,0:T(8,128)(2,1)S(1)}, bf16[64,1024]{1,0:T(8,128)(2,1)S(1)}, u32[]{:S(2)}, u32[]{:S(2)}) %collective-permute-start.13) | collective-permute-done | bytes 131104 | tf_op jit(solution)/shard_map/ppermute | solution.py:429
  55.1 1.8 %right_side.1 = (f32[304,1024]{1,0:T(8,128)S(1)}, bf16[512,1024]{1,0:T(8,128)(2,1)S(1)}, bf16[304,128]{1,0:T(8,128)(2,1)S(1)}, bf16[16,304]{1,0:T(8,128)(2,1)S(1)}, bf16[304,128]{1,0:T(8,128)(2,1)S(1)}) custom-call(bf16[64,1024]{1,0:T(8,128)(2,1)S(1)} %copy-done, bf16[64,1024]{1,0:T(8,128)(2,1)S(1)} %collective-permute-done.2.refs_1_, ...), custom_call_target="tpu_custom_call" | custom-call | tf_op jit(solution)/shard_map/right_side/pallas_call | solution.py:30
  56.8 1.2 %collective-permute-start.18 = (bf16[16,304]{1,0:T(8,128)(2,1)S(1)}, bf16[16,304]{1,0:T(8,128)(2,1)S(1)}, u32[]{:S(2)}, u32[]{:S(2)}) collective-permute-start(bf16[16,304]{1,0:T(8,128)(2,1)S(1)} %get-tuple-element.104), channel_id=1, source_target_pairs={{0,32},{32,64},{64,96},{96,128},{128,160},{160,192},{192,224},{224... | collective-permute-start | bytes 29192 | tf_op jit(solution)/shard_map/ppermute | solution.py:429
  58.1 1.1 collective-permute-start.19
  59.2 4.9 %collective-permute-start.16 = (bf16[304,128]{1,0:T(8,128)(2,1)S(1)}, bf16[304,128]{1,0:T(8,128)(2,1)S(1)}, u32[]{:S(2)}, u32[]{:S(2)}) collective-permute-start(bf16[304,128]{1,0:T(8,128)(2,1)S(1)} %get-tuple-element.102), channel_id=1, source_target_pairs={{0,1},{1,2},{2,3},{3,4},{4,5},{5,6},{6,7},{7,8},{8,9},{9,10},{10,1... | collective-permute-start | bytes 233480 | tf_op jit(solution)/shard_map/ppermute | solution.py:429
  64.1 3.4 %collective-permute-start.17 = (bf16[304,128]{1,0:T(8,128)(2,1)S(1)}, bf16[304,128]{1,0:T(8,128)(2,1)S(1)}, u32[]{:S(2)}, u32[]{:S(2)}) collective-permute-start(bf16[304,128]{1,0:T(8,128)(2,1)S(1)} %get-tuple-element.103), channel_id=1, source_target_pairs={{0,31},{1,0},{2,1},{3,2},{4,3},{5,4},{6,5},{7,6},{8,7},{9,8},{10,9... | collective-permute-start | bytes 233480 | tf_op jit(solution)/shard_map/ppermute | solution.py:429
  67.5 0.3 pad_maximum_fusion.refs_2_
  67.8 3.4 %apply0.1 = (f32[304,1024]{1,0:T(8,128)S(1)}, f32[3,8,128]{2,1,0:T(8,128)S(1)}) custom-call(f32[304,1024]{1,0:T(8,128)S(1)} %get-tuple-element.99.refs_0_.refs_4_.basis.zero, bf16[512,1024]{1,0:T(8,128)(2,1)S(1)} %get-tuple-element.100.refs_1_, bf16[512,608]{1,0:T(8,128)(2,1)S(1)} %pad_maximum_fusion.refs_2_, ...), custom_call_target="tpu_custom_call" | custom-call | tf_op jit(solution)/shard_map/apply0/pallas_call | solution.py:30
  71.2 0.7 add_halo1.1
  71.9 5.4 %collective-permute-start.21 = (bf16[304,128]{1,0:T(8,128)(2,1)S(1)}, bf16[304,128]{1,0:T(8,128)(2,1)S(1)}, u32[]{:S(2)}, u32[]{:S(2)}) collective-permute-start(bf16[304,128]{1,0:T(8,128)(2,1)S(1)} %get-tuple-element.108), channel_id=1, source_target_pairs={{0,31},{1,0},{2,1},{3,2},{4,3},{5,4},{6,5},{7,6},{8,7},{9,8},{10,9... | collective-permute-start | bytes 233480 | tf_op jit(solution)/shard_map/ppermute | solution.py:429
  77.3 1.7 %collective-permute-start.23 = (bf16[16,304]{1,0:T(8,128)(2,1)S(1)}, bf16[16,304]{1,0:T(8,128)(2,1)S(1)}, u32[]{:S(2)}, u32[]{:S(2)}) collective-permute-start(bf16[16,304]{1,0:T(8,128)(2,1)S(1)} %get-tuple-element.109), channel_id=1, source_target_pairs={{0,224},{32,0},{64,32},{96,64},{128,96},{160,128},{192,160},{224,1... | collective-permute-start | bytes 29192 | tf_op jit(solution)/shard_map/ppermute | solution.py:429
  79.0 3.4 %apply1.1 = (f32[304,1024]{1,0:T(8,128)S(1)}, f32[3,8,128]{2,1,0:T(8,128)S(1)}) custom-call(f32[304,1024]{1,0:T(8,128)S(1)} %get-tuple-element.105.refs_0_.refs_4_.one, bf16[512,1024]{1,0:T(8,128)(2,1)S(1)} %get-tuple-element.100.refs_1_, bf16[512,608]{1,0:T(8,128)(2,1)S(1)} %pad_maximum_fusion.refs_2_, ...), custom_call_target="tpu_custom_call" | custom-call | tf_op jit(solution)/shard_map/apply1/pallas_call | solution.py:30
  82.5 0.7 add_halo2.1
  83.2 0.2 collective-permute-start.24
  83.4 1.1 collective-permute-start.25
  84.5 3.5 %apply2.1.two = f32[3,8,128]{2,1,0:T(8,128)S(1)} custom-call(f32[304,1024]{1,0:T(8,128)S(1)} %get-tuple-element.110.refs_0_.field.two, bf16[512,1024]{1,0:T(8,128)(2,1)S(1)} %get-tuple-element.100.refs_1_, bf16[512,608]{1,0:T(8,128)(2,1)S(1)} %pad_maximum_fusion.refs_2_, bf16[304,512]{1,0:T(8,128)(2,1)S(1)} %subtract_convert_fusion.1.refs_16_.refs_3_, ...), custom_call_target="tpu_custom_call" | custom-call | tf_op jit(solution)/shard_map/apply2/pallas_call | solution.py:30
  87.9 3.9 %collective-permute-done.24.above = bf16[304,128]{1,0:T(8,128)(2,1)S(1)} collective-permute-done((bf16[304,128]{1,0:T(8,128)(2,1)S(1)}, bf16[304,128]{1,0:T(8,128)(2,1)S(1)}, u32[]{:S(2)}, u32[]{:S(2)}) %collective-permute-start.24) | collective-permute-done | bytes 77856 | tf_op jit(solution)/shard_map/ppermute | solution.py:429
  91.8 0.6 all_moments.1
  92.6 1.0 collective-permute-done.26
  93.6 3.5 %collective-permute-done.27 = f32[1,128]{1,0:T(1,128)S(1)} collective-permute-done((f32[1,128]{1,0:T(1,128)S(1)}, f32[1,128]{1,0:T(1,128)S(1)}, u32[]{:S(2)}, u32[]{:S(2)}) %collective-permute-start.27) | collective-permute-done | bytes 544 | tf_op jit(solution)/shard_map/ppermute | solution.py:429
  97.1 1.7 %collective-permute-start.28 = (f32[1,128]{1,0:T(1,128)S(1)}, f32[1,128]{1,0:T(1,128)S(1)}, u32[]{:S(2)}, u32[]{:S(2)}) collective-permute-start(f32[1,128]{1,0:T(1,128)S(1)} %add.70.one), channel_id=1, source_target_pairs={{0,128},{32,160},{64,192},{96,224},{128,0},{160,32},{192,64},{224,... | collective-permute-start | bytes 1544 | tf_op jit(solution)/shard_map/ppermute | solution.py:429
  98.8 3.3 %collective-permute-done.28.two = f32[1,128]{1,0:T(1,128)S(1)} collective-permute-done((f32[1,128]{1,0:T(1,128)S(1)}, f32[1,128]{1,0:T(1,128)S(1)}, u32[]{:S(2)}, u32[]{:S(2)}) %collective-permute-start.28) | collective-permute-done | bytes 544 | tf_op jit(solution)/shard_map/ppermute | solution.py:429
  102.2 14.4 %all_to_all.10.parts = f32[32,1,128]{2,1,0:T(1,128)S(1)} all-to-all(f32[32,1,128]{2,1,0:T(1,128)S(1)} %add_and_spread.1), channel_id=1, replica_groups=mesh['ifg'=8,'rows'=32] {'rows'}, dimensions={0} | all-to-all | bytes 32768 | tf_op jit(solution)/shard_map/all_to_all | solution.py:588
  116.6 1.3 %combine.1 = f32[2400,128]{1,0:T(8,128)} custom-call(f32[32,1,128]{2,1,0:T(1,128)S(1)} %all_to_all.10.parts, f32[304,1024]{1,0:T(8,128)S(1)} %get-tuple-element.99.refs_0_.refs_4_.basis.zero, f32[304,1024]{1,0:T(8,128)S(1)} %get-tuple-element.105.refs_0_.refs_4_.one, f32[304,1024]{1,0:T(8,128)S(1)} %get-tuple-element.110.refs_0_.field.two), custom_call_target="tpu_custom_call" | custom-call | tf_op jit(solution)/shard_map/combine/pallas_call | solution.py:30
  (58 shorter events, 1.2 us)
Async XLA Ops:
  0.6 10.7 %copy-start.5 = (s32[64,8]{0,1:T(8,128)S(1)}, s32[64,8]{0,1:T(8,128)}, u32[]{:S(2)}) copy-start(s32[64,8]{0,1:T(8,128)} %param.8) | copy-start | bytes 6148
  0.6 10.8 %copy-start.6 = (s32[512,2]{0,1:T(2,128)S(1)}, s32[512,2]{0,1:T(2,128)}, u32[]{:S(2)}) copy-start(s32[512,2]{0,1:T(2,128)} %param.9) | copy-start | bytes 12292
  0.7 11.6 %copy-start.1 = (f32[8,1024]{1,0:T(8,128)S(1)}, f32[8,1024]{1,0:T(8,128)}, u32[]{:S(2)}) copy-start(f32[8,1024]{1,0:T(8,128)} %height.5) | copy-start | bytes 98308
  2.8 14.7 %collective-permute-start = (bf16[128,1024]{1,0:T(8,128)(2,1)S(1)}, bf16[128,1024]{1,0:T(8,128)(2,1)S(1)}, u32[]{:S(2)}, u32[]{:S(2)}) collective-permute-start(bf16[128,1024]{1,0:T(8,128)(2,1)S(1)} %get-tuple-element.61), channel_id=1, source_target_pairs={{0,1},{1,2},{2,3},{3,4},{4,5},{5,6},{6,7},{7,8},{8,9},{9,10},{10,1... | collective-permute-start | bytes 786440 | tf_op jit(solution)/shard_map/ppermute | solution.py:429
  4.8 12.7 %collective-permute-start.1 = (bf16[128,1024]{1,0:T(8,128)(2,1)S(1)}, bf16[128,1024]{1,0:T(8,128)(2,1)S(1)}, u32[]{:S(2)}, u32[]{:S(2)}) collective-permute-start(bf16[128,1024]{1,0:T(8,128)(2,1)S(1)} %get-tuple-element.62), channel_id=1, source_target_pairs={{0,31},{1,0},{2,1},{3,2},{4,3},{5,4},{6,5},{7,6},{8,7},{9,8},{10,9... | collective-permute-start | bytes 786440 | tf_op jit(solution)/shard_map/ppermute | solution.py:429
  20.1 4.0 %collective-permute-start.2 = (bf16[64,1024]{1,0:T(8,128)(2,1)}, bf16[64,1024]{1,0:T(8,128)(2,1)S(1)}, u32[]{:S(2)}, u32[]{:S(2)}) collective-permute-start(bf16[64,1024]{1,0:T(8,128)(2,1)} %get-tuple-element.75), channel_id=1, source_target_pairs={{0,32},{32,0},{64,96},{96,64},{128,160},{160,128},{192,224},{224,1... | collective-permute-start | bytes 393224 | tf_op jit(solution)/shard_map/ppermute | solution.py:429
  20.2 15.0 %collective-permute-start.3 = (bf16[64,1024]{1,0:T(8,128)(2,1)}, bf16[64,1024]{1,0:T(8,128)(2,1)S(1)}, u32[]{:S(2)}, u32[]{:S(2)}) collective-permute-start(bf16[64,1024]{1,0:T(8,128)(2,1)} %get-tuple-element.78), channel_id=1, source_target_pairs={{0,128},{32,160},{64,192},{96,224},{128,0},{160,32},{192,64},{224,... | collective-permute-start | bytes 393224 | tf_op jit(solution)/shard_map/ppermute | solution.py:429
  21.7 14.9 %collective-permute-start.4 = (bf16[64,1024]{1,0:T(8,128)(2,1)}, bf16[64,1024]{1,0:T(8,128)(2,1)S(1)}, u32[]{:S(2)}, u32[]{:S(2)}) collective-permute-start(bf16[64,1024]{1,0:T(8,128)(2,1)} %get-tuple-element.79), channel_id=1, source_target_pairs={{0,160},{32,128},{64,224},{96,192},{128,32},{160,0},{192,96},{224,... | collective-permute-start | bytes 393224 | tf_op jit(solution)/shard_map/ppermute | solution.py:429
  23.5 13.0 %collective-permute-start.5 = (bf16[64,1024]{1,0:T(8,128)(2,1)}, bf16[64,1024]{1,0:T(8,128)(2,1)S(1)}, u32[]{:S(2)}, u32[]{:S(2)}) collective-permute-start(bf16[64,1024]{1,0:T(8,128)(2,1)} %get-tuple-element.80), channel_id=1, source_target_pairs={{0,64},{32,96},{64,128},{96,160},{128,192},{160,224},{192,0},{224,... | collective-permute-start | bytes 393224 | tf_op jit(solution)/shard_map/ppermute | solution.py:429
  24.0 16.6 %all-to-all-start = ((f32[32,1,128]{2,1,0:T(1,128)}), f32[32,1,128]{2,1,0:T(1,128)S(1)}, u32[]{:S(2)}, u32[]{:S(2)}) async-start(f32[32,1,128]{2,1,0:T(1,128)} %get-tuple-element.77), calls=%async_computation | async-start | bytes 32768 | tf_op jit(solution)/shard_map/all_to_all | solution.py:503
  31.8 1.6 %copy-start.3 = (bf16[64,1024]{1,0:T(8,128)(2,1)S(1)}, bf16[64,1024]{1,0:T(8,128)(2,1)}, u32[]{:S(2)}) copy-start(bf16[64,1024]{1,0:T(8,128)(2,1)} %get-tuple-element.84) | copy-start | bytes 393220
  31.8 2.6 %copy-start.4 = (bf16[64,1024]{1,0:T(8,128)(2,1)S(1)}, bf16[64,1024]{1,0:T(8,128)(2,1)}, u32[]{:S(2)}) copy-start(bf16[64,1024]{1,0:T(8,128)(2,1)} %get-tuple-element.85) | copy-start | bytes 393220
  33.4 21.6 %copy-start = (bf16[64,1024]{1,0:T(8,128)(2,1)S(1)}, bf16[64,1024]{1,0:T(8,128)(2,1)}, u32[]{:S(2)}) copy-start(bf16[64,1024]{1,0:T(8,128)(2,1)} %get-tuple-element.73.refs_0_) | copy-start | bytes 393220
  33.4 10.4 %collective-permute-start.6 = (bf16[64,1024]{1,0:T(8,128)(2,1)S(1)}, bf16[64,1024]{1,0:T(8,128)(2,1)S(1)}, u32[]{:S(2)}, u32[]{:S(2)}) collective-permute-start(bf16[64,1024]{1,0:T(8,128)(2,1)S(1)} %copy-done.3), channel_id=1, source_target_pairs={{0,96},{32,64},{64,160},{96,128},{128,224},{160,192},{192,32},{224... | collective-permute-start | bytes 393224 | tf_op jit(solution)/shard_map/ppermute | solution.py:429
  34.4 11.4 %collective-permute-start.7 = (bf16[64,1024]{1,0:T(8,128)(2,1)S(1)}, bf16[64,1024]{1,0:T(8,128)(2,1)S(1)}, u32[]{:S(2)}, u32[]{:S(2)}) collective-permute-start(bf16[64,1024]{1,0:T(8,128)(2,1)S(1)} %copy-done.4), channel_id=1, source_target_pairs={{0,192},{32,224},{64,0},{96,32},{128,64},{160,96},{192,128},{224,1... | collective-permute-start | bytes 393224 | tf_op jit(solution)/shard_map/ppermute | solution.py:429
  35.2 12.3 %collective-permute-start.8 = (bf16[64,1024]{1,0:T(8,128)(2,1)}, bf16[64,1024]{1,0:T(8,128)(2,1)S(1)}, u32[]{:S(2)}, u32[]{:S(2)}) collective-permute-start(bf16[64,1024]{1,0:T(8,128)(2,1)} %get-tuple-element.86), channel_id=1, source_target_pairs={{0,224},{32,192},{64,32},{96,0},{128,96},{160,64},{192,160},{224,1... | collective-permute-start | bytes 393224 | tf_op jit(solution)/shard_map/ppermute | solution.py:429
  41.2 6.8 %collective-permute-start.10 = (bf16[64,1024]{1,0:T(8,128)(2,1)S(1)}, bf16[64,1024]{1,0:T(8,128)(2,1)S(1)}, u32[]{:S(2)}, u32[]{:S(2)}) collective-permute-start(bf16[64,1024]{1,0:T(8,128)(2,1)S(1)} %get-tuple-element.93), channel_id=1, source_target_pairs={{0,128},{32,160},{64,192},{96,224},{128,0},{160,32},{192,64},{224,... | collective-permute-start | bytes 393224 | tf_op jit(solution)/shard_map/ppermute | solution.py:429
  43.7 23.8 %copy-start.2 = (bf16[512,304]{1,0:T(8,128)(2,1)S(1)}, bf16[512,304]{1,0:T(8,128)(2,1)}, u32[]{:S(2)}) copy-start(bf16[512,304]{1,0:T(8,128)(2,1)} %subtract_convert_fusion) | copy-start | bytes 933892
  43.7 6.9 %collective-permute-start.11 = (bf16[64,1024]{1,0:T(8,128)(2,1)S(1)}, bf16[64,1024]{1,0:T(8,128)(2,1)S(1)}, u32[]{:S(2)}, u32[]{:S(2)}) collective-permute-start(bf16[64,1024]{1,0:T(8,128)(2,1)S(1)} %get-tuple-element.94), channel_id=1, source_target_pairs={{0,160},{32,128},{64,224},{96,192},{128,32},{160,0},{192,96},{224,... | collective-permute-start | bytes 393224 | tf_op jit(solution)/shard_map/ppermute | solution.py:429
  43.9 7.5 %collective-permute-start.12 = (bf16[64,1024]{1,0:T(8,128)(2,1)S(1)}, bf16[64,1024]{1,0:T(8,128)(2,1)S(1)}, u32[]{:S(2)}, u32[]{:S(2)}) collective-permute-start(bf16[64,1024]{1,0:T(8,128)(2,1)S(1)} %get-tuple-element.95), channel_id=1, source_target_pairs={{0,64},{32,96},{64,128},{96,160},{128,192},{160,224},{192,0},{224,... | collective-permute-start | bytes 393224 | tf_op jit(solution)/shard_map/ppermute | solution.py:429
  45.8 9.2 %collective-permute-start.13 = (bf16[64,1024]{1,0:T(8,128)(2,1)S(1)}, bf16[64,1024]{1,0:T(8,128)(2,1)S(1)}, u32[]{:S(2)}, u32[]{:S(2)}) collective-permute-start(bf16[64,1024]{1,0:T(8,128)(2,1)S(1)} %get-tuple-element.96), channel_id=1, source_target_pairs={{0,96},{32,64},{64,160},{96,128},{128,224},{160,192},{192,32},{224... | collective-permute-start | bytes 393224 | tf_op jit(solution)/shard_map/ppermute | solution.py:429
  47.5 7.5 %collective-permute-start.14 = (bf16[64,1024]{1,0:T(8,128)(2,1)S(1)}, bf16[64,1024]{1,0:T(8,128)(2,1)S(1)}, u32[]{:S(2)}, u32[]{:S(2)}) collective-permute-start(bf16[64,1024]{1,0:T(8,128)(2,1)S(1)} %get-tuple-element.97), channel_id=1, source_target_pairs={{0,192},{32,224},{64,0},{96,32},{128,64},{160,96},{192,128},{224,1... | collective-permute-start | bytes 393224 | tf_op jit(solution)/shard_map/ppermute | solution.py:429
  48.0 7.0 %collective-permute-start.15 = (bf16[64,1024]{1,0:T(8,128)(2,1)S(1)}, bf16[64,1024]{1,0:T(8,128)(2,1)S(1)}, u32[]{:S(2)}, u32[]{:S(2)}) collective-permute-start(bf16[64,1024]{1,0:T(8,128)(2,1)S(1)} %get-tuple-element.98), channel_id=1, source_target_pairs={{0,224},{32,192},{64,32},{96,0},{128,96},{160,64},{192,160},{224,1... | collective-permute-start | bytes 393224 | tf_op jit(solution)/shard_map/ppermute | solution.py:429
  50.6 4.5 %collective-permute-start.9 = (bf16[64,1024]{1,0:T(8,128)(2,1)S(1)}, bf16[64,1024]{1,0:T(8,128)(2,1)S(1)}, u32[]{:S(2)}, u32[]{:S(2)}) collective-permute-start(bf16[64,1024]{1,0:T(8,128)(2,1)S(1)} %get-tuple-element.92), channel_id=1, source_target_pairs={{0,32},{32,0},{64,96},{96,64},{128,160},{160,128},{192,224},{224,1... | collective-permute-start | bytes 393224 | tf_op jit(solution)/shard_map/ppermute | solution.py:429
  56.8 14.3 %collective-permute-start.18 = (bf16[16,304]{1,0:T(8,128)(2,1)S(1)}, bf16[16,304]{1,0:T(8,128)(2,1)S(1)}, u32[]{:S(2)}, u32[]{:S(2)}) collective-permute-start(bf16[16,304]{1,0:T(8,128)(2,1)S(1)} %get-tuple-element.104), channel_id=1, source_target_pairs={{0,32},{32,64},{64,96},{96,128},{128,160},{160,192},{192,224},{224... | collective-permute-start | bytes 29192 | tf_op jit(solution)/shard_map/ppermute | solution.py:429
  58.1 13.1 %collective-permute-start.19 = (bf16[16,304]{1,0:T(8,128)(2,1)S(1)}, bf16[16,304]{1,0:T(8,128)(2,1)S(1)}, u32[]{:S(2)}, u32[]{:S(2)}) collective-permute-start(bf16[16,304]{1,0:T(8,128)(2,1)S(1)} %get-tuple-element.104), channel_id=1, source_target_pairs={{0,224},{32,0},{64,32},{96,64},{128,96},{160,128},{192,160},{224,1... | collective-permute-start | bytes 29192 | tf_op jit(solution)/shard_map/ppermute | solution.py:429
  59.2 12.0 %collective-permute-start.16 = (bf16[304,128]{1,0:T(8,128)(2,1)S(1)}, bf16[304,128]{1,0:T(8,128)(2,1)S(1)}, u32[]{:S(2)}, u32[]{:S(2)}) collective-permute-start(bf16[304,128]{1,0:T(8,128)(2,1)S(1)} %get-tuple-element.102), channel_id=1, source_target_pairs={{0,1},{1,2},{2,3},{3,4},{4,5},{5,6},{6,7},{7,8},{8,9},{9,10},{10,1... | collective-permute-start | bytes 233480 | tf_op jit(solution)/shard_map/ppermute | solution.py:429
  64.1 7.1 %collective-permute-start.17 = (bf16[304,128]{1,0:T(8,128)(2,1)S(1)}, bf16[304,128]{1,0:T(8,128)(2,1)S(1)}, u32[]{:S(2)}, u32[]{:S(2)}) collective-permute-start(bf16[304,128]{1,0:T(8,128)(2,1)S(1)} %get-tuple-element.103), channel_id=1, source_target_pairs={{0,31},{1,0},{2,1},{3,2},{4,3},{5,4},{6,5},{7,6},{8,7},{9,8},{10,9... | collective-permute-start | bytes 233480 | tf_op jit(solution)/shard_map/ppermute | solution.py:429
  71.9 10.5 %collective-permute-start.20 = (bf16[304,128]{1,0:T(8,128)(2,1)S(1)}, bf16[304,128]{1,0:T(8,128)(2,1)S(1)}, u32[]{:S(2)}, u32[]{:S(2)}) collective-permute-start(bf16[304,128]{1,0:T(8,128)(2,1)S(1)} %get-tuple-element.107), channel_id=1, source_target_pairs={{0,1},{1,2},{2,3},{3,4},{4,5},{5,6},{6,7},{7,8},{8,9},{9,10},{10,1... | collective-permute-start | bytes 233480 | tf_op jit(solution)/shard_map/ppermute | solution.py:429
  71.9 10.5 %collective-permute-start.21 = (bf16[304,128]{1,0:T(8,128)(2,1)S(1)}, bf16[304,128]{1,0:T(8,128)(2,1)S(1)}, u32[]{:S(2)}, u32[]{:S(2)}) collective-permute-start(bf16[304,128]{1,0:T(8,128)(2,1)S(1)} %get-tuple-element.108), channel_id=1, source_target_pairs={{0,31},{1,0},{2,1},{3,2},{4,3},{5,4},{6,5},{7,6},{8,7},{9,8},{10,9... | collective-permute-start | bytes 233480 | tf_op jit(solution)/shard_map/ppermute | solution.py:429
  77.3 5.2 %collective-permute-start.22 = (bf16[16,304]{1,0:T(8,128)(2,1)S(1)}, bf16[16,304]{1,0:T(8,128)(2,1)S(1)}, u32[]{:S(2)}, u32[]{:S(2)}) collective-permute-start(bf16[16,304]{1,0:T(8,128)(2,1)S(1)} %get-tuple-element.109), channel_id=1, source_target_pairs={{0,32},{32,64},{64,96},{96,128},{128,160},{160,192},{192,224},{224... | collective-permute-start | bytes 29192 | tf_op jit(solution)/shard_map/ppermute | solution.py:429
  77.3 5.2 %collective-permute-start.23 = (bf16[16,304]{1,0:T(8,128)(2,1)S(1)}, bf16[16,304]{1,0:T(8,128)(2,1)S(1)}, u32[]{:S(2)}, u32[]{:S(2)}) collective-permute-start(bf16[16,304]{1,0:T(8,128)(2,1)S(1)} %get-tuple-element.109), channel_id=1, source_target_pairs={{0,224},{32,0},{64,32},{96,64},{128,96},{160,128},{192,160},{224,1... | collective-permute-start | bytes 29192 | tf_op jit(solution)/shard_map/ppermute | solution.py:429
  83.2 8.7 %collective-permute-start.24 = (bf16[304,128]{1,0:T(8,128)(2,1)S(1)}, bf16[304,128]{1,0:T(8,128)(2,1)S(1)}, u32[]{:S(2)}, u32[]{:S(2)}) collective-permute-start(bf16[304,128]{1,0:T(8,128)(2,1)S(1)} %get-tuple-element.111), channel_id=1, source_target_pairs={{0,1},{1,2},{2,3},{3,4},{4,5},{5,6},{6,7},{7,8},{8,9},{9,10},{10,1... | collective-permute-start | bytes 233480 | tf_op jit(solution)/shard_map/ppermute | solution.py:429
  83.4 4.5 %collective-permute-start.25 = (bf16[16,304]{1,0:T(8,128)(2,1)S(1)}, bf16[16,304]{1,0:T(8,128)(2,1)S(1)}, u32[]{:S(2)}, u32[]{:S(2)}) collective-permute-start(bf16[16,304]{1,0:T(8,128)(2,1)S(1)} %get-tuple-element.112), channel_id=1, source_target_pairs={{0,32},{32,64},{64,96},{96,128},{128,160},{160,192},{192,224},{224... | collective-permute-start | bytes 29192 | tf_op jit(solution)/shard_map/ppermute | solution.py:429
  92.4 1.1 collective-permute-start.26
  93.6 3.5 %collective-permute-start.27 = (f32[1,128]{1,0:T(1,128)S(1)}, f32[1,128]{1,0:T(1,128)S(1)}, u32[]{:S(2)}, u32[]{:S(2)}) collective-permute-start(f32[1,128]{1,0:T(1,128)S(1)} %add.69), channel_id=1, source_target_pairs={{0,64},{32,96},{64,0},{96,32},{128,192},{160,224},{192,128},{224,1... | collective-permute-start | bytes 1544 | tf_op jit(solution)/shard_map/ppermute | solution.py:429
  97.1 5.0 %collective-permute-start.28 = (f32[1,128]{1,0:T(1,128)S(1)}, f32[1,128]{1,0:T(1,128)S(1)}, u32[]{:S(2)}, u32[]{:S(2)}) collective-permute-start(f32[1,128]{1,0:T(1,128)S(1)} %add.70.one), channel_id=1, source_target_pairs={{0,128},{32,160},{64,192},{96,224},{128,0},{160,32},{192,64},{224,... | collective-permute-start | bytes 1544 | tf_op jit(solution)/shard_map/ppermute | solution.py:429

commit v9 on v8

--- a/solution.py
+++ b/solution.py
@@ -82,11 +82,46 @@
     return values + left + right
 
 
-def fold_lanes(values):
-    total = values[:, :128]
-    for tile in range(1, 8):
-        total += values[:, tile * 128 : tile * 128 + 128]
+def regression_sums(phase_t, coher_t, height, above, below, out, box_one, box_two, totals):
+    lane = lax.broadcasted_iota(jnp.int32, (8, 1024), 1)
+    sub = lax.broadcasted_iota(jnp.int32, (8, 1024), 0)
+    my_row = lax.axis_index("rows")
+    here = height[...]
+    upper = jnp.where(my_row > 0, above[...], 0.0)
+    lower = jnp.where(my_row < lax.axis_size("rows") - 1, below[...], 0.0)
+    up = jnp.where(sub == 0, upper, pltpu.roll(here, 1, 0))
+    down = jnp.where(sub == 7, lower, pltpu.roll(here, 7, 0))
+    box_one[...] = shifted_sum(here + up + down, lane, 1023)
+    box_two[...] = shifted_sum(here * here + up * up + down * down, lane, 1023)
+
+    def group(block, _):
+        ifgs, lows = block_of(block)
+        top = jnp.zeros((16, 128), F32)
+        low = jnp.zeros((16, 128), F32)
+        for row in range(8):
+            for tile in range(8):
+                lanes = pl.ds(tile * 128, 128)
+                coher = coher_t[row, ifgs, lanes].astype(F32)
+                phase = phase_t[row, ifgs, lanes].astype(F32)
+                top += coher * phase * box_one[pl.ds(row, 1), lanes]
+                low += coher * box_two[pl.ds(row, 1), lanes]
+        totals[ifgs, :] = top
+        totals[lows, :] = low
+        return 0
+
+    lax.fori_loop(0, 4, group, 0)
+    out[...] = jnp.broadcast_to(jnp.sum(totals[...].T, axis=0)[None, None, :], out.shape)
+
+
+def add_parts(parts):
+    total = parts[0]
+    for index in range(1, parts.shape[0]):
+        total += parts[index]
     return total
+
+
+def sum_and_spread(parts, out):
+    out[...] = jnp.broadcast_to(add_parts(parts)[None], out.shape)
 
 
 OFFSETS = ((0, 0), (0, 1), (2, 0), (2, 1), (1, 0), (1, 1), (3, 0), (3, 1))
@@ -100,12 +135,10 @@
     return other(lax.axis_index("ifg"), *OFFSETS[step])
 
 
-def smooth_row(rows, lane, mask, terrain):
+def smooth_row(rows, lane, mask):
     denom = shifted_sum(rows[0][0] + rows[1][0] + rows[2][0], lane, 1023)
     numer = shifted_sum(rows[0][1] + rows[1][1] + rows[2][1], lane, 1023)
-    top = fold_lanes(numer * terrain)
-    low = fold_lanes(denom * (terrain * terrain))
-    return numer / denom, (mask * (denom / 9.0)).astype(BF16), top, low
+    return numer / denom, (mask * (denom / 9.0)).astype(BF16)
 
 
 def load_row(phase_t, coher_t, row, ifgs):
@@ -117,7 +150,7 @@
     return pl.ds(pl.multiple_of(block * 16, 16), 16), pl.ds(pl.multiple_of(block * 16 + 64, 16), 16)
 
 
-def inner_rows(phase_t, coher_t, mask, height, smooth_out, totals, *rest):
+def inner_rows(phase_t, coher_t, mask, smooth_out, *rest):
     outs, weights, smooth, sems = rest[:8], *rest[8:]
     lane = lax.broadcasted_iota(jnp.int32, (16, 1024), 1)
 
@@ -131,24 +164,16 @@
         ] + [pltpu.make_async_copy(smooth.at[:, ifgs], smooth_out.at[pl.ds(1, 6), ifgs], sems.at[block, 8])]
 
     def group(block, _):
-        ifgs, lows = block_of(block)
+        ifgs, _ = block_of(block)
         masks = mask[ifgs, :]
         rows = [load_row(phase_t, coher_t, row, ifgs) for row in (0, 1)]
-        top = jnp.zeros((16, 128), F32)
-        low = jnp.zeros((16, 128), F32)
         for row in range(1, 7):
             rows.append(load_row(phase_t, coher_t, row + 1, ifgs))
-            value, weight, more_top, more_low = smooth_row(
-                rows, lane, masks[:, row : row + 1], height[pl.ds(row, 1), :]
-            )
+            value, weight = smooth_row(rows, lane, masks[:, row : row + 1])
             rows = rows[1:]
-            top += more_top
-            low += more_low
             smooth[row - 1, ifgs, :] = value
             for tile in range(8):
                 weights[tile, ifgs, pl.ds((row - 1) * 128, 128)] = weight[:, tile * 128 : tile * 128 + 128]
-        totals[ifgs, :] = top
-        totals[lows, :] = low
         for copy in copies(block):
             copy.start()
         return 0
@@ -159,9 +184,9 @@
             copy.wait()
 
 
-def border_rows(phase_t, coher_t, above, below, mask, height, totals, *rest):
-    smooth_out, sums, outs = rest[9], rest[10], rest[11:19]
-    weights, smooth, added, sems = rest[19:]
+def border_rows(phase_t, coher_t, above, below, mask, *rest):
+    smooth_out, outs = rest[9], rest[10:18]
+    weights, smooth, sems = rest[18:]
     lane = lax.broadcasted_iota(jnp.int32, (16, 1024), 1)
     my_row = lax.axis_index("rows")
     valid = (my_row > 0, my_row < lax.axis_size("rows") - 1)
@@ -169,22 +194,14 @@
     def group(block, _):
         ifgs, lows = block_of(block)
         masks = mask[ifgs, :]
-        top = totals[ifgs, :]
-        low = totals[lows, :]
         for side, (edge, row) in enumerate(((above, 0), (below, 7))):
             coher = jnp.where(valid[side], edge[lows, :].astype(F32), 0.0)
             rows = [(coher, coher * edge[ifgs, :].astype(F32))]
             rows += [load_row(phase_t, coher_t, near, ifgs) for near in (row, 1 if row == 0 else 6)]
-            value, weight, more_top, more_low = smooth_row(
-                rows, lane, masks[:, row : row + 1], height[pl.ds(row, 1), :]
-            )
-            top += more_top
-            low += more_low
+            value, weight = smooth_row(rows, lane, masks[:, row : row + 1])
             smooth[side, ifgs, :] = value
             for tile in range(8):
                 weights[side, tile, ifgs, :] = weight[:, tile * 128 : tile * 128 + 128]
-        added[ifgs, :] = top
-        added[lows, :] = low
         return 0
 
     lax.fori_loop(0, 4, group, 0)
@@ -198,7 +215,6 @@
             )
     for copy in copies:
         copy.start()
-    sums[...] = jnp.broadcast_to(jnp.sum(added[...].T, axis=0)[None, None, :], sums.shape)
     for copy in copies:
         copy.wait()
 
@@ -216,9 +232,7 @@
 
 def correction(sums, smooth, height, slope_row, *rest):
     outs, blocks = rest[:8], rest[8]
-    total = sums[0]
-    for index in range(1, sums.shape[0]):
-        total += sums[index]
+    total = add_parts(sums)
     slope_row[...] = total / pltpu.roll(total, 64, 1)
     column = jnp.broadcast_to(total, (128, 128)).T
     slope = column[:64, :] / column[64:, :]
@@ -387,9 +401,7 @@
 
 
 def combine(parts, zero, one, two, out, field, sems):
-    total = parts[0]
-    for index in range(1, parts.shape[0]):
-        total += parts[index]
+    total = add_parts(parts)
     m0, m1, m2, m3, m4, m5 = (jnp.broadcast_to(total[:, i : i + 1], (1, 128)) for i in range(6))
     t00, t01, t11 = m1 + SHIFT * m0, m2 + SHIFT * m1, m3 + SHIFT * m2
     t12, t22 = m4 + SHIFT * m3, m5 + SHIFT * m4
@@ -434,6 +446,7 @@
     def backward(values, axis):
         return permute(values, axis, lambda i: (i - 1) % lax.axis_size(axis))
 
+    height_above, height_below = forward(height[7:8], "rows"), backward(height[0:1], "rows")
     stacked = sds((8, 64, 1024), BF16)
     edge = sds((128, 1024), BF16)
     phase_t, coher_t, first, last = call(
@@ -452,15 +465,29 @@
     )
     above, below = forward(last, "rows"), backward(first, "rows")
     mask = gap_mask.astype(F32)
+    sums = call(
+        regression_sums,
+        sds((8, 1, 128), F32),
+        phase_t,
+        coher_t,
+        height,
+        height_above,
+        height_below,
+        scratch=(pltpu.VMEM((8, 1024), F32), pltpu.VMEM((8, 1024), F32), pltpu.VMEM((128, 128), F32)),
+        name="regression_sums",
+    )
+    near = [[8 * y + z for z in range(8)] for y in range(4)]
+    far = [[8 * y + z for y in range(4)] for z in range(8)]
+    sums = lax.all_to_all(sums, "rows", 0, 0, tiled=True, axis_index_groups=near)
+    sums = call(sum_and_spread, sds((4, 1, 128), F32), sums, name="sum_and_spread")
     pieces = [in_hbm((64, 1024), BF16)] * 8
-    smooth, totals, *weight_parts = call(
+    smooth, *weight_parts = call(
         inner_rows,
-        [in_hbm((8, 64, 1024), F32), sds((128, 128), F32)] + pieces,
+        [in_hbm((8, 64, 1024), F32)] + pieces,
         phase_t,
         coher_t,
         mask,
-        height,
-        out_specs=[pltpu.HBM, pltpu.VMEM] + [pltpu.HBM] * 8,
+        out_specs=[pltpu.HBM] * 9,
         scratch=(
             pltpu.VMEM((8, 64, 768), BF16),
             pltpu.VMEM((6, 64, 1024), F32),
@@ -468,27 +495,24 @@
         ),
         name="inner_rows",
     )
-    smooth, sums, *weight_parts = call(
+    smooth, *weight_parts = call(
         border_rows,
-        [in_hbm((8, 64, 1024), F32), sds((n_rows, 1, 128), F32)] + pieces,
+        [in_hbm((8, 64, 1024), F32)] + pieces,
         phase_t,
         coher_t,
         above,
         below,
         mask,
-        height,
-        totals,
         smooth,
         *weight_parts,
-        specs=[pltpu.VMEM] * 7 + [pltpu.HBM] * 9,
-        out_specs=[pltpu.HBM, pltpu.VMEM] + [pltpu.HBM] * 8,
+        specs=[pltpu.VMEM] * 5 + [pltpu.HBM] * 9,
+        out_specs=[pltpu.HBM] * 9,
         scratch=(
             pltpu.VMEM((2, 8, 64, 128), BF16),
             pltpu.VMEM((2, 64, 1024), F32),
-            pltpu.VMEM((128, 128), F32),
             pltpu.SemaphoreType.DMA((2, 9)),
         ),
-        aliases={7: 0, **{8 + step: 2 + step for step in range(8)}},
+        aliases={5 + step: step for step in range(9)},
         name="border_rows",
     )
 
@@ -500,7 +524,7 @@
 
     weight_parts = exchange(weight_parts)
     sums, weight_parts[1] = lax.optimization_barrier((sums, weight_parts[1]))
-    sums = lax.all_to_all(sums, "rows", 0, 0, tiled=True)
+    sums = lax.all_to_all(sums, "rows", 0, 0, tiled=True, axis_index_groups=far)
     sums, *weight_parts[2:5] = lax.optimization_barrier((sums, *weight_parts[2:5]))
     smooth = call(
         stage,

time: 118 us -> 126 us (1.068)
  starting transfers between devices: 50.1 us -> 54.2 us
  waiting for transfers between devices: 24.2 us -> 25.9 us
  Pallas kernels: 25.5 us -> 26.8 us
    ppermute x29 -> x31, starting transfers between devices: 43.2 us -> 47.8 us  [permute(): lax.ppermute(values, axis, [(i, target(i)) for i in range(lax.axis_size(a...]
    all_to_all x1 -> x2, waiting for transfers between devices: 4.09 us -> 5.49 us  [the longest x1 5.49 us: per_device(): lax.all_to_all(sums, 'rows', 0, 0, tiled=True, axis_index_groups=near)]
    pallas_call x14 -> x16, Pallas kernels: 25.5 us -> 26.8 us  [call(): pl.pallas_call(body, out_shape=outs, in_specs=[pl.BlockSpec(memory_space=...]
    all_to_all x1 -> x2, starting transfers between devices: 6.81 us -> 6.36 us  [the longest x1 3.23 us: per_device(): lax.all_to_all(sums, 'rows', 0, 0, tiled=True, axis_index_groups=near)]
    ppermute x29 -> x31, waiting for transfers between devices: 20.1 us -> 20.4 us  [permute(): lax.ppermute(values, axis, [(i, target(i)) for i in range(lax.axis_size(a...]
  transfers between devices with their start and end apart: 30 -> 33, of which waited for: 9 -> 10; matrix products, arithmetic and copies ran while one was open for 2% -> 2% of each run, Pallas kernels for 13% -> 16%
where the time goes in v9:
time: 126 us
  starting transfers between devices  54.2 us (43%)
  Pallas kernels  26.8 us (21%)
  waiting for transfers between devices  25.9 us (21%)
  blocking collectives  15 us (12%)
  local copies, waits for them, and re-layouts  1.48 us (1%)
  other arithmetic  1.4 us (1%)
    ppermute x31, starting transfers between devices, permute(): lax.ppermute(values, axis, [(i, target(i)) for i in range(lax.axis_size(a...  47.8 us
    pallas_call x16, Pallas kernels, call(): pl.pallas_call(body, out_shape=outs, in_specs=[pl.BlockSpec(memory_space=...  26.8 us
    ppermute x31, waiting for transfers between devices, permute(): lax.ppermute(values, axis, [(i, target(i)) for i in range(lax.axis_size(a...  20.4 us
    all_to_all x1, blocking collectives, per_device(): parts = lax.all_to_all(parts, 'rows', 0, 0, tiled=True)  15 us
    all_to_all x1, waiting for transfers between devices, per_device(): lax.all_to_all(sums, 'rows', 0, 0, tiled=True, axis_index_groups=near)  5.49 us
    all_to_all x1, starting transfers between devices, per_device(): lax.all_to_all(sums, 'rows', 0, 0, tiled=True, axis_index_groups=near)  3.23 us
    all_to_all x1, starting transfers between devices, per_device(): sums = lax.all_to_all(sums, 'rows', 0, 0, tiled=True, axis_index_groups=far)  3.14 us
  transfers between devices with their start and end apart: 33, of which 10 were waited for; matrix products, arithmetic and copies ran while one was open for 2% of the time, Pallas kernels for 16%

profile of v9, /device:TPU:6, one launch (start us, length us, event | category | flops | bytes accessed | tf_op | source)
XLA Modules:
  0.0 125.9 jit_solution(13742028705711053268)
XLA Ops:
  0.7 2.2 %rows_first.1 = (bf16[8,64,1024]{2,1,0:T(8,128)(2,1)S(1)}, bf16[8,64,1024]{2,1,0:T(8,128)(2,1)S(1)}, bf16[128,1024]{1,0:T(8,128)(2,1)S(1)}, bf16[128,1024]{1,0:T(8,128)(2,1)S(1)}) custom-call(bf16[64,8,1024]{2,1,0:T(8,128)(2,1)} %phase.1, bf16[64,8,1024]{2,1,0:T(8,128)(2,1)} %coher.1), custom_call_target="tpu_custom_call" | custom-call | tf_op jit(solution)/shard_map/rows_first/pallas_call | solution.py:30
  2.8 2.0 %collective-permute-start = (bf16[128,1024]{1,0:T(8,128)(2,1)S(1)}, bf16[128,1024]{1,0:T(8,128)(2,1)S(1)}, u32[]{:S(2)}, u32[]{:S(2)}) collective-permute-start(bf16[128,1024]{1,0:T(8,128)(2,1)S(1)} %get-tuple-element.59), channel_id=1, source_target_pairs={{0,1},{1,2},{2,3},{3,4},{4,5},{5,6},{6,7},{7,8},{8,9},{9,10},{10,1... | collective-permute-start | bytes 786440 | tf_op jit(solution)/shard_map/ppermute | solution.py:441
  4.8 6.5 %collective-permute-start.1 = (bf16[128,1024]{1,0:T(8,128)(2,1)S(1)}, bf16[128,1024]{1,0:T(8,128)(2,1)S(1)}, u32[]{:S(2)}, u32[]{:S(2)}) collective-permute-start(bf16[128,1024]{1,0:T(8,128)(2,1)S(1)} %get-tuple-element.60), channel_id=1, source_target_pairs={{0,31},{1,0},{2,1},{3,2},{4,3},{5,4},{6,5},{7,6},{8,7},{9,8},{10,9... | collective-permute-start | bytes 786440 | tf_op jit(solution)/shard_map/ppermute | solution.py:441
  11.4 5.3 %collective-permute-start.3 = (f32[1,1024]{1,0:T(1,128)S(1)}, f32[1,1024]{1,0:T(1,128)S(1)}, u32[]{:S(2)}, u32[]{:S(2)}) collective-permute-start(f32[1,1024]{1,0:T(1,128)S(1)} %get-tuple-element.112), channel_id=1, source_target_pairs={{0,31},{1,0},{2,1},{3,2},{4,3},{5,4},{6,5},{7,6},{8,7},{9,8},{10,9... | collective-permute-start | bytes 12296 | tf_op jit(solution)/shard_map/ppermute | solution.py:441
  17.7 3.2 %inner_rows.1 = (f32[8,64,1024]{2,1,0:T(8,128)}, bf16[64,1024]{1,0:T(8,128)(2,1)}, bf16[64,1024]{1,0:T(8,128)(2,1)}, bf16[64,1024]{1,0:T(8,128)(2,1)}, bf16[64,1...) custom-call(bf16[8,64,1024]{2,1,0:T(8,128)(2,1)S(1)} %get-tuple-elem, ...), custom_call_target="tpu_custom_call" | custom-call | tf_op jit(solution)/shard_map/inner_rows/pallas_call | solution.py:30
  20.9 1.5 %regression_sums.1 = f32[8,1,128]{2,1,0:T(1,128)} custom-call(bf16[8,64,1024]{2,1,0:T(8,128)(2,1)S(1)} %get-tuple-element.57.phase_t, bf16[8,64,1024]{2,1,0:T(8,128)(2,1)S(1)} %get-tuple-element.58.coher_t, f32[8,1024]{1,0:T(8,128)S(1)} %copy-done.1, f32[1,1024]{1,0:T(1,128)S(1)} %collective-permute-done.2.above, f32[1,1024]{1,0:T(1,128)S(1)} %collective-permute-done.3.below), custom_call_target="tpu_custom_call" | custom-call | tf_op jit(solution)/shard_map/regression_sums/pallas_call | solution.py:30
  22.4 3.2 %all-to-all-start = ((f32[8,1,128]{2,1,0:T(1,128)}), f32[8,1,128]{2,1,0:T(1,128)S(1)}, u32[]{:S(2)}, u32[]{:S(2)}) async-start(f32[8,1,128]{2,1,0:T(1,128)} %regression_sums.1), calls=%async_computation | async-start | bytes 8192 | tf_op jit(solution)/shard_map/all_to_all | solution.py:481
  25.6 2.0 %border_rows.1 = (f32[8,64,1024]{2,1,0:T(8,128)}, bf16[64,1024]{1,0:T(8,128)(2,1)}, bf16[64,1024]{1,0:T(8,128)(2,1)}, bf16[64,1024]{1,0:T(8,128)(2,1)}, bf16[64,...) custom-call(bf16[8,64,1024]{2,1,0:T(8,128)(2,1)S(1)} %get-tuple-elem, ...), custom_call_target="tpu_custom_call", output_to_operand_aliasing={{0}: (5, {}), {1}: (6, {}), {2}: (7, {}), {3}: (8, {}), {4}... | custom-call | tf_op jit(solution)/shard_map/border_rows/pallas_call | solution.py:30
  27.7 5.5 %all-to-all-done.parts = f32[8,1,128]{2,1,0:T(1,128)S(1)} async-done(((f32[8,1,128]{2,1,0:T(1,128)}), f32[8,1,128]{2,1,0:T(1,128)S(1)}, u32[]{:S(2)}, u32[]{:S(2)}) %all-to-all-start) | async-done | bytes 4128 | tf_op jit(solution)/shard_map/all_to_all | solution.py:481
  33.2 0.6 sum_and_spread.1
  33.8 1.4 %collective-permute-start.5 = (bf16[64,1024]{1,0:T(8,128)(2,1)}, bf16[64,1024]{1,0:T(8,128)(2,1)S(1)}, u32[]{:S(2)}, u32[]{:S(2)}) collective-permute-start(bf16[64,1024]{1,0:T(8,128)(2,1)} %get-tuple-element.74), channel_id=1, source_target_pairs={{0,128},{32,160},{64,192},{96,224},{128,0},{160,32},{192,64},{224,... | collective-permute-start | bytes 393224 | tf_op jit(solution)/shard_map/ppermute | solution.py:441
  35.2 2.1 %collective-permute-start.7 = (bf16[64,1024]{1,0:T(8,128)(2,1)}, bf16[64,1024]{1,0:T(8,128)(2,1)S(1)}, u32[]{:S(2)}, u32[]{:S(2)}) collective-permute-start(bf16[64,1024]{1,0:T(8,128)(2,1)} %get-tuple-element.76), channel_id=1, source_target_pairs={{0,64},{32,96},{64,128},{96,160},{128,192},{160,224},{192,0},{224,... | collective-permute-start | bytes 393224 | tf_op jit(solution)/shard_map/ppermute | solution.py:441
  37.3 3.1 %all-to-all-start.1 = ((f32[4,1,128]{2,1,0:T(1,128)}), f32[4,1,128]{2,1,0:T(1,128)S(1)}, u32[]{:S(2)}, u32[]{:S(2)}) async-start(f32[4,1,128]{2,1,0:T(1,128)} %sum_and_spread.1), calls=%async_computation.1 | async-start | bytes 4096 | tf_op jit(solution)/shard_map/all_to_all | solution.py:527
  40.4 1.0 subtract_convert_fusion
  41.4 1.6 %stage.1.smooth = f32[8,64,1024]{2,1,0:T(8,128)S(1)} custom-call(f32[8,64,1024]{2,1,0:T(8,128)} %get-tuple-element.84.source), custom_call_target="tpu_custom_call" | custom-call | tf_op jit(solution)/shard_map/stage/pallas_call | solution.py:30
  43.0 1.6 %collective-permute-start.10 = (bf16[64,1024]{1,0:T(8,128)(2,1)}, bf16[64,1024]{1,0:T(8,128)(2,1)S(1)}, u32[]{:S(2)}, u32[]{:S(2)}) collective-permute-start(bf16[64,1024]{1,0:T(8,128)(2,1)} %get-tuple-element.82), channel_id=1, source_target_pairs={{0,224},{32,192},{64,32},{96,0},{128,96},{160,64},{192,160},{224,1... | collective-permute-start | bytes 393224 | tf_op jit(solution)/shard_map/ppermute | solution.py:441
  44.6 1.5 %collective-permute-start.8 = (bf16[64,1024]{1,0:T(8,128)(2,1)S(1)}, bf16[64,1024]{1,0:T(8,128)(2,1)S(1)}, u32[]{:S(2)}, u32[]{:S(2)}) collective-permute-start(bf16[64,1024]{1,0:T(8,128)(2,1)S(1)} %copy-done.3), channel_id=1, source_target_pairs={{0,96},{32,64},{64,160},{96,128},{128,224},{160,192},{192,32},{224... | collective-permute-start | bytes 393224 | tf_op jit(solution)/shard_map/ppermute | solution.py:441
  47.1 1.5 %collective-permute-start.12 = (bf16[64,1024]{1,0:T(8,128)(2,1)S(1)}, bf16[64,1024]{1,0:T(8,128)(2,1)S(1)}, u32[]{:S(2)}, u32[]{:S(2)}) collective-permute-start(bf16[64,1024]{1,0:T(8,128)(2,1)S(1)} %get-tuple-element.89), channel_id=1, source_target_pairs={{0,128},{32,160},{64,192},{96,224},{128,0},{160,32},{192,64},{224,... | collective-permute-start | bytes 393224 | tf_op jit(solution)/shard_map/ppermute | solution.py:441
  48.7 1.1 collective-permute-done.10.refs_7_
  49.9 1.3 %collective-permute-start.13 = (bf16[64,1024]{1,0:T(8,128)(2,1)S(1)}, bf16[64,1024]{1,0:T(8,128)(2,1)S(1)}, u32[]{:S(2)}, u32[]{:S(2)}) collective-permute-start(bf16[64,1024]{1,0:T(8,128)(2,1)S(1)} %get-tuple-element.90), channel_id=1, source_target_pairs={{0,160},{32,128},{64,224},{96,192},{128,32},{160,0},{192,96},{224,... | collective-permute-start | bytes 393224 | tf_op jit(solution)/shard_map/ppermute | solution.py:441
  51.2 2.4 %collective-permute-start.14 = (bf16[64,1024]{1,0:T(8,128)(2,1)S(1)}, bf16[64,1024]{1,0:T(8,128)(2,1)S(1)}, u32[]{:S(2)}, u32[]{:S(2)}) collective-permute-start(bf16[64,1024]{1,0:T(8,128)(2,1)S(1)} %get-tuple-element.91), channel_id=1, source_target_pairs={{0,64},{32,96},{64,128},{96,160},{128,192},{160,224},{192,0},{224,... | collective-permute-start | bytes 393224 | tf_op jit(solution)/shard_map/ppermute | solution.py:441
  53.6 4.9 %collective-permute-done.9.refs_6_ = bf16[64,1024]{1,0:T(8,128)(2,1)S(1)} collective-permute-done((bf16[64,1024]{1,0:T(8,128)(2,1)S(1)}, bf16[64,1024]{1,0:T(8,128)(2,1)S(1)}, u32[]{:S(2)}, u32[]{:S(2)}) %collective-permute-start.9) | collective-permute-done | bytes 131104 | tf_op jit(solution)/shard_map/ppermute | solution.py:441
  58.5 0.8 collective-permute-start.16
  59.3 1.0 collective-permute-start.17
  60.8 2.8 %collective-permute-done.15.refs_13_ = bf16[64,1024]{1,0:T(8,128)(2,1)S(1)} collective-permute-done((bf16[64,1024]{1,0:T(8,128)(2,1)S(1)}, bf16[64,1024]{1,0:T(8,128)(2,1)S(1)}, u32[]{:S(2)}, u32[]{:S(2)}) %collective-permute-start.15) | collective-permute-done | bytes 131104 | tf_op jit(solution)/shard_map/ppermute | solution.py:441
  63.6 2.2 %collective-permute-done.16.refs_14_ = bf16[64,1024]{1,0:T(8,128)(2,1)S(1)} collective-permute-done((bf16[64,1024]{1,0:T(8,128)(2,1)S(1)}, bf16[64,1024]{1,0:T(8,128)(2,1)S(1)}, u32[]{:S(2)}, u32[]{:S(2)}) %collective-permute-start.16) | collective-permute-done | bytes 131104 | tf_op jit(solution)/shard_map/ppermute | solution.py:441
  66.3 1.8 %right_side.1 = (f32[304,1024]{1,0:T(8,128)S(1)}, bf16[512,1024]{1,0:T(8,128)(2,1)S(1)}, bf16[304,128]{1,0:T(8,128)(2,1)S(1)}, bf16[16,304]{1,0:T(8,128)(2,1)S(1)}, bf16[304,128]{1,0:T(8,128)(2,1)S(1)}) custom-call(bf16[64,1024]{1,0:T(8,128)(2,1)S(1)} %copy-done, bf16[64,1024]{1,0:T(8,128)(2,1)S(1)} %collective-permute-done.4.refs_1_, ...), custom_call_target="tpu_custom_call" | custom-call | tf_op jit(solution)/shard_map/right_side/pallas_call | solution.py:30
  68.1 1.0 collective-permute-start.20
  69.1 0.7 collective-permute-start.21
  69.8 0.6 collective-permute-start.18
  70.4 4.8 %collective-permute-start.19 = (bf16[304,128]{1,0:T(8,128)(2,1)S(1)}, bf16[304,128]{1,0:T(8,128)(2,1)S(1)}, u32[]{:S(2)}, u32[]{:S(2)}) collective-permute-start(bf16[304,128]{1,0:T(8,128)(2,1)S(1)} %get-tuple-element.99), channel_id=1, source_target_pairs={{0,31},{1,0},{2,1},{3,2},{4,3},{5,4},{6,5},{7,6},{8,7},{9,8},{10,9... | collective-permute-start | bytes 233480 | tf_op jit(solution)/shard_map/ppermute | solution.py:441
  75.4 3.4 %apply0.1 = (f32[304,1024]{1,0:T(8,128)S(1)}, f32[3,8,128]{2,1,0:T(8,128)S(1)}) custom-call(f32[304,1024]{1,0:T(8,128)S(1)} %get-tuple-element.95.refs_0_.refs_4_.basis.zero, bf16[512,1024]{1,0:T(8,128)(2,1)S(1)} %get-tuple-element.96.refs_1_, bf16[512,608]{1,0:T(8,128)(2,1)S(1)} %pad_maximum_fusion.refs_2_, ...), custom_call_target="tpu_custom_call" | custom-call | tf_op jit(solution)/shard_map/apply0/pallas_call | solution.py:30
  78.9 0.7 add_halo1.1
  79.6 5.4 %collective-permute-start.23 = (bf16[304,128]{1,0:T(8,128)(2,1)S(1)}, bf16[304,128]{1,0:T(8,128)(2,1)S(1)}, u32[]{:S(2)}, u32[]{:S(2)}) collective-permute-start(bf16[304,128]{1,0:T(8,128)(2,1)S(1)} %get-tuple-element.104), channel_id=1, source_target_pairs={{0,31},{1,0},{2,1},{3,2},{4,3},{5,4},{6,5},{7,6},{8,7},{9,8},{10,9... | collective-permute-start | bytes 233480 | tf_op jit(solution)/shard_map/ppermute | solution.py:441
  84.9 1.7 %collective-permute-start.25 = (bf16[16,304]{1,0:T(8,128)(2,1)S(1)}, bf16[16,304]{1,0:T(8,128)(2,1)S(1)}, u32[]{:S(2)}, u32[]{:S(2)}) collective-permute-start(bf16[16,304]{1,0:T(8,128)(2,1)S(1)} %get-tuple-element.105), channel_id=1, source_target_pairs={{0,224},{32,0},{64,32},{96,64},{128,96},{160,128},{192,160},{224,1... | collective-permute-start | bytes 29192 | tf_op jit(solution)/shard_map/ppermute | solution.py:441
  86.7 3.4 %apply1.1 = (f32[304,1024]{1,0:T(8,128)S(1)}, f32[3,8,128]{2,1,0:T(8,128)S(1)}) custom-call(f32[304,1024]{1,0:T(8,128)S(1)} %get-tuple-element.101.refs_0_.refs_4_.one, bf16[512,1024]{1,0:T(8,128)(2,1)S(1)} %get-tuple-element.96.refs_1_, bf16[512,608]{1,0:T(8,128)(2,1)S(1)} %pad_maximum_fusion.refs_2_, ...), custom_call_target="tpu_custom_call" | custom-call | tf_op jit(solution)/shard_map/apply1/pallas_call | solution.py:30
  90.1 0.7 add_halo2.1
  90.8 1.4 %collective-permute-start.27 = (bf16[16,304]{1,0:T(8,128)(2,1)S(1)}, bf16[16,304]{1,0:T(8,128)(2,1)S(1)}, u32[]{:S(2)}, u32[]{:S(2)}) collective-permute-start(bf16[16,304]{1,0:T(8,128)(2,1)S(1)} %get-tuple-element.108), channel_id=1, source_target_pairs={{0,32},{32,64},{64,96},{96,128},{128,160},{160,192},{192,224},{224... | collective-permute-start | bytes 29192 | tf_op jit(solution)/shard_map/ppermute | solution.py:441
  92.2 3.5 %apply2.1.two = f32[3,8,128]{2,1,0:T(8,128)S(1)} custom-call(f32[304,1024]{1,0:T(8,128)S(1)} %get-tuple-element.106.refs_0_.field.two, bf16[512,1024]{1,0:T(8,128)(2,1)S(1)} %get-tuple-element.96.refs_1_, bf16[512,608]{1,0:T(8,128)(2,1)S(1)} %pad_maximum_fusion.refs_2_, bf16[304,512]{1,0:T(8,128)(2,1)S(1)} %subtract_convert_fusion.1.refs_16_.refs_3_, ...), custom_call_target="tpu_custom_call" | custom-call | tf_op jit(solution)/shard_map/apply2/pallas_call | solution.py:30
  95.7 3.3 %collective-permute-done.26.above = bf16[304,128]{1,0:T(8,128)(2,1)S(1)} collective-permute-done((bf16[304,128]{1,0:T(8,128)(2,1)S(1)}, bf16[304,128]{1,0:T(8,128)(2,1)S(1)}, u32[]{:S(2)}, u32[]{:S(2)}) %collective-permute-start.26) | collective-permute-done | bytes 77856 | tf_op jit(solution)/shard_map/ppermute | solution.py:441
  99.1 0.6 all_moments.1
  99.8 1.0 collective-permute-done.28
  100.8 1.7 %collective-permute-start.29 = (f32[1,128]{1,0:T(1,128)S(1)}, f32[1,128]{1,0:T(1,128)S(1)}, u32[]{:S(2)}, u32[]{:S(2)}) collective-permute-start(f32[1,128]{1,0:T(1,128)S(1)} %add.69), channel_id=1, source_target_pairs={{0,64},{32,96},{64,0},{96,32},{128,192},{160,224},{192,128},{224,1... | collective-permute-start | bytes 1544 | tf_op jit(solution)/shard_map/ppermute | solution.py:441
  102.5 1.9 %collective-permute-done.29 = f32[1,128]{1,0:T(1,128)S(1)} collective-permute-done((f32[1,128]{1,0:T(1,128)S(1)}, f32[1,128]{1,0:T(1,128)S(1)}, u32[]{:S(2)}, u32[]{:S(2)}) %collective-permute-start.29) | collective-permute-done | bytes 544 | tf_op jit(solution)/shard_map/ppermute | solution.py:441
  104.3 2.3 %collective-permute-start.30 = (f32[1,128]{1,0:T(1,128)S(1)}, f32[1,128]{1,0:T(1,128)S(1)}, u32[]{:S(2)}, u32[]{:S(2)}) collective-permute-start(f32[1,128]{1,0:T(1,128)S(1)} %add.70.one), channel_id=1, source_target_pairs={{0,128},{32,160},{64,192},{96,224},{128,0},{160,32},{192,64},{224,... | collective-permute-start | bytes 1544 | tf_op jit(solution)/shard_map/ppermute | solution.py:441
  106.6 2.8 %collective-permute-done.30.two = f32[1,128]{1,0:T(1,128)S(1)} collective-permute-done((f32[1,128]{1,0:T(1,128)S(1)}, f32[1,128]{1,0:T(1,128)S(1)}, u32[]{:S(2)}, u32[]{:S(2)}) %collective-permute-start.30) | collective-permute-done | bytes 544 | tf_op jit(solution)/shard_map/ppermute | solution.py:441
  109.4 15.0 %all_to_all.15.parts = f32[32,1,128]{2,1,0:T(1,128)S(1)} all-to-all(f32[32,1,128]{2,1,0:T(1,128)S(1)} %add_and_spread.1), channel_id=1, replica_groups=mesh['ifg'=8,'rows'=32] {'rows'}, dimensions={0} | all-to-all | bytes 32768 | tf_op jit(solution)/shard_map/all_to_all | solution.py:612
  124.4 1.3 %combine.1 = f32[2400,128]{1,0:T(8,128)} custom-call(f32[32,1,128]{2,1,0:T(1,128)S(1)} %all_to_all.15.parts, f32[304,1024]{1,0:T(8,128)S(1)} %get-tuple-element.95.refs_0_.refs_4_.basis.zero, f32[304,1024]{1,0:T(8,128)S(1)} %get-tuple-element.101.refs_0_.refs_4_.one, f32[304,1024]{1,0:T(8,128)S(1)} %get-tuple-element.106.refs_0_.field.two), custom_call_target="tpu_custom_call" | custom-call | tf_op jit(solution)/shard_map/combine/pallas_call | solution.py:30
  (67 shorter events, 3.8 us)
Async XLA Ops:
  0.6 10.7 %copy-start.1 = (f32[8,1024]{1,0:T(8,128)S(1)}, f32[8,1024]{1,0:T(8,128)}, u32[]{:S(2)}) copy-start(f32[8,1024]{1,0:T(8,128)} %height.3) | copy-start | bytes 98308
  0.6 16.2 %copy-start.5 = (s32[64,8]{0,1:T(8,128)S(1)}, s32[64,8]{0,1:T(8,128)}, u32[]{:S(2)}) copy-start(s32[64,8]{0,1:T(8,128)} %param.8) | copy-start | bytes 6148
  0.7 16.3 %copy-start.6 = (s32[512,2]{0,1:T(2,128)S(1)}, s32[512,2]{0,1:T(2,128)}, u32[]{:S(2)}) copy-start(s32[512,2]{0,1:T(2,128)} %param.9) | copy-start | bytes 12292
  2.8 22.8 %collective-permute-start = (bf16[128,1024]{1,0:T(8,128)(2,1)S(1)}, bf16[128,1024]{1,0:T(8,128)(2,1)S(1)}, u32[]{:S(2)}, u32[]{:S(2)}) collective-permute-start(bf16[128,1024]{1,0:T(8,128)(2,1)S(1)} %get-tuple-element.59), channel_id=1, source_target_pairs={{0,1},{1,2},{2,3},{3,4},{4,5},{5,6},{6,7},{7,8},{8,9},{9,10},{10,1... | collective-permute-start | bytes 786440 | tf_op jit(solution)/shard_map/ppermute | solution.py:441
  4.8 20.8 %collective-permute-start.1 = (bf16[128,1024]{1,0:T(8,128)(2,1)S(1)}, bf16[128,1024]{1,0:T(8,128)(2,1)S(1)}, u32[]{:S(2)}, u32[]{:S(2)}) collective-permute-start(bf16[128,1024]{1,0:T(8,128)(2,1)S(1)} %get-tuple-element.60), channel_id=1, source_target_pairs={{0,31},{1,0},{2,1},{3,2},{4,3},{5,4},{6,5},{7,6},{8,7},{9,8},{10,9... | collective-permute-start | bytes 786440 | tf_op jit(solution)/shard_map/ppermute | solution.py:441
  11.3 9.6 %collective-permute-start.2 = (f32[1,1024]{1,0:T(1,128)S(1)}, f32[1,1024]{1,0:T(1,128)S(1)}, u32[]{:S(2)}, u32[]{:S(2)}) collective-permute-start(f32[1,1024]{1,0:T(1,128)S(1)} %get-tuple-element.113), channel_id=1, source_target_pairs={{0,1},{1,2},{2,3},{3,4},{4,5},{5,6},{6,7},{7,8},{8,9},{9,10},{10,1... | collective-permute-start | bytes 12296 | tf_op jit(solution)/shard_map/ppermute | solution.py:441
  11.4 9.5 %collective-permute-start.3 = (f32[1,1024]{1,0:T(1,128)S(1)}, f32[1,1024]{1,0:T(1,128)S(1)}, u32[]{:S(2)}, u32[]{:S(2)}) collective-permute-start(f32[1,1024]{1,0:T(1,128)S(1)} %get-tuple-element.112), channel_id=1, source_target_pairs={{0,31},{1,0},{2,1},{3,2},{4,3},{5,4},{6,5},{7,6},{8,7},{9,8},{10,9... | collective-permute-start | bytes 12296 | tf_op jit(solution)/shard_map/ppermute | solution.py:441
  22.4 10.8 %all-to-all-start = ((f32[8,1,128]{2,1,0:T(1,128)}), f32[8,1,128]{2,1,0:T(1,128)S(1)}, u32[]{:S(2)}, u32[]{:S(2)}) async-start(f32[8,1,128]{2,1,0:T(1,128)} %regression_sums.1), calls=%async_computation | async-start | bytes 8192 | tf_op jit(solution)/shard_map/all_to_all | solution.py:481
  27.6 9.7 %collective-permute-start.4 = (bf16[64,1024]{1,0:T(8,128)(2,1)}, bf16[64,1024]{1,0:T(8,128)(2,1)S(1)}, u32[]{:S(2)}, u32[]{:S(2)}) collective-permute-start(bf16[64,1024]{1,0:T(8,128)(2,1)} %get-tuple-element.71), channel_id=1, source_target_pairs={{0,32},{32,0},{64,96},{96,64},{128,160},{160,128},{192,224},{224,1... | collective-permute-start | bytes 393224 | tf_op jit(solution)/shard_map/ppermute | solution.py:441
  33.8 12.3 %collective-permute-start.5 = (bf16[64,1024]{1,0:T(8,128)(2,1)}, bf16[64,1024]{1,0:T(8,128)(2,1)S(1)}, u32[]{:S(2)}, u32[]{:S(2)}) collective-permute-start(bf16[64,1024]{1,0:T(8,128)(2,1)} %get-tuple-element.74), channel_id=1, source_target_pairs={{0,128},{32,160},{64,192},{96,224},{128,0},{160,32},{192,64},{224,... | collective-permute-start | bytes 393224 | tf_op jit(solution)/shard_map/ppermute | solution.py:441
  35.2 10.9 %collective-permute-start.6 = (bf16[64,1024]{1,0:T(8,128)(2,1)}, bf16[64,1024]{1,0:T(8,128)(2,1)S(1)}, u32[]{:S(2)}, u32[]{:S(2)}) collective-permute-start(bf16[64,1024]{1,0:T(8,128)(2,1)} %get-tuple-element.75), channel_id=1, source_target_pairs={{0,160},{32,128},{64,224},{96,192},{128,32},{160,0},{192,96},{224,... | collective-permute-start | bytes 393224 | tf_op jit(solution)/shard_map/ppermute | solution.py:441
  35.2 10.9 %collective-permute-start.7 = (bf16[64,1024]{1,0:T(8,128)(2,1)}, bf16[64,1024]{1,0:T(8,128)(2,1)S(1)}, u32[]{:S(2)}, u32[]{:S(2)}) collective-permute-start(bf16[64,1024]{1,0:T(8,128)(2,1)} %get-tuple-element.76), channel_id=1, source_target_pairs={{0,64},{32,96},{64,128},{96,160},{128,192},{160,224},{192,0},{224,... | collective-permute-start | bytes 393224 | tf_op jit(solution)/shard_map/ppermute | solution.py:441
  37.3 8.8 %all-to-all-start.1 = ((f32[4,1,128]{2,1,0:T(1,128)}), f32[4,1,128]{2,1,0:T(1,128)S(1)}, u32[]{:S(2)}, u32[]{:S(2)}) async-start(f32[4,1,128]{2,1,0:T(1,128)} %sum_and_spread.1), calls=%async_computation.1 | async-start | bytes 4096 | tf_op jit(solution)/shard_map/all_to_all | solution.py:527
  41.4 3.2 %copy-start.3 = (bf16[64,1024]{1,0:T(8,128)(2,1)S(1)}, bf16[64,1024]{1,0:T(8,128)(2,1)}, u32[]{:S(2)}) copy-start(bf16[64,1024]{1,0:T(8,128)(2,1)} %get-tuple-element.80) | copy-start | bytes 393220
  41.4 4.7 %copy-start.4 = (bf16[64,1024]{1,0:T(8,128)(2,1)S(1)}, bf16[64,1024]{1,0:T(8,128)(2,1)}, u32[]{:S(2)}) copy-start(bf16[64,1024]{1,0:T(8,128)(2,1)} %get-tuple-element.81) | copy-start | bytes 393220
  43.0 23.3 %copy-start = (bf16[64,1024]{1,0:T(8,128)(2,1)S(1)}, bf16[64,1024]{1,0:T(8,128)(2,1)}, u32[]{:S(2)}) copy-start(bf16[64,1024]{1,0:T(8,128)(2,1)} %get-tuple-element.70.refs_0_) | copy-start | bytes 393220
  43.0 6.8 %collective-permute-start.10 = (bf16[64,1024]{1,0:T(8,128)(2,1)}, bf16[64,1024]{1,0:T(8,128)(2,1)S(1)}, u32[]{:S(2)}, u32[]{:S(2)}) collective-permute-start(bf16[64,1024]{1,0:T(8,128)(2,1)} %get-tuple-element.82), channel_id=1, source_target_pairs={{0,224},{32,192},{64,32},{96,0},{128,96},{160,64},{192,160},{224,1... | collective-permute-start | bytes 393224 | tf_op jit(solution)/shard_map/ppermute | solution.py:441
  44.6 6.6 %collective-permute-start.8 = (bf16[64,1024]{1,0:T(8,128)(2,1)S(1)}, bf16[64,1024]{1,0:T(8,128)(2,1)S(1)}, u32[]{:S(2)}, u32[]{:S(2)}) collective-permute-start(bf16[64,1024]{1,0:T(8,128)(2,1)S(1)} %copy-done.3), channel_id=1, source_target_pairs={{0,96},{32,64},{64,160},{96,128},{128,224},{160,192},{192,32},{224... | collective-permute-start | bytes 393224 | tf_op jit(solution)/shard_map/ppermute | solution.py:441
  46.1 12.4 %collective-permute-start.9 = (bf16[64,1024]{1,0:T(8,128)(2,1)S(1)}, bf16[64,1024]{1,0:T(8,128)(2,1)S(1)}, u32[]{:S(2)}, u32[]{:S(2)}) collective-permute-start(bf16[64,1024]{1,0:T(8,128)(2,1)S(1)} %copy-done.4), channel_id=1, source_target_pairs={{0,192},{32,224},{64,0},{96,32},{128,64},{160,96},{192,128},{224,1... | collective-permute-start | bytes 393224 | tf_op jit(solution)/shard_map/ppermute | solution.py:441
  46.6 11.9 %collective-permute-start.11 = (bf16[64,1024]{1,0:T(8,128)(2,1)S(1)}, bf16[64,1024]{1,0:T(8,128)(2,1)S(1)}, u32[]{:S(2)}, u32[]{:S(2)}) collective-permute-start(bf16[64,1024]{1,0:T(8,128)(2,1)S(1)} %get-tuple-element.88), channel_id=1, source_target_pairs={{0,32},{32,0},{64,96},{96,64},{128,160},{160,128},{192,224},{224,1... | collective-permute-start | bytes 393224 | tf_op jit(solution)/shard_map/ppermute | solution.py:441
  47.1 28.1 %copy-start.2 = (bf16[512,304]{1,0:T(8,128)(2,1)S(1)}, bf16[512,304]{1,0:T(8,128)(2,1)}, u32[]{:S(2)}) copy-start(bf16[512,304]{1,0:T(8,128)(2,1)} %subtract_convert_fusion) | copy-start | bytes 933892
  47.1 12.2 %collective-permute-start.12 = (bf16[64,1024]{1,0:T(8,128)(2,1)S(1)}, bf16[64,1024]{1,0:T(8,128)(2,1)S(1)}, u32[]{:S(2)}, u32[]{:S(2)}) collective-permute-start(bf16[64,1024]{1,0:T(8,128)(2,1)S(1)} %get-tuple-element.89), channel_id=1, source_target_pairs={{0,128},{32,160},{64,192},{96,224},{128,0},{160,32},{192,64},{224,... | collective-permute-start | bytes 393224 | tf_op jit(solution)/shard_map/ppermute | solution.py:441
  49.9 11.0 %collective-permute-start.13 = (bf16[64,1024]{1,0:T(8,128)(2,1)S(1)}, bf16[64,1024]{1,0:T(8,128)(2,1)S(1)}, u32[]{:S(2)}, u32[]{:S(2)}) collective-permute-start(bf16[64,1024]{1,0:T(8,128)(2,1)S(1)} %get-tuple-element.90), channel_id=1, source_target_pairs={{0,160},{32,128},{64,224},{96,192},{128,32},{160,0},{192,96},{224,... | collective-permute-start | bytes 393224 | tf_op jit(solution)/shard_map/ppermute | solution.py:441
  51.2 9.6 %collective-permute-start.14 = (bf16[64,1024]{1,0:T(8,128)(2,1)S(1)}, bf16[64,1024]{1,0:T(8,128)(2,1)S(1)}, u32[]{:S(2)}, u32[]{:S(2)}) collective-permute-start(bf16[64,1024]{1,0:T(8,128)(2,1)S(1)} %get-tuple-element.91), channel_id=1, source_target_pairs={{0,64},{32,96},{64,128},{96,160},{128,192},{160,224},{192,0},{224,... | collective-permute-start | bytes 393224 | tf_op jit(solution)/shard_map/ppermute | solution.py:441
  58.5 5.1 %collective-permute-start.15 = (bf16[64,1024]{1,0:T(8,128)(2,1)S(1)}, bf16[64,1024]{1,0:T(8,128)(2,1)S(1)}, u32[]{:S(2)}, u32[]{:S(2)}) collective-permute-start(bf16[64,1024]{1,0:T(8,128)(2,1)S(1)} %get-tuple-element.92), channel_id=1, source_target_pairs={{0,96},{32,64},{64,160},{96,128},{128,224},{160,192},{192,32},{224... | collective-permute-start | bytes 393224 | tf_op jit(solution)/shard_map/ppermute | solution.py:441
  58.5 7.4 %collective-permute-start.16 = (bf16[64,1024]{1,0:T(8,128)(2,1)S(1)}, bf16[64,1024]{1,0:T(8,128)(2,1)S(1)}, u32[]{:S(2)}, u32[]{:S(2)}) collective-permute-start(bf16[64,1024]{1,0:T(8,128)(2,1)S(1)} %get-tuple-element.93), channel_id=1, source_target_pairs={{0,192},{32,224},{64,0},{96,32},{128,64},{160,96},{192,128},{224,1... | collective-permute-start | bytes 393224 | tf_op jit(solution)/shard_map/ppermute | solution.py:441
  59.3 7.0 %collective-permute-start.17 = (bf16[64,1024]{1,0:T(8,128)(2,1)S(1)}, bf16[64,1024]{1,0:T(8,128)(2,1)S(1)}, u32[]{:S(2)}, u32[]{:S(2)}) collective-permute-start(bf16[64,1024]{1,0:T(8,128)(2,1)S(1)} %get-tuple-element.94), channel_id=1, source_target_pairs={{0,224},{32,192},{64,32},{96,0},{128,96},{160,64},{192,160},{224,1... | collective-permute-start | bytes 393224 | tf_op jit(solution)/shard_map/ppermute | solution.py:441
  68.1 10.8 %collective-permute-start.20 = (bf16[16,304]{1,0:T(8,128)(2,1)S(1)}, bf16[16,304]{1,0:T(8,128)(2,1)S(1)}, u32[]{:S(2)}, u32[]{:S(2)}) collective-permute-start(bf16[16,304]{1,0:T(8,128)(2,1)S(1)} %get-tuple-element.100), channel_id=1, source_target_pairs={{0,32},{32,64},{64,96},{96,128},{128,160},{160,192},{192,224},{224... | collective-permute-start | bytes 29192 | tf_op jit(solution)/shard_map/ppermute | solution.py:441
  69.1 9.7 %collective-permute-start.21 = (bf16[16,304]{1,0:T(8,128)(2,1)S(1)}, bf16[16,304]{1,0:T(8,128)(2,1)S(1)}, u32[]{:S(2)}, u32[]{:S(2)}) collective-permute-start(bf16[16,304]{1,0:T(8,128)(2,1)S(1)} %get-tuple-element.100), channel_id=1, source_target_pairs={{0,224},{32,0},{64,32},{96,64},{128,96},{160,128},{192,160},{224,1... | collective-permute-start | bytes 29192 | tf_op jit(solution)/shard_map/ppermute | solution.py:441
  69.8 9.0 %collective-permute-start.18 = (bf16[304,128]{1,0:T(8,128)(2,1)S(1)}, bf16[304,128]{1,0:T(8,128)(2,1)S(1)}, u32[]{:S(2)}, u32[]{:S(2)}) collective-permute-start(bf16[304,128]{1,0:T(8,128)(2,1)S(1)} %get-tuple-element.98), channel_id=1, source_target_pairs={{0,1},{1,2},{2,3},{3,4},{4,5},{5,6},{6,7},{7,8},{8,9},{9,10},{10,1... | collective-permute-start | bytes 233480 | tf_op jit(solution)/shard_map/ppermute | solution.py:441
  70.4 8.4 %collective-permute-start.19 = (bf16[304,128]{1,0:T(8,128)(2,1)S(1)}, bf16[304,128]{1,0:T(8,128)(2,1)S(1)}, u32[]{:S(2)}, u32[]{:S(2)}) collective-permute-start(bf16[304,128]{1,0:T(8,128)(2,1)S(1)} %get-tuple-element.99), channel_id=1, source_target_pairs={{0,31},{1,0},{2,1},{3,2},{4,3},{5,4},{6,5},{7,6},{8,7},{9,8},{10,9... | collective-permute-start | bytes 233480 | tf_op jit(solution)/shard_map/ppermute | solution.py:441
  79.6 10.5 %collective-permute-start.22 = (bf16[304,128]{1,0:T(8,128)(2,1)S(1)}, bf16[304,128]{1,0:T(8,128)(2,1)S(1)}, u32[]{:S(2)}, u32[]{:S(2)}) collective-permute-start(bf16[304,128]{1,0:T(8,128)(2,1)S(1)} %get-tuple-element.103), channel_id=1, source_target_pairs={{0,1},{1,2},{2,3},{3,4},{4,5},{5,6},{6,7},{7,8},{8,9},{9,10},{10,1... | collective-permute-start | bytes 233480 | tf_op jit(solution)/shard_map/ppermute | solution.py:441
  79.6 10.5 %collective-permute-start.23 = (bf16[304,128]{1,0:T(8,128)(2,1)S(1)}, bf16[304,128]{1,0:T(8,128)(2,1)S(1)}, u32[]{:S(2)}, u32[]{:S(2)}) collective-permute-start(bf16[304,128]{1,0:T(8,128)(2,1)S(1)} %get-tuple-element.104), channel_id=1, source_target_pairs={{0,31},{1,0},{2,1},{3,2},{4,3},{5,4},{6,5},{7,6},{8,7},{9,8},{10,9... | collective-permute-start | bytes 233480 | tf_op jit(solution)/shard_map/ppermute | solution.py:441
  84.9 5.2 %collective-permute-start.24 = (bf16[16,304]{1,0:T(8,128)(2,1)S(1)}, bf16[16,304]{1,0:T(8,128)(2,1)S(1)}, u32[]{:S(2)}, u32[]{:S(2)}) collective-permute-start(bf16[16,304]{1,0:T(8,128)(2,1)S(1)} %get-tuple-element.105), channel_id=1, source_target_pairs={{0,32},{32,64},{64,96},{96,128},{128,160},{160,192},{192,224},{224... | collective-permute-start | bytes 29192 | tf_op jit(solution)/shard_map/ppermute | solution.py:441
  84.9 5.2 %collective-permute-start.25 = (bf16[16,304]{1,0:T(8,128)(2,1)S(1)}, bf16[16,304]{1,0:T(8,128)(2,1)S(1)}, u32[]{:S(2)}, u32[]{:S(2)}) collective-permute-start(bf16[16,304]{1,0:T(8,128)(2,1)S(1)} %get-tuple-element.105), channel_id=1, source_target_pairs={{0,224},{32,0},{64,32},{96,64},{128,96},{160,128},{192,160},{224,1... | collective-permute-start | bytes 29192 | tf_op jit(solution)/shard_map/ppermute | solution.py:441
  90.8 8.2 %collective-permute-start.26 = (bf16[304,128]{1,0:T(8,128)(2,1)S(1)}, bf16[304,128]{1,0:T(8,128)(2,1)S(1)}, u32[]{:S(2)}, u32[]{:S(2)}) collective-permute-start(bf16[304,128]{1,0:T(8,128)(2,1)S(1)} %get-tuple-element.107), channel_id=1, source_target_pairs={{0,1},{1,2},{2,3},{3,4},{4,5},{5,6},{6,7},{7,8},{8,9},{9,10},{10,1... | collective-permute-start | bytes 233480 | tf_op jit(solution)/shard_map/ppermute | solution.py:441
  90.8 4.9 %collective-permute-start.27 = (bf16[16,304]{1,0:T(8,128)(2,1)S(1)}, bf16[16,304]{1,0:T(8,128)(2,1)S(1)}, u32[]{:S(2)}, u32[]{:S(2)}) collective-permute-start(bf16[16,304]{1,0:T(8,128)(2,1)S(1)} %get-tuple-element.108), channel_id=1, source_target_pairs={{0,32},{32,64},{64,96},{96,128},{128,160},{160,192},{192,224},{224... | collective-permute-start | bytes 29192 | tf_op jit(solution)/shard_map/ppermute | solution.py:441
  99.7 1.1 collective-permute-start.28
  100.8 3.5 %collective-permute-start.29 = (f32[1,128]{1,0:T(1,128)S(1)}, f32[1,128]{1,0:T(1,128)S(1)}, u32[]{:S(2)}, u32[]{:S(2)}) collective-permute-start(f32[1,128]{1,0:T(1,128)S(1)} %add.69), channel_id=1, source_target_pairs={{0,64},{32,96},{64,0},{96,32},{128,192},{160,224},{192,128},{224,1... | collective-permute-start | bytes 1544 | tf_op jit(solution)/shard_map/ppermute | solution.py:441
  104.3 5.0 %collective-permute-start.30 = (f32[1,128]{1,0:T(1,128)S(1)}, f32[1,128]{1,0:T(1,128)S(1)}, u32[]{:S(2)}, u32[]{:S(2)}) collective-permute-start(f32[1,128]{1,0:T(1,128)S(1)} %add.70.one), channel_id=1, source_target_pairs={{0,128},{32,160},{64,192},{96,224},{128,0},{160,32},{192,64},{224,... | collective-permute-start | bytes 1544 | tf_op jit(solution)/shard_map/ppermute | solution.py:441

commit v10 on v8

--- a/solution.py
+++ b/solution.py
@@ -89,7 +89,7 @@
     return total
 
 
-OFFSETS = ((0, 0), (0, 1), (2, 0), (2, 1), (1, 0), (1, 1), (3, 0), (3, 1))
+OFFSETS = ((0, 0), (0, 1), (2, 0), (1, 0), (3, 0), (2, 1), (1, 1), (3, 1))
 
 
 def other(index, chips, core):

time: 118 us -> 117 us (level)
  waiting for transfers between devices: 24.2 us -> 20.2 us
  starting transfers between devices: 50.1 us -> 51.4 us
  blocking collectives: 14.4 us -> 15.6 us
    ppermute x29, waiting for transfers between devices: 20.1 us -> 17 us  [permute(): lax.ppermute(values, axis, [(i, target(i)) for i in range(lax.axis_size(a...]
    ppermute x29, starting transfers between devices: 43.2 us -> 44.6 us  [permute(): lax.ppermute(values, axis, [(i, target(i)) for i in range(lax.axis_size(a...]
where the time goes in v10:
time: 117 us
  starting transfers between devices  51.4 us (44%)
  Pallas kernels  25.5 us (22%)
  waiting for transfers between devices  20.2 us (17%)
  blocking collectives  15.6 us (13%)
  local copies, waits for them, and re-layouts  1.48 us (1%)
  other arithmetic  1.4 us (1%)
    ppermute x29, starting transfers between devices, permute(): lax.ppermute(values, axis, [(i, target(i)) for i in range(lax.axis_size(a...  44.6 us
    pallas_call x14, Pallas kernels, call(): pl.pallas_call(body, out_shape=outs, in_specs=[pl.BlockSpec(memory_space=...  25.5 us
    ppermute x29, waiting for transfers between devices, permute(): lax.ppermute(values, axis, [(i, target(i)) for i in range(lax.axis_size(a...  17 us
    all_to_all x1, blocking collectives, per_device(): parts = lax.all_to_all(parts, 'rows', 0, 0, tiled=True)  15.6 us
    all_to_all x1, starting transfers between devices, per_device(): sums = lax.all_to_all(sums, 'rows', 0, 0, tiled=True)  6.81 us
    all_to_all x1, waiting for transfers between devices, per_device(): sums = lax.all_to_all(sums, 'rows', 0, 0, tiled=True)  3.21 us
  transfers between devices with their start and end apart: 30, of which 9 were waited for; matrix products, arithmetic and copies ran while one was open for 2% of the time, Pallas kernels for 13%

profile of v10, /device:TPU:6, one launch (start us, length us, event | category | flops | bytes accessed | tf_op | source)
XLA Modules:
  0.0 116.6 jit_solution(12685651051748509260)
XLA Ops:
  0.7 2.2 %rows_first.1 = (bf16[8,64,1024]{2,1,0:T(8,128)(2,1)S(1)}, bf16[8,64,1024]{2,1,0:T(8,128)(2,1)S(1)}, bf16[128,1024]{1,0:T(8,128)(2,1)S(1)}, bf16[128,1024]{1,0:T(8,128)(2,1)S(1)}) custom-call(bf16[64,8,1024]{2,1,0:T(8,128)(2,1)} %phase.1, bf16[64,8,1024]{2,1,0:T(8,128)(2,1)} %coher.1), custom_call_target="tpu_custom_call" | custom-call | tf_op jit(solution)/shard_map/rows_first/pallas_call | solution.py:30
  2.8 2.0 %collective-permute-start = (bf16[128,1024]{1,0:T(8,128)(2,1)S(1)}, bf16[128,1024]{1,0:T(8,128)(2,1)S(1)}, u32[]{:S(2)}, u32[]{:S(2)}) collective-permute-start(bf16[128,1024]{1,0:T(8,128)(2,1)S(1)} %get-tuple-element.61), channel_id=1, source_target_pairs={{0,1},{1,2},{2,3},{3,4},{4,5},{5,6},{6,7},{7,8},{8,9},{9,10},{10,1... | collective-permute-start | bytes 786440 | tf_op jit(solution)/shard_map/ppermute | solution.py:429
  4.8 6.5 %collective-permute-start.1 = (bf16[128,1024]{1,0:T(8,128)(2,1)S(1)}, bf16[128,1024]{1,0:T(8,128)(2,1)S(1)}, u32[]{:S(2)}, u32[]{:S(2)}) collective-permute-start(bf16[128,1024]{1,0:T(8,128)(2,1)S(1)} %get-tuple-element.62), channel_id=1, source_target_pairs={{0,31},{1,0},{2,1},{3,2},{4,3},{5,4},{6,5},{7,6},{8,7},{9,8},{10,9... | collective-permute-start | bytes 786440 | tf_op jit(solution)/shard_map/ppermute | solution.py:429
  11.6 0.6 gather_fusion
  12.3 3.3 %inner_rows.1 = (f32[8,64,1024]{2,1,0:T(8,128)}, f32[128,128]{1,0:T(8,128)S(1)}, bf16[64,1024]{1,0:T(8,128)(2,1)}, bf16[64,1024]{1,0:T(8,128)(2,1)}, bf16[64,102...) custom-call(bf16[8,64,1024]{2,1,0:T(8,128)(2,1)S(1)} %get-tuple-elem, ...), custom_call_target="tpu_custom_call" | custom-call | tf_op jit(solution)/shard_map/inner_rows/pallas_call | solution.py:30
  15.6 1.9 %collective-permute-done.above = bf16[128,1024]{1,0:T(8,128)(2,1)S(1)} collective-permute-done((bf16[128,1024]{1,0:T(8,128)(2,1)S(1)}, bf16[128,1024]{1,0:T(8,128)(2,1)S(1)}, u32[]{:S(2)}, u32[]{:S(2)}) %collective-permute-start) | collective-permute-done | bytes 262176 | tf_op jit(solution)/shard_map/ppermute | solution.py:429
  17.5 2.5 %border_rows.1 = (f32[8,64,1024]{2,1,0:T(8,128)}, f32[32,1,128]{2,1,0:T(1,128)}, bf16[64,1024]{1,0:T(8,128)(2,1)}, bf16[64,1024]{1,0:T(8,128)(2,1)}, bf16[64,102...) custom-call(bf16[8,64,1024]{2,1,0:T(8,128)(2,1)S(1)} %get-tuple-elem, ...), custom_call_target="tpu_custom_call", output_to_operand_aliasing={{0}: (7, {}), {2}: (8, {}), {3}: (9, {}), {4}: (10, {}), {5... | custom-call | tf_op jit(solution)/shard_map/border_rows/pallas_call | solution.py:30
  20.2 1.5 %collective-permute-start.3 = (bf16[64,1024]{1,0:T(8,128)(2,1)}, bf16[64,1024]{1,0:T(8,128)(2,1)S(1)}, u32[]{:S(2)}, u32[]{:S(2)}) collective-permute-start(bf16[64,1024]{1,0:T(8,128)(2,1)} %get-tuple-element.78), channel_id=1, source_target_pairs={{0,128},{32,160},{64,192},{96,224},{128,0},{160,32},{192,64},{224,... | collective-permute-start | bytes 393224 | tf_op jit(solution)/shard_map/ppermute | solution.py:429
  21.7 2.1 %collective-permute-start.4 = (bf16[64,1024]{1,0:T(8,128)(2,1)}, bf16[64,1024]{1,0:T(8,128)(2,1)S(1)}, u32[]{:S(2)}, u32[]{:S(2)}) collective-permute-start(bf16[64,1024]{1,0:T(8,128)(2,1)} %get-tuple-element.79), channel_id=1, source_target_pairs={{0,64},{32,96},{64,128},{96,160},{128,192},{160,224},{192,0},{224,... | collective-permute-start | bytes 393224 | tf_op jit(solution)/shard_map/ppermute | solution.py:429
  23.8 6.8 %all-to-all-start = ((f32[32,1,128]{2,1,0:T(1,128)}), f32[32,1,128]{2,1,0:T(1,128)S(1)}, u32[]{:S(2)}, u32[]{:S(2)}) async-start(f32[32,1,128]{2,1,0:T(1,128)} %get-tuple-element.77), calls=%async_computation | async-start | bytes 32768 | tf_op jit(solution)/shard_map/all_to_all | solution.py:503
  30.6 1.0 subtract_convert_fusion
  31.5 1.6 %stage.1.smooth = f32[8,64,1024]{2,1,0:T(8,128)S(1)} custom-call(f32[8,64,1024]{2,1,0:T(8,128)} %get-tuple-element.88.source), custom_call_target="tpu_custom_call" | custom-call | tf_op jit(solution)/shard_map/stage/pallas_call | solution.py:30
  33.2 1.1 collective-permute-start.6
  34.2 1.4 %collective-permute-start.7 = (bf16[64,1024]{1,0:T(8,128)(2,1)S(1)}, bf16[64,1024]{1,0:T(8,128)(2,1)S(1)}, u32[]{:S(2)}, u32[]{:S(2)}) collective-permute-start(bf16[64,1024]{1,0:T(8,128)(2,1)S(1)} %copy-done.4), channel_id=1, source_target_pairs={{0,96},{32,64},{64,160},{96,128},{128,224},{160,192},{192,32},{224... | collective-permute-start | bytes 393224 | tf_op jit(solution)/shard_map/ppermute | solution.py:429
  35.6 1.5 %collective-permute-start.8 = (bf16[64,1024]{1,0:T(8,128)(2,1)}, bf16[64,1024]{1,0:T(8,128)(2,1)S(1)}, u32[]{:S(2)}, u32[]{:S(2)}) collective-permute-start(bf16[64,1024]{1,0:T(8,128)(2,1)} %get-tuple-element.86), channel_id=1, source_target_pairs={{0,224},{32,192},{64,32},{96,0},{128,96},{160,64},{192,160},{224,1... | collective-permute-start | bytes 393224 | tf_op jit(solution)/shard_map/ppermute | solution.py:429
  37.2 3.2 %all-to-all-done.sums = f32[32,1,128]{2,1,0:T(1,128)S(1)} async-done(((f32[32,1,128]{2,1,0:T(1,128)}), f32[32,1,128]{2,1,0:T(1,128)S(1)}, u32[]{:S(2)}, u32[]{:S(2)}) %all-to-all-start) | async-done | bytes 16416 | tf_op jit(solution)/shard_map/all_to_all | solution.py:503
  40.4 0.6 correction.1
  40.9 2.1 %collective-permute-start.10 = (bf16[64,1024]{1,0:T(8,128)(2,1)S(1)}, bf16[64,1024]{1,0:T(8,128)(2,1)S(1)}, u32[]{:S(2)}, u32[]{:S(2)}) collective-permute-start(bf16[64,1024]{1,0:T(8,128)(2,1)S(1)} %get-tuple-element.93), channel_id=1, source_target_pairs={{0,128},{32,160},{64,192},{96,224},{128,0},{160,32},{192,64},{224,... | collective-permute-start | bytes 393224 | tf_op jit(solution)/shard_map/ppermute | solution.py:429
  43.1 1.3 %collective-permute-start.11 = (bf16[64,1024]{1,0:T(8,128)(2,1)S(1)}, bf16[64,1024]{1,0:T(8,128)(2,1)S(1)}, u32[]{:S(2)}, u32[]{:S(2)}) collective-permute-start(bf16[64,1024]{1,0:T(8,128)(2,1)S(1)} %get-tuple-element.94), channel_id=1, source_target_pairs={{0,64},{32,96},{64,128},{96,160},{128,192},{160,224},{192,0},{224,... | collective-permute-start | bytes 393224 | tf_op jit(solution)/shard_map/ppermute | solution.py:429
  44.5 0.8 collective-permute-start.12
  45.4 4.4 %collective-permute-start.14 = (bf16[64,1024]{1,0:T(8,128)(2,1)S(1)}, bf16[64,1024]{1,0:T(8,128)(2,1)S(1)}, u32[]{:S(2)}, u32[]{:S(2)}) collective-permute-start(bf16[64,1024]{1,0:T(8,128)(2,1)S(1)} %get-tuple-element.97), channel_id=1, source_target_pairs={{0,96},{32,64},{64,160},{96,128},{128,224},{160,192},{192,32},{224... | collective-permute-start | bytes 393224 | tf_op jit(solution)/shard_map/ppermute | solution.py:429
  49.9 0.5 slice_bitcast_fusion
  50.4 3.2 %collective-permute-done.12.refs_12_ = bf16[64,1024]{1,0:T(8,128)(2,1)S(1)} collective-permute-done((bf16[64,1024]{1,0:T(8,128)(2,1)S(1)}, bf16[64,1024]{1,0:T(8,128)(2,1)S(1)}, u32[]{:S(2)}, u32[]{:S(2)}) %collective-permute-start.12) | collective-permute-done | bytes 131104 | tf_op jit(solution)/shard_map/ppermute | solution.py:429
  53.6 1.6 %collective-permute-done.14.refs_14_ = bf16[64,1024]{1,0:T(8,128)(2,1)S(1)} collective-permute-done((bf16[64,1024]{1,0:T(8,128)(2,1)S(1)}, bf16[64,1024]{1,0:T(8,128)(2,1)S(1)}, u32[]{:S(2)}, u32[]{:S(2)}) %collective-permute-start.14) | collective-permute-done | bytes 131104 | tf_op jit(solution)/shard_map/ppermute | solution.py:429
  55.2 1.2 %collective-permute-done.15.refs_15_ = bf16[64,1024]{1,0:T(8,128)(2,1)S(1)} collective-permute-done((bf16[64,1024]{1,0:T(8,128)(2,1)S(1)}, bf16[64,1024]{1,0:T(8,128)(2,1)S(1)}, u32[]{:S(2)}, u32[]{:S(2)}) %collective-permute-start.15) | collective-permute-done | bytes 131104 | tf_op jit(solution)/shard_map/ppermute | solution.py:429
  56.4 1.8 %right_side.1 = (f32[304,1024]{1,0:T(8,128)S(1)}, bf16[512,1024]{1,0:T(8,128)(2,1)S(1)}, bf16[304,128]{1,0:T(8,128)(2,1)S(1)}, bf16[16,304]{1,0:T(8,128)(2,1)S(1)}, bf16[304,128]{1,0:T(8,128)(2,1)S(1)}) custom-call(bf16[64,1024]{1,0:T(8,128)(2,1)S(1)} %copy-done, bf16[64,1024]{1,0:T(8,128)(2,1)S(1)} %collective-permute-done.2.refs_1_, ...), custom_call_target="tpu_custom_call" | custom-call | tf_op jit(solution)/shard_map/right_side/pallas_call | solution.py:30
  58.2 1.7 %collective-permute-start.19 = (bf16[16,304]{1,0:T(8,128)(2,1)S(1)}, bf16[16,304]{1,0:T(8,128)(2,1)S(1)}, u32[]{:S(2)}, u32[]{:S(2)}) collective-permute-start(bf16[16,304]{1,0:T(8,128)(2,1)S(1)} %get-tuple-element.104), channel_id=1, source_target_pairs={{0,224},{32,0},{64,32},{96,64},{128,96},{160,128},{192,160},{224,1... | collective-permute-start | bytes 29192 | tf_op jit(solution)/shard_map/ppermute | solution.py:429
  59.9 0.7 collective-permute-start.16
  60.6 4.6 %collective-permute-start.17 = (bf16[304,128]{1,0:T(8,128)(2,1)S(1)}, bf16[304,128]{1,0:T(8,128)(2,1)S(1)}, u32[]{:S(2)}, u32[]{:S(2)}) collective-permute-start(bf16[304,128]{1,0:T(8,128)(2,1)S(1)} %get-tuple-element.103), channel_id=1, source_target_pairs={{0,31},{1,0},{2,1},{3,2},{4,3},{5,4},{6,5},{7,6},{8,7},{9,8},{10,9... | collective-permute-start | bytes 233480 | tf_op jit(solution)/shard_map/ppermute | solution.py:429
  65.3 0.3 pad_maximum_fusion.refs_2_
  65.6 3.4 %apply0.1 = (f32[304,1024]{1,0:T(8,128)S(1)}, f32[3,8,128]{2,1,0:T(8,128)S(1)}) custom-call(f32[304,1024]{1,0:T(8,128)S(1)} %get-tuple-element.99.refs_0_.refs_4_.basis.zero, bf16[512,1024]{1,0:T(8,128)(2,1)S(1)} %get-tuple-element.100.refs_1_, bf16[512,608]{1,0:T(8,128)(2,1)S(1)} %pad_maximum_fusion.refs_2_, ...), custom_call_target="tpu_custom_call" | custom-call | tf_op jit(solution)/shard_map/apply0/pallas_call | solution.py:30
  69.0 0.7 add_halo1.1
  69.7 5.4 %collective-permute-start.21 = (bf16[304,128]{1,0:T(8,128)(2,1)S(1)}, bf16[304,128]{1,0:T(8,128)(2,1)S(1)}, u32[]{:S(2)}, u32[]{:S(2)}) collective-permute-start(bf16[304,128]{1,0:T(8,128)(2,1)S(1)} %get-tuple-element.108), channel_id=1, source_target_pairs={{0,31},{1,0},{2,1},{3,2},{4,3},{5,4},{6,5},{7,6},{8,7},{9,8},{10,9... | collective-permute-start | bytes 233480 | tf_op jit(solution)/shard_map/ppermute | solution.py:429
  75.1 1.7 %collective-permute-start.23 = (bf16[16,304]{1,0:T(8,128)(2,1)S(1)}, bf16[16,304]{1,0:T(8,128)(2,1)S(1)}, u32[]{:S(2)}, u32[]{:S(2)}) collective-permute-start(bf16[16,304]{1,0:T(8,128)(2,1)S(1)} %get-tuple-element.109), channel_id=1, source_target_pairs={{0,224},{32,0},{64,32},{96,64},{128,96},{160,128},{192,160},{224,1... | collective-permute-start | bytes 29192 | tf_op jit(solution)/shard_map/ppermute | solution.py:429
  76.8 3.4 %apply1.1 = (f32[304,1024]{1,0:T(8,128)S(1)}, f32[3,8,128]{2,1,0:T(8,128)S(1)}) custom-call(f32[304,1024]{1,0:T(8,128)S(1)} %get-tuple-element.105.refs_0_.refs_4_.one, bf16[512,1024]{1,0:T(8,128)(2,1)S(1)} %get-tuple-element.100.refs_1_, bf16[512,608]{1,0:T(8,128)(2,1)S(1)} %pad_maximum_fusion.refs_2_, ...), custom_call_target="tpu_custom_call" | custom-call | tf_op jit(solution)/shard_map/apply1/pallas_call | solution.py:30
  80.2 0.7 add_halo2.1
  81.0 0.2 collective-permute-start.24
  81.2 1.8 %collective-permute-start.25 = (bf16[16,304]{1,0:T(8,128)(2,1)S(1)}, bf16[16,304]{1,0:T(8,128)(2,1)S(1)}, u32[]{:S(2)}, u32[]{:S(2)}) collective-permute-start(bf16[16,304]{1,0:T(8,128)(2,1)S(1)} %get-tuple-element.112), channel_id=1, source_target_pairs={{0,32},{32,64},{64,96},{96,128},{128,160},{160,192},{192,224},{224... | collective-permute-start | bytes 29192 | tf_op jit(solution)/shard_map/ppermute | solution.py:429
  83.0 3.5 %apply2.1.two = f32[3,8,128]{2,1,0:T(8,128)S(1)} custom-call(f32[304,1024]{1,0:T(8,128)S(1)} %get-tuple-element.110.refs_0_.field.two, bf16[512,1024]{1,0:T(8,128)(2,1)S(1)} %get-tuple-element.100.refs_1_, bf16[512,608]{1,0:T(8,128)(2,1)S(1)} %pad_maximum_fusion.refs_2_, bf16[304,512]{1,0:T(8,128)(2,1)S(1)} %subtract_convert_fusion.1.refs_16_.refs_3_, ...), custom_call_target="tpu_custom_call" | custom-call | tf_op jit(solution)/shard_map/apply2/pallas_call | solution.py:30
  86.4 2.5 %collective-permute-done.24.above = bf16[304,128]{1,0:T(8,128)(2,1)S(1)} collective-permute-done((bf16[304,128]{1,0:T(8,128)(2,1)S(1)}, bf16[304,128]{1,0:T(8,128)(2,1)S(1)}, u32[]{:S(2)}, u32[]{:S(2)}) %collective-permute-start.24) | collective-permute-done | bytes 77856 | tf_op jit(solution)/shard_map/ppermute | solution.py:429
  88.9 0.6 all_moments.1
  89.5 0.6 collective-permute-start.26
  90.1 0.8 collective-permute-done.26
  91.0 3.5 %collective-permute-done.27 = f32[1,128]{1,0:T(1,128)S(1)} collective-permute-done((f32[1,128]{1,0:T(1,128)S(1)}, f32[1,128]{1,0:T(1,128)S(1)}, u32[]{:S(2)}, u32[]{:S(2)}) %collective-permute-start.27) | collective-permute-done | bytes 544 | tf_op jit(solution)/shard_map/ppermute | solution.py:429
  94.5 2.8 %collective-permute-start.28 = (f32[1,128]{1,0:T(1,128)S(1)}, f32[1,128]{1,0:T(1,128)S(1)}, u32[]{:S(2)}, u32[]{:S(2)}) collective-permute-start(f32[1,128]{1,0:T(1,128)S(1)} %add.70.one), channel_id=1, source_target_pairs={{0,128},{32,160},{64,192},{96,224},{128,0},{160,32},{192,64},{224,... | collective-permute-start | bytes 1544 | tf_op jit(solution)/shard_map/ppermute | solution.py:429
  97.3 2.2 %collective-permute-done.28.two = f32[1,128]{1,0:T(1,128)S(1)} collective-permute-done((f32[1,128]{1,0:T(1,128)S(1)}, f32[1,128]{1,0:T(1,128)S(1)}, u32[]{:S(2)}, u32[]{:S(2)}) %collective-permute-start.28) | collective-permute-done | bytes 544 | tf_op jit(solution)/shard_map/ppermute | solution.py:429
  99.6 15.6 %all_to_all.10.parts = f32[32,1,128]{2,1,0:T(1,128)S(1)} all-to-all(f32[32,1,128]{2,1,0:T(1,128)S(1)} %add_and_spread.1), channel_id=1, replica_groups=mesh['ifg'=8,'rows'=32] {'rows'}, dimensions={0} | all-to-all | bytes 32768 | tf_op jit(solution)/shard_map/all_to_all | solution.py:588
  115.1 1.3 %combine.1 = f32[2400,128]{1,0:T(8,128)} custom-call(f32[32,1,128]{2,1,0:T(1,128)S(1)} %all_to_all.10.parts, f32[304,1024]{1,0:T(8,128)S(1)} %get-tuple-element.99.refs_0_.refs_4_.basis.zero, f32[304,1024]{1,0:T(8,128)S(1)} %get-tuple-element.105.refs_0_.refs_4_.one, f32[304,1024]{1,0:T(8,128)S(1)} %get-tuple-element.110.refs_0_.field.two), custom_call_target="tpu_custom_call" | custom-call | tf_op jit(solution)/shard_map/combine/pallas_call | solution.py:30
  (58 shorter events, 0.9 us)
Async XLA Ops:
  0.6 10.7 %copy-start.5 = (s32[64,8]{0,1:T(8,128)S(1)}, s32[64,8]{0,1:T(8,128)}, u32[]{:S(2)}) copy-start(s32[64,8]{0,1:T(8,128)} %param.8) | copy-start | bytes 6148
  0.6 10.8 %copy-start.6 = (s32[512,2]{0,1:T(2,128)S(1)}, s32[512,2]{0,1:T(2,128)}, u32[]{:S(2)}) copy-start(s32[512,2]{0,1:T(2,128)} %param.9) | copy-start | bytes 12292
  0.7 11.6 %copy-start.1 = (f32[8,1024]{1,0:T(8,128)S(1)}, f32[8,1024]{1,0:T(8,128)}, u32[]{:S(2)}) copy-start(f32[8,1024]{1,0:T(8,128)} %height.5) | copy-start | bytes 98308
  2.8 14.7 %collective-permute-start = (bf16[128,1024]{1,0:T(8,128)(2,1)S(1)}, bf16[128,1024]{1,0:T(8,128)(2,1)S(1)}, u32[]{:S(2)}, u32[]{:S(2)}) collective-permute-start(bf16[128,1024]{1,0:T(8,128)(2,1)S(1)} %get-tuple-element.61), channel_id=1, source_target_pairs={{0,1},{1,2},{2,3},{3,4},{4,5},{5,6},{6,7},{7,8},{8,9},{9,10},{10,1... | collective-permute-start | bytes 786440 | tf_op jit(solution)/shard_map/ppermute | solution.py:429
  4.8 12.7 %collective-permute-start.1 = (bf16[128,1024]{1,0:T(8,128)(2,1)S(1)}, bf16[128,1024]{1,0:T(8,128)(2,1)S(1)}, u32[]{:S(2)}, u32[]{:S(2)}) collective-permute-start(bf16[128,1024]{1,0:T(8,128)(2,1)S(1)} %get-tuple-element.62), channel_id=1, source_target_pairs={{0,31},{1,0},{2,1},{3,2},{4,3},{5,4},{6,5},{7,6},{8,7},{9,8},{10,9... | collective-permute-start | bytes 786440 | tf_op jit(solution)/shard_map/ppermute | solution.py:429
  20.1 3.7 %collective-permute-start.2 = (bf16[64,1024]{1,0:T(8,128)(2,1)}, bf16[64,1024]{1,0:T(8,128)(2,1)S(1)}, u32[]{:S(2)}, u32[]{:S(2)}) collective-permute-start(bf16[64,1024]{1,0:T(8,128)(2,1)} %get-tuple-element.75), channel_id=1, source_target_pairs={{0,32},{32,0},{64,96},{96,64},{128,160},{160,128},{192,224},{224,1... | collective-permute-start | bytes 393224 | tf_op jit(solution)/shard_map/ppermute | solution.py:429
  20.2 15.5 %collective-permute-start.3 = (bf16[64,1024]{1,0:T(8,128)(2,1)}, bf16[64,1024]{1,0:T(8,128)(2,1)S(1)}, u32[]{:S(2)}, u32[]{:S(2)}) collective-permute-start(bf16[64,1024]{1,0:T(8,128)(2,1)} %get-tuple-element.78), channel_id=1, source_target_pairs={{0,128},{32,160},{64,192},{96,224},{128,0},{160,32},{192,64},{224,... | collective-permute-start | bytes 393224 | tf_op jit(solution)/shard_map/ppermute | solution.py:429
  21.7 15.5 %collective-permute-start.4 = (bf16[64,1024]{1,0:T(8,128)(2,1)}, bf16[64,1024]{1,0:T(8,128)(2,1)S(1)}, u32[]{:S(2)}, u32[]{:S(2)}) collective-permute-start(bf16[64,1024]{1,0:T(8,128)(2,1)} %get-tuple-element.79), channel_id=1, source_target_pairs={{0,64},{32,96},{64,128},{96,160},{128,192},{160,224},{192,0},{224,... | collective-permute-start | bytes 393224 | tf_op jit(solution)/shard_map/ppermute | solution.py:429
  23.8 13.4 %collective-permute-start.5 = (bf16[64,1024]{1,0:T(8,128)(2,1)}, bf16[64,1024]{1,0:T(8,128)(2,1)S(1)}, u32[]{:S(2)}, u32[]{:S(2)}) collective-permute-start(bf16[64,1024]{1,0:T(8,128)(2,1)} %get-tuple-element.80), channel_id=1, source_target_pairs={{0,192},{32,224},{64,0},{96,32},{128,64},{160,96},{192,128},{224,1... | collective-permute-start | bytes 393224 | tf_op jit(solution)/shard_map/ppermute | solution.py:429
  23.8 16.6 %all-to-all-start = ((f32[32,1,128]{2,1,0:T(1,128)}), f32[32,1,128]{2,1,0:T(1,128)S(1)}, u32[]{:S(2)}, u32[]{:S(2)}) async-start(f32[32,1,128]{2,1,0:T(1,128)} %get-tuple-element.77), calls=%async_computation | async-start | bytes 32768 | tf_op jit(solution)/shard_map/all_to_all | solution.py:503
  31.5 1.6 %copy-start.3 = (bf16[64,1024]{1,0:T(8,128)(2,1)S(1)}, bf16[64,1024]{1,0:T(8,128)(2,1)}, u32[]{:S(2)}) copy-start(bf16[64,1024]{1,0:T(8,128)(2,1)} %get-tuple-element.84) | copy-start | bytes 393220
  31.5 2.7 %copy-start.4 = (bf16[64,1024]{1,0:T(8,128)(2,1)S(1)}, bf16[64,1024]{1,0:T(8,128)(2,1)}, u32[]{:S(2)}) copy-start(bf16[64,1024]{1,0:T(8,128)(2,1)} %get-tuple-element.85) | copy-start | bytes 393220
  33.1 23.3 %copy-start = (bf16[64,1024]{1,0:T(8,128)(2,1)S(1)}, bf16[64,1024]{1,0:T(8,128)(2,1)}, u32[]{:S(2)}) copy-start(bf16[64,1024]{1,0:T(8,128)(2,1)} %get-tuple-element.73.refs_0_) | copy-start | bytes 393220
  33.2 11.3 %collective-permute-start.6 = (bf16[64,1024]{1,0:T(8,128)(2,1)S(1)}, bf16[64,1024]{1,0:T(8,128)(2,1)S(1)}, u32[]{:S(2)}, u32[]{:S(2)}) collective-permute-start(bf16[64,1024]{1,0:T(8,128)(2,1)S(1)} %copy-done.3), channel_id=1, source_target_pairs={{0,160},{32,128},{64,224},{96,192},{128,32},{160,0},{192,96},{224,... | collective-permute-start | bytes 393224 | tf_op jit(solution)/shard_map/ppermute | solution.py:429
  34.2 11.1 %collective-permute-start.7 = (bf16[64,1024]{1,0:T(8,128)(2,1)S(1)}, bf16[64,1024]{1,0:T(8,128)(2,1)S(1)}, u32[]{:S(2)}, u32[]{:S(2)}) collective-permute-start(bf16[64,1024]{1,0:T(8,128)(2,1)S(1)} %copy-done.4), channel_id=1, source_target_pairs={{0,96},{32,64},{64,160},{96,128},{128,224},{160,192},{192,32},{224... | collective-permute-start | bytes 393224 | tf_op jit(solution)/shard_map/ppermute | solution.py:429
  35.6 9.7 %collective-permute-start.8 = (bf16[64,1024]{1,0:T(8,128)(2,1)}, bf16[64,1024]{1,0:T(8,128)(2,1)S(1)}, u32[]{:S(2)}, u32[]{:S(2)}) collective-permute-start(bf16[64,1024]{1,0:T(8,128)(2,1)} %get-tuple-element.86), channel_id=1, source_target_pairs={{0,224},{32,192},{64,32},{96,0},{128,96},{160,64},{192,160},{224,1... | collective-permute-start | bytes 393224 | tf_op jit(solution)/shard_map/ppermute | solution.py:429
  40.9 8.9 %collective-permute-start.10 = (bf16[64,1024]{1,0:T(8,128)(2,1)S(1)}, bf16[64,1024]{1,0:T(8,128)(2,1)S(1)}, u32[]{:S(2)}, u32[]{:S(2)}) collective-permute-start(bf16[64,1024]{1,0:T(8,128)(2,1)S(1)} %get-tuple-element.93), channel_id=1, source_target_pairs={{0,128},{32,160},{64,192},{96,224},{128,0},{160,32},{192,64},{224,... | collective-permute-start | bytes 393224 | tf_op jit(solution)/shard_map/ppermute | solution.py:429
  43.1 22.2 %copy-start.2 = (bf16[512,304]{1,0:T(8,128)(2,1)S(1)}, bf16[512,304]{1,0:T(8,128)(2,1)}, u32[]{:S(2)}) copy-start(bf16[512,304]{1,0:T(8,128)(2,1)} %subtract_convert_fusion) | copy-start | bytes 933892
  43.1 6.7 %collective-permute-start.11 = (bf16[64,1024]{1,0:T(8,128)(2,1)S(1)}, bf16[64,1024]{1,0:T(8,128)(2,1)S(1)}, u32[]{:S(2)}, u32[]{:S(2)}) collective-permute-start(bf16[64,1024]{1,0:T(8,128)(2,1)S(1)} %get-tuple-element.94), channel_id=1, source_target_pairs={{0,64},{32,96},{64,128},{96,160},{128,192},{160,224},{192,0},{224,... | collective-permute-start | bytes 393224 | tf_op jit(solution)/shard_map/ppermute | solution.py:429
  44.5 9.1 %collective-permute-start.12 = (bf16[64,1024]{1,0:T(8,128)(2,1)S(1)}, bf16[64,1024]{1,0:T(8,128)(2,1)S(1)}, u32[]{:S(2)}, u32[]{:S(2)}) collective-permute-start(bf16[64,1024]{1,0:T(8,128)(2,1)S(1)} %get-tuple-element.95), channel_id=1, source_target_pairs={{0,192},{32,224},{64,0},{96,32},{128,64},{160,96},{192,128},{224,1... | collective-permute-start | bytes 393224 | tf_op jit(solution)/shard_map/ppermute | solution.py:429
  45.4 8.2 %collective-permute-start.13 = (bf16[64,1024]{1,0:T(8,128)(2,1)S(1)}, bf16[64,1024]{1,0:T(8,128)(2,1)S(1)}, u32[]{:S(2)}, u32[]{:S(2)}) collective-permute-start(bf16[64,1024]{1,0:T(8,128)(2,1)S(1)} %get-tuple-element.96), channel_id=1, source_target_pairs={{0,160},{32,128},{64,224},{96,192},{128,32},{160,0},{192,96},{224,... | collective-permute-start | bytes 393224 | tf_op jit(solution)/shard_map/ppermute | solution.py:429
  45.4 9.8 %collective-permute-start.14 = (bf16[64,1024]{1,0:T(8,128)(2,1)S(1)}, bf16[64,1024]{1,0:T(8,128)(2,1)S(1)}, u32[]{:S(2)}, u32[]{:S(2)}) collective-permute-start(bf16[64,1024]{1,0:T(8,128)(2,1)S(1)} %get-tuple-element.97), channel_id=1, source_target_pairs={{0,96},{32,64},{64,160},{96,128},{128,224},{160,192},{192,32},{224... | collective-permute-start | bytes 393224 | tf_op jit(solution)/shard_map/ppermute | solution.py:429
  49.8 6.6 %collective-permute-start.15 = (bf16[64,1024]{1,0:T(8,128)(2,1)S(1)}, bf16[64,1024]{1,0:T(8,128)(2,1)S(1)}, u32[]{:S(2)}, u32[]{:S(2)}) collective-permute-start(bf16[64,1024]{1,0:T(8,128)(2,1)S(1)} %get-tuple-element.98), channel_id=1, source_target_pairs={{0,224},{32,192},{64,32},{96,0},{128,96},{160,64},{192,160},{224,1... | collective-permute-start | bytes 393224 | tf_op jit(solution)/shard_map/ppermute | solution.py:429
  49.8 6.6 %collective-permute-start.9 = (bf16[64,1024]{1,0:T(8,128)(2,1)S(1)}, bf16[64,1024]{1,0:T(8,128)(2,1)S(1)}, u32[]{:S(2)}, u32[]{:S(2)}) collective-permute-start(bf16[64,1024]{1,0:T(8,128)(2,1)S(1)} %get-tuple-element.92), channel_id=1, source_target_pairs={{0,32},{32,0},{64,96},{96,64},{128,160},{160,128},{192,224},{224,1... | collective-permute-start | bytes 393224 | tf_op jit(solution)/shard_map/ppermute | solution.py:429
  58.2 10.8 %collective-permute-start.18 = (bf16[16,304]{1,0:T(8,128)(2,1)S(1)}, bf16[16,304]{1,0:T(8,128)(2,1)S(1)}, u32[]{:S(2)}, u32[]{:S(2)}) collective-permute-start(bf16[16,304]{1,0:T(8,128)(2,1)S(1)} %get-tuple-element.104), channel_id=1, source_target_pairs={{0,32},{32,64},{64,96},{96,128},{128,160},{160,192},{192,224},{224... | collective-permute-start | bytes 29192 | tf_op jit(solution)/shard_map/ppermute | solution.py:429
  58.2 10.7 %collective-permute-start.19 = (bf16[16,304]{1,0:T(8,128)(2,1)S(1)}, bf16[16,304]{1,0:T(8,128)(2,1)S(1)}, u32[]{:S(2)}, u32[]{:S(2)}) collective-permute-start(bf16[16,304]{1,0:T(8,128)(2,1)S(1)} %get-tuple-element.104), channel_id=1, source_target_pairs={{0,224},{32,0},{64,32},{96,64},{128,96},{160,128},{192,160},{224,1... | collective-permute-start | bytes 29192 | tf_op jit(solution)/shard_map/ppermute | solution.py:429
  59.9 9.0 %collective-permute-start.16 = (bf16[304,128]{1,0:T(8,128)(2,1)S(1)}, bf16[304,128]{1,0:T(8,128)(2,1)S(1)}, u32[]{:S(2)}, u32[]{:S(2)}) collective-permute-start(bf16[304,128]{1,0:T(8,128)(2,1)S(1)} %get-tuple-element.102), channel_id=1, source_target_pairs={{0,1},{1,2},{2,3},{3,4},{4,5},{5,6},{6,7},{7,8},{8,9},{9,10},{10,1... | collective-permute-start | bytes 233480 | tf_op jit(solution)/shard_map/ppermute | solution.py:429
  60.6 8.3 %collective-permute-start.17 = (bf16[304,128]{1,0:T(8,128)(2,1)S(1)}, bf16[304,128]{1,0:T(8,128)(2,1)S(1)}, u32[]{:S(2)}, u32[]{:S(2)}) collective-permute-start(bf16[304,128]{1,0:T(8,128)(2,1)S(1)} %get-tuple-element.103), channel_id=1, source_target_pairs={{0,31},{1,0},{2,1},{3,2},{4,3},{5,4},{6,5},{7,6},{8,7},{9,8},{10,9... | collective-permute-start | bytes 233480 | tf_op jit(solution)/shard_map/ppermute | solution.py:429
  69.7 10.5 %collective-permute-start.20 = (bf16[304,128]{1,0:T(8,128)(2,1)S(1)}, bf16[304,128]{1,0:T(8,128)(2,1)S(1)}, u32[]{:S(2)}, u32[]{:S(2)}) collective-permute-start(bf16[304,128]{1,0:T(8,128)(2,1)S(1)} %get-tuple-element.107), channel_id=1, source_target_pairs={{0,1},{1,2},{2,3},{3,4},{4,5},{5,6},{6,7},{7,8},{8,9},{9,10},{10,1... | collective-permute-start | bytes 233480 | tf_op jit(solution)/shard_map/ppermute | solution.py:429
  69.7 10.5 %collective-permute-start.21 = (bf16[304,128]{1,0:T(8,128)(2,1)S(1)}, bf16[304,128]{1,0:T(8,128)(2,1)S(1)}, u32[]{:S(2)}, u32[]{:S(2)}) collective-permute-start(bf16[304,128]{1,0:T(8,128)(2,1)S(1)} %get-tuple-element.108), channel_id=1, source_target_pairs={{0,31},{1,0},{2,1},{3,2},{4,3},{5,4},{6,5},{7,6},{8,7},{9,8},{10,9... | collective-permute-start | bytes 233480 | tf_op jit(solution)/shard_map/ppermute | solution.py:429
  75.0 5.2 %collective-permute-start.22 = (bf16[16,304]{1,0:T(8,128)(2,1)S(1)}, bf16[16,304]{1,0:T(8,128)(2,1)S(1)}, u32[]{:S(2)}, u32[]{:S(2)}) collective-permute-start(bf16[16,304]{1,0:T(8,128)(2,1)S(1)} %get-tuple-element.109), channel_id=1, source_target_pairs={{0,32},{32,64},{64,96},{96,128},{128,160},{160,192},{192,224},{224... | collective-permute-start | bytes 29192 | tf_op jit(solution)/shard_map/ppermute | solution.py:429
  75.1 5.2 %collective-permute-start.23 = (bf16[16,304]{1,0:T(8,128)(2,1)S(1)}, bf16[16,304]{1,0:T(8,128)(2,1)S(1)}, u32[]{:S(2)}, u32[]{:S(2)}) collective-permute-start(bf16[16,304]{1,0:T(8,128)(2,1)S(1)} %get-tuple-element.109), channel_id=1, source_target_pairs={{0,224},{32,0},{64,32},{96,64},{128,96},{160,128},{192,160},{224,1... | collective-permute-start | bytes 29192 | tf_op jit(solution)/shard_map/ppermute | solution.py:429
  81.0 8.0 %collective-permute-start.24 = (bf16[304,128]{1,0:T(8,128)(2,1)S(1)}, bf16[304,128]{1,0:T(8,128)(2,1)S(1)}, u32[]{:S(2)}, u32[]{:S(2)}) collective-permute-start(bf16[304,128]{1,0:T(8,128)(2,1)S(1)} %get-tuple-element.111), channel_id=1, source_target_pairs={{0,1},{1,2},{2,3},{3,4},{4,5},{5,6},{6,7},{7,8},{8,9},{9,10},{10,1... | collective-permute-start | bytes 233480 | tf_op jit(solution)/shard_map/ppermute | solution.py:429
  81.2 5.3 %collective-permute-start.25 = (bf16[16,304]{1,0:T(8,128)(2,1)S(1)}, bf16[16,304]{1,0:T(8,128)(2,1)S(1)}, u32[]{:S(2)}, u32[]{:S(2)}) collective-permute-start(bf16[16,304]{1,0:T(8,128)(2,1)S(1)} %get-tuple-element.112), channel_id=1, source_target_pairs={{0,32},{32,64},{64,96},{96,128},{128,160},{160,192},{192,224},{224... | collective-permute-start | bytes 29192 | tf_op jit(solution)/shard_map/ppermute | solution.py:429
  89.5 1.5 %collective-permute-start.26 = (f32[1,128]{1,0:T(1,128)S(1)}, f32[1,128]{1,0:T(1,128)S(1)}, u32[]{:S(2)}, u32[]{:S(2)}) collective-permute-start(f32[1,128]{1,0:T(1,128)S(1)} %all_moments.1), channel_id=1, source_target_pairs={{0,32},{32,0},{64,96},{96,64},{128,160},{160,128},{192,224},{224,1... | collective-permute-start | bytes 1544 | tf_op jit(solution)/shard_map/ppermute | solution.py:429
  91.0 3.5 %collective-permute-start.27 = (f32[1,128]{1,0:T(1,128)S(1)}, f32[1,128]{1,0:T(1,128)S(1)}, u32[]{:S(2)}, u32[]{:S(2)}) collective-permute-start(f32[1,128]{1,0:T(1,128)S(1)} %add.69), channel_id=1, source_target_pairs={{0,64},{32,96},{64,0},{96,32},{128,192},{160,224},{192,128},{224,1... | collective-permute-start | bytes 1544 | tf_op jit(solution)/shard_map/ppermute | solution.py:429
  94.5 5.0 %collective-permute-start.28 = (f32[1,128]{1,0:T(1,128)S(1)}, f32[1,128]{1,0:T(1,128)S(1)}, u32[]{:S(2)}, u32[]{:S(2)}) collective-permute-start(f32[1,128]{1,0:T(1,128)S(1)} %add.70.one), channel_id=1, source_target_pairs={{0,128},{32,160},{64,192},{96,224},{128,0},{160,32},{192,64},{224,... | collective-permute-start | bytes 1544 | tf_op jit(solution)/shard_map/ppermute | solution.py:429

commit v11 on v10

--- a/solution.py
+++ b/solution.py
@@ -279,12 +279,17 @@
     return pl.ds(pl.multiple_of(row * 128, 128), 128)
 
 
-def local_image(field, weights, design, design_t, chunk):
+def local_image(field, weights, design, design_t, chunk, with_image):
     lanes = pl.ds(pl.multiple_of(chunk * 256, 256), 256)
     high, low = split(field[:, lanes])
-    scaled = dot(design[...], jnp.concatenate([high, low], axis=0)) * weights[:, lanes].astype(F32)
-    high, low = split(scaled)
-    back = dot(design_t[...], high) + dot(design_t[...], low)
+    across = dot(design[...], jnp.concatenate([high, low], axis=0))
+    scaled = across * weights[:, lanes].astype(F32)
+    back, square = None, None
+    if with_image:
+        high, low = split(scaled)
+        back = dot(design_t[...], high) + dot(design_t[...], low)
+    else:
+        square = across * scaled
     lane = lax.broadcasted_iota(jnp.int32, (DP, 128), 1)
     parts = []
     for offset in range(2):
@@ -294,13 +299,15 @@
         around += jnp.where(lane == 127, 0.0, pltpu.roll(here, 127, 1))
         around += jnp.where(row > 0, field[:, row_lanes(jnp.maximum(row - 1, 0))], 0.0)
         around += jnp.where(row < 7, field[:, row_lanes(jnp.minimum(row + 1, 7))], 0.0)
-        part = back[:, offset * 128 : offset * 128 + 128] + CENTRE * here - SMOOTHING_WEIGHT * around
+        part = CENTRE * here - SMOOTHING_WEIGHT * around
+        if with_image:
+            part = back[:, offset * 128 : offset * 128 + 128] + part
         parts.append((row, part))
-    return parts
+    return parts, square
 
 
 def fold(values):
-    return jnp.sum(values.reshape(DP // 8, 8, 128), axis=0)
+    return jnp.sum(values.reshape(-1, 8, 128), axis=0)
 
 
 def apply_local(with_before, with_image, *refs):
@@ -316,7 +323,10 @@
 
     def one_chunk(chunk, totals):
         square, cross, ahead = totals
-        for row, part in local_image(field, weights, design, design_t, chunk):
+        parts, across = local_image(field, weights, design, design_t, chunk, with_image)
+        if not with_image:
+            ahead += fold(across[:, :128]) + fold(across[:, 128:])
+        for row, part in parts:
             here = field[:, row_lanes(row)]
             square += fold(here * here)
             if with_before:

time: 117 us -> 116 us (level); the launches traced: 117 us -> 114 us
  Pallas kernels: 25.5 us -> 23.3 us
  blocking collectives: 15.6 us -> 13.4 us
  waiting for transfers between devices: 20.2 us -> 22.3 us
    pallas_call x14, Pallas kernels: 25.5 us -> 23.3 us  [call(): pl.pallas_call(body, out_shape=outs, in_specs=[pl.BlockSpec(memory_space=...]
    all_to_all x1, blocking collectives: 15.6 us -> 13.4 us  [per_device(): parts = lax.all_to_all(parts, 'rows', 0, 0, tiled=True)]
    ppermute x29, waiting for transfers between devices: 17 us -> 19.1 us  [permute(): lax.ppermute(values, axis, [(i, target(i)) for i in range(lax.axis_size(a...]
  transfers between devices with their start and end apart: 30 -> 30, of which waited for: 9 -> 9; matrix products, arithmetic and copies ran while one was open for 2% -> 2% of each run, Pallas kernels for 13% -> 12%
where the time goes in v11:
time: 116 us; the launch traced here: 114 us
  starting transfers between devices  51.4 us (44%)
  Pallas kernels  23.3 us (20%)
  waiting for transfers between devices  22.3 us (19%)
  blocking collectives  13.4 us (12%)
  local copies, waits for them, and re-layouts  1.48 us (1%)
  other arithmetic  1.4 us (1%)
    ppermute x29, starting transfers between devices, permute(): lax.ppermute(values, axis, [(i, target(i)) for i in range(lax.axis_size(a...  44.6 us
    pallas_call x14, Pallas kernels, call(): pl.pallas_call(body, out_shape=outs, in_specs=[pl.BlockSpec(memory_space=...  23.3 us
    ppermute x29, waiting for transfers between devices, permute(): lax.ppermute(values, axis, [(i, target(i)) for i in range(lax.axis_size(a...  19.1 us
    all_to_all x1, blocking collectives, per_device(): parts = lax.all_to_all(parts, 'rows', 0, 0, tiled=True)  13.4 us
    all_to_all x1, starting transfers between devices, per_device(): sums = lax.all_to_all(sums, 'rows', 0, 0, tiled=True)  6.81 us
    all_to_all x1, waiting for transfers between devices, per_device(): sums = lax.all_to_all(sums, 'rows', 0, 0, tiled=True)  3.21 us
  transfers between devices with their start and end apart: 30, of which 9 were waited for; matrix products, arithmetic and copies ran while one was open for 2% of the time, Pallas kernels for 12%

profile of v11, /device:TPU:6, one launch (start us, length us, event | category | flops | bytes accessed | tf_op | source)
XLA Modules:
  0.0 114.4 jit_solution(5463893101351655225)
XLA Ops:
  0.7 2.2 %rows_first.1 = (bf16[8,64,1024]{2,1,0:T(8,128)(2,1)S(1)}, bf16[8,64,1024]{2,1,0:T(8,128)(2,1)S(1)}, bf16[128,1024]{1,0:T(8,128)(2,1)S(1)}, bf16[128,1024]{1,0:T(8,128)(2,1)S(1)}) custom-call(bf16[64,8,1024]{2,1,0:T(8,128)(2,1)} %phase.1, bf16[64,8,1024]{2,1,0:T(8,128)(2,1)} %coher.1), custom_call_target="tpu_custom_call" | custom-call | tf_op jit(solution)/shard_map/rows_first/pallas_call | solution.py:30
  2.8 2.0 %collective-permute-start = (bf16[128,1024]{1,0:T(8,128)(2,1)S(1)}, bf16[128,1024]{1,0:T(8,128)(2,1)S(1)}, u32[]{:S(2)}, u32[]{:S(2)}) collective-permute-start(bf16[128,1024]{1,0:T(8,128)(2,1)S(1)} %get-tuple-element.61), channel_id=1, source_target_pairs={{0,1},{1,2},{2,3},{3,4},{4,5},{5,6},{6,7},{7,8},{8,9},{9,10},{10,1... | collective-permute-start | bytes 786440 | tf_op jit(solution)/shard_map/ppermute | solution.py:439
  4.8 6.5 %collective-permute-start.1 = (bf16[128,1024]{1,0:T(8,128)(2,1)S(1)}, bf16[128,1024]{1,0:T(8,128)(2,1)S(1)}, u32[]{:S(2)}, u32[]{:S(2)}) collective-permute-start(bf16[128,1024]{1,0:T(8,128)(2,1)S(1)} %get-tuple-element.62), channel_id=1, source_target_pairs={{0,31},{1,0},{2,1},{3,2},{4,3},{5,4},{6,5},{7,6},{8,7},{9,8},{10,9... | collective-permute-start | bytes 786440 | tf_op jit(solution)/shard_map/ppermute | solution.py:439
  11.6 0.6 gather_fusion
  12.3 3.3 %inner_rows.1 = (f32[8,64,1024]{2,1,0:T(8,128)}, f32[128,128]{1,0:T(8,128)S(1)}, bf16[64,1024]{1,0:T(8,128)(2,1)}, bf16[64,1024]{1,0:T(8,128)(2,1)}, bf16[64,102...) custom-call(bf16[8,64,1024]{2,1,0:T(8,128)(2,1)S(1)} %get-tuple-elem, ...), custom_call_target="tpu_custom_call" | custom-call | tf_op jit(solution)/shard_map/inner_rows/pallas_call | solution.py:30
  15.6 1.9 %collective-permute-done.above = bf16[128,1024]{1,0:T(8,128)(2,1)S(1)} collective-permute-done((bf16[128,1024]{1,0:T(8,128)(2,1)S(1)}, bf16[128,1024]{1,0:T(8,128)(2,1)S(1)}, u32[]{:S(2)}, u32[]{:S(2)}) %collective-permute-start) | collective-permute-done | bytes 262176 | tf_op jit(solution)/shard_map/ppermute | solution.py:439
  17.5 2.5 %border_rows.1 = (f32[8,64,1024]{2,1,0:T(8,128)}, f32[32,1,128]{2,1,0:T(1,128)}, bf16[64,1024]{1,0:T(8,128)(2,1)}, bf16[64,1024]{1,0:T(8,128)(2,1)}, bf16[64,102...) custom-call(bf16[8,64,1024]{2,1,0:T(8,128)(2,1)S(1)} %get-tuple-elem, ...), custom_call_target="tpu_custom_call", output_to_operand_aliasing={{0}: (7, {}), {2}: (8, {}), {3}: (9, {}), {4}: (10, {}), {5... | custom-call | tf_op jit(solution)/shard_map/border_rows/pallas_call | solution.py:30
  20.2 1.5 %collective-permute-start.3 = (bf16[64,1024]{1,0:T(8,128)(2,1)}, bf16[64,1024]{1,0:T(8,128)(2,1)S(1)}, u32[]{:S(2)}, u32[]{:S(2)}) collective-permute-start(bf16[64,1024]{1,0:T(8,128)(2,1)} %get-tuple-element.78), channel_id=1, source_target_pairs={{0,128},{32,160},{64,192},{96,224},{128,0},{160,32},{192,64},{224,... | collective-permute-start | bytes 393224 | tf_op jit(solution)/shard_map/ppermute | solution.py:439
  21.7 2.1 %collective-permute-start.4 = (bf16[64,1024]{1,0:T(8,128)(2,1)}, bf16[64,1024]{1,0:T(8,128)(2,1)S(1)}, u32[]{:S(2)}, u32[]{:S(2)}) collective-permute-start(bf16[64,1024]{1,0:T(8,128)(2,1)} %get-tuple-element.79), channel_id=1, source_target_pairs={{0,64},{32,96},{64,128},{96,160},{128,192},{160,224},{192,0},{224,... | collective-permute-start | bytes 393224 | tf_op jit(solution)/shard_map/ppermute | solution.py:439
  23.8 6.8 %all-to-all-start = ((f32[32,1,128]{2,1,0:T(1,128)}), f32[32,1,128]{2,1,0:T(1,128)S(1)}, u32[]{:S(2)}, u32[]{:S(2)}) async-start(f32[32,1,128]{2,1,0:T(1,128)} %get-tuple-element.77), calls=%async_computation | async-start | bytes 32768 | tf_op jit(solution)/shard_map/all_to_all | solution.py:513
  30.6 1.0 subtract_convert_fusion
  31.5 1.6 %stage.1.smooth = f32[8,64,1024]{2,1,0:T(8,128)S(1)} custom-call(f32[8,64,1024]{2,1,0:T(8,128)} %get-tuple-element.88.source), custom_call_target="tpu_custom_call" | custom-call | tf_op jit(solution)/shard_map/stage/pallas_call | solution.py:30
  33.2 1.1 collective-permute-start.6
  34.2 1.4 %collective-permute-start.7 = (bf16[64,1024]{1,0:T(8,128)(2,1)S(1)}, bf16[64,1024]{1,0:T(8,128)(2,1)S(1)}, u32[]{:S(2)}, u32[]{:S(2)}) collective-permute-start(bf16[64,1024]{1,0:T(8,128)(2,1)S(1)} %copy-done.4), channel_id=1, source_target_pairs={{0,96},{32,64},{64,160},{96,128},{128,224},{160,192},{192,32},{224... | collective-permute-start | bytes 393224 | tf_op jit(solution)/shard_map/ppermute | solution.py:439
  35.6 1.5 %collective-permute-start.8 = (bf16[64,1024]{1,0:T(8,128)(2,1)}, bf16[64,1024]{1,0:T(8,128)(2,1)S(1)}, u32[]{:S(2)}, u32[]{:S(2)}) collective-permute-start(bf16[64,1024]{1,0:T(8,128)(2,1)} %get-tuple-element.86), channel_id=1, source_target_pairs={{0,224},{32,192},{64,32},{96,0},{128,96},{160,64},{192,160},{224,1... | collective-permute-start | bytes 393224 | tf_op jit(solution)/shard_map/ppermute | solution.py:439
  37.2 3.2 %all-to-all-done.sums = f32[32,1,128]{2,1,0:T(1,128)S(1)} async-done(((f32[32,1,128]{2,1,0:T(1,128)}), f32[32,1,128]{2,1,0:T(1,128)S(1)}, u32[]{:S(2)}, u32[]{:S(2)}) %all-to-all-start) | async-done | bytes 16416 | tf_op jit(solution)/shard_map/all_to_all | solution.py:513
  40.4 0.6 correction.1
  40.9 2.1 %collective-permute-start.10 = (bf16[64,1024]{1,0:T(8,128)(2,1)S(1)}, bf16[64,1024]{1,0:T(8,128)(2,1)S(1)}, u32[]{:S(2)}, u32[]{:S(2)}) collective-permute-start(bf16[64,1024]{1,0:T(8,128)(2,1)S(1)} %get-tuple-element.93), channel_id=1, source_target_pairs={{0,128},{32,160},{64,192},{96,224},{128,0},{160,32},{192,64},{224,... | collective-permute-start | bytes 393224 | tf_op jit(solution)/shard_map/ppermute | solution.py:439
  43.1 1.3 %collective-permute-start.11 = (bf16[64,1024]{1,0:T(8,128)(2,1)S(1)}, bf16[64,1024]{1,0:T(8,128)(2,1)S(1)}, u32[]{:S(2)}, u32[]{:S(2)}) collective-permute-start(bf16[64,1024]{1,0:T(8,128)(2,1)S(1)} %get-tuple-element.94), channel_id=1, source_target_pairs={{0,64},{32,96},{64,128},{96,160},{128,192},{160,224},{192,0},{224,... | collective-permute-start | bytes 393224 | tf_op jit(solution)/shard_map/ppermute | solution.py:439
  44.5 0.8 collective-permute-start.12
  45.4 4.4 %collective-permute-start.14 = (bf16[64,1024]{1,0:T(8,128)(2,1)S(1)}, bf16[64,1024]{1,0:T(8,128)(2,1)S(1)}, u32[]{:S(2)}, u32[]{:S(2)}) collective-permute-start(bf16[64,1024]{1,0:T(8,128)(2,1)S(1)} %get-tuple-element.97), channel_id=1, source_target_pairs={{0,96},{32,64},{64,160},{96,128},{128,224},{160,192},{192,32},{224... | collective-permute-start | bytes 393224 | tf_op jit(solution)/shard_map/ppermute | solution.py:439
  49.9 0.5 slice_bitcast_fusion
  50.4 3.2 %collective-permute-done.12.refs_12_ = bf16[64,1024]{1,0:T(8,128)(2,1)S(1)} collective-permute-done((bf16[64,1024]{1,0:T(8,128)(2,1)S(1)}, bf16[64,1024]{1,0:T(8,128)(2,1)S(1)}, u32[]{:S(2)}, u32[]{:S(2)}) %collective-permute-start.12) | collective-permute-done | bytes 131104 | tf_op jit(solution)/shard_map/ppermute | solution.py:439
  53.6 1.6 %collective-permute-done.14.refs_14_ = bf16[64,1024]{1,0:T(8,128)(2,1)S(1)} collective-permute-done((bf16[64,1024]{1,0:T(8,128)(2,1)S(1)}, bf16[64,1024]{1,0:T(8,128)(2,1)S(1)}, u32[]{:S(2)}, u32[]{:S(2)}) %collective-permute-start.14) | collective-permute-done | bytes 131104 | tf_op jit(solution)/shard_map/ppermute | solution.py:439
  55.2 1.2 %collective-permute-done.15.refs_15_ = bf16[64,1024]{1,0:T(8,128)(2,1)S(1)} collective-permute-done((bf16[64,1024]{1,0:T(8,128)(2,1)S(1)}, bf16[64,1024]{1,0:T(8,128)(2,1)S(1)}, u32[]{:S(2)}, u32[]{:S(2)}) %collective-permute-start.15) | collective-permute-done | bytes 131104 | tf_op jit(solution)/shard_map/ppermute | solution.py:439
  56.4 1.8 %right_side.1 = (f32[304,1024]{1,0:T(8,128)S(1)}, bf16[512,1024]{1,0:T(8,128)(2,1)S(1)}, bf16[304,128]{1,0:T(8,128)(2,1)S(1)}, bf16[16,304]{1,0:T(8,128)(2,1)S(1)}, bf16[304,128]{1,0:T(8,128)(2,1)S(1)}) custom-call(bf16[64,1024]{1,0:T(8,128)(2,1)S(1)} %copy-done, bf16[64,1024]{1,0:T(8,128)(2,1)S(1)} %collective-permute-done.2.refs_1_, ...), custom_call_target="tpu_custom_call" | custom-call | tf_op jit(solution)/shard_map/right_side/pallas_call | solution.py:30
  58.2 1.7 %collective-permute-start.19 = (bf16[16,304]{1,0:T(8,128)(2,1)S(1)}, bf16[16,304]{1,0:T(8,128)(2,1)S(1)}, u32[]{:S(2)}, u32[]{:S(2)}) collective-permute-start(bf16[16,304]{1,0:T(8,128)(2,1)S(1)} %get-tuple-element.104), channel_id=1, source_target_pairs={{0,224},{32,0},{64,32},{96,64},{128,96},{160,128},{192,160},{224,1... | collective-permute-start | bytes 29192 | tf_op jit(solution)/shard_map/ppermute | solution.py:439
  59.9 0.7 collective-permute-start.16
  60.6 4.6 %collective-permute-start.17 = (bf16[304,128]{1,0:T(8,128)(2,1)S(1)}, bf16[304,128]{1,0:T(8,128)(2,1)S(1)}, u32[]{:S(2)}, u32[]{:S(2)}) collective-permute-start(bf16[304,128]{1,0:T(8,128)(2,1)S(1)} %get-tuple-element.103), channel_id=1, source_target_pairs={{0,31},{1,0},{2,1},{3,2},{4,3},{5,4},{6,5},{7,6},{8,7},{9,8},{10,9... | collective-permute-start | bytes 233480 | tf_op jit(solution)/shard_map/ppermute | solution.py:439
  65.3 0.3 pad_maximum_fusion.refs_2_
  65.6 3.4 %apply0.1 = (f32[304,1024]{1,0:T(8,128)S(1)}, f32[3,8,128]{2,1,0:T(8,128)S(1)}) custom-call(f32[304,1024]{1,0:T(8,128)S(1)} %get-tuple-element.99.refs_0_.refs_4_.basis.zero, bf16[512,1024]{1,0:T(8,128)(2,1)S(1)} %get-tuple-element.100.refs_1_, bf16[512,608]{1,0:T(8,128)(2,1)S(1)} %pad_maximum_fusion.refs_2_, ...), custom_call_target="tpu_custom_call" | custom-call | tf_op jit(solution)/shard_map/apply0/pallas_call | solution.py:30
  69.0 0.7 add_halo1.1
  69.7 5.4 %collective-permute-start.21 = (bf16[304,128]{1,0:T(8,128)(2,1)S(1)}, bf16[304,128]{1,0:T(8,128)(2,1)S(1)}, u32[]{:S(2)}, u32[]{:S(2)}) collective-permute-start(bf16[304,128]{1,0:T(8,128)(2,1)S(1)} %get-tuple-element.108), channel_id=1, source_target_pairs={{0,31},{1,0},{2,1},{3,2},{4,3},{5,4},{6,5},{7,6},{8,7},{9,8},{10,9... | collective-permute-start | bytes 233480 | tf_op jit(solution)/shard_map/ppermute | solution.py:439
  75.0 1.7 %collective-permute-start.23 = (bf16[16,304]{1,0:T(8,128)(2,1)S(1)}, bf16[16,304]{1,0:T(8,128)(2,1)S(1)}, u32[]{:S(2)}, u32[]{:S(2)}) collective-permute-start(bf16[16,304]{1,0:T(8,128)(2,1)S(1)} %get-tuple-element.109), channel_id=1, source_target_pairs={{0,224},{32,0},{64,32},{96,64},{128,96},{160,128},{192,160},{224,1... | collective-permute-start | bytes 29192 | tf_op jit(solution)/shard_map/ppermute | solution.py:439
  76.8 3.4 %apply1.1 = (f32[304,1024]{1,0:T(8,128)S(1)}, f32[3,8,128]{2,1,0:T(8,128)S(1)}) custom-call(f32[304,1024]{1,0:T(8,128)S(1)} %get-tuple-element.105.refs_0_.refs_4_.one, bf16[512,1024]{1,0:T(8,128)(2,1)S(1)} %get-tuple-element.100.refs_1_, bf16[512,608]{1,0:T(8,128)(2,1)S(1)} %pad_maximum_fusion.refs_2_, ...), custom_call_target="tpu_custom_call" | custom-call | tf_op jit(solution)/shard_map/apply1/pallas_call | solution.py:30
  80.2 0.7 add_halo2.1
  80.9 0.2 collective-permute-start.24
  81.1 1.8 %collective-permute-start.25 = (bf16[16,304]{1,0:T(8,128)(2,1)S(1)}, bf16[16,304]{1,0:T(8,128)(2,1)S(1)}, u32[]{:S(2)}, u32[]{:S(2)}) collective-permute-start(bf16[16,304]{1,0:T(8,128)(2,1)S(1)} %get-tuple-element.112), channel_id=1, source_target_pairs={{0,32},{32,64},{64,96},{96,128},{128,160},{160,192},{192,224},{224... | collective-permute-start | bytes 29192 | tf_op jit(solution)/shard_map/ppermute | solution.py:439
  83.0 1.3 %apply2.1.two = f32[3,8,128]{2,1,0:T(8,128)S(1)} custom-call(f32[304,1024]{1,0:T(8,128)S(1)} %get-tuple-element.110.refs_0_.field.two, bf16[512,1024]{1,0:T(8,128)(2,1)S(1)} %get-tuple-element.100.refs_1_, bf16[512,608]{1,0:T(8,128)(2,1)S(1)} %pad_maximum_fusion.refs_2_, bf16[304,512]{1,0:T(8,128)(2,1)S(1)} %subtract_convert_fusion.1.refs_16_.refs_3_, ...), custom_call_target="tpu_custom_call" | custom-call | tf_op jit(solution)/shard_map/apply2/pallas_call | solution.py:30
  84.3 4.6 %collective-permute-done.24.above = bf16[304,128]{1,0:T(8,128)(2,1)S(1)} collective-permute-done((bf16[304,128]{1,0:T(8,128)(2,1)S(1)}, bf16[304,128]{1,0:T(8,128)(2,1)S(1)}, u32[]{:S(2)}, u32[]{:S(2)}) %collective-permute-start.24) | collective-permute-done | bytes 77856 | tf_op jit(solution)/shard_map/ppermute | solution.py:439
  88.8 0.6 all_moments.1
  89.4 0.7 collective-permute-start.26
  90.1 0.8 collective-permute-done.26
  90.9 3.5 %collective-permute-done.27 = f32[1,128]{1,0:T(1,128)S(1)} collective-permute-done((f32[1,128]{1,0:T(1,128)S(1)}, f32[1,128]{1,0:T(1,128)S(1)}, u32[]{:S(2)}, u32[]{:S(2)}) %collective-permute-start.27) | collective-permute-done | bytes 544 | tf_op jit(solution)/shard_map/ppermute | solution.py:439
  94.5 2.8 %collective-permute-start.28 = (f32[1,128]{1,0:T(1,128)S(1)}, f32[1,128]{1,0:T(1,128)S(1)}, u32[]{:S(2)}, u32[]{:S(2)}) collective-permute-start(f32[1,128]{1,0:T(1,128)S(1)} %add.70.one), channel_id=1, source_target_pairs={{0,128},{32,160},{64,192},{96,224},{128,0},{160,32},{192,64},{224,... | collective-permute-start | bytes 1544 | tf_op jit(solution)/shard_map/ppermute | solution.py:439
  97.3 2.2 %collective-permute-done.28.two = f32[1,128]{1,0:T(1,128)S(1)} collective-permute-done((f32[1,128]{1,0:T(1,128)S(1)}, f32[1,128]{1,0:T(1,128)S(1)}, u32[]{:S(2)}, u32[]{:S(2)}) %collective-permute-start.28) | collective-permute-done | bytes 544 | tf_op jit(solution)/shard_map/ppermute | solution.py:439
  99.5 13.4 %all_to_all.10.parts = f32[32,1,128]{2,1,0:T(1,128)S(1)} all-to-all(f32[32,1,128]{2,1,0:T(1,128)S(1)} %add_and_spread.1), channel_id=1, replica_groups=mesh['ifg'=8,'rows'=32] {'rows'}, dimensions={0} | all-to-all | bytes 32768 | tf_op jit(solution)/shard_map/all_to_all | solution.py:598
  113.0 1.3 %combine.1 = f32[2400,128]{1,0:T(8,128)} custom-call(f32[32,1,128]{2,1,0:T(1,128)S(1)} %all_to_all.10.parts, f32[304,1024]{1,0:T(8,128)S(1)} %get-tuple-element.99.refs_0_.refs_4_.basis.zero, f32[304,1024]{1,0:T(8,128)S(1)} %get-tuple-element.105.refs_0_.refs_4_.one, f32[304,1024]{1,0:T(8,128)S(1)} %get-tuple-element.110.refs_0_.field.two), custom_call_target="tpu_custom_call" | custom-call | tf_op jit(solution)/shard_map/combine/pallas_call | solution.py:30
  (58 shorter events, 0.9 us)
Async XLA Ops:
  0.6 10.7 %copy-start.5 = (s32[64,8]{0,1:T(8,128)S(1)}, s32[64,8]{0,1:T(8,128)}, u32[]{:S(2)}) copy-start(s32[64,8]{0,1:T(8,128)} %param.8) | copy-start | bytes 6148
  0.6 10.8 %copy-start.6 = (s32[512,2]{0,1:T(2,128)S(1)}, s32[512,2]{0,1:T(2,128)}, u32[]{:S(2)}) copy-start(s32[512,2]{0,1:T(2,128)} %param.9) | copy-start | bytes 12292
  0.7 11.6 %copy-start.1 = (f32[8,1024]{1,0:T(8,128)S(1)}, f32[8,1024]{1,0:T(8,128)}, u32[]{:S(2)}) copy-start(f32[8,1024]{1,0:T(8,128)} %height.5) | copy-start | bytes 98308
  2.8 14.7 %collective-permute-start = (bf16[128,1024]{1,0:T(8,128)(2,1)S(1)}, bf16[128,1024]{1,0:T(8,128)(2,1)S(1)}, u32[]{:S(2)}, u32[]{:S(2)}) collective-permute-start(bf16[128,1024]{1,0:T(8,128)(2,1)S(1)} %get-tuple-element.61), channel_id=1, source_target_pairs={{0,1},{1,2},{2,3},{3,4},{4,5},{5,6},{6,7},{7,8},{8,9},{9,10},{10,1... | collective-permute-start | bytes 786440 | tf_op jit(solution)/shard_map/ppermute | solution.py:439
  4.8 12.7 %collective-permute-start.1 = (bf16[128,1024]{1,0:T(8,128)(2,1)S(1)}, bf16[128,1024]{1,0:T(8,128)(2,1)S(1)}, u32[]{:S(2)}, u32[]{:S(2)}) collective-permute-start(bf16[128,1024]{1,0:T(8,128)(2,1)S(1)} %get-tuple-element.62), channel_id=1, source_target_pairs={{0,31},{1,0},{2,1},{3,2},{4,3},{5,4},{6,5},{7,6},{8,7},{9,8},{10,9... | collective-permute-start | bytes 786440 | tf_op jit(solution)/shard_map/ppermute | solution.py:439
  20.1 3.7 %collective-permute-start.2 = (bf16[64,1024]{1,0:T(8,128)(2,1)}, bf16[64,1024]{1,0:T(8,128)(2,1)S(1)}, u32[]{:S(2)}, u32[]{:S(2)}) collective-permute-start(bf16[64,1024]{1,0:T(8,128)(2,1)} %get-tuple-element.75), channel_id=1, source_target_pairs={{0,32},{32,0},{64,96},{96,64},{128,160},{160,128},{192,224},{224,1... | collective-permute-start | bytes 393224 | tf_op jit(solution)/shard_map/ppermute | solution.py:439
  20.2 15.5 %collective-permute-start.3 = (bf16[64,1024]{1,0:T(8,128)(2,1)}, bf16[64,1024]{1,0:T(8,128)(2,1)S(1)}, u32[]{:S(2)}, u32[]{:S(2)}) collective-permute-start(bf16[64,1024]{1,0:T(8,128)(2,1)} %get-tuple-element.78), channel_id=1, source_target_pairs={{0,128},{32,160},{64,192},{96,224},{128,0},{160,32},{192,64},{224,... | collective-permute-start | bytes 393224 | tf_op jit(solution)/shard_map/ppermute | solution.py:439
  21.7 15.5 %collective-permute-start.4 = (bf16[64,1024]{1,0:T(8,128)(2,1)}, bf16[64,1024]{1,0:T(8,128)(2,1)S(1)}, u32[]{:S(2)}, u32[]{:S(2)}) collective-permute-start(bf16[64,1024]{1,0:T(8,128)(2,1)} %get-tuple-element.79), channel_id=1, source_target_pairs={{0,64},{32,96},{64,128},{96,160},{128,192},{160,224},{192,0},{224,... | collective-permute-start | bytes 393224 | tf_op jit(solution)/shard_map/ppermute | solution.py:439
  23.8 13.4 %collective-permute-start.5 = (bf16[64,1024]{1,0:T(8,128)(2,1)}, bf16[64,1024]{1,0:T(8,128)(2,1)S(1)}, u32[]{:S(2)}, u32[]{:S(2)}) collective-permute-start(bf16[64,1024]{1,0:T(8,128)(2,1)} %get-tuple-element.80), channel_id=1, source_target_pairs={{0,192},{32,224},{64,0},{96,32},{128,64},{160,96},{192,128},{224,1... | collective-permute-start | bytes 393224 | tf_op jit(solution)/shard_map/ppermute | solution.py:439
  23.8 16.6 %all-to-all-start = ((f32[32,1,128]{2,1,0:T(1,128)}), f32[32,1,128]{2,1,0:T(1,128)S(1)}, u32[]{:S(2)}, u32[]{:S(2)}) async-start(f32[32,1,128]{2,1,0:T(1,128)} %get-tuple-element.77), calls=%async_computation | async-start | bytes 32768 | tf_op jit(solution)/shard_map/all_to_all | solution.py:513
  31.5 1.6 %copy-start.3 = (bf16[64,1024]{1,0:T(8,128)(2,1)S(1)}, bf16[64,1024]{1,0:T(8,128)(2,1)}, u32[]{:S(2)}) copy-start(bf16[64,1024]{1,0:T(8,128)(2,1)} %get-tuple-element.84) | copy-start | bytes 393220
  31.5 2.7 %copy-start.4 = (bf16[64,1024]{1,0:T(8,128)(2,1)S(1)}, bf16[64,1024]{1,0:T(8,128)(2,1)}, u32[]{:S(2)}) copy-start(bf16[64,1024]{1,0:T(8,128)(2,1)} %get-tuple-element.85) | copy-start | bytes 393220
  33.1 23.3 %copy-start = (bf16[64,1024]{1,0:T(8,128)(2,1)S(1)}, bf16[64,1024]{1,0:T(8,128)(2,1)}, u32[]{:S(2)}) copy-start(bf16[64,1024]{1,0:T(8,128)(2,1)} %get-tuple-element.73.refs_0_) | copy-start | bytes 393220
  33.2 11.3 %collective-permute-start.6 = (bf16[64,1024]{1,0:T(8,128)(2,1)S(1)}, bf16[64,1024]{1,0:T(8,128)(2,1)S(1)}, u32[]{:S(2)}, u32[]{:S(2)}) collective-permute-start(bf16[64,1024]{1,0:T(8,128)(2,1)S(1)} %copy-done.3), channel_id=1, source_target_pairs={{0,160},{32,128},{64,224},{96,192},{128,32},{160,0},{192,96},{224,... | collective-permute-start | bytes 393224 | tf_op jit(solution)/shard_map/ppermute | solution.py:439
  34.2 11.1 %collective-permute-start.7 = (bf16[64,1024]{1,0:T(8,128)(2,1)S(1)}, bf16[64,1024]{1,0:T(8,128)(2,1)S(1)}, u32[]{:S(2)}, u32[]{:S(2)}) collective-permute-start(bf16[64,1024]{1,0:T(8,128)(2,1)S(1)} %copy-done.4), channel_id=1, source_target_pairs={{0,96},{32,64},{64,160},{96,128},{128,224},{160,192},{192,32},{224... | collective-permute-start | bytes 393224 | tf_op jit(solution)/shard_map/ppermute | solution.py:439
  35.6 9.7 %collective-permute-start.8 = (bf16[64,1024]{1,0:T(8,128)(2,1)}, bf16[64,1024]{1,0:T(8,128)(2,1)S(1)}, u32[]{:S(2)}, u32[]{:S(2)}) collective-permute-start(bf16[64,1024]{1,0:T(8,128)(2,1)} %get-tuple-element.86), channel_id=1, source_target_pairs={{0,224},{32,192},{64,32},{96,0},{128,96},{160,64},{192,160},{224,1... | collective-permute-start | bytes 393224 | tf_op jit(solution)/shard_map/ppermute | solution.py:439
  40.9 8.9 %collective-permute-start.10 = (bf16[64,1024]{1,0:T(8,128)(2,1)S(1)}, bf16[64,1024]{1,0:T(8,128)(2,1)S(1)}, u32[]{:S(2)}, u32[]{:S(2)}) collective-permute-start(bf16[64,1024]{1,0:T(8,128)(2,1)S(1)} %get-tuple-element.93), channel_id=1, source_target_pairs={{0,128},{32,160},{64,192},{96,224},{128,0},{160,32},{192,64},{224,... | collective-permute-start | bytes 393224 | tf_op jit(solution)/shard_map/ppermute | solution.py:439
  43.1 22.2 %copy-start.2 = (bf16[512,304]{1,0:T(8,128)(2,1)S(1)}, bf16[512,304]{1,0:T(8,128)(2,1)}, u32[]{:S(2)}) copy-start(bf16[512,304]{1,0:T(8,128)(2,1)} %subtract_convert_fusion) | copy-start | bytes 933892
  43.1 6.7 %collective-permute-start.11 = (bf16[64,1024]{1,0:T(8,128)(2,1)S(1)}, bf16[64,1024]{1,0:T(8,128)(2,1)S(1)}, u32[]{:S(2)}, u32[]{:S(2)}) collective-permute-start(bf16[64,1024]{1,0:T(8,128)(2,1)S(1)} %get-tuple-element.94), channel_id=1, source_target_pairs={{0,64},{32,96},{64,128},{96,160},{128,192},{160,224},{192,0},{224,... | collective-permute-start | bytes 393224 | tf_op jit(solution)/shard_map/ppermute | solution.py:439
  44.5 9.1 %collective-permute-start.12 = (bf16[64,1024]{1,0:T(8,128)(2,1)S(1)}, bf16[64,1024]{1,0:T(8,128)(2,1)S(1)}, u32[]{:S(2)}, u32[]{:S(2)}) collective-permute-start(bf16[64,1024]{1,0:T(8,128)(2,1)S(1)} %get-tuple-element.95), channel_id=1, source_target_pairs={{0,192},{32,224},{64,0},{96,32},{128,64},{160,96},{192,128},{224,1... | collective-permute-start | bytes 393224 | tf_op jit(solution)/shard_map/ppermute | solution.py:439
  45.4 8.2 %collective-permute-start.13 = (bf16[64,1024]{1,0:T(8,128)(2,1)S(1)}, bf16[64,1024]{1,0:T(8,128)(2,1)S(1)}, u32[]{:S(2)}, u32[]{:S(2)}) collective-permute-start(bf16[64,1024]{1,0:T(8,128)(2,1)S(1)} %get-tuple-element.96), channel_id=1, source_target_pairs={{0,160},{32,128},{64,224},{96,192},{128,32},{160,0},{192,96},{224,... | collective-permute-start | bytes 393224 | tf_op jit(solution)/shard_map/ppermute | solution.py:439
  45.4 9.8 %collective-permute-start.14 = (bf16[64,1024]{1,0:T(8,128)(2,1)S(1)}, bf16[64,1024]{1,0:T(8,128)(2,1)S(1)}, u32[]{:S(2)}, u32[]{:S(2)}) collective-permute-start(bf16[64,1024]{1,0:T(8,128)(2,1)S(1)} %get-tuple-element.97), channel_id=1, source_target_pairs={{0,96},{32,64},{64,160},{96,128},{128,224},{160,192},{192,32},{224... | collective-permute-start | bytes 393224 | tf_op jit(solution)/shard_map/ppermute | solution.py:439
  49.8 6.6 %collective-permute-start.15 = (bf16[64,1024]{1,0:T(8,128)(2,1)S(1)}, bf16[64,1024]{1,0:T(8,128)(2,1)S(1)}, u32[]{:S(2)}, u32[]{:S(2)}) collective-permute-start(bf16[64,1024]{1,0:T(8,128)(2,1)S(1)} %get-tuple-element.98), channel_id=1, source_target_pairs={{0,224},{32,192},{64,32},{96,0},{128,96},{160,64},{192,160},{224,1... | collective-permute-start | bytes 393224 | tf_op jit(solution)/shard_map/ppermute | solution.py:439
  49.8 6.6 %collective-permute-start.9 = (bf16[64,1024]{1,0:T(8,128)(2,1)S(1)}, bf16[64,1024]{1,0:T(8,128)(2,1)S(1)}, u32[]{:S(2)}, u32[]{:S(2)}) collective-permute-start(bf16[64,1024]{1,0:T(8,128)(2,1)S(1)} %get-tuple-element.92), channel_id=1, source_target_pairs={{0,32},{32,0},{64,96},{96,64},{128,160},{160,128},{192,224},{224,1... | collective-permute-start | bytes 393224 | tf_op jit(solution)/shard_map/ppermute | solution.py:439
  58.2 10.7 %collective-permute-start.18 = (bf16[16,304]{1,0:T(8,128)(2,1)S(1)}, bf16[16,304]{1,0:T(8,128)(2,1)S(1)}, u32[]{:S(2)}, u32[]{:S(2)}) collective-permute-start(bf16[16,304]{1,0:T(8,128)(2,1)S(1)} %get-tuple-element.104), channel_id=1, source_target_pairs={{0,32},{32,64},{64,96},{96,128},{128,160},{160,192},{192,224},{224... | collective-permute-start | bytes 29192 | tf_op jit(solution)/shard_map/ppermute | solution.py:439
  58.2 10.7 %collective-permute-start.19 = (bf16[16,304]{1,0:T(8,128)(2,1)S(1)}, bf16[16,304]{1,0:T(8,128)(2,1)S(1)}, u32[]{:S(2)}, u32[]{:S(2)}) collective-permute-start(bf16[16,304]{1,0:T(8,128)(2,1)S(1)} %get-tuple-element.104), channel_id=1, source_target_pairs={{0,224},{32,0},{64,32},{96,64},{128,96},{160,128},{192,160},{224,1... | collective-permute-start | bytes 29192 | tf_op jit(solution)/shard_map/ppermute | solution.py:439
  59.9 9.0 %collective-permute-start.16 = (bf16[304,128]{1,0:T(8,128)(2,1)S(1)}, bf16[304,128]{1,0:T(8,128)(2,1)S(1)}, u32[]{:S(2)}, u32[]{:S(2)}) collective-permute-start(bf16[304,128]{1,0:T(8,128)(2,1)S(1)} %get-tuple-element.102), channel_id=1, source_target_pairs={{0,1},{1,2},{2,3},{3,4},{4,5},{5,6},{6,7},{7,8},{8,9},{9,10},{10,1... | collective-permute-start | bytes 233480 | tf_op jit(solution)/shard_map/ppermute | solution.py:439
  60.6 8.3 %collective-permute-start.17 = (bf16[304,128]{1,0:T(8,128)(2,1)S(1)}, bf16[304,128]{1,0:T(8,128)(2,1)S(1)}, u32[]{:S(2)}, u32[]{:S(2)}) collective-permute-start(bf16[304,128]{1,0:T(8,128)(2,1)S(1)} %get-tuple-element.103), channel_id=1, source_target_pairs={{0,31},{1,0},{2,1},{3,2},{4,3},{5,4},{6,5},{7,6},{8,7},{9,8},{10,9... | collective-permute-start | bytes 233480 | tf_op jit(solution)/shard_map/ppermute | solution.py:439
  69.7 10.5 %collective-permute-start.20 = (bf16[304,128]{1,0:T(8,128)(2,1)S(1)}, bf16[304,128]{1,0:T(8,128)(2,1)S(1)}, u32[]{:S(2)}, u32[]{:S(2)}) collective-permute-start(bf16[304,128]{1,0:T(8,128)(2,1)S(1)} %get-tuple-element.107), channel_id=1, source_target_pairs={{0,1},{1,2},{2,3},{3,4},{4,5},{5,6},{6,7},{7,8},{8,9},{9,10},{10,1... | collective-permute-start | bytes 233480 | tf_op jit(solution)/shard_map/ppermute | solution.py:439
  69.7 10.5 %collective-permute-start.21 = (bf16[304,128]{1,0:T(8,128)(2,1)S(1)}, bf16[304,128]{1,0:T(8,128)(2,1)S(1)}, u32[]{:S(2)}, u32[]{:S(2)}) collective-permute-start(bf16[304,128]{1,0:T(8,128)(2,1)S(1)} %get-tuple-element.108), channel_id=1, source_target_pairs={{0,31},{1,0},{2,1},{3,2},{4,3},{5,4},{6,5},{7,6},{8,7},{9,8},{10,9... | collective-permute-start | bytes 233480 | tf_op jit(solution)/shard_map/ppermute | solution.py:439
  75.0 5.1 %collective-permute-start.22 = (bf16[16,304]{1,0:T(8,128)(2,1)S(1)}, bf16[16,304]{1,0:T(8,128)(2,1)S(1)}, u32[]{:S(2)}, u32[]{:S(2)}) collective-permute-start(bf16[16,304]{1,0:T(8,128)(2,1)S(1)} %get-tuple-element.109), channel_id=1, source_target_pairs={{0,32},{32,64},{64,96},{96,128},{128,160},{160,192},{192,224},{224... | collective-permute-start | bytes 29192 | tf_op jit(solution)/shard_map/ppermute | solution.py:439
  75.0 5.1 %collective-permute-start.23 = (bf16[16,304]{1,0:T(8,128)(2,1)S(1)}, bf16[16,304]{1,0:T(8,128)(2,1)S(1)}, u32[]{:S(2)}, u32[]{:S(2)}) collective-permute-start(bf16[16,304]{1,0:T(8,128)(2,1)S(1)} %get-tuple-element.109), channel_id=1, source_target_pairs={{0,224},{32,0},{64,32},{96,64},{128,96},{160,128},{192,160},{224,1... | collective-permute-start | bytes 29192 | tf_op jit(solution)/shard_map/ppermute | solution.py:439
  80.9 7.9 %collective-permute-start.24 = (bf16[304,128]{1,0:T(8,128)(2,1)S(1)}, bf16[304,128]{1,0:T(8,128)(2,1)S(1)}, u32[]{:S(2)}, u32[]{:S(2)}) collective-permute-start(bf16[304,128]{1,0:T(8,128)(2,1)S(1)} %get-tuple-element.111), channel_id=1, source_target_pairs={{0,1},{1,2},{2,3},{3,4},{4,5},{5,6},{6,7},{7,8},{8,9},{9,10},{10,1... | collective-permute-start | bytes 233480 | tf_op jit(solution)/shard_map/ppermute | solution.py:439
  81.1 3.1 %collective-permute-start.25 = (bf16[16,304]{1,0:T(8,128)(2,1)S(1)}, bf16[16,304]{1,0:T(8,128)(2,1)S(1)}, u32[]{:S(2)}, u32[]{:S(2)}) collective-permute-start(bf16[16,304]{1,0:T(8,128)(2,1)S(1)} %get-tuple-element.112), channel_id=1, source_target_pairs={{0,32},{32,64},{64,96},{96,128},{128,160},{160,192},{192,224},{224... | collective-permute-start | bytes 29192 | tf_op jit(solution)/shard_map/ppermute | solution.py:439
  89.4 1.5 %collective-permute-start.26 = (f32[1,128]{1,0:T(1,128)S(1)}, f32[1,128]{1,0:T(1,128)S(1)}, u32[]{:S(2)}, u32[]{:S(2)}) collective-permute-start(f32[1,128]{1,0:T(1,128)S(1)} %all_moments.1), channel_id=1, source_target_pairs={{0,32},{32,0},{64,96},{96,64},{128,160},{160,128},{192,224},{224,1... | collective-permute-start | bytes 1544 | tf_op jit(solution)/shard_map/ppermute | solution.py:439
  90.9 3.5 %collective-permute-start.27 = (f32[1,128]{1,0:T(1,128)S(1)}, f32[1,128]{1,0:T(1,128)S(1)}, u32[]{:S(2)}, u32[]{:S(2)}) collective-permute-start(f32[1,128]{1,0:T(1,128)S(1)} %add.69), channel_id=1, source_target_pairs={{0,64},{32,96},{64,0},{96,32},{128,192},{160,224},{192,128},{224,1... | collective-permute-start | bytes 1544 | tf_op jit(solution)/shard_map/ppermute | solution.py:439
  94.5 5.0 %collective-permute-start.28 = (f32[1,128]{1,0:T(1,128)S(1)}, f32[1,128]{1,0:T(1,128)S(1)}, u32[]{:S(2)}, u32[]{:S(2)}) collective-permute-start(f32[1,128]{1,0:T(1,128)S(1)} %add.70.one), channel_id=1, source_target_pairs={{0,128},{32,160},{64,192},{96,224},{128,0},{160,32},{192,64},{224,... | collective-permute-start | bytes 1544 | tf_op jit(solution)/shard_map/ppermute | solution.py:439

commit v12 on v11

--- a/solution.py
+++ b/solution.py
@@ -271,7 +271,7 @@
         field[:, lanes] = dot(design_t[...], high) + dot(design_t[...], low)
         return 0
 
-    lax.fori_loop(0, 4, one_chunk, 0)
+    lax.fori_loop(0, 4, one_chunk, 0, unroll=True)
     write_edges(field, *edges)
 
 

time: 116 us -> 116 us (level)
  no operation moved by 1% of the time
where the time goes in v12:
time: 116 us; the launch traced here: 114 us
  starting transfers between devices  51.4 us (44%)
  Pallas kernels  22.7 us (20%)
  waiting for transfers between devices  22.3 us (19%)
  blocking collectives  13.4 us (12%)
  local copies, waits for them, and re-layouts  1.48 us (1%)
  other arithmetic  1.4 us (1%)
    ppermute x29, starting transfers between devices, permute(): lax.ppermute(values, axis, [(i, target(i)) for i in range(lax.axis_size(a...  44.6 us
    pallas_call x14, Pallas kernels, call(): pl.pallas_call(body, out_shape=outs, in_specs=[pl.BlockSpec(memory_space=...  22.7 us
    ppermute x29, waiting for transfers between devices, permute(): lax.ppermute(values, axis, [(i, target(i)) for i in range(lax.axis_size(a...  19.1 us
    all_to_all x1, blocking collectives, per_device(): parts = lax.all_to_all(parts, 'rows', 0, 0, tiled=True)  13.4 us
    all_to_all x1, starting transfers between devices, per_device(): sums = lax.all_to_all(sums, 'rows', 0, 0, tiled=True)  6.81 us
    all_to_all x1, waiting for transfers between devices, per_device(): sums = lax.all_to_all(sums, 'rows', 0, 0, tiled=True)  3.21 us
  transfers between devices with their start and end apart: 30, of which 9 were waited for; matrix products, arithmetic and copies ran while one was open for 2% of the time, Pallas kernels for 12%

profile of v12, /device:TPU:6, one launch (start us, length us, event | category | flops | bytes accessed | tf_op | source)
XLA Modules:
  0.0 113.8 jit_solution(1920698399945501625)
XLA Ops:
  0.7 2.2 %rows_first.1 = (bf16[8,64,1024]{2,1,0:T(8,128)(2,1)S(1)}, bf16[8,64,1024]{2,1,0:T(8,128)(2,1)S(1)}, bf16[128,1024]{1,0:T(8,128)(2,1)S(1)}, bf16[128,1024]{1,0:T(8,128)(2,1)S(1)}) custom-call(bf16[64,8,1024]{2,1,0:T(8,128)(2,1)} %phase.1, bf16[64,8,1024]{2,1,0:T(8,128)(2,1)} %coher.1), custom_call_target="tpu_custom_call" | custom-call | tf_op jit(solution)/shard_map/rows_first/pallas_call | solution.py:30
  2.8 2.0 %collective-permute-start = (bf16[128,1024]{1,0:T(8,128)(2,1)S(1)}, bf16[128,1024]{1,0:T(8,128)(2,1)S(1)}, u32[]{:S(2)}, u32[]{:S(2)}) collective-permute-start(bf16[128,1024]{1,0:T(8,128)(2,1)S(1)} %get-tuple-element.61), channel_id=1, source_target_pairs={{0,1},{1,2},{2,3},{3,4},{4,5},{5,6},{6,7},{7,8},{8,9},{9,10},{10,1... | collective-permute-start | bytes 786440 | tf_op jit(solution)/shard_map/ppermute | solution.py:439
  4.8 6.5 %collective-permute-start.1 = (bf16[128,1024]{1,0:T(8,128)(2,1)S(1)}, bf16[128,1024]{1,0:T(8,128)(2,1)S(1)}, u32[]{:S(2)}, u32[]{:S(2)}) collective-permute-start(bf16[128,1024]{1,0:T(8,128)(2,1)S(1)} %get-tuple-element.62), channel_id=1, source_target_pairs={{0,31},{1,0},{2,1},{3,2},{4,3},{5,4},{6,5},{7,6},{8,7},{9,8},{10,9... | collective-permute-start | bytes 786440 | tf_op jit(solution)/shard_map/ppermute | solution.py:439
  11.6 0.6 gather_fusion
  12.3 3.3 %inner_rows.1 = (f32[8,64,1024]{2,1,0:T(8,128)}, f32[128,128]{1,0:T(8,128)S(1)}, bf16[64,1024]{1,0:T(8,128)(2,1)}, bf16[64,1024]{1,0:T(8,128)(2,1)}, bf16[64,102...) custom-call(bf16[8,64,1024]{2,1,0:T(8,128)(2,1)S(1)} %get-tuple-elem, ...), custom_call_target="tpu_custom_call" | custom-call | tf_op jit(solution)/shard_map/inner_rows/pallas_call | solution.py:30
  15.6 1.9 %collective-permute-done.above = bf16[128,1024]{1,0:T(8,128)(2,1)S(1)} collective-permute-done((bf16[128,1024]{1,0:T(8,128)(2,1)S(1)}, bf16[128,1024]{1,0:T(8,128)(2,1)S(1)}, u32[]{:S(2)}, u32[]{:S(2)}) %collective-permute-start) | collective-permute-done | bytes 262176 | tf_op jit(solution)/shard_map/ppermute | solution.py:439
  17.5 2.5 %border_rows.1 = (f32[8,64,1024]{2,1,0:T(8,128)}, f32[32,1,128]{2,1,0:T(1,128)}, bf16[64,1024]{1,0:T(8,128)(2,1)}, bf16[64,1024]{1,0:T(8,128)(2,1)}, bf16[64,102...) custom-call(bf16[8,64,1024]{2,1,0:T(8,128)(2,1)S(1)} %get-tuple-elem, ...), custom_call_target="tpu_custom_call", output_to_operand_aliasing={{0}: (7, {}), {2}: (8, {}), {3}: (9, {}), {4}: (10, {}), {5... | custom-call | tf_op jit(solution)/shard_map/border_rows/pallas_call | solution.py:30
  20.2 1.5 %collective-permute-start.3 = (bf16[64,1024]{1,0:T(8,128)(2,1)}, bf16[64,1024]{1,0:T(8,128)(2,1)S(1)}, u32[]{:S(2)}, u32[]{:S(2)}) collective-permute-start(bf16[64,1024]{1,0:T(8,128)(2,1)} %get-tuple-element.78), channel_id=1, source_target_pairs={{0,128},{32,160},{64,192},{96,224},{128,0},{160,32},{192,64},{224,... | collective-permute-start | bytes 393224 | tf_op jit(solution)/shard_map/ppermute | solution.py:439
  21.7 2.1 %collective-permute-start.4 = (bf16[64,1024]{1,0:T(8,128)(2,1)}, bf16[64,1024]{1,0:T(8,128)(2,1)S(1)}, u32[]{:S(2)}, u32[]{:S(2)}) collective-permute-start(bf16[64,1024]{1,0:T(8,128)(2,1)} %get-tuple-element.79), channel_id=1, source_target_pairs={{0,64},{32,96},{64,128},{96,160},{128,192},{160,224},{192,0},{224,... | collective-permute-start | bytes 393224 | tf_op jit(solution)/shard_map/ppermute | solution.py:439
  23.8 6.8 %all-to-all-start = ((f32[32,1,128]{2,1,0:T(1,128)}), f32[32,1,128]{2,1,0:T(1,128)S(1)}, u32[]{:S(2)}, u32[]{:S(2)}) async-start(f32[32,1,128]{2,1,0:T(1,128)} %get-tuple-element.77), calls=%async_computation | async-start | bytes 32768 | tf_op jit(solution)/shard_map/all_to_all | solution.py:513
  30.6 1.0 subtract_convert_fusion
  31.5 1.6 %stage.1.smooth = f32[8,64,1024]{2,1,0:T(8,128)S(1)} custom-call(f32[8,64,1024]{2,1,0:T(8,128)} %get-tuple-element.88.source), custom_call_target="tpu_custom_call" | custom-call | tf_op jit(solution)/shard_map/stage/pallas_call | solution.py:30
  33.2 1.1 collective-permute-start.6
  34.2 1.4 %collective-permute-start.7 = (bf16[64,1024]{1,0:T(8,128)(2,1)S(1)}, bf16[64,1024]{1,0:T(8,128)(2,1)S(1)}, u32[]{:S(2)}, u32[]{:S(2)}) collective-permute-start(bf16[64,1024]{1,0:T(8,128)(2,1)S(1)} %copy-done.4), channel_id=1, source_target_pairs={{0,96},{32,64},{64,160},{96,128},{128,224},{160,192},{192,32},{224... | collective-permute-start | bytes 393224 | tf_op jit(solution)/shard_map/ppermute | solution.py:439
  35.6 1.5 %collective-permute-start.8 = (bf16[64,1024]{1,0:T(8,128)(2,1)}, bf16[64,1024]{1,0:T(8,128)(2,1)S(1)}, u32[]{:S(2)}, u32[]{:S(2)}) collective-permute-start(bf16[64,1024]{1,0:T(8,128)(2,1)} %get-tuple-element.86), channel_id=1, source_target_pairs={{0,224},{32,192},{64,32},{96,0},{128,96},{160,64},{192,160},{224,1... | collective-permute-start | bytes 393224 | tf_op jit(solution)/shard_map/ppermute | solution.py:439
  37.2 3.2 %all-to-all-done.sums = f32[32,1,128]{2,1,0:T(1,128)S(1)} async-done(((f32[32,1,128]{2,1,0:T(1,128)}), f32[32,1,128]{2,1,0:T(1,128)S(1)}, u32[]{:S(2)}, u32[]{:S(2)}) %all-to-all-start) | async-done | bytes 16416 | tf_op jit(solution)/shard_map/all_to_all | solution.py:513
  40.4 0.6 correction.1
  40.9 2.1 %collective-permute-start.10 = (bf16[64,1024]{1,0:T(8,128)(2,1)S(1)}, bf16[64,1024]{1,0:T(8,128)(2,1)S(1)}, u32[]{:S(2)}, u32[]{:S(2)}) collective-permute-start(bf16[64,1024]{1,0:T(8,128)(2,1)S(1)} %get-tuple-element.93), channel_id=1, source_target_pairs={{0,128},{32,160},{64,192},{96,224},{128,0},{160,32},{192,64},{224,... | collective-permute-start | bytes 393224 | tf_op jit(solution)/shard_map/ppermute | solution.py:439
  43.1 1.3 %collective-permute-start.11 = (bf16[64,1024]{1,0:T(8,128)(2,1)S(1)}, bf16[64,1024]{1,0:T(8,128)(2,1)S(1)}, u32[]{:S(2)}, u32[]{:S(2)}) collective-permute-start(bf16[64,1024]{1,0:T(8,128)(2,1)S(1)} %get-tuple-element.94), channel_id=1, source_target_pairs={{0,64},{32,96},{64,128},{96,160},{128,192},{160,224},{192,0},{224,... | collective-permute-start | bytes 393224 | tf_op jit(solution)/shard_map/ppermute | solution.py:439
  44.5 0.8 collective-permute-start.12
  45.4 4.4 %collective-permute-start.14 = (bf16[64,1024]{1,0:T(8,128)(2,1)S(1)}, bf16[64,1024]{1,0:T(8,128)(2,1)S(1)}, u32[]{:S(2)}, u32[]{:S(2)}) collective-permute-start(bf16[64,1024]{1,0:T(8,128)(2,1)S(1)} %get-tuple-element.97), channel_id=1, source_target_pairs={{0,96},{32,64},{64,160},{96,128},{128,224},{160,192},{192,32},{224... | collective-permute-start | bytes 393224 | tf_op jit(solution)/shard_map/ppermute | solution.py:439
  49.9 0.5 slice_bitcast_fusion
  50.4 3.2 %collective-permute-done.12.refs_12_ = bf16[64,1024]{1,0:T(8,128)(2,1)S(1)} collective-permute-done((bf16[64,1024]{1,0:T(8,128)(2,1)S(1)}, bf16[64,1024]{1,0:T(8,128)(2,1)S(1)}, u32[]{:S(2)}, u32[]{:S(2)}) %collective-permute-start.12) | collective-permute-done | bytes 131104 | tf_op jit(solution)/shard_map/ppermute | solution.py:439
  53.6 1.6 %collective-permute-done.14.refs_14_ = bf16[64,1024]{1,0:T(8,128)(2,1)S(1)} collective-permute-done((bf16[64,1024]{1,0:T(8,128)(2,1)S(1)}, bf16[64,1024]{1,0:T(8,128)(2,1)S(1)}, u32[]{:S(2)}, u32[]{:S(2)}) %collective-permute-start.14) | collective-permute-done | bytes 131104 | tf_op jit(solution)/shard_map/ppermute | solution.py:439
  55.2 1.2 %collective-permute-done.15.refs_15_ = bf16[64,1024]{1,0:T(8,128)(2,1)S(1)} collective-permute-done((bf16[64,1024]{1,0:T(8,128)(2,1)S(1)}, bf16[64,1024]{1,0:T(8,128)(2,1)S(1)}, u32[]{:S(2)}, u32[]{:S(2)}) %collective-permute-start.15) | collective-permute-done | bytes 131104 | tf_op jit(solution)/shard_map/ppermute | solution.py:439
  56.4 1.2 %right_side.1 = (f32[304,1024]{1,0:T(8,128)S(1)}, bf16[512,1024]{1,0:T(8,128)(2,1)S(1)}, bf16[304,128]{1,0:T(8,128)(2,1)S(1)}, bf16[16,304]{1,0:T(8,128)(2,1)S(1)}, bf16[304,128]{1,0:T(8,128)(2,1)S(1)}) custom-call(bf16[64,1024]{1,0:T(8,128)(2,1)S(1)} %copy-done, bf16[64,1024]{1,0:T(8,128)(2,1)S(1)} %collective-permute-done.2.refs_1_, ...), custom_call_target="tpu_custom_call" | custom-call | tf_op jit(solution)/shard_map/right_side/pallas_call | solution.py:30
  57.6 1.8 %collective-permute-start.19 = (bf16[16,304]{1,0:T(8,128)(2,1)S(1)}, bf16[16,304]{1,0:T(8,128)(2,1)S(1)}, u32[]{:S(2)}, u32[]{:S(2)}) collective-permute-start(bf16[16,304]{1,0:T(8,128)(2,1)S(1)} %get-tuple-element.104), channel_id=1, source_target_pairs={{0,224},{32,0},{64,32},{96,64},{128,96},{160,128},{192,160},{224,1... | collective-permute-start | bytes 29192 | tf_op jit(solution)/shard_map/ppermute | solution.py:439
  59.3 0.7 collective-permute-start.16
  60.0 4.6 %collective-permute-start.17 = (bf16[304,128]{1,0:T(8,128)(2,1)S(1)}, bf16[304,128]{1,0:T(8,128)(2,1)S(1)}, u32[]{:S(2)}, u32[]{:S(2)}) collective-permute-start(bf16[304,128]{1,0:T(8,128)(2,1)S(1)} %get-tuple-element.103), channel_id=1, source_target_pairs={{0,31},{1,0},{2,1},{3,2},{4,3},{5,4},{6,5},{7,6},{8,7},{9,8},{10,9... | collective-permute-start | bytes 233480 | tf_op jit(solution)/shard_map/ppermute | solution.py:439
  64.7 0.3 pad_maximum_fusion.refs_2_
  64.9 3.4 %apply0.1 = (f32[304,1024]{1,0:T(8,128)S(1)}, f32[3,8,128]{2,1,0:T(8,128)S(1)}) custom-call(f32[304,1024]{1,0:T(8,128)S(1)} %get-tuple-element.99.refs_0_.refs_4_.basis.zero, bf16[512,1024]{1,0:T(8,128)(2,1)S(1)} %get-tuple-element.100.refs_1_, bf16[512,608]{1,0:T(8,128)(2,1)S(1)} %pad_maximum_fusion.refs_2_, ...), custom_call_target="tpu_custom_call" | custom-call | tf_op jit(solution)/shard_map/apply0/pallas_call | solution.py:30
  68.3 0.7 add_halo1.1
  69.1 5.4 %collective-permute-start.21 = (bf16[304,128]{1,0:T(8,128)(2,1)S(1)}, bf16[304,128]{1,0:T(8,128)(2,1)S(1)}, u32[]{:S(2)}, u32[]{:S(2)}) collective-permute-start(bf16[304,128]{1,0:T(8,128)(2,1)S(1)} %get-tuple-element.108), channel_id=1, source_target_pairs={{0,31},{1,0},{2,1},{3,2},{4,3},{5,4},{6,5},{7,6},{8,7},{9,8},{10,9... | collective-permute-start | bytes 233480 | tf_op jit(solution)/shard_map/ppermute | solution.py:439
  74.4 1.7 %collective-permute-start.23 = (bf16[16,304]{1,0:T(8,128)(2,1)S(1)}, bf16[16,304]{1,0:T(8,128)(2,1)S(1)}, u32[]{:S(2)}, u32[]{:S(2)}) collective-permute-start(bf16[16,304]{1,0:T(8,128)(2,1)S(1)} %get-tuple-element.109), channel_id=1, source_target_pairs={{0,224},{32,0},{64,32},{96,64},{128,96},{160,128},{192,160},{224,1... | collective-permute-start | bytes 29192 | tf_op jit(solution)/shard_map/ppermute | solution.py:439
  76.2 3.4 %apply1.1 = (f32[304,1024]{1,0:T(8,128)S(1)}, f32[3,8,128]{2,1,0:T(8,128)S(1)}) custom-call(f32[304,1024]{1,0:T(8,128)S(1)} %get-tuple-element.105.refs_0_.refs_4_.one, bf16[512,1024]{1,0:T(8,128)(2,1)S(1)} %get-tuple-element.100.refs_1_, bf16[512,608]{1,0:T(8,128)(2,1)S(1)} %pad_maximum_fusion.refs_2_, ...), custom_call_target="tpu_custom_call" | custom-call | tf_op jit(solution)/shard_map/apply1/pallas_call | solution.py:30
  79.6 0.7 add_halo2.1
  80.3 0.2 collective-permute-start.24
  80.5 1.8 %collective-permute-start.25 = (bf16[16,304]{1,0:T(8,128)(2,1)S(1)}, bf16[16,304]{1,0:T(8,128)(2,1)S(1)}, u32[]{:S(2)}, u32[]{:S(2)}) collective-permute-start(bf16[16,304]{1,0:T(8,128)(2,1)S(1)} %get-tuple-element.112), channel_id=1, source_target_pairs={{0,32},{32,64},{64,96},{96,128},{128,160},{160,192},{192,224},{224... | collective-permute-start | bytes 29192 | tf_op jit(solution)/shard_map/ppermute | solution.py:439
  82.3 1.3 %apply2.1.two = f32[3,8,128]{2,1,0:T(8,128)S(1)} custom-call(f32[304,1024]{1,0:T(8,128)S(1)} %get-tuple-element.110.refs_0_.field.two, bf16[512,1024]{1,0:T(8,128)(2,1)S(1)} %get-tuple-element.100.refs_1_, bf16[512,608]{1,0:T(8,128)(2,1)S(1)} %pad_maximum_fusion.refs_2_, bf16[304,512]{1,0:T(8,128)(2,1)S(1)} %subtract_convert_fusion.1.refs_16_.refs_3_, ...), custom_call_target="tpu_custom_call" | custom-call | tf_op jit(solution)/shard_map/apply2/pallas_call | solution.py:30
  83.7 4.6 %collective-permute-done.24.above = bf16[304,128]{1,0:T(8,128)(2,1)S(1)} collective-permute-done((bf16[304,128]{1,0:T(8,128)(2,1)S(1)}, bf16[304,128]{1,0:T(8,128)(2,1)S(1)}, u32[]{:S(2)}, u32[]{:S(2)}) %collective-permute-start.24) | collective-permute-done | bytes 77856 | tf_op jit(solution)/shard_map/ppermute | solution.py:439
  88.2 0.6 all_moments.1
  88.8 0.7 collective-permute-start.26
  89.5 0.8 collective-permute-done.26
  90.3 3.5 %collective-permute-done.27 = f32[1,128]{1,0:T(1,128)S(1)} collective-permute-done((f32[1,128]{1,0:T(1,128)S(1)}, f32[1,128]{1,0:T(1,128)S(1)}, u32[]{:S(2)}, u32[]{:S(2)}) %collective-permute-start.27) | collective-permute-done | bytes 544 | tf_op jit(solution)/shard_map/ppermute | solution.py:439
  93.9 2.8 %collective-permute-start.28 = (f32[1,128]{1,0:T(1,128)S(1)}, f32[1,128]{1,0:T(1,128)S(1)}, u32[]{:S(2)}, u32[]{:S(2)}) collective-permute-start(f32[1,128]{1,0:T(1,128)S(1)} %add.70.one), channel_id=1, source_target_pairs={{0,128},{32,160},{64,192},{96,224},{128,0},{160,32},{192,64},{224,... | collective-permute-start | bytes 1544 | tf_op jit(solution)/shard_map/ppermute | solution.py:439
  96.7 2.2 %collective-permute-done.28.two = f32[1,128]{1,0:T(1,128)S(1)} collective-permute-done((f32[1,128]{1,0:T(1,128)S(1)}, f32[1,128]{1,0:T(1,128)S(1)}, u32[]{:S(2)}, u32[]{:S(2)}) %collective-permute-start.28) | collective-permute-done | bytes 544 | tf_op jit(solution)/shard_map/ppermute | solution.py:439
  98.9 13.4 %all_to_all.10.parts = f32[32,1,128]{2,1,0:T(1,128)S(1)} all-to-all(f32[32,1,128]{2,1,0:T(1,128)S(1)} %add_and_spread.1), channel_id=1, replica_groups=mesh['ifg'=8,'rows'=32] {'rows'}, dimensions={0} | all-to-all | bytes 32768 | tf_op jit(solution)/shard_map/all_to_all | solution.py:598
  112.3 1.3 %combine.1 = f32[2400,128]{1,0:T(8,128)} custom-call(f32[32,1,128]{2,1,0:T(1,128)S(1)} %all_to_all.10.parts, f32[304,1024]{1,0:T(8,128)S(1)} %get-tuple-element.99.refs_0_.refs_4_.basis.zero, f32[304,1024]{1,0:T(8,128)S(1)} %get-tuple-element.105.refs_0_.refs_4_.one, f32[304,1024]{1,0:T(8,128)S(1)} %get-tuple-element.110.refs_0_.field.two), custom_call_target="tpu_custom_call" | custom-call | tf_op jit(solution)/shard_map/combine/pallas_call | solution.py:30
  (58 shorter events, 0.9 us)
Async XLA Ops:
  0.6 10.7 %copy-start.5 = (s32[64,8]{0,1:T(8,128)S(1)}, s32[64,8]{0,1:T(8,128)}, u32[]{:S(2)}) copy-start(s32[64,8]{0,1:T(8,128)} %param.8) | copy-start | bytes 6148
  0.6 10.8 %copy-start.6 = (s32[512,2]{0,1:T(2,128)S(1)}, s32[512,2]{0,1:T(2,128)}, u32[]{:S(2)}) copy-start(s32[512,2]{0,1:T(2,128)} %param.9) | copy-start | bytes 12292
  0.7 11.6 %copy-start.1 = (f32[8,1024]{1,0:T(8,128)S(1)}, f32[8,1024]{1,0:T(8,128)}, u32[]{:S(2)}) copy-start(f32[8,1024]{1,0:T(8,128)} %height.5) | copy-start | bytes 98308
  2.8 14.7 %collective-permute-start = (bf16[128,1024]{1,0:T(8,128)(2,1)S(1)}, bf16[128,1024]{1,0:T(8,128)(2,1)S(1)}, u32[]{:S(2)}, u32[]{:S(2)}) collective-permute-start(bf16[128,1024]{1,0:T(8,128)(2,1)S(1)} %get-tuple-element.61), channel_id=1, source_target_pairs={{0,1},{1,2},{2,3},{3,4},{4,5},{5,6},{6,7},{7,8},{8,9},{9,10},{10,1... | collective-permute-start | bytes 786440 | tf_op jit(solution)/shard_map/ppermute | solution.py:439
  4.8 12.7 %collective-permute-start.1 = (bf16[128,1024]{1,0:T(8,128)(2,1)S(1)}, bf16[128,1024]{1,0:T(8,128)(2,1)S(1)}, u32[]{:S(2)}, u32[]{:S(2)}) collective-permute-start(bf16[128,1024]{1,0:T(8,128)(2,1)S(1)} %get-tuple-element.62), channel_id=1, source_target_pairs={{0,31},{1,0},{2,1},{3,2},{4,3},{5,4},{6,5},{7,6},{8,7},{9,8},{10,9... | collective-permute-start | bytes 786440 | tf_op jit(solution)/shard_map/ppermute | solution.py:439
  20.1 3.7 %collective-permute-start.2 = (bf16[64,1024]{1,0:T(8,128)(2,1)}, bf16[64,1024]{1,0:T(8,128)(2,1)S(1)}, u32[]{:S(2)}, u32[]{:S(2)}) collective-permute-start(bf16[64,1024]{1,0:T(8,128)(2,1)} %get-tuple-element.75), channel_id=1, source_target_pairs={{0,32},{32,0},{64,96},{96,64},{128,160},{160,128},{192,224},{224,1... | collective-permute-start | bytes 393224 | tf_op jit(solution)/shard_map/ppermute | solution.py:439
  20.2 15.5 %collective-permute-start.3 = (bf16[64,1024]{1,0:T(8,128)(2,1)}, bf16[64,1024]{1,0:T(8,128)(2,1)S(1)}, u32[]{:S(2)}, u32[]{:S(2)}) collective-permute-start(bf16[64,1024]{1,0:T(8,128)(2,1)} %get-tuple-element.78), channel_id=1, source_target_pairs={{0,128},{32,160},{64,192},{96,224},{128,0},{160,32},{192,64},{224,... | collective-permute-start | bytes 393224 | tf_op jit(solution)/shard_map/ppermute | solution.py:439
  21.7 15.5 %collective-permute-start.4 = (bf16[64,1024]{1,0:T(8,128)(2,1)}, bf16[64,1024]{1,0:T(8,128)(2,1)S(1)}, u32[]{:S(2)}, u32[]{:S(2)}) collective-permute-start(bf16[64,1024]{1,0:T(8,128)(2,1)} %get-tuple-element.79), channel_id=1, source_target_pairs={{0,64},{32,96},{64,128},{96,160},{128,192},{160,224},{192,0},{224,... | collective-permute-start | bytes 393224 | tf_op jit(solution)/shard_map/ppermute | solution.py:439
  23.8 13.4 %collective-permute-start.5 = (bf16[64,1024]{1,0:T(8,128)(2,1)}, bf16[64,1024]{1,0:T(8,128)(2,1)S(1)}, u32[]{:S(2)}, u32[]{:S(2)}) collective-permute-start(bf16[64,1024]{1,0:T(8,128)(2,1)} %get-tuple-element.80), channel_id=1, source_target_pairs={{0,192},{32,224},{64,0},{96,32},{128,64},{160,96},{192,128},{224,1... | collective-permute-start | bytes 393224 | tf_op jit(solution)/shard_map/ppermute | solution.py:439
  23.8 16.6 %all-to-all-start = ((f32[32,1,128]{2,1,0:T(1,128)}), f32[32,1,128]{2,1,0:T(1,128)S(1)}, u32[]{:S(2)}, u32[]{:S(2)}) async-start(f32[32,1,128]{2,1,0:T(1,128)} %get-tuple-element.77), calls=%async_computation | async-start | bytes 32768 | tf_op jit(solution)/shard_map/all_to_all | solution.py:513
  31.5 1.6 %copy-start.3 = (bf16[64,1024]{1,0:T(8,128)(2,1)S(1)}, bf16[64,1024]{1,0:T(8,128)(2,1)}, u32[]{:S(2)}) copy-start(bf16[64,1024]{1,0:T(8,128)(2,1)} %get-tuple-element.84) | copy-start | bytes 393220
  31.5 2.7 %copy-start.4 = (bf16[64,1024]{1,0:T(8,128)(2,1)S(1)}, bf16[64,1024]{1,0:T(8,128)(2,1)}, u32[]{:S(2)}) copy-start(bf16[64,1024]{1,0:T(8,128)(2,1)} %get-tuple-element.85) | copy-start | bytes 393220
  33.1 23.3 %copy-start = (bf16[64,1024]{1,0:T(8,128)(2,1)S(1)}, bf16[64,1024]{1,0:T(8,128)(2,1)}, u32[]{:S(2)}) copy-start(bf16[64,1024]{1,0:T(8,128)(2,1)} %get-tuple-element.73.refs_0_) | copy-start | bytes 393220
  33.2 11.3 %collective-permute-start.6 = (bf16[64,1024]{1,0:T(8,128)(2,1)S(1)}, bf16[64,1024]{1,0:T(8,128)(2,1)S(1)}, u32[]{:S(2)}, u32[]{:S(2)}) collective-permute-start(bf16[64,1024]{1,0:T(8,128)(2,1)S(1)} %copy-done.3), channel_id=1, source_target_pairs={{0,160},{32,128},{64,224},{96,192},{128,32},{160,0},{192,96},{224,... | collective-permute-start | bytes 393224 | tf_op jit(solution)/shard_map/ppermute | solution.py:439
  34.2 11.1 %collective-permute-start.7 = (bf16[64,1024]{1,0:T(8,128)(2,1)S(1)}, bf16[64,1024]{1,0:T(8,128)(2,1)S(1)}, u32[]{:S(2)}, u32[]{:S(2)}) collective-permute-start(bf16[64,1024]{1,0:T(8,128)(2,1)S(1)} %copy-done.4), channel_id=1, source_target_pairs={{0,96},{32,64},{64,160},{96,128},{128,224},{160,192},{192,32},{224... | collective-permute-start | bytes 393224 | tf_op jit(solution)/shard_map/ppermute | solution.py:439
  35.6 9.7 %collective-permute-start.8 = (bf16[64,1024]{1,0:T(8,128)(2,1)}, bf16[64,1024]{1,0:T(8,128)(2,1)S(1)}, u32[]{:S(2)}, u32[]{:S(2)}) collective-permute-start(bf16[64,1024]{1,0:T(8,128)(2,1)} %get-tuple-element.86), channel_id=1, source_target_pairs={{0,224},{32,192},{64,32},{96,0},{128,96},{160,64},{192,160},{224,1... | collective-permute-start | bytes 393224 | tf_op jit(solution)/shard_map/ppermute | solution.py:439
  40.9 8.9 %collective-permute-start.10 = (bf16[64,1024]{1,0:T(8,128)(2,1)S(1)}, bf16[64,1024]{1,0:T(8,128)(2,1)S(1)}, u32[]{:S(2)}, u32[]{:S(2)}) collective-permute-start(bf16[64,1024]{1,0:T(8,128)(2,1)S(1)} %get-tuple-element.93), channel_id=1, source_target_pairs={{0,128},{32,160},{64,192},{96,224},{128,0},{160,32},{192,64},{224,... | collective-permute-start | bytes 393224 | tf_op jit(solution)/shard_map/ppermute | solution.py:439
  43.1 21.6 %copy-start.2 = (bf16[512,304]{1,0:T(8,128)(2,1)S(1)}, bf16[512,304]{1,0:T(8,128)(2,1)}, u32[]{:S(2)}) copy-start(bf16[512,304]{1,0:T(8,128)(2,1)} %subtract_convert_fusion) | copy-start | bytes 933892
  43.1 6.7 %collective-permute-start.11 = (bf16[64,1024]{1,0:T(8,128)(2,1)S(1)}, bf16[64,1024]{1,0:T(8,128)(2,1)S(1)}, u32[]{:S(2)}, u32[]{:S(2)}) collective-permute-start(bf16[64,1024]{1,0:T(8,128)(2,1)S(1)} %get-tuple-element.94), channel_id=1, source_target_pairs={{0,64},{32,96},{64,128},{96,160},{128,192},{160,224},{192,0},{224,... | collective-permute-start | bytes 393224 | tf_op jit(solution)/shard_map/ppermute | solution.py:439
  44.5 9.1 %collective-permute-start.12 = (bf16[64,1024]{1,0:T(8,128)(2,1)S(1)}, bf16[64,1024]{1,0:T(8,128)(2,1)S(1)}, u32[]{:S(2)}, u32[]{:S(2)}) collective-permute-start(bf16[64,1024]{1,0:T(8,128)(2,1)S(1)} %get-tuple-element.95), channel_id=1, source_target_pairs={{0,192},{32,224},{64,0},{96,32},{128,64},{160,96},{192,128},{224,1... | collective-permute-start | bytes 393224 | tf_op jit(solution)/shard_map/ppermute | solution.py:439
  45.4 8.2 %collective-permute-start.13 = (bf16[64,1024]{1,0:T(8,128)(2,1)S(1)}, bf16[64,1024]{1,0:T(8,128)(2,1)S(1)}, u32[]{:S(2)}, u32[]{:S(2)}) collective-permute-start(bf16[64,1024]{1,0:T(8,128)(2,1)S(1)} %get-tuple-element.96), channel_id=1, source_target_pairs={{0,160},{32,128},{64,224},{96,192},{128,32},{160,0},{192,96},{224,... | collective-permute-start | bytes 393224 | tf_op jit(solution)/shard_map/ppermute | solution.py:439
  45.4 9.8 %collective-permute-start.14 = (bf16[64,1024]{1,0:T(8,128)(2,1)S(1)}, bf16[64,1024]{1,0:T(8,128)(2,1)S(1)}, u32[]{:S(2)}, u32[]{:S(2)}) collective-permute-start(bf16[64,1024]{1,0:T(8,128)(2,1)S(1)} %get-tuple-element.97), channel_id=1, source_target_pairs={{0,96},{32,64},{64,160},{96,128},{128,224},{160,192},{192,32},{224... | collective-permute-start | bytes 393224 | tf_op jit(solution)/shard_map/ppermute | solution.py:439
  49.8 6.6 %collective-permute-start.15 = (bf16[64,1024]{1,0:T(8,128)(2,1)S(1)}, bf16[64,1024]{1,0:T(8,128)(2,1)S(1)}, u32[]{:S(2)}, u32[]{:S(2)}) collective-permute-start(bf16[64,1024]{1,0:T(8,128)(2,1)S(1)} %get-tuple-element.98), channel_id=1, source_target_pairs={{0,224},{32,192},{64,32},{96,0},{128,96},{160,64},{192,160},{224,1... | collective-permute-start | bytes 393224 | tf_op jit(solution)/shard_map/ppermute | solution.py:439
  49.8 6.6 %collective-permute-start.9 = (bf16[64,1024]{1,0:T(8,128)(2,1)S(1)}, bf16[64,1024]{1,0:T(8,128)(2,1)S(1)}, u32[]{:S(2)}, u32[]{:S(2)}) collective-permute-start(bf16[64,1024]{1,0:T(8,128)(2,1)S(1)} %get-tuple-element.92), channel_id=1, source_target_pairs={{0,32},{32,0},{64,96},{96,64},{128,160},{160,128},{192,224},{224,1... | collective-permute-start | bytes 393224 | tf_op jit(solution)/shard_map/ppermute | solution.py:439
  57.6 10.7 %collective-permute-start.18 = (bf16[16,304]{1,0:T(8,128)(2,1)S(1)}, bf16[16,304]{1,0:T(8,128)(2,1)S(1)}, u32[]{:S(2)}, u32[]{:S(2)}) collective-permute-start(bf16[16,304]{1,0:T(8,128)(2,1)S(1)} %get-tuple-element.104), channel_id=1, source_target_pairs={{0,32},{32,64},{64,96},{96,128},{128,160},{160,192},{192,224},{224... | collective-permute-start | bytes 29192 | tf_op jit(solution)/shard_map/ppermute | solution.py:439
  57.6 10.7 %collective-permute-start.19 = (bf16[16,304]{1,0:T(8,128)(2,1)S(1)}, bf16[16,304]{1,0:T(8,128)(2,1)S(1)}, u32[]{:S(2)}, u32[]{:S(2)}) collective-permute-start(bf16[16,304]{1,0:T(8,128)(2,1)S(1)} %get-tuple-element.104), channel_id=1, source_target_pairs={{0,224},{32,0},{64,32},{96,64},{128,96},{160,128},{192,160},{224,1... | collective-permute-start | bytes 29192 | tf_op jit(solution)/shard_map/ppermute | solution.py:439
  59.3 9.0 %collective-permute-start.16 = (bf16[304,128]{1,0:T(8,128)(2,1)S(1)}, bf16[304,128]{1,0:T(8,128)(2,1)S(1)}, u32[]{:S(2)}, u32[]{:S(2)}) collective-permute-start(bf16[304,128]{1,0:T(8,128)(2,1)S(1)} %get-tuple-element.102), channel_id=1, source_target_pairs={{0,1},{1,2},{2,3},{3,4},{4,5},{5,6},{6,7},{7,8},{8,9},{9,10},{10,1... | collective-permute-start | bytes 233480 | tf_op jit(solution)/shard_map/ppermute | solution.py:439
  60.0 8.3 %collective-permute-start.17 = (bf16[304,128]{1,0:T(8,128)(2,1)S(1)}, bf16[304,128]{1,0:T(8,128)(2,1)S(1)}, u32[]{:S(2)}, u32[]{:S(2)}) collective-permute-start(bf16[304,128]{1,0:T(8,128)(2,1)S(1)} %get-tuple-element.103), channel_id=1, source_target_pairs={{0,31},{1,0},{2,1},{3,2},{4,3},{5,4},{6,5},{7,6},{8,7},{9,8},{10,9... | collective-permute-start | bytes 233480 | tf_op jit(solution)/shard_map/ppermute | solution.py:439
  69.1 10.5 %collective-permute-start.20 = (bf16[304,128]{1,0:T(8,128)(2,1)S(1)}, bf16[304,128]{1,0:T(8,128)(2,1)S(1)}, u32[]{:S(2)}, u32[]{:S(2)}) collective-permute-start(bf16[304,128]{1,0:T(8,128)(2,1)S(1)} %get-tuple-element.107), channel_id=1, source_target_pairs={{0,1},{1,2},{2,3},{3,4},{4,5},{5,6},{6,7},{7,8},{8,9},{9,10},{10,1... | collective-permute-start | bytes 233480 | tf_op jit(solution)/shard_map/ppermute | solution.py:439
  69.1 10.5 %collective-permute-start.21 = (bf16[304,128]{1,0:T(8,128)(2,1)S(1)}, bf16[304,128]{1,0:T(8,128)(2,1)S(1)}, u32[]{:S(2)}, u32[]{:S(2)}) collective-permute-start(bf16[304,128]{1,0:T(8,128)(2,1)S(1)} %get-tuple-element.108), channel_id=1, source_target_pairs={{0,31},{1,0},{2,1},{3,2},{4,3},{5,4},{6,5},{7,6},{8,7},{9,8},{10,9... | collective-permute-start | bytes 233480 | tf_op jit(solution)/shard_map/ppermute | solution.py:439
  74.4 5.1 %collective-permute-start.22 = (bf16[16,304]{1,0:T(8,128)(2,1)S(1)}, bf16[16,304]{1,0:T(8,128)(2,1)S(1)}, u32[]{:S(2)}, u32[]{:S(2)}) collective-permute-start(bf16[16,304]{1,0:T(8,128)(2,1)S(1)} %get-tuple-element.109), channel_id=1, source_target_pairs={{0,32},{32,64},{64,96},{96,128},{128,160},{160,192},{192,224},{224... | collective-permute-start | bytes 29192 | tf_op jit(solution)/shard_map/ppermute | solution.py:439
  74.4 5.1 %collective-permute-start.23 = (bf16[16,304]{1,0:T(8,128)(2,1)S(1)}, bf16[16,304]{1,0:T(8,128)(2,1)S(1)}, u32[]{:S(2)}, u32[]{:S(2)}) collective-permute-start(bf16[16,304]{1,0:T(8,128)(2,1)S(1)} %get-tuple-element.109), channel_id=1, source_target_pairs={{0,224},{32,0},{64,32},{96,64},{128,96},{160,128},{192,160},{224,1... | collective-permute-start | bytes 29192 | tf_op jit(solution)/shard_map/ppermute | solution.py:439
  80.3 7.9 %collective-permute-start.24 = (bf16[304,128]{1,0:T(8,128)(2,1)S(1)}, bf16[304,128]{1,0:T(8,128)(2,1)S(1)}, u32[]{:S(2)}, u32[]{:S(2)}) collective-permute-start(bf16[304,128]{1,0:T(8,128)(2,1)S(1)} %get-tuple-element.111), channel_id=1, source_target_pairs={{0,1},{1,2},{2,3},{3,4},{4,5},{5,6},{6,7},{7,8},{8,9},{9,10},{10,1... | collective-permute-start | bytes 233480 | tf_op jit(solution)/shard_map/ppermute | solution.py:439
  80.5 3.1 %collective-permute-start.25 = (bf16[16,304]{1,0:T(8,128)(2,1)S(1)}, bf16[16,304]{1,0:T(8,128)(2,1)S(1)}, u32[]{:S(2)}, u32[]{:S(2)}) collective-permute-start(bf16[16,304]{1,0:T(8,128)(2,1)S(1)} %get-tuple-element.112), channel_id=1, source_target_pairs={{0,32},{32,64},{64,96},{96,128},{128,160},{160,192},{192,224},{224... | collective-permute-start | bytes 29192 | tf_op jit(solution)/shard_map/ppermute | solution.py:439
  88.8 1.5 %collective-permute-start.26 = (f32[1,128]{1,0:T(1,128)S(1)}, f32[1,128]{1,0:T(1,128)S(1)}, u32[]{:S(2)}, u32[]{:S(2)}) collective-permute-start(f32[1,128]{1,0:T(1,128)S(1)} %all_moments.1), channel_id=1, source_target_pairs={{0,32},{32,0},{64,96},{96,64},{128,160},{160,128},{192,224},{224,1... | collective-permute-start | bytes 1544 | tf_op jit(solution)/shard_map/ppermute | solution.py:439
  90.3 3.5 %collective-permute-start.27 = (f32[1,128]{1,0:T(1,128)S(1)}, f32[1,128]{1,0:T(1,128)S(1)}, u32[]{:S(2)}, u32[]{:S(2)}) collective-permute-start(f32[1,128]{1,0:T(1,128)S(1)} %add.69), channel_id=1, source_target_pairs={{0,64},{32,96},{64,0},{96,32},{128,192},{160,224},{192,128},{224,1... | collective-permute-start | bytes 1544 | tf_op jit(solution)/shard_map/ppermute | solution.py:439
  93.9 5.0 %collective-permute-start.28 = (f32[1,128]{1,0:T(1,128)S(1)}, f32[1,128]{1,0:T(1,128)S(1)}, u32[]{:S(2)}, u32[]{:S(2)}) collective-permute-start(f32[1,128]{1,0:T(1,128)S(1)} %add.70.one), channel_id=1, source_target_pairs={{0,128},{32,160},{64,192},{96,224},{128,0},{160,32},{192,64},{224,... | collective-permute-start | bytes 1544 | tf_op jit(solution)/shard_map/ppermute | solution.py:439
